TPU v7x, 32 devices: a whole 2x2x4 slice. The times are simulated.
32 devices in a mesh: dp: 8 (over y, x, core), ctx: 4 (over z).
Axes of the slice: x: 2, y: 2, z: 4, core: 2. Of those that a mesh axis runs over, the one named last changes fastest.
Arguments:
- tokens: bfloat16 [8, 2048, 1024], P('dp', 'ctx'), may hold values from -6 to 6
- lengths: int32 [8], P('dp'), may hold values from 1 to 2048, 12288 in all
- cotangent: bfloat16 [8, 2048, 1024], P('dp', 'ctx'), may hold values from -6 to 6
- query_weight: bfloat16 [1024, 1024], P(('dp', 'ctx')), may hold values from -0.1875 to 0.1875
- key_weight: bfloat16 [1024, 1024], P(('dp', 'ctx')), may hold values from -0.1875 to 0.1875
- value_weight: bfloat16 [1024, 1024], P(('dp', 'ctx')), may hold values from -0.1875 to 0.1875
- output_weight: bfloat16 [1024, 1024], P(('dp', 'ctx')), may hold values from -4 to 4
- gate_weight: bfloat16 [1024, 4096], P(('dp', 'ctx')), may hold values from -0.1875 to 0.1875
- up_weight: bfloat16 [1024, 4096], P(('dp', 'ctx')), may hold values from -0.1875 to 0.1875
- down_weight: bfloat16 [4096, 1024], P(('dp', 'ctx')), may hold values from -0.09375 to 0.09375
- attention_gain: bfloat16 [1024], P(('dp', 'ctx')), may hold values from 0.099609375 to 1.8984375
- attention_shift: bfloat16 [1024], P(('dp', 'ctx')), may hold values from -1.5 to 1.5
- feed_gain: bfloat16 [1024], P(('dp', 'ctx')), may hold values from 0.099609375 to 1.8984375
- feed_shift: bfloat16 [1024], P(('dp', 'ctx')), may hold values from -1.5 to 1.5
Outputs:
- output: bfloat16 [8, 2048, 1024], P('dp', 'ctx')
- tokens_grad: bfloat16 [8, 2048, 1024], P('dp', 'ctx')
- query_grad: float32 [1024, 1024], P(('dp', 'ctx'))
- key_grad: float32 [1024, 1024], P(('dp', 'ctx'))
- value_grad: float32 [1024, 1024], P(('dp', 'ctx'))
- output_grad: float32 [1024, 1024], P(('dp', 'ctx'))
- gate_grad: float32 [1024, 4096], P(('dp', 'ctx'))
- up_grad: float32 [1024, 4096], P(('dp', 'ctx'))
- down_grad: float32 [4096, 1024], P(('dp', 'ctx'))
- attention_gain_grad: float32 [1024], P(('dp', 'ctx'))
- attention_shift_grad: float32 [1024], P(('dp', 'ctx'))
- feed_gain_grad: float32 [1024], P(('dp', 'ctx'))
- feed_shift_grad: float32 [1024], P(('dp', 'ctx'))
Inputs may be any that keep to these rules, and one draw needn't show every extreme that they name: `lengths`: positions below a window's length are real, the rest padding; some window has length 2048.
All inputs are finite; a program needn't handle non-finite values. No bound on the sum of `lengths` on one device may be relied on, other than what follows from the above.
Results may differ from a plain program's by a relative error of at most 0.023.
Values may be sent and summed in bfloat16 or wider, within the bound.
No kernel may reach another device: no remote copies, remote signals or barrier semaphores. Data moves between devices by JAX's collectives and lax.ppermute only.
A program may use at most 192 MiB of HBM per device.

v0:
```python
import math

import jax
import jax.numpy as jnp
from jax import lax
from jax.sharding import PartitionSpec as P

H = 16
HD = 64
L = 2048


epsilon = 1e-05
masked_score = -1e30


def layer_norm(values, gain, shift):
    centre = values - jnp.mean(values, axis=-1, keepdims=True)
    spread = jnp.mean(centre * centre, axis=-1, keepdims=True)
    return centre * lax.rsqrt(spread + epsilon) * gain + shift


def rotary_tables(positions):
    half = HD // 2
    freqs = jnp.exp(jnp.arange(half, dtype=jnp.float32) * (-2.0 * math.log(10000.0) / HD))
    angles = positions.astype(jnp.float32)[:, None] * freqs[None, :]
    cosine = jnp.concatenate([jnp.cos(angles), jnp.cos(angles)], axis=-1)
    sine = jnp.concatenate([jnp.sin(angles), jnp.sin(angles)], axis=-1)
    return (cosine, sine)


def rotate(values, cosine, sine):
    half = HD // 2
    turned = jnp.concatenate([-values[..., half:], values[..., :half]], axis=-1)
    return values * cosine[:, None, :] + turned * sine[:, None, :]


def shards(
    tokens,
    lengths,
    cotangent,
    query_weight,
    key_weight,
    value_weight,
    output_weight,
    gate_weight,
    up_weight,
    down_weight,
    attention_gain,
    attention_shift,
    feed_gain,
    feed_shift,
):
    weights = (
        lax.all_gather(query_weight, ("dp", "ctx"), axis=0, tiled=True),
        lax.all_gather(key_weight, ("dp", "ctx"), axis=0, tiled=True),
        lax.all_gather(value_weight, ("dp", "ctx"), axis=0, tiled=True),
        lax.all_gather(output_weight, ("dp", "ctx"), axis=0, tiled=True),
        lax.all_gather(gate_weight, ("dp", "ctx"), axis=0, tiled=True),
        lax.all_gather(up_weight, ("dp", "ctx"), axis=0, tiled=True),
        lax.all_gather(down_weight, ("dp", "ctx"), axis=0, tiled=True),
        lax.all_gather(attention_gain, ("dp", "ctx"), axis=0, tiled=True),
        lax.all_gather(attention_shift, ("dp", "ctx"), axis=0, tiled=True),
        lax.all_gather(feed_gain, ("dp", "ctx"), axis=0, tiled=True),
        lax.all_gather(feed_shift, ("dp", "ctx"), axis=0, tiled=True),
    )
    windows, local_len, width = tokens.shape
    total_rows = windows * local_len
    scale = 1.0 / math.sqrt(HD)
    local_pos = lax.axis_index("ctx") * local_len + jnp.arange(local_len, dtype=jnp.int32)
    row_valid = (local_pos[None, :] < lengths[:, None]).astype(jnp.float32)
    cosine, sine = rotary_tables(local_pos)
    inputs = tokens.astype(jnp.float32).reshape(total_rows, width)
    gain_one = weights[7].astype(jnp.float32)
    shift_one = weights[8].astype(jnp.float32)
    gain_two = weights[9].astype(jnp.float32)
    shift_two = weights[10].astype(jnp.float32)
    normed_one = layer_norm(inputs, gain_one, shift_one)
    normed_low = normed_one.astype(jnp.bfloat16)
    query_raw = jnp.dot(normed_low, weights[0], preferred_element_type=jnp.float32)
    key_raw = jnp.dot(normed_low, weights[1], preferred_element_type=jnp.float32)
    value_flat = (
        jnp.dot(normed_low, weights[2], preferred_element_type=jnp.float32)
        .astype(jnp.bfloat16)
        .reshape(windows, local_len, width)
    )
    queries = rotate(query_raw.reshape(windows, local_len, H, HD), cosine, sine).astype(
        jnp.bfloat16
    )
    keys_flat = (
        rotate(key_raw.reshape(windows, local_len, H, HD), cosine, sine)
        .astype(jnp.bfloat16)
        .reshape(windows, local_len, width)
    )
    start_state = (
        jnp.full((windows, H, local_len), masked_score, jnp.float32),
        jnp.zeros((windows, H, local_len), jnp.float32),
        jnp.zeros((windows, local_len, H, HD), jnp.float32),
    )
    key_piece = lax.all_gather(keys_flat, "ctx", axis=1, tiled=True)
    value_piece = lax.all_gather(value_flat, "ctx", axis=1, tiled=True)
    piece_len = key_piece.shape[1]
    attend_block = math.gcd(piece_len, 256)

    def one_block(inner, index):
        maxima, totals, accum = inner
        offset = index * attend_block
        key_block = lax.dynamic_slice_in_dim(key_piece, offset, attend_block, 1).reshape(
            windows, attend_block, H, HD
        )
        value_block = lax.dynamic_slice_in_dim(value_piece, offset, attend_block, 1).reshape(
            windows, attend_block, H, HD
        )
        key_pos = offset + jnp.arange(attend_block, dtype=jnp.int32)
        allowed = (key_pos[None, :] < lengths[:, None])[:, None, None, :]
        scores = (
            jnp.einsum("wqhd,wkhd->whqk", queries, key_block, preferred_element_type=jnp.float32)
            * scale
        )
        scores = jnp.where(allowed, scores, masked_score)
        new_max = jnp.maximum(maxima, jnp.max(scores, axis=-1))
        expo = jnp.where(allowed, jnp.exp(scores - new_max[..., None]), 0.0)
        factor = jnp.exp(maxima - new_max)
        totals = totals * factor + jnp.sum(expo, axis=-1)
        update = jnp.einsum(
            "whqk,wkhd->wqhd",
            expo.astype(jnp.bfloat16),
            value_block,
            preferred_element_type=jnp.float32,
        )
        accum = accum * jnp.transpose(factor, (0, 2, 1))[..., None] + update
        return ((new_max, totals, accum), None)

    result, unused = lax.scan(one_block, start_state, jnp.arange(piece_len // attend_block))
    maxima, totals, accum = result
    log_total = maxima + jnp.log(totals)
    attended = accum / jnp.transpose(totals, (0, 2, 1))[..., None]
    attn_low = attended.reshape(total_rows, width).astype(jnp.bfloat16)
    resid = inputs + jnp.dot(attn_low, weights[3], preferred_element_type=jnp.float32)
    normed_two = layer_norm(resid, gain_two, shift_two)
    two_low = normed_two.astype(jnp.bfloat16)
    gate_pre = jnp.dot(two_low, weights[4], preferred_element_type=jnp.float32)
    up_pre = jnp.dot(two_low, weights[5], preferred_element_type=jnp.float32)
    sigma = jax.nn.sigmoid(gate_pre)
    activ = gate_pre * sigma
    hidden = (activ * up_pre).astype(jnp.bfloat16)
    result_rows = resid + jnp.dot(hidden, weights[6], preferred_element_type=jnp.float32)
    output = result_rows.astype(jnp.bfloat16).reshape(windows, local_len, width)
    back_weights = (
        lax.all_gather(query_weight, ("dp", "ctx"), axis=0, tiled=True),
        lax.all_gather(key_weight, ("dp", "ctx"), axis=0, tiled=True),
        lax.all_gather(value_weight, ("dp", "ctx"), axis=0, tiled=True),
        lax.all_gather(output_weight, ("dp", "ctx"), axis=0, tiled=True),
        lax.all_gather(gate_weight, ("dp", "ctx"), axis=0, tiled=True),
        lax.all_gather(up_weight, ("dp", "ctx"), axis=0, tiled=True),
        lax.all_gather(down_weight, ("dp", "ctx"), axis=0, tiled=True),
        lax.all_gather(attention_gain, ("dp", "ctx"), axis=0, tiled=True),
        lax.all_gather(attention_shift, ("dp", "ctx"), axis=0, tiled=True),
        lax.all_gather(feed_gain, ("dp", "ctx"), axis=0, tiled=True),
        lax.all_gather(feed_shift, ("dp", "ctx"), axis=0, tiled=True),
    )
    upstream = cotangent.astype(jnp.float32).reshape(total_rows, width) * row_valid.reshape(
        total_rows, 1
    )
    upstream_low = upstream.astype(jnp.bfloat16)
    grad_down = jnp.dot(hidden.T, upstream_low, preferred_element_type=jnp.float32)
    grad_hidden = jnp.dot(upstream_low, back_weights[6].T, preferred_element_type=jnp.float32)
    grad_gate = (grad_hidden * up_pre * sigma * (1.0 + gate_pre * (1.0 - sigma))).astype(
        jnp.bfloat16
    )
    grad_up = (grad_hidden * activ).astype(jnp.bfloat16)
    grad_gate_w = jnp.dot(two_low.T, grad_gate, preferred_element_type=jnp.float32)
    grad_up_w = jnp.dot(two_low.T, grad_up, preferred_element_type=jnp.float32)
    grad_normed_two = jnp.dot(
        grad_gate, back_weights[4].T, preferred_element_type=jnp.float32
    ) + jnp.dot(grad_up, back_weights[5].T, preferred_element_type=jnp.float32)
    unused_two, pull_two = jax.vjp(layer_norm, resid, gain_two, shift_two)
    grad_resid_norm, grad_gain_two, grad_shift_two = pull_two(grad_normed_two)
    grad_resid = upstream + grad_resid_norm
    branch_low = grad_resid.astype(jnp.bfloat16)
    grad_out_w = jnp.dot(attn_low.T, branch_low, preferred_element_type=jnp.float32)
    grad_attn = (
        jnp.dot(branch_low, back_weights[3].T, preferred_element_type=jnp.float32)
        .astype(jnp.bfloat16)
        .reshape(windows, local_len, H, HD)
    )
    delta = jnp.transpose(jnp.sum(grad_attn.astype(jnp.float32) * attended, axis=-1), (0, 2, 1))
    key_all, value_all = (
        lax.all_gather(keys_flat, "ctx", axis=1, tiled=True),
        lax.all_gather(value_flat, "ctx", axis=1, tiled=True),
    )
    block = min(256, L)

    def back_block(carry, index):
        grad_query, kv_grads = carry
        offset = index * block
        key_block = lax.dynamic_slice_in_dim(key_all, offset, block, 1).reshape(
            windows, block, H, HD
        )
        value_block = lax.dynamic_slice_in_dim(value_all, offset, block, 1).reshape(
            windows, block, H, HD
        )
        key_pos = offset + jnp.arange(block, dtype=jnp.int32)
        allowed = (key_pos[None, :] < lengths[:, None])[:, None, None, :]
        scores = (
            jnp.einsum("wqhd,wkhd->whqk", queries, key_block, preferred_element_type=jnp.float32)
            * scale
        )
        probs = jnp.where(allowed, jnp.exp(scores - log_total[..., None]), 0.0)
        grad_probs = jnp.einsum(
            "wqhd,wkhd->whqk", grad_attn, value_block, preferred_element_type=jnp.float32
        )
        grad_scores = (probs * (grad_probs - delta[..., None])).astype(jnp.bfloat16)
        grad_query = (
            grad_query
            + jnp.einsum(
                "whqk,wkhd->wqhd", grad_scores, key_block, preferred_element_type=jnp.float32
            )
            * scale
        )
        grad_key_blk = (
            jnp.einsum("whqk,wqhd->wkhd", grad_scores, queries, preferred_element_type=jnp.float32)
            * scale
        )
        grad_value_blk = jnp.einsum(
            "whqk,wqhd->wkhd",
            probs.astype(jnp.bfloat16),
            grad_attn,
            preferred_element_type=jnp.float32,
        )
        joined = jnp.concatenate(
            [
                grad_key_blk.reshape(windows, block, width),
                grad_value_blk.reshape(windows, block, width),
            ],
            axis=-1,
        )
        kv_grads = lax.dynamic_update_slice_in_dim(kv_grads, joined, offset, 1)
        return ((grad_query, kv_grads), None)

    start_back = (
        jnp.zeros((windows, local_len, H, HD), jnp.float32),
        jnp.zeros((windows, L, 2 * width), jnp.float32),
    )
    back_state, unused = lax.scan(back_block, start_back, jnp.arange(L // block))
    grad_query, kv_grads = back_state
    kv_share = lax.psum_scatter(
        kv_grads.astype(jnp.bfloat16), "ctx", scatter_dimension=1, tiled=True
    ).astype(jnp.float32)
    grad_key = kv_share[..., :width].reshape(windows, local_len, H, HD)
    grad_value = kv_share[..., width:].reshape(total_rows, width).astype(jnp.bfloat16)
    grad_query_raw = (
        rotate(grad_query, cosine, -sine).reshape(total_rows, width).astype(jnp.bfloat16)
    )
    grad_key_raw = rotate(grad_key, cosine, -sine).reshape(total_rows, width).astype(jnp.bfloat16)
    grad_query_w = jnp.dot(normed_low.T, grad_query_raw, preferred_element_type=jnp.float32)
    grad_key_w = jnp.dot(normed_low.T, grad_key_raw, preferred_element_type=jnp.float32)
    grad_value_w = jnp.dot(normed_low.T, grad_value, preferred_element_type=jnp.float32)
    grad_normed_one = jnp.dot(grad_query_raw, back_weights[0].T, preferred_element_type=jnp.float32)
    grad_normed_one = grad_normed_one + jnp.dot(
        grad_key_raw, back_weights[1].T, preferred_element_type=jnp.float32
    )
    grad_normed_one = grad_normed_one + jnp.dot(
        grad_value, back_weights[2].T, preferred_element_type=jnp.float32
    )
    unused_one, pull_one = jax.vjp(layer_norm, inputs, gain_one, shift_one)
    grad_inputs_norm, grad_gain_one, grad_shift_one = pull_one(grad_normed_one)
    tokens_grad = (
        (grad_resid + grad_inputs_norm).astype(jnp.bfloat16).reshape(windows, local_len, width)
    )
    summed = (
        lax.psum_scatter(grad_query_w, ("dp", "ctx"), scatter_dimension=0, tiled=True),
        lax.psum_scatter(grad_key_w, ("dp", "ctx"), scatter_dimension=0, tiled=True),
        lax.psum_scatter(grad_value_w, ("dp", "ctx"), scatter_dimension=0, tiled=True),
        lax.psum_scatter(grad_out_w, ("dp", "ctx"), scatter_dimension=0, tiled=True),
        lax.psum_scatter(grad_gate_w, ("dp", "ctx"), scatter_dimension=0, tiled=True),
        lax.psum_scatter(grad_up_w, ("dp", "ctx"), scatter_dimension=0, tiled=True),
        lax.psum_scatter(grad_down, ("dp", "ctx"), scatter_dimension=0, tiled=True),
        lax.psum_scatter(grad_gain_one, ("dp", "ctx"), scatter_dimension=0, tiled=True),
        lax.psum_scatter(grad_shift_one, ("dp", "ctx"), scatter_dimension=0, tiled=True),
        lax.psum_scatter(grad_gain_two, ("dp", "ctx"), scatter_dimension=0, tiled=True),
        lax.psum_scatter(grad_shift_two, ("dp", "ctx"), scatter_dimension=0, tiled=True),
    )
    return (
        output,
        tokens_grad,
        summed[0],
        summed[1],
        summed[2],
        summed[3],
        summed[4],
        summed[5],
        summed[6],
        summed[7],
        summed[8],
        summed[9],
        summed[10],
    )


def solution(mesh):
    return jax.shard_map(
        shards,
        mesh=mesh,
        in_specs=(
            P("dp", "ctx", None),
            P("dp"),
            P("dp", "ctx", None),
            P(("dp", "ctx"), None),
            P(("dp", "ctx"), None),
            P(("dp", "ctx"), None),
            P(("dp", "ctx"), None),
            P(("dp", "ctx"), None),
            P(("dp", "ctx"), None),
            P(("dp", "ctx"), None),
            P(("dp", "ctx")),
            P(("dp", "ctx")),
            P(("dp", "ctx")),
            P(("dp", "ctx")),
        ),
        out_specs=(
            P("dp", "ctx", None),
            P("dp", "ctx", None),
            P(("dp", "ctx"), None),
            P(("dp", "ctx"), None),
            P(("dp", "ctx"), None),
            P(("dp", "ctx"), None),
            P(("dp", "ctx"), None),
            P(("dp", "ctx"), None),
            P(("dp", "ctx"), None),
            P(("dp", "ctx")),
            P(("dp", "ctx")),
            P(("dp", "ctx")),
            P(("dp", "ctx")),
        ),
        check_vma=False,
    )
```

profile of v0, /device:TPU:0, one launch (start us, length us, event | category | flops | bytes accessed | tf_op | source)
XLA Modules:
  0.0 2675.3 jit_solution(3709941379202044671)
XLA Ops:
  12.8 42.2 %all-reduce.9 = (bf16[1024]{0:T(1024)(128)(2,1)S(1)}, bf16[1024]{0:T(1024)(128)(2,1)S(1)}, bf16[1024]{0:T(1024)(128)(2,1)S(1)}, bf16[1024]{0:T(1024)(128)(2,1)S(1)}) all-reduce(bf16[1024]{0:T(1024)(128)(2,1)S(1)} %dynamic-update-slice.1, bf16[1024]{0:T(1024)(128)(2,1)S(1)} %dynamic-update-slice, ...), channel_id=1, replica_groups=mesh['dp'=8,'ctx'=4] {'dp','ctx'}, use_global_device_ids=true, to_apply=%add.1 | all-reduce | flops 4096 | bytes 16384
  61.0 9.2 all-gather.12.cloned.1.call-done
  78.7 5.3 add_convert_fusion.3
  84.0 44.3 %all-gather.16.cloned.1.call-done = bf16[1024,1024]{1,0:T(8,128)(2,1)} async-done(((bf16[32,1024]{1,0:T(8,128)(2,1)}), bf16[1024,1024]{1,0:T(8,128)(2,1)}) %all-gather.16.cloned.1.call-update) | async-done | bytes 2097168 | tf_op jit(solution)/shard_map/all_gather | solution.py:57
  135.8 50.7 %all-gather.14.cloned.1.call-done = bf16[1024,1024]{1,0:T(8,128)(2,1)} async-done(((bf16[32,1024]{1,0:T(8,128)(2,1)}), bf16[1024,1024]{1,0:T(8,128)(2,1)}) %all-gather.14.cloned.1.call-update) | async-done | bytes 2097168 | tf_op jit(solution)/shard_map/all_gather | solution.py:55
  190.5 77.6 %all-gather.26.cloned.1.call-done = bf16[2048,1024]{1,0:T(8,128)(2,1)} async-done(((bf16[512,1024]{1,0:T(8,128)(2,1)}), bf16[2048,1024]{1,0:T(8,128)(2,1)}) %all-gather.26.cloned.1.call-update) | async-done | bytes 4194320 | tf_op jit(solution)/shard_map/all_gather | solution.py:100
  268.1 7.0 copy.58
  275.1 74.3 %all-gather.28.cloned.1.call-done = bf16[2048,1024]{1,0:T(8,128)(2,1)} async-done(((bf16[512,1024]{1,0:T(8,128)(2,1)}), bf16[2048,1024]{1,0:T(8,128)(2,1)}) %all-gather.28.cloned.1.call-update) | async-done | bytes 4194320 | tf_op jit(solution)/shard_map/all_gather | solution.py:101
  349.4 6.6 copy.59
  355.9 147.6 %while.28 = (s32[]{:T(128)}, f32[1,16,512]{2,1,0:T(8,128)S(1)}, f32[1,16,512]{2,1,0:T(8,128)S(1)}, f32[1,512,16,64]{1,3,2,0:T(8,128)}, s32[8]{0:T(128)S(1)}, /*i...) while((s32[]{:T(128)}, f32[1,16,512]{2,1,0:T(8,128)S(1)}, ...), condition=%wide.region_5.6_spmd.clone, body=%wide.region_2.5_spmd.clone.sunk | while | flops 565756416 | bytes 67634408 | solution.py:134
  359.1 5.2 bitcast_reduce_fusion.2
  364.3 7.0 bitcast_add_fusion.7
  376.9 5.2 bitcast_reduce_fusion.2
  382.1 7.6 bitcast_add_fusion.7
  395.3 5.2 bitcast_reduce_fusion.2
  400.5 7.7 bitcast_add_fusion.7
  413.7 5.2 bitcast_reduce_fusion.2
  418.9 7.6 bitcast_add_fusion.7
  432.0 5.2 bitcast_reduce_fusion.2
  437.2 7.7 bitcast_add_fusion.7
  450.4 5.2 bitcast_reduce_fusion.2
  455.6 8.7 bitcast_add_fusion.7
  469.7 5.2 bitcast_reduce_fusion.2
  474.9 7.7 bitcast_add_fusion.7
  488.1 5.2 bitcast_reduce_fusion.2
  493.3 7.9 bitcast_add_fusion.7
  510.6 10.6 fusion.89
  521.2 43.4 %all-gather.22.cloned.1.call-done = bf16[1024,4096]{1,0:T(8,128)(2,1)} async-done(((bf16[32,4096]{1,0:T(8,128)(2,1)}), bf16[1024,4096]{1,0:T(8,128)(2,1)}) %all-gather.22.cloned.1.call-update) | async-done | bytes 8388624 | tf_op jit(solution)/shard_map/all_gather | solution.py:60
  564.6 10.0 fusion.90
  574.6 68.6 %all-gather.24.cloned.1.call-done = bf16[4096,1024]{1,0:T(8,128)(2,1)} async-done(((bf16[128,1024]{1,0:T(8,128)(2,1)}), bf16[4096,1024]{1,0:T(8,128)(2,1)}) %all-gather.24.cloned.1.call-update) | async-done | bytes 8388624 | tf_op jit(solution)/shard_map/all_gather | solution.py:61
  643.3 16.4 multiply_convert_fusion.1
  659.7 10.7 fusion.91
  670.3 7.3 multiply_reduce_fusion
  689.1 139.4 %while.29 = (s32[]{:T(128)}, f32[1,512,16,64]{1,3,2,0:T(8,128)}, bf16[1,2048,2048]{1,2,0:T(8,128)(2,1)}, s32[8]{0:T(128)S(1)}, bf16[1,2048,1024]{1,2,0:T(8,128)(...) while((s32[]{:T(128)}, f32[1,512,16,64]{1,3,2,0:T(8,128)}, ...), condition=%wide.region_12.13_spmd.clone, body=%wide.region_11.12_spmd.clone.sunk | while | flops 1367343616 | bytes 69829632 | solution.py:245
  841.3 130.6 %reduce-scatter.9.cloned.1.call-done = bf16[1,512,2048]{1,2,0:T(8,128)(2,1)} async-done(((bf16[1,2048,2048]{1,2,0:T(8,128)(2,1)}), bf16[1,512,2048]{1,2,0:T(8,128)(2,1)}) %reduce-scatter.9.cloned.1.call-update) | async-done | bytes 2097168 | tf_op jit(solution)/shard_map/reduce_scatter | solution.py:247
  980.8 5.2 fusion.67
  986.0 12.8 fusion.95
  998.9 12.9 fusion.96
  1012.1 12.9 fusion.63
  1028.8 8.6 fusion.55
  1044.7 41.8 %all-reduce.8 = (f32[1024]{0:T(1024)S(1)}, f32[1024]{0:T(1024)S(1)}, f32[1024]{0:T(1024)S(1)}, f32[1024]{0:T(1024)S(1)}) all-reduce(f32[1024]{0:T(1024)S(1)} %get-tuple-element.253, f32[1024]{0:T(1024)S(1)} %get-tuple-element.256, f32[1024]{0:T(1024)S(1)} %copy-done.39, ...), channel_id=12, replica_groups=mesh['dp'=8,'ctx'=4] {'dp','ctx'}, use_global_device_ids=true, to_apply=%region_24.25.clone | all-reduce | flops 4096 | bytes 32768
  1092.2 32.6 %reduce-scatter.17.cloned.1.call-done = f32[32,1024]{1,0:T(8,128)} async-done(((f32[1024,1024]{1,0:T(8,128)}), f32[32,1024]{1,0:T(8,128)}) %reduce-scatter.17.cloned.1.call-update) | async-done | bytes 131088 | tf_op jit(solution)/shard_map/reduce_scatter | solution.py:275
  1124.8 151.2 %reduce-scatter.11.cloned.1.call-done = f32[32,1024]{1,0:T(8,128)} async-done(((f32[1024,1024]{1,0:T(8,128)}), f32[32,1024]{1,0:T(8,128)}) %reduce-scatter.11.cloned.1.call-update) | async-done | bytes 131088 | tf_op jit(solution)/shard_map/reduce_scatter | solution.py:272
  1276.0 150.2 %reduce-scatter.13.cloned.1.call-done = f32[32,1024]{1,0:T(8,128)} async-done(((f32[1024,1024]{1,0:T(8,128)}), f32[32,1024]{1,0:T(8,128)}) %reduce-scatter.13.cloned.1.call-update) | async-done | bytes 131088 | tf_op jit(solution)/shard_map/reduce_scatter | solution.py:273
  1426.2 150.9 %reduce-scatter.15.cloned.1.call-done = f32[32,1024]{1,0:T(8,128)} async-done(((f32[1024,1024]{1,0:T(8,128)}), f32[32,1024]{1,0:T(8,128)}) %reduce-scatter.15.cloned.1.call-update) | async-done | bytes 131088 | tf_op jit(solution)/shard_map/reduce_scatter | solution.py:274
  1577.1 362.0 %reduce-scatter.19.cloned.1.call-done = f32[32,4096]{1,0:T(8,128)} async-done(((f32[1024,4096]{1,0:T(8,128)}), f32[32,4096]{1,0:T(8,128)}) %reduce-scatter.19.cloned.1.call-update) | async-done | bytes 524304 | tf_op jit(solution)/shard_map/reduce_scatter | solution.py:276
  1939.1 364.7 %reduce-scatter.21.cloned.1.call-done = f32[32,4096]{1,0:T(8,128)} async-done(((f32[1024,4096]{1,0:T(8,128)}), f32[32,4096]{1,0:T(8,128)}) %reduce-scatter.21.cloned.1.call-update) | async-done | bytes 524304 | tf_op jit(solution)/shard_map/reduce_scatter | solution.py:277
  2303.8 364.7 %reduce-scatter.23.cloned.1.call-done = f32[128,1024]{1,0:T(8,128)} async-done(((f32[4096,1024]{1,0:T(8,128)}), f32[128,1024]{1,0:T(8,128)}) %reduce-scatter.23.cloned.1.call-update) | async-done | bytes 524304 | tf_op jit(solution)/shard_map/reduce_scatter | solution.py:278
  (358 shorter events, 259.8 us)
Async XLA Ops:
  7.2 63.0 %all-gather.12.cloned.1.call-start = ((), (), s32[]{:S(2)}) async-start(), calls=%async_computation.8 | async-start | bytes 2162688 | tf_op jit(solution)/shard_map/all_gather | solution.py:56
  7.9 120.4 %all-gather.16.cloned.1.call-start = ((), (), s32[]{:S(2)}) async-start(), calls=%async_computation.10 | async-start | bytes 2162688 | tf_op jit(solution)/shard_map/all_gather | solution.py:57
  8.7 177.8 %all-gather.14.cloned.1.call-start = ((), (), s32[]{:S(2)}) async-start(), calls=%async_computation.9 | async-start | bytes 2162688 | tf_op jit(solution)/shard_map/all_gather | solution.py:55
  9.4 258.7 %all-gather.26.cloned.1.call-start = ((), (), s32[]{:S(2)}) async-start(), calls=%async_computation.23 | async-start | bytes 5242880 | tf_op jit(solution)/shard_map/all_gather | solution.py:100
  55.0 131.5 %copy-start.27 = (f32[1024]{0:T(1024)}, f32[1024]{0:T(1024)S(1)}, u32[]{:S(2)}) copy-start(f32[1024]{0:T(1024)S(1)} %convert_element_type.150) | copy-start | bytes 12292
  55.0 131.5 %copy-start.37 = (f32[1024]{0:T(1024)}, f32[1024]{0:T(1024)S(1)}, u32[]{:S(2)}) copy-start(f32[1024]{0:T(1024)S(1)} %convert_element_type.151) | copy-start | bytes 12292
  55.4 134.5 %copy-start.15 = (f32[512,64]{0,1:T(8,128)}, f32[512,64]{0,1:T(8,128)S(1)}, u32[]{:S(2)}) copy-start(f32[512,64]{0,1:T(8,128)S(1)} %pad_maximum_fusion.2) | copy-start | bytes 393220
  60.5 126.0 %copy-start.29 = (f32[512]{0:T(512)}, f32[512]{0:T(512)S(1)}, u32[]{:S(2)}) copy-start(f32[512]{0:T(512)S(1)} %broadcast_multiply_fusion.1) | copy-start | bytes 6148
  61.0 13.5 copy-start.35
  61.0 125.5 %copy-start.33 = (f32[512]{0:T(512)}, f32[512]{0:T(512)S(1)}, u32[]{:S(2)}) copy-start(f32[512]{0:T(512)S(1)} %fusion.74) | copy-start | bytes 6148
  84.0 265.4 %all-gather.28.cloned.1.call-start = ((), (), s32[]{:S(2)}) async-start(), calls=%async_computation.24 | async-start | bytes 5242880 | tf_op jit(solution)/shard_map/all_gather | solution.py:101
  132.2 373.2 %all-gather.18.cloned.1.call-start = ((), (), s32[]{:S(2)}) async-start(), calls=%async_computation.11 | async-start | bytes 2162688 | tf_op jit(solution)/shard_map/all_gather | solution.py:58
  132.8 377.8 %all-gather.20.cloned.1.call-start = ((), (), s32[]{:S(2)}) async-start(), calls=%async_computation.12 | async-start | bytes 8650752 | tf_op jit(solution)/shard_map/all_gather | solution.py:59
  133.5 431.1 %all-gather.22.cloned.1.call-start = ((), (), s32[]{:S(2)}) async-start(), calls=%async_computation.13 | async-start | bytes 8650752 | tf_op jit(solution)/shard_map/all_gather | solution.py:60
  134.3 509.0 %all-gather.24.cloned.1.call-start = ((), (), s32[]{:S(2)}) async-start(), calls=%async_computation.14 | async-start | bytes 8650752 | tf_op jit(solution)/shard_map/all_gather | solution.py:61
  135.0 836.9 %reduce-scatter.9.cloned.1.call-start = ((), (), s32[]{:S(2)}) async-start(), calls=%async_computation.15 | async-start | bytes 10485760 | tf_op jit(solution)/shard_map/reduce_scatter | solution.py:247
  364.3 7.0 copy-start
  382.1 7.7 copy-start
  400.4 7.7 copy-start
  418.9 7.6 copy-start
  437.2 7.7 copy-start
  455.6 8.7 copy-start
  474.9 7.7 copy-start
  493.3 7.9 copy-start
  505.4 3.4 copy-start.18
  510.5 54.1 %copy-start.13 = (bf16[512,1024]{1,0:T(8,128)(2,1)}, bf16[512,1024]{1,0:T(8,128)(2,1)S(1)}, u32[]{:S(2)}) copy-start(bf16[512,1024]{1,0:T(8,128)(2,1)S(1)} %add_convert_fusion.2) | copy-start | bytes 3145732
  521.2 122.0 %copy-start.17 = (bf16[1,512,1024]{2,1,0:T(8,128)(2,1)S(1)}, bf16[1,512,1024]{2,1,0:T(8,128)(2,1)}, u32[]{:S(2)}) copy-start(bf16[1,512,1024]{2,1,0:T(8,128)(2,1)} %param.20) | copy-start | bytes 3145732
  659.6 10.7 copy-start.6
  659.7 10.7 copy-start.20
  659.7 10.7 copy-start.41
  678.3 2.5 copy-start.22
  713.9 2.0 copy-start.1
  766.2 2.0 copy-start.1
  783.7 2.0 copy-start.1
  828.5 296.3 %reduce-scatter.17.cloned.1.call-start = ((), (), s32[]{:S(2)}) async-start(), calls=%async_computation.19 | async-start | bytes 4325376 | tf_op jit(solution)/shard_map/reduce_scatter | solution.py:275
  833.3 442.7 %reduce-scatter.11.cloned.1.call-start = ((), (), s32[]{:S(2)}) async-start(), calls=%async_computation.16 | async-start | bytes 4325376 | tf_op jit(solution)/shard_map/reduce_scatter | solution.py:272
  841.2 585.0 %reduce-scatter.13.cloned.1.call-start = ((), (), s32[]{:S(2)}) async-start(), calls=%async_computation.17 | async-start | bytes 4325376 | tf_op jit(solution)/shard_map/reduce_scatter | solution.py:273
  980.5 596.6 %reduce-scatter.15.cloned.1.call-start = ((), (), s32[]{:S(2)}) async-start(), calls=%async_computation.18 | async-start | bytes 4325376 | tf_op jit(solution)/shard_map/reduce_scatter | solution.py:274
  986.0 953.1 %reduce-scatter.19.cloned.1.call-start = ((), (), s32[]{:S(2)}) async-start(), calls=%async_computation.20 | async-start | bytes 17301504 | tf_op jit(solution)/shard_map/reduce_scatter | solution.py:276
  998.9 1304.9 %reduce-scatter.21.cloned.1.call-start = ((), (), s32[]{:S(2)}) async-start(), calls=%async_computation.21 | async-start | bytes 17301504 | tf_op jit(solution)/shard_map/reduce_scatter | solution.py:277
  1011.8 1656.6 %reduce-scatter.23.cloned.1.call-start = ((), (), s32[]{:S(2)}) async-start(), calls=%async_computation.22 | async-start | bytes 17301504 | tf_op jit(solution)/shard_map/reduce_scatter | solution.py:278
  1025.0 3.4 copy-start.7
  1025.0 3.8 copy-start.43
  1028.8 8.6 copy-start.9
  1042.5 2.3 copy-start.39
  1042.5 2.3 copy-start.40
  1042.5 46.4 %copy-start.11 = (f32[512,1024]{1,0:T(8,128)S(1)}, f32[512,1024]{1,0:T(8,128)}, u32[]{:S(2)}) copy-start(f32[512,1024]{1,0:T(8,128)} %copy-done.10) | copy-start | bytes 6291460
  1042.5 46.3 %copy-start.32 = (f32[512]{0:T(512)S(1)}, f32[512]{0:T(512)}, u32[]{:S(2)}) copy-start(f32[512]{0:T(512)} %copy-done.31) | copy-start | bytes 6148
  (27 other events, 42.6 us)
Sparse Core Ops, SparseCore 0:
  10.9 59.1 all-gather.11
  73.1 55.2 all-gather.15
  131.2 55.1 all-gather.13
  188.5 79.5 all-gather.25
  270.1 79.2 all-gather.27
  352.1 54.8 all-gather.17
  410.0 75.9 all-gather.19
  488.8 75.7 all-gather.21
  567.5 75.6 all-gather.23
  828.6 143.2 reduce-scatter.8
  974.7 150.0 reduce-scatter.16
  1127.5 148.4 reduce-scatter.10
  1278.8 147.3 reduce-scatter.12
  1428.9 148.1 reduce-scatter.14
  1579.9 359.1 reduce-scatter.18
  1941.8 361.9 reduce-scatter.20
  2306.5 361.9 reduce-scatter.22
where the time goes:
time: 2680 us
  waiting for transfers between devices  2080 us (78%)
  matrix products  342 us (13%)
  blocking collectives  83.9 us (3%)
  local copies, waits for them, and re-layouts  81.6 us (3%)
  other arithmetic  59.4 us (2%)
    reduce_scatter x1, waiting for transfers between devices, shards(): lax.psum_scatter(grad_up_w, ('dp', 'ctx'), scatter_dimension=0, tiled=True)  365 us
    reduce_scatter x1, waiting for transfers between devices, shards(): lax.psum_scatter(grad_down, ('dp', 'ctx'), scatter_dimension=0, tiled=True)  365 us
    reduce_scatter x1, waiting for transfers between devices, shards(): lax.psum_scatter(grad_gate_w, ('dp', 'ctx'), scatter_dimension=0, tiled=T...  362 us
    reduce_scatter x1, waiting for transfers between devices, shards(): lax.psum_scatter(grad_query_w, ('dp', 'ctx'), scatter_dimension=0, tiled=...  151 us
    reduce_scatter x1, waiting for transfers between devices, shards(): lax.psum_scatter(grad_value_w, ('dp', 'ctx'), scatter_dimension=0, tiled=...  151 us
    reduce_scatter x1, waiting for transfers between devices, shards(): lax.psum_scatter(grad_key_w, ('dp', 'ctx'), scatter_dimension=0, tiled=True)  150 us
    reduce_scatter x1, waiting for transfers between devices, shards(): lax.psum_scatter(kv_grads.astype(jnp.bfloat16), 'ctx', scatter_dimension=...  131 us
    unnamed x2, blocking collectives  83.9 us
  transfers between devices with their start and end apart: 17, of which 15 were waited for; matrix products, arithmetic and copies ran while one was open for 11% of the time, Pallas kernels for 0%

commit v1 on v0

--- a/solution.py
+++ b/solution.py
@@ -1,8 +1,13 @@
+import functools
 import math
+
+import numpy as np
 
 import jax
 import jax.numpy as jnp
 from jax import lax
+from jax.experimental import pallas as pl
+from jax.experimental.pallas import tpu as pltpu
 from jax.sharding import PartitionSpec as P
 
 H = 16
@@ -35,7 +40,168 @@
     return values * cosine[:, None, :] + turned * sine[:, None, :]
 
 
+AXES = ("dp", "ctx")
+BF = jnp.bfloat16
+
+
+class Plan:
+    def __init__(self, mesh):
+        self.dp, self.ctx = mesh.shape["dp"], mesh.shape["ctx"]
+        self.stages = self.dp.bit_length() - 2
+        self.ctx_bits = self.ctx.bit_length() - 1
+        orders = (list(range(1, self.stages + 1)), list(range(self.stages, 0, -1)))
+        self.core = self.pairs(lambda d, z: (d ^ 1, z))
+        self.stage = [
+            self.pairs(lambda d, z, t=t: (d ^ (1 << orders[d & 1][t]), z)) for t in range(self.stages)
+        ]
+        self.along = [self.pairs(lambda d, z, b=b: (d, z ^ (1 << b))) for b in range(self.ctx_bits)]
+        half = self.dp // 2
+        table = np.zeros((self.dp, self.dp), np.int32)
+        for d in range(self.dp):
+            for j in range(self.dp):
+                owner = d ^ 1 if j >= half else d
+                block = owner
+                for t in range(self.stages):
+                    if (j % half) >> (self.stages - 1 - t) & 1:
+                        block ^= 1 << orders[owner & 1][t]
+                table[d, j] = block
+        self.table = table
+
+    def pairs(self, target):
+        found = []
+        for d in range(self.dp):
+            for z in range(self.ctx):
+                other, place = target(d, z)
+                found.append((d * self.ctx + z, other * self.ctx + place))
+        return found
+
+    def slots(self):
+        return jnp.asarray(self.table)[lax.axis_index("dp")]
+
+
+def assemble(slots, pieces, rows):
+    blocks = slots.shape[0]
+    width = pieces[0].shape[1]
+    sizes = [piece.shape[0] // rows for piece in pieces]
+    starts = [sum(sizes[:i]) for i in range(len(sizes))]
+
+    def body(order, *refs):
+        slot = pl.program_id(0)
+        out = refs[-1]
+        for piece, start, size in zip(refs, starts, sizes):
+
+            @pl.when((slot >= start) & (slot < start + size))
+            def _(piece=piece):
+                out[...] = piece[...]
+
+    specs = [
+        pl.BlockSpec(
+            (rows, width),
+            lambda j, order, start=start, size=size: (jnp.clip(j - start, 0, size - 1), 0),
+        )
+        for start, size in zip(starts, sizes)
+    ]
+    return pl.pallas_call(
+        body,
+        out_shape=jax.ShapeDtypeStruct((blocks * rows, width), pieces[0].dtype),
+        grid_spec=pltpu.PrefetchScalarGridSpec(
+            num_scalar_prefetch=1,
+            grid=(blocks,),
+            in_specs=specs,
+            out_specs=pl.BlockSpec((rows, width), lambda j, order: (order[j], 0)),
+        ),
+        name="assemble",
+    )(slots, *pieces)
+
+
+def gather_rows(plan, slots, shard):
+    place = lax.axis_index("ctx")
+    run = shard
+    for bit, pairs in enumerate(plan.along):
+        other = lax.ppermute(run, AXES, pairs)
+        upper = (place >> bit) & 1 == 1
+        run = jnp.where(upper, jnp.concatenate([other, run]), jnp.concatenate([run, other]))
+    rows = run.shape[0]
+    pieces = [run]
+    for pairs in reversed(plan.stage):
+        other = lax.ppermute(run, AXES, pairs)
+        pieces.append(other)
+        run = jnp.concatenate([run, other])
+    pieces.append(lax.ppermute(run, AXES, plan.core))
+    return assemble(slots, pieces, rows)
+
+
+def to_slots(slots, values):
+    blocks = slots.shape[0]
+    rows, width = values.shape
+    part = width // blocks
+    if part % 128:
+        cut = values.reshape(rows, blocks, part)
+        return jnp.take(cut, slots, axis=1).reshape(rows, width)
+
+    def body(order, source, out):
+        out[...] = source[...]
+
+    return pl.pallas_call(
+        body,
+        out_shape=jax.ShapeDtypeStruct((rows, width), values.dtype),
+        grid_spec=pltpu.PrefetchScalarGridSpec(
+            num_scalar_prefetch=1,
+            grid=(blocks,),
+            in_specs=[pl.BlockSpec((rows, part), lambda j, order: (0, order[j]))],
+            out_specs=pl.BlockSpec((rows, part), lambda j, order: (0, j)),
+        ),
+        name="to_slots",
+    )(slots, values)
+
+
+def sum_rows(plan, left, right):
+    place = lax.axis_index("ctx")
+    rows = left.shape[1] // plan.dp
+    half = plan.dp // 2
+
+    def product(start, end, add=None):
+        part = lax.slice_in_dim(left, start * rows, end * rows, axis=1)
+        found = jnp.dot(part.T, right, preferred_element_type=jnp.float32)
+        if add is not None:
+            found = found + add.astype(jnp.float32)
+        return found.astype(BF)
+
+    def total(a, b):
+        return (a.astype(jnp.float32) + b.astype(jnp.float32)).astype(BF)
+
+    other = lax.ppermute(product(half, plan.dp), AXES, plan.core)
+    size = half // 2
+    upper = product(size, half, other[size * rows :])
+    other_upper = lax.ppermute(upper, AXES, plan.stage[0])
+    held = total(product(0, size, other[: size * rows]), other_upper)
+    for pairs in plan.stage[1:]:
+        size //= 2
+        other = lax.ppermute(held[size * rows :], AXES, pairs)
+        held = total(held[: size * rows], other)
+    for bit in reversed(range(plan.ctx_bits)):
+        cut = held.shape[0] // 2
+        above = (place >> bit) & 1 == 1
+        low, high = held[:cut], held[cut:]
+        other = lax.ppermute(jnp.where(above, low, high), AXES, plan.along[bit])
+        held = jnp.where(above, high, low).astype(jnp.float32) + other.astype(jnp.float32)
+        if bit:
+            held = held.astype(BF)
+    return held
+
+
+def sum_vectors(plan, vectors):
+    count = plan.dp * plan.ctx
+    packed = jnp.stack(vectors).reshape(len(vectors), count, -1).transpose(1, 0, 2)
+    part = packed.shape[2]
+    packed = packed.reshape(count, len(vectors) * part)
+    came = lax.all_to_all(packed, AXES, split_axis=0, concat_axis=0, tiled=True)
+    whole = jnp.sum(came, axis=0)
+    return [whole[i * part : (i + 1) * part] for i in range(len(vectors))]
+
+
 def shards(
+    plan,
     tokens,
     lengths,
     cotangent,
@@ -51,18 +217,24 @@
     feed_gain,
     feed_shift,
 ):
+    slots = plan.slots()
+    edge = jnp.stack([attention_gain, attention_shift, feed_gain, feed_shift], axis=1)
+    edge = jnp.pad(edge, ((0, 0), (0, 124)))
+    mixed = jnp.concatenate([query_weight, key_weight, value_weight, output_weight, edge], axis=1)
+    mixed = gather_rows(plan, slots, mixed)
+    vectors = mixed[:, 4096:4100].T
     weights = (
-        lax.all_gather(query_weight, ("dp", "ctx"), axis=0, tiled=True),
-        lax.all_gather(key_weight, ("dp", "ctx"), axis=0, tiled=True),
-        lax.all_gather(value_weight, ("dp", "ctx"), axis=0, tiled=True),
-        lax.all_gather(output_weight, ("dp", "ctx"), axis=0, tiled=True),
-        lax.all_gather(gate_weight, ("dp", "ctx"), axis=0, tiled=True),
-        lax.all_gather(up_weight, ("dp", "ctx"), axis=0, tiled=True),
-        lax.all_gather(down_weight, ("dp", "ctx"), axis=0, tiled=True),
-        lax.all_gather(attention_gain, ("dp", "ctx"), axis=0, tiled=True),
-        lax.all_gather(attention_shift, ("dp", "ctx"), axis=0, tiled=True),
-        lax.all_gather(feed_gain, ("dp", "ctx"), axis=0, tiled=True),
-        lax.all_gather(feed_shift, ("dp", "ctx"), axis=0, tiled=True),
+        mixed[:, :1024],
+        mixed[:, 1024:2048],
+        mixed[:, 2048:3072],
+        mixed[:, 3072:4096],
+        gather_rows(plan, slots, gate_weight),
+        gather_rows(plan, slots, up_weight),
+        gather_rows(plan, slots, down_weight),
+        vectors[0],
+        vectors[1],
+        vectors[2],
+        vectors[3],
     )
     windows, local_len, width = tokens.shape
     total_rows = windows * local_len
@@ -146,31 +318,20 @@
     hidden = (activ * up_pre).astype(jnp.bfloat16)
     result_rows = resid + jnp.dot(hidden, weights[6], preferred_element_type=jnp.float32)
     output = result_rows.astype(jnp.bfloat16).reshape(windows, local_len, width)
-    back_weights = (
-        lax.all_gather(query_weight, ("dp", "ctx"), axis=0, tiled=True),
-        lax.all_gather(key_weight, ("dp", "ctx"), axis=0, tiled=True),
-        lax.all_gather(value_weight, ("dp", "ctx"), axis=0, tiled=True),
-        lax.all_gather(output_weight, ("dp", "ctx"), axis=0, tiled=True),
-        lax.all_gather(gate_weight, ("dp", "ctx"), axis=0, tiled=True),
-        lax.all_gather(up_weight, ("dp", "ctx"), axis=0, tiled=True),
-        lax.all_gather(down_weight, ("dp", "ctx"), axis=0, tiled=True),
-        lax.all_gather(attention_gain, ("dp", "ctx"), axis=0, tiled=True),
-        lax.all_gather(attention_shift, ("dp", "ctx"), axis=0, tiled=True),
-        lax.all_gather(feed_gain, ("dp", "ctx"), axis=0, tiled=True),
-        lax.all_gather(feed_shift, ("dp", "ctx"), axis=0, tiled=True),
-    )
+    back_weights = weights
     upstream = cotangent.astype(jnp.float32).reshape(total_rows, width) * row_valid.reshape(
         total_rows, 1
     )
     upstream_low = upstream.astype(jnp.bfloat16)
-    grad_down = jnp.dot(hidden.T, upstream_low, preferred_element_type=jnp.float32)
+    grad_down = sum_rows(plan, to_slots(slots, hidden), upstream_low)
     grad_hidden = jnp.dot(upstream_low, back_weights[6].T, preferred_element_type=jnp.float32)
     grad_gate = (grad_hidden * up_pre * sigma * (1.0 + gate_pre * (1.0 - sigma))).astype(
         jnp.bfloat16
     )
     grad_up = (grad_hidden * activ).astype(jnp.bfloat16)
-    grad_gate_w = jnp.dot(two_low.T, grad_gate, preferred_element_type=jnp.float32)
-    grad_up_w = jnp.dot(two_low.T, grad_up, preferred_element_type=jnp.float32)
+    two_slots = to_slots(slots, two_low)
+    grad_gate_w = sum_rows(plan, two_slots, grad_gate)
+    grad_up_w = sum_rows(plan, two_slots, grad_up)
     grad_normed_two = jnp.dot(
         grad_gate, back_weights[4].T, preferred_element_type=jnp.float32
     ) + jnp.dot(grad_up, back_weights[5].T, preferred_element_type=jnp.float32)
@@ -178,7 +339,7 @@
     grad_resid_norm, grad_gain_two, grad_shift_two = pull_two(grad_normed_two)
     grad_resid = upstream + grad_resid_norm
     branch_low = grad_resid.astype(jnp.bfloat16)
-    grad_out_w = jnp.dot(attn_low.T, branch_low, preferred_element_type=jnp.float32)
+    grad_out_w = sum_rows(plan, to_slots(slots, attn_low), branch_low)
     grad_attn = (
         jnp.dot(branch_low, back_weights[3].T, preferred_element_type=jnp.float32)
         .astype(jnp.bfloat16)
@@ -253,9 +414,11 @@
         rotate(grad_query, cosine, -sine).reshape(total_rows, width).astype(jnp.bfloat16)
     )
     grad_key_raw = rotate(grad_key, cosine, -sine).reshape(total_rows, width).astype(jnp.bfloat16)
-    grad_query_w = jnp.dot(normed_low.T, grad_query_raw, preferred_element_type=jnp.float32)
-    grad_key_w = jnp.dot(normed_low.T, grad_key_raw, preferred_element_type=jnp.float32)
-    grad_value_w = jnp.dot(normed_low.T, grad_value, preferred_element_type=jnp.float32)
+    raw = jnp.concatenate([grad_query_raw, grad_key_raw, grad_value], axis=1)
+    grad_raw_w = sum_rows(plan, to_slots(slots, normed_low), raw)
+    grad_query_w = grad_raw_w[:, :width]
+    grad_key_w = grad_raw_w[:, width : 2 * width]
+    grad_value_w = grad_raw_w[:, 2 * width :]
     grad_normed_one = jnp.dot(grad_query_raw, back_weights[0].T, preferred_element_type=jnp.float32)
     grad_normed_one = grad_normed_one + jnp.dot(
         grad_key_raw, back_weights[1].T, preferred_element_type=jnp.float32
@@ -268,18 +431,18 @@
     tokens_grad = (
         (grad_resid + grad_inputs_norm).astype(jnp.bfloat16).reshape(windows, local_len, width)
     )
+    vectors_grad = sum_vectors(
+        plan, (grad_gain_one, grad_shift_one, grad_gain_two, grad_shift_two)
+    )
     summed = (
-        lax.psum_scatter(grad_query_w, ("dp", "ctx"), scatter_dimension=0, tiled=True),
-        lax.psum_scatter(grad_key_w, ("dp", "ctx"), scatter_dimension=0, tiled=True),
-        lax.psum_scatter(grad_value_w, ("dp", "ctx"), scatter_dimension=0, tiled=True),
-        lax.psum_scatter(grad_out_w, ("dp", "ctx"), scatter_dimension=0, tiled=True),
-        lax.psum_scatter(grad_gate_w, ("dp", "ctx"), scatter_dimension=0, tiled=True),
-        lax.psum_scatter(grad_up_w, ("dp", "ctx"), scatter_dimension=0, tiled=True),
-        lax.psum_scatter(grad_down, ("dp", "ctx"), scatter_dimension=0, tiled=True),
-        lax.psum_scatter(grad_gain_one, ("dp", "ctx"), scatter_dimension=0, tiled=True),
-        lax.psum_scatter(grad_shift_one, ("dp", "ctx"), scatter_dimension=0, tiled=True),
-        lax.psum_scatter(grad_gain_two, ("dp", "ctx"), scatter_dimension=0, tiled=True),
-        lax.psum_scatter(grad_shift_two, ("dp", "ctx"), scatter_dimension=0, tiled=True),
+        grad_query_w,
+        grad_key_w,
+        grad_value_w,
+        grad_out_w,
+        grad_gate_w,
+        grad_up_w,
+        grad_down,
+        *vectors_grad,
     )
     return (
         output,
@@ -300,7 +463,7 @@
 
 def solution(mesh):
     return jax.shard_map(
-        shards,
+        functools.partial(shards, Plan(mesh)),
         mesh=mesh,
         in_specs=(
             P("dp", "ctx", None),

time: 2680 us -> 1080 us (0.40)
  waiting for transfers between devices: 2080 us -> 347 us
  blocking collectives: 83.9 us -> 0 us
  Pallas kernels: 0 us -> 69.5 us
  starting transfers between devices: 1.07 us -> 70.1 us
  other arithmetic: 59.4 us -> 121 us
    reduce_scatter x7 -> x0, waiting for transfers between devices: 1580 us -> none  [the longest x1 365 us: shards(): lax.psum_scatter(grad_up_w, ('dp', 'ctx'), scatter_dimension=0, tiled=True)]
    ppermute x0 -> x45, waiting for transfers between devices: none -> 326 us  [the longest x16 159 us: gather_rows(): other = lax.ppermute(run, AXES, pairs)]
    all_gather x7 -> x0, waiting for transfers between devices: 216 us -> none  [the longest x1 68.6 us: shards(): lax.all_gather(down_weight, ('dp', 'ctx'), axis=0, tiled=True)]
    reduce_scatter x1, waiting for transfers between devices: 131 us -> 0.01 us  [shards(): lax.psum_scatter(kv_grads.astype(jnp.bfloat16), 'ctx', scatter_dimension=...]
    unnamed x2 -> x0, blocking collectives: 83.9 us -> none
    all_gather x1, waiting for transfers between devices: 74.3 us -> 0.02 us  [shards(): value_piece = lax.all_gather(value_flat, 'ctx', axis=1, tiled=True)]
    pallas_call x0 -> x8, Pallas kernels: none -> 69.5 us  [the longest x4 43.6 us: assemble(): pl.pallas_call(body, out_shape=jax.ShapeDtypeStruct((blocks * rows, width...]
    ppermute x0 -> x45, starting transfers between devices: none -> 66.1 us  [the longest x16 23.3 us: gather_rows(): other = lax.ppermute(run, AXES, pairs)]
  transfers between devices with their start and end apart: 17 -> 49, of which waited for: 15 -> 27; matrix products, arithmetic and copies ran while one was open for 11% -> 17% of each run, Pallas kernels for 0% -> 6%
where the time goes in v1:
time: 1080 us; the launch traced here: 1070 us
  waiting for transfers between devices  347 us (32%)
  matrix products  344 us (32%)
  other arithmetic  121 us (11%)
  local copies, waits for them, and re-layouts  90.4 us (8%)
  starting transfers between devices  70.1 us (6%)
  Pallas kernels  69.5 us (6%)
  between operations  16 us (1%)
  loops' own time  11.4 us (1%)
    ppermute x16, waiting for transfers between devices, gather_rows(): other = lax.ppermute(run, AXES, pairs)  159 us
    ppermute x10, waiting for transfers between devices, sum_rows(): other = lax.ppermute(jnp.where(above, low, high), AXES, plan.along[bit])  75.2 us
    ppermute x5, waiting for transfers between devices, sum_rows(): other_upper = lax.ppermute(upper, AXES, plan.stage[0])  72 us
    dot_general x8, matrix products, one_block(): jnp.einsum('whqk,wkhd->wqhd', expo.astype(jnp.bfloat16), value_block, pre...  60.4 us
    dot_general x15, matrix products, product(): found = jnp.dot(part.T, right, preferred_element_type=jnp.float32)  52.1 us
    pallas_call x4, Pallas kernels, assemble(): pl.pallas_call(body, out_shape=jax.ShapeDtypeStruct((blocks * rows, width...  43.6 us
    dot_general x8, matrix products, one_block(): jnp.einsum('wqhd,wkhd->whqk', queries, key_block, preferred_element_type=...  41.4 us
    dot_general x8, matrix products, back_block(): jnp.einsum('whqk,wkhd->wqhd', grad_scores, key_block, preferred_element_t...  39.6 us
  transfers between devices with their start and end apart: 49, of which 27 were waited for; matrix products, arithmetic and copies ran while one was open for 17% of the time, Pallas kernels for 6%

profile of v1, /device:TPU:0, one launch (start us, length us, event | category | flops | bytes accessed | tf_op | source)
XLA Modules:
  0.0 1068.8 jit_solution(5579842121404192698)
XLA Ops:
  14.6 6.5 collective-permute-done
  23.9 23.2 %collective-permute-done.1 = bf16[64,4224]{1,0:T(8,128)(2,1)S(1)} collective-permute-done((bf16[64,4224]{1,0:T(8,128)(2,1)S(1)}, bf16[64,4224]{1,0:T(8,128)(2,1)S(1)}, u32[]{:S(2)}, u32[]{:S(2)}) %collective-permute-start.1) | collective-permute-done | bytes 540704 | tf_op jit(solution)/shard_map/ppermute | solution.py:121
  48.8 13.7 %collective-permute-done.2.refs_1_ = bf16[128,4224]{1,0:T(8,128)(2,1)S(1)} collective-permute-done((bf16[128,4224]{1,0:T(8,128)(2,1)S(1)}, bf16[128,4224]{1,0:T(8,128)(2,1)S(1)}, u32[]{:S(2)}, u32[]{:S(2)}) %collective-permute-start.2) | collective-permute-done | bytes 1081376 | tf_op jit(solution)/shard_map/ppermute | solution.py:127
  64.2 25.4 %collective-permute-done.3.refs_2_ = bf16[256,4224]{1,0:T(8,128)(2,1)S(1)} collective-permute-done((bf16[256,4224]{1,0:T(8,128)(2,1)S(1)}, bf16[256,4224]{1,0:T(8,128)(2,1)S(1)}, u32[]{:S(2)}, u32[]{:S(2)}) %collective-permute-start.3) | collective-permute-done | bytes 2162720 | tf_op jit(solution)/shard_map/ppermute | solution.py:127
  106.6 13.2 %collective-permute-done.15 = bf16[128,1024]{1,0:T(8,128)(2,1)S(1)} collective-permute-done((bf16[128,1024]{1,0:T(8,128)(2,1)S(1)}, bf16[128,1024]{1,0:T(8,128)(2,1)S(1)}, u32[]{:S(2)}, u32[]{:S(2)}) %collective-permute-start.15) | collective-permute-done | bytes 262176 | tf_op jit(solution)/shard_map/ppermute | solution.py:121
  125.8 28.0 %collective-permute-done.11 = bf16[64,4096]{1,0:T(8,128)(2,1)S(1)} collective-permute-done((bf16[64,4096]{1,0:T(8,128)(2,1)S(1)}, bf16[64,4096]{1,0:T(8,128)(2,1)S(1)}, u32[]{:S(2)}, u32[]{:S(2)}) %collective-permute-start.11) | collective-permute-done | bytes 524320 | tf_op jit(solution)/shard_map/ppermute | solution.py:121
  155.3 10.9 %assemble.4 = bf16[1024,4224]{1,0:T(8,128)(2,1)} custom-call(s32[8]{0:T(128)} %dynamic-slice_bitcast_fusion.order, bf16[128,4224]{1,0:T(8,128)(2,1)} %copy-done.16, bf16[128,4224]{1,0:T(8,128)(2,1)} %copy-done.24, bf16[256,4224]{1,0:T(8,128)(2,1)} %copy-done.29, bf16[512,4224]{1,0:T(8,128)(2,1)} %collective-permute-done.4.refs_3_), custom_call_target="tpu_custom_call" | custom-call | tf_op jit(solution)/shard_map/assemble/pallas_call | solution.py:104
  185.0 15.7 %collective-permute-done.17.refs_1_ = bf16[512,1024]{1,0:T(8,128)(2,1)S(1)} collective-permute-done((bf16[512,1024]{1,0:T(8,128)(2,1)S(1)}, bf16[512,1024]{1,0:T(8,128)(2,1)S(1)}, u32[]{:S(2)}, u32[]{:S(2)}) %collective-permute-start.17) | collective-permute-done | bytes 1048608 | tf_op jit(solution)/shard_map/ppermute | solution.py:127
  204.8 18.4 %collective-permute-done.7.refs_1_ = bf16[128,4096]{1,0:T(8,128)(2,1)S(1)} collective-permute-done((bf16[128,4096]{1,0:T(8,128)(2,1)S(1)}, bf16[128,4096]{1,0:T(8,128)(2,1)S(1)}, u32[]{:S(2)}, u32[]{:S(2)}) %collective-permute-start.7) | collective-permute-done | bytes 1048608 | tf_op jit(solution)/shard_map/ppermute | solution.py:127
  244.6 6.7 collective-permute-start.19
  260.3 13.2 %collective-permute-start.9 = (bf16[512,4096]{1,0:T(8,128)(2,1)}, bf16[512,4096]{1,0:T(8,128)(2,1)}, u32[]{:S(2)}, u32[]{:S(2)}) collective-permute-start(bf16[512,4096]{1,0:T(8,128)(2,1)} %pad_maximum_fusion.1), channel_id=1, source_target_pairs={{0,4},{1,5},{2,6},{3,7},{4,0},{5,1},{6,2},{7,3},{8,12},{9,13},{10,... | collective-permute-start | bytes 12582920 | tf_op jit(solution)/shard_map/ppermute | solution.py:130
  293.2 10.9 %assemble.6 = bf16[1024,4096]{1,0:T(8,128)(2,1)} custom-call(s32[8]{0:T(128)} %dynamic-slice_bitcast_fusion.order, bf16[128,4096]{1,0:T(8,128)(2,1)} %copy-done.19, bf16[128,4096]{1,0:T(8,128)(2,1)} %collective-permute-done.12.refs_1_, bf16[256,4096]{1,0:T(8,128)(2,1)} %collective-permute-done.13.refs_2_, bf16[512,4096]{1,0:T(8,128)(2,1)} %collective-permute-done.14.refs_3_), custom_call_target="tpu_custom_call" | custom-call | tf_op jit(solution)/shard_map/assemble/pallas_call | solution.py:104
  304.1 10.8 %assemble.7 = bf16[4096,1024]{1,0:T(8,128)(2,1)} custom-call(s32[8]{0:T(128)} %dynamic-slice_bitcast_fusion.order, bf16[512,1024]{1,0:T(8,128)(2,1)} %copy-done.20, bf16[512,1024]{1,0:T(8,128)(2,1)} %copy-done.25, bf16[1024,1024]{1,0:T(8,128)(2,1)} %collective-permute-done.18.refs_2_, bf16[2048,1024]{1,0:T(8,128)(2,1)} %collective-permute-done.19.refs_3_), custom_call_target="tpu_custom_call" | custom-call | tf_op jit(solution)/shard_map/assemble/pallas_call | solution.py:104
  314.9 10.9 %assemble.5 = bf16[1024,4096]{1,0:T(8,128)(2,1)} custom-call(s32[8]{0:T(128)} %dynamic-slice_bitcast_fusion.order, bf16[128,4096]{1,0:T(8,128)(2,1)} %copy-done.21, bf16[128,4096]{1,0:T(8,128)(2,1)} %copy-done.27, bf16[256,4096]{1,0:T(8,128)(2,1)} %collective-permute-done.8.refs_2_, bf16[512,4096]{1,0:T(8,128)(2,1)} %collective-permute-done.9.refs_3_), custom_call_target="tpu_custom_call" | custom-call | tf_op jit(solution)/shard_map/assemble/pallas_call | solution.py:104
  325.9 10.3 fusion.124
  336.1 6.0 to_slots.4
  346.1 6.6 copy.72
  352.7 20.9 %all-gather.5.cloned.1.call-done = bf16[2048,1024]{1,0:T(8,128)(2,1)} async-done(((bf16[512,1024]{1,0:T(8,128)(2,1)}), bf16[2048,1024]{1,0:T(8,128)(2,1)}) %all-gather.5.cloned.1.call-update) | async-done | bytes 4194320 | tf_op jit(solution)/shard_map/all_gather | solution.py:272
  373.6 6.5 copy.71
  380.2 146.2 %while.28 = (s32[]{:T(128)}, f32[1,16,512]{2,1,0:T(8,128)S(1)}, f32[1,16,512]{2,1,0:T(8,128)S(1)}, f32[1,512,16,64]{1,3,2,0:T(8,128)}, s32[8]{0:T(128)S(1)}, /*i...) while((s32[]{:T(128)}, f32[1,16,512]{2,1,0:T(8,128)S(1)}, ...), condition=%wide.region_5.6_spmd.clone, body=%wide.region_2.5_spmd.clone.sunk | while | flops 565756416 | bytes 67634408 | solution.py:306
  388.6 7.0 bitcast_add_fusion.7
  406.3 7.6 bitcast_add_fusion.7
  424.6 7.6 bitcast_add_fusion.7
  443.0 7.6 bitcast_add_fusion.7
  461.3 7.6 bitcast_add_fusion.7
  479.6 7.6 bitcast_add_fusion.7
  498.0 7.6 bitcast_add_fusion.7
  516.3 7.6 bitcast_add_fusion.7
  534.4 6.1 to_slots.6
  540.4 10.0 fusion.130
  550.4 15.3 %multiply_convert_fusion.2 = (bf16[512,4096]{1,0:T(8,128)(2,1)S(1)}, bf16[512,4096]{1,0:T(8,128)(2,1)S(1)}, bf16[512,4096]{1,0:T(8,128)(2,1)}) fusion(f32[512,4096]{1,0:T(8,128)} %fusion.124, f32[512,4096]{1,0:T(8,128)} %fusion.130, bf16[512,1024]{1,0:T(8,128)(2,1)S(1)} %copy-done.46, bf16[1024,4096]{1,0:T(8,128)(2,1)} %assemble.5), kind=kOutput, calls=%fused_computation.44 | convolution fusion | flops 4326424576 | bytes 38797312 | tf_op jit(solution)/shard_map/dot_general | solution.py:314
  565.7 9.9 fusion.131
  575.7 8.6 multiply_reduce_fusion
  599.6 139.1 %while.29 = (s32[]{:T(128)}, f32[1,512,16,64]{1,3,2,0:T(8,128)}, bf16[1,2048,2048]{1,2,0:T(8,128)(2,1)}, s32[8]{0:T(128)S(1)}, bf16[1,2048,1024]{1,2,0:T(8,128)(...) while((s32[]{:T(128)}, f32[1,512,16,64]{1,3,2,0:T(8,128)}, ...), condition=%wide.region_12.13_spmd.clone, body=%wide.region_11.12_spmd.clone.sunk | while | flops 1367343616 | bytes 69829632 | solution.py:406
  738.8 7.7 to_slots.7
  746.5 6.1 convolution_convert_fusion.3
  757.7 8.3 fusion.76
  767.3 6.2 to_slots.5
  841.9 27.3 %collective-permute-done.36 = bf16[256,4096]{1,0:T(8,128)(2,1)} collective-permute-done((bf16[256,4096]{1,0:T(8,128)(2,1)}, bf16[256,4096]{1,0:T(8,128)(2,1)}, u32[]{:S(2)}, u32[]{:S(2)}) %collective-permute-start.36) | collective-permute-done | bytes 2097184 | tf_op jit(solution)/shard_map/ppermute | solution.py:176
  874.2 28.5 %collective-permute-done.31 = bf16[256,4096]{1,0:T(8,128)(2,1)S(1)} collective-permute-done((bf16[256,4096]{1,0:T(8,128)(2,1)}, bf16[256,4096]{1,0:T(8,128)(2,1)S(1)}, u32[]{:S(2)}, u32[]{:S(2)}) %collective-permute-start.31) | collective-permute-done | bytes 2097184 | tf_op jit(solution)/shard_map/ppermute | solution.py:176
  909.3 9.5 collective-permute-done.32
  921.9 29.9 %collective-permute-done.43 = bf16[256,1024]{1,0:T(8,128)(2,1)S(1)} collective-permute-done((bf16[256,1024]{1,0:T(8,128)(2,1)S(1)}, bf16[256,1024]{1,0:T(8,128)(2,1)S(1)}, u32[]{:S(2)}, u32[]{:S(2)}) %collective-permute-start.43) | collective-permute-done | bytes 524320 | tf_op jit(solution)/shard_map/ppermute | solution.py:186
  952.9 10.2 collective-permute-done.38
  969.1 6.0 convolution_convert_fusion.2
  978.6 7.0 collective-permute-done.39
  1007.9 9.8 collective-permute-done.21
  1039.1 13.7 %collective-permute-done.23 = bf16[64,3072]{1,0:T(8,128)(2,1)S(1)} collective-permute-done((bf16[64,3072]{1,0:T(8,128)(2,1)}, bf16[64,3072]{1,0:T(8,128)(2,1)S(1)}, u32[]{:S(2)}, u32[]{:S(2)}) %collective-permute-start.23) | collective-permute-done | bytes 393248 | tf_op jit(solution)/shard_map/ppermute | solution.py:186
  1054.8 6.2 collective-permute-done.24
  (542 shorter events, 496.9 us)
Async XLA Ops:
  7.2 338.9 %all-gather.7.cloned.1.call-start = ((), (), s32[]{:S(2)}) async-start(), calls=%async_computation.4 | async-start | bytes 5242880 | tf_op jit(solution)/shard_map/all_gather | solution.py:273
  11.4 9.6 collective-permute-start
  21.1 26.0 %collective-permute-start.1 = (bf16[64,4224]{1,0:T(8,128)(2,1)S(1)}, bf16[64,4224]{1,0:T(8,128)(2,1)S(1)}, u32[]{:S(2)}, u32[]{:S(2)}) collective-permute-start(bf16[64,4224]{1,0:T(8,128)(2,1)S(1)} %maximum_select_fusion.4), channel_id=1, source_target_pairs={{0,2},{1,3},{2,0},{3,1},{4,6},{5,7},{6,4},{7,5},{8,10},{9,11},{10,... | collective-permute-start | bytes 1622024 | tf_op jit(solution)/shard_map/ppermute | solution.py:121
  47.3 15.2 %collective-permute-start.2 = (bf16[128,4224]{1,0:T(8,128)(2,1)S(1)}, bf16[128,4224]{1,0:T(8,128)(2,1)S(1)}, u32[]{:S(2)}, u32[]{:S(2)}) collective-permute-start(bf16[128,4224]{1,0:T(8,128)(2,1)S(1)} %maximum_select_fusion.refs_0_), channel_id=1, source_target_pairs={{0,16},{1,17},{2,18},{3,19},{4,12},{5,13},{6,14},{7,15},{8,24},{9,... | collective-permute-start | bytes 3244040 | tf_op jit(solution)/shard_map/ppermute | solution.py:127
  62.7 26.8 %collective-permute-start.3 = (bf16[256,4224]{1,0:T(8,128)(2,1)S(1)}, bf16[256,4224]{1,0:T(8,128)(2,1)S(1)}, u32[]{:S(2)}, u32[]{:S(2)}) collective-permute-start(bf16[256,4224]{1,0:T(8,128)(2,1)S(1)} %pad_maximum_fusion.5), channel_id=1, source_target_pairs={{0,8},{1,9},{2,10},{3,11},{4,20},{5,21},{6,22},{7,23},{8,0},{9,1},... | collective-permute-start | bytes 6488072 | tf_op jit(solution)/shard_map/ppermute | solution.py:127
  95.3 60.1 %collective-permute-start.4 = (bf16[512,4224]{1,0:T(8,128)(2,1)}, bf16[512,4224]{1,0:T(8,128)(2,1)}, u32[]{:S(2)}, u32[]{:S(2)}) collective-permute-start(bf16[512,4224]{1,0:T(8,128)(2,1)} %pad_maximum_fusion), channel_id=1, source_target_pairs={{0,4},{1,5},{2,6},{3,7},{4,0},{5,1},{6,2},{7,3},{8,12},{9,13},{10,... | collective-permute-start | bytes 12976136 | tf_op jit(solution)/shard_map/ppermute | solution.py:130
  95.3 9.2 collective-permute-start.10
  95.9 23.9 %collective-permute-start.15 = (bf16[128,1024]{1,0:T(8,128)(2,1)S(1)}, bf16[128,1024]{1,0:T(8,128)(2,1)S(1)}, u32[]{:S(2)}, u32[]{:S(2)}) collective-permute-start(bf16[128,1024]{1,0:T(8,128)(2,1)S(1)} %copy-done.59), channel_id=1, source_target_pairs={{0,1},{1,0},{2,3},{3,2},{4,5},{5,4},{6,7},{7,6},{8,9},{9,8},{10,11... | collective-permute-start | bytes 786440 | tf_op jit(solution)/shard_map/ppermute | solution.py:121
  97.4 27.5 %collective-permute-start.5 = (bf16[32,4096]{1,0:T(8,128)(2,1)S(1)}, bf16[32,4096]{1,0:T(8,128)(2,1)S(1)}, u32[]{:S(2)}, u32[]{:S(2)}) collective-permute-start(bf16[32,4096]{1,0:T(8,128)(2,1)S(1)} %copy-done.60), channel_id=1, source_target_pairs={{0,1},{1,0},{2,3},{3,2},{4,5},{5,4},{6,7},{7,6},{8,9},{9,8},{10,11... | collective-permute-start | bytes 786440 | tf_op jit(solution)/shard_map/ppermute | solution.py:121
  104.6 49.1 %collective-permute-start.11 = (bf16[64,4096]{1,0:T(8,128)(2,1)S(1)}, bf16[64,4096]{1,0:T(8,128)(2,1)S(1)}, u32[]{:S(2)}, u32[]{:S(2)}) collective-permute-start(bf16[64,4096]{1,0:T(8,128)(2,1)S(1)} %maximum_select_fusion.6), channel_id=1, source_target_pairs={{0,2},{1,3},{2,0},{3,1},{4,6},{5,7},{6,4},{7,5},{8,10},{9,11},{10,... | collective-permute-start | bytes 1572872 | tf_op jit(solution)/shard_map/ppermute | solution.py:121
  120.0 54.6 %collective-permute-start.16 = (bf16[256,1024]{1,0:T(8,128)(2,1)S(1)}, bf16[256,1024]{1,0:T(8,128)(2,1)}, u32[]{:S(2)}, u32[]{:S(2)}) collective-permute-start(bf16[256,1024]{1,0:T(8,128)(2,1)S(1)} %maximum_select_fusion.7), channel_id=1, source_target_pairs={{0,2},{1,3},{2,0},{3,1},{4,6},{5,7},{6,4},{7,5},{8,10},{9,11},{10,... | collective-permute-start | bytes 1572872 | tf_op jit(solution)/shard_map/ppermute | solution.py:121
  125.8 51.6 %collective-permute-start.6 = (bf16[64,4096]{1,0:T(8,128)(2,1)}, bf16[64,4096]{1,0:T(8,128)(2,1)}, u32[]{:S(2)}, u32[]{:S(2)}) collective-permute-start(bf16[64,4096]{1,0:T(8,128)(2,1)} %maximum_select_fusion.5), channel_id=1, source_target_pairs={{0,2},{1,3},{2,0},{3,1},{4,6},{5,7},{6,4},{7,5},{8,10},{9,11},{10,... | collective-permute-start | bytes 1572872 | tf_op jit(solution)/shard_map/ppermute | solution.py:121
  154.0 26.7 %collective-permute-start.12 = (bf16[128,4096]{1,0:T(8,128)(2,1)S(1)}, bf16[128,4096]{1,0:T(8,128)(2,1)}, u32[]{:S(2)}, u32[]{:S(2)}) collective-permute-start(bf16[128,4096]{1,0:T(8,128)(2,1)S(1)} %maximum_select_fusion.2.refs_0_), channel_id=1, source_target_pairs={{0,16},{1,17},{2,18},{3,19},{4,12},{5,13},{6,14},{7,15},{8,24},{9,... | collective-permute-start | bytes 3145736 | tf_op jit(solution)/shard_map/ppermute | solution.py:127
  174.3 199.3 %all-gather.5.cloned.1.call-start = ((), (), s32[]{:S(2)}) async-start(), calls=%async_computation.3 | async-start | bytes 5242880 | tf_op jit(solution)/shard_map/all_gather | solution.py:272
  176.6 24.1 %collective-permute-start.17 = (bf16[512,1024]{1,0:T(8,128)(2,1)S(1)}, bf16[512,1024]{1,0:T(8,128)(2,1)S(1)}, u32[]{:S(2)}, u32[]{:S(2)}) collective-permute-start(bf16[512,1024]{1,0:T(8,128)(2,1)S(1)} %maximum_select_fusion.3.refs_0_), channel_id=1, source_target_pairs={{0,16},{1,17},{2,18},{3,19},{4,12},{5,13},{6,14},{7,15},{8,24},{9,... | collective-permute-start | bytes 3145736 | tf_op jit(solution)/shard_map/ppermute | solution.py:127
  179.4 43.8 %collective-permute-start.7 = (bf16[128,4096]{1,0:T(8,128)(2,1)S(1)}, bf16[128,4096]{1,0:T(8,128)(2,1)S(1)}, u32[]{:S(2)}, u32[]{:S(2)}) collective-permute-start(bf16[128,4096]{1,0:T(8,128)(2,1)S(1)} %maximum_select_fusion.1.refs_0_), channel_id=1, source_target_pairs={{0,16},{1,17},{2,18},{3,19},{4,12},{5,13},{6,14},{7,15},{8,24},{9,... | collective-permute-start | bytes 3145736 | tf_op jit(solution)/shard_map/ppermute | solution.py:127
  183.6 53.7 %collective-permute-start.13 = (bf16[256,4096]{1,0:T(8,128)(2,1)}, bf16[256,4096]{1,0:T(8,128)(2,1)}, u32[]{:S(2)}, u32[]{:S(2)}) collective-permute-start(bf16[256,4096]{1,0:T(8,128)(2,1)} %pad_maximum_fusion.8), channel_id=1, source_target_pairs={{0,8},{1,9},{2,10},{3,11},{4,20},{5,21},{6,22},{7,23},{8,0},{9,1},... | collective-permute-start | bytes 6291464 | tf_op jit(solution)/shard_map/ppermute | solution.py:127
  202.4 38.6 %collective-permute-start.18 = (bf16[1024,1024]{1,0:T(8,128)(2,1)}, bf16[1024,1024]{1,0:T(8,128)(2,1)}, u32[]{:S(2)}, u32[]{:S(2)}) collective-permute-start(bf16[1024,1024]{1,0:T(8,128)(2,1)} %pad_maximum_fusion.9), channel_id=1, source_target_pairs={{0,8},{1,9},{2,10},{3,11},{4,20},{5,21},{6,22},{7,23},{8,0},{9,1},... | collective-permute-start | bytes 6291464 | tf_op jit(solution)/shard_map/ppermute | solution.py:127
  224.9 31.9 %collective-permute-start.8 = (bf16[256,4096]{1,0:T(8,128)(2,1)}, bf16[256,4096]{1,0:T(8,128)(2,1)}, u32[]{:S(2)}, u32[]{:S(2)}) collective-permute-start(bf16[256,4096]{1,0:T(8,128)(2,1)} %pad_maximum_fusion.7), channel_id=1, source_target_pairs={{0,8},{1,9},{2,10},{3,11},{4,20},{5,21},{6,22},{7,23},{8,0},{9,1},... | collective-permute-start | bytes 6291464 | tf_op jit(solution)/shard_map/ppermute | solution.py:127
  241.0 52.2 %collective-permute-start.14 = (bf16[512,4096]{1,0:T(8,128)(2,1)}, bf16[512,4096]{1,0:T(8,128)(2,1)}, u32[]{:S(2)}, u32[]{:S(2)}) collective-permute-start(bf16[512,4096]{1,0:T(8,128)(2,1)} %pad_maximum_fusion.2), channel_id=1, source_target_pairs={{0,4},{1,5},{2,6},{3,7},{4,0},{5,1},{6,2},{7,3},{8,12},{9,13},{10,... | collective-permute-start | bytes 12582920 | tf_op jit(solution)/shard_map/ppermute | solution.py:130
  244.6 59.5 %collective-permute-start.19 = (bf16[2048,1024]{1,0:T(8,128)(2,1)}, bf16[2048,1024]{1,0:T(8,128)(2,1)}, u32[]{:S(2)}, u32[]{:S(2)}) collective-permute-start(bf16[2048,1024]{1,0:T(8,128)(2,1)} %pad_maximum_fusion.3), channel_id=1, source_target_pairs={{0,4},{1,5},{2,6},{3,7},{4,0},{5,1},{6,2},{7,3},{8,12},{9,13},{10,... | collective-permute-start | bytes 12582920 | tf_op jit(solution)/shard_map/ppermute | solution.py:130
  260.3 54.6 %collective-permute-start.9 = (bf16[512,4096]{1,0:T(8,128)(2,1)}, bf16[512,4096]{1,0:T(8,128)(2,1)}, u32[]{:S(2)}, u32[]{:S(2)}) collective-permute-start(bf16[512,4096]{1,0:T(8,128)(2,1)} %pad_maximum_fusion.1), channel_id=1, source_target_pairs={{0,4},{1,5},{2,6},{3,7},{4,0},{5,1},{6,2},{7,3},{8,12},{9,13},{10,... | collective-permute-start | bytes 12582920 | tf_op jit(solution)/shard_map/ppermute | solution.py:130
  292.0 672.1 %reduce-scatter.2.cloned.1.call-start = ((), (), s32[]{:S(2)}) async-start(), calls=%async_computation.2 | async-start | bytes 10485760 | tf_op jit(solution)/shard_map/reduce_scatter | solution.py:408
  752.6 52.2 %collective-permute-start.40 = (bf16[2048,1024]{1,0:T(8,128)(2,1)}, bf16[2048,1024]{1,0:T(8,128)(2,1)}, u32[]{:S(2)}, u32[]{:S(2)}) collective-permute-start(bf16[2048,1024]{1,0:T(8,128)(2,1)} %convolution_convert_fusion.3), channel_id=1, source_target_pairs={{0,4},{1,5},{2,6},{3,7},{4,0},{5,1},{6,2},{7,3},{8,12},{9,13},{10,... | collective-permute-start | bytes 12582920 | tf_op jit(solution)/shard_map/ppermute | solution.py:173
  757.2 53.4 %collective-permute-start.35 = (bf16[512,4096]{1,0:T(8,128)(2,1)}, bf16[512,4096]{1,0:T(8,128)(2,1)}, u32[]{:S(2)}, u32[]{:S(2)}) collective-permute-start(bf16[512,4096]{1,0:T(8,128)(2,1)} %convolution_convert_fusion), channel_id=1, source_target_pairs={{0,4},{1,5},{2,6},{3,7},{4,0},{5,1},{6,2},{7,3},{8,12},{9,13},{10,... | collective-permute-start | bytes 12582920 | tf_op jit(solution)/shard_map/ppermute | solution.py:173
  775.2 12.1 %collective-permute-start.25 = (bf16[512,1024]{1,0:T(8,128)(2,1)S(1)}, bf16[512,1024]{1,0:T(8,128)(2,1)S(1)}, u32[]{:S(2)}, u32[]{:S(2)}) collective-permute-start(bf16[512,1024]{1,0:T(8,128)(2,1)S(1)} %convolution_convert_fusion.4), channel_id=1, source_target_pairs={{0,4},{1,5},{2,6},{3,7},{4,0},{5,1},{6,2},{7,3},{8,12},{9,13},{10,... | collective-permute-start | bytes 3145736 | tf_op jit(solution)/shard_map/ppermute | solution.py:173
  780.1 41.4 %collective-permute-start.30 = (bf16[512,4096]{1,0:T(8,128)(2,1)S(1)}, bf16[512,4096]{1,0:T(8,128)(2,1)S(1)}, u32[]{:S(2)}, u32[]{:S(2)}) collective-permute-start(bf16[512,4096]{1,0:T(8,128)(2,1)S(1)} %convolution_convert_fusion.1), channel_id=1, source_target_pairs={{0,4},{1,5},{2,6},{3,7},{4,0},{5,1},{6,2},{7,3},{8,12},{9,13},{10,... | collective-permute-start | bytes 12582920 | tf_op jit(solution)/shard_map/ppermute | solution.py:173
  787.9 9.2 collective-permute-start.26
  803.9 16.9 %collective-permute-start.28 = (bf16[64,1024]{1,0:T(8,128)(2,1)S(1)}, bf16[64,1024]{1,0:T(8,128)(2,1)S(1)}, u32[]{:S(2)}, u32[]{:S(2)}) collective-permute-start(bf16[64,1024]{1,0:T(8,128)(2,1)S(1)} %broadcast_select_fusion.8), channel_id=1, source_target_pairs={{0,2},{1,3},{2,0},{3,1},{4,6},{5,7},{6,4},{7,5},{8,10},{9,11},{10,... | collective-permute-start | bytes 393224 | tf_op jit(solution)/shard_map/ppermute | solution.py:186
  809.1 26.4 %collective-permute-start.41 = (bf16[1024,1024]{1,0:T(8,128)(2,1)}, bf16[1024,1024]{1,0:T(8,128)(2,1)}, u32[]{:S(2)}, u32[]{:S(2)}) collective-permute-start(bf16[1024,1024]{1,0:T(8,128)(2,1)} %add_convert_fusion.1), channel_id=1, source_target_pairs={{0,8},{1,9},{2,10},{3,11},{4,20},{5,21},{6,22},{7,23},{8,0},{9,1},... | collective-permute-start | bytes 6291464 | tf_op jit(solution)/shard_map/ppermute | solution.py:176
  814.9 54.2 %collective-permute-start.36 = (bf16[256,4096]{1,0:T(8,128)(2,1)}, bf16[256,4096]{1,0:T(8,128)(2,1)}, u32[]{:S(2)}, u32[]{:S(2)}) collective-permute-start(bf16[256,4096]{1,0:T(8,128)(2,1)} %add_convert_fusion.4), channel_id=1, source_target_pairs={{0,8},{1,9},{2,10},{3,11},{4,20},{5,21},{6,22},{7,23},{8,0},{9,1},... | collective-permute-start | bytes 6291464 | tf_op jit(solution)/shard_map/ppermute | solution.py:176
  821.5 10.0 collective-permute-start.29
  824.4 78.3 %collective-permute-start.31 = (bf16[256,4096]{1,0:T(8,128)(2,1)}, bf16[256,4096]{1,0:T(8,128)(2,1)S(1)}, u32[]{:S(2)}, u32[]{:S(2)}) collective-permute-start(bf16[256,4096]{1,0:T(8,128)(2,1)} %add_convert_fusion.7), channel_id=1, source_target_pairs={{0,8},{1,9},{2,10},{3,11},{4,20},{5,21},{6,22},{7,23},{8,0},{9,1},... | collective-permute-start | bytes 6291464 | tf_op jit(solution)/shard_map/ppermute | solution.py:176
  840.3 65.1 %collective-permute-start.42 = (bf16[512,1024]{1,0:T(8,128)(2,1)S(1)}, bf16[512,1024]{1,0:T(8,128)(2,1)S(1)}, u32[]{:S(2)}, u32[]{:S(2)}) collective-permute-start(bf16[512,1024]{1,0:T(8,128)(2,1)S(1)} %slice.387), channel_id=1, source_target_pairs={{0,16},{1,17},{2,18},{3,19},{4,12},{5,13},{6,14},{7,15},{8,24},{9,... | collective-permute-start | bytes 3145736 | tf_op jit(solution)/shard_map/ppermute | solution.py:180
  872.7 35.4 %collective-permute-start.37 = (bf16[128,4096]{1,0:T(8,128)(2,1)S(1)}, bf16[128,4096]{1,0:T(8,128)(2,1)S(1)}, u32[]{:S(2)}, u32[]{:S(2)}) collective-permute-start(bf16[128,4096]{1,0:T(8,128)(2,1)S(1)} %slice.376), channel_id=1, source_target_pairs={{0,16},{1,17},{2,18},{3,19},{4,12},{5,13},{6,14},{7,15},{8,24},{9,... | collective-permute-start | bytes 3145736 | tf_op jit(solution)/shard_map/ppermute | solution.py:180
  903.9 14.9 %collective-permute-start.32 = (bf16[128,4096]{1,0:T(8,128)(2,1)S(1)}, bf16[128,4096]{1,0:T(8,128)(2,1)S(1)}, u32[]{:S(2)}, u32[]{:S(2)}) collective-permute-start(bf16[128,4096]{1,0:T(8,128)(2,1)S(1)} %slice.368), channel_id=1, source_target_pairs={{0,16},{1,17},{2,18},{3,19},{4,12},{5,13},{6,14},{7,15},{8,24},{9,... | collective-permute-start | bytes 3145736 | tf_op jit(solution)/shard_map/ppermute | solution.py:180
  905.9 45.9 %collective-permute-start.43 = (bf16[256,1024]{1,0:T(8,128)(2,1)S(1)}, bf16[256,1024]{1,0:T(8,128)(2,1)S(1)}, u32[]{:S(2)}, u32[]{:S(2)}) collective-permute-start(bf16[256,1024]{1,0:T(8,128)(2,1)S(1)} %broadcast_select_fusion), channel_id=1, source_target_pairs={{0,2},{1,3},{2,0},{3,1},{4,6},{5,7},{6,4},{7,5},{8,10},{9,11},{10,... | collective-permute-start | bytes 1572872 | tf_op jit(solution)/shard_map/ppermute | solution.py:186
  908.4 54.8 %collective-permute-start.38 = (bf16[64,4096]{1,0:T(8,128)(2,1)S(1)}, bf16[64,4096]{1,0:T(8,128)(2,1)S(1)}, u32[]{:S(2)}, u32[]{:S(2)}) collective-permute-start(bf16[64,4096]{1,0:T(8,128)(2,1)S(1)} %broadcast_select_fusion.1), channel_id=1, source_target_pairs={{0,2},{1,3},{2,0},{3,1},{4,6},{5,7},{6,4},{7,5},{8,10},{9,11},{10,... | collective-permute-start | bytes 1572872 | tf_op jit(solution)/shard_map/ppermute | solution.py:186
  919.8 55.4 %collective-permute-start.33 = (bf16[64,4096]{1,0:T(8,128)(2,1)}, bf16[64,4096]{1,0:T(8,128)(2,1)}, u32[]{:S(2)}, u32[]{:S(2)}) collective-permute-start(bf16[64,4096]{1,0:T(8,128)(2,1)} %broadcast_select_fusion.2), channel_id=1, source_target_pairs={{0,2},{1,3},{2,0},{3,1},{4,6},{5,7},{6,4},{7,5},{8,10},{9,11},{10,... | collective-permute-start | bytes 1572872 | tf_op jit(solution)/shard_map/ppermute | solution.py:186
  952.8 45.0 %collective-permute-start.44 = (bf16[128,1024]{1,0:T(8,128)(2,1)}, bf16[128,1024]{1,0:T(8,128)(2,1)}, u32[]{:S(2)}, u32[]{:S(2)}) collective-permute-start(bf16[128,1024]{1,0:T(8,128)(2,1)} %broadcast_select_fusion.4), channel_id=1, source_target_pairs={{0,1},{1,0},{2,3},{3,2},{4,5},{5,4},{6,7},{7,6},{8,9},{9,8},{10,11... | collective-permute-start | bytes 786440 | tf_op jit(solution)/shard_map/ppermute | solution.py:186
  964.1 21.4 %collective-permute-start.39 = (bf16[32,4096]{1,0:T(8,128)(2,1)}, bf16[32,4096]{1,0:T(8,128)(2,1)}, u32[]{:S(2)}, u32[]{:S(2)}) collective-permute-start(bf16[32,4096]{1,0:T(8,128)(2,1)} %broadcast_select_fusion.5), channel_id=1, source_target_pairs={{0,1},{1,0},{2,3},{3,2},{4,5},{5,4},{6,7},{7,6},{8,9},{9,8},{10,11... | collective-permute-start | bytes 786440 | tf_op jit(solution)/shard_map/ppermute | solution.py:186
  975.1 16.7 %collective-permute-start.20 = (bf16[512,3072]{1,0:T(8,128)(2,1)S(1)}, bf16[512,3072]{1,0:T(8,128)(2,1)S(1)}, u32[]{:S(2)}, u32[]{:S(2)}) collective-permute-start(bf16[512,3072]{1,0:T(8,128)(2,1)S(1)} %convolution_convert_fusion.2), channel_id=1, source_target_pairs={{0,4},{1,5},{2,6},{3,7},{4,0},{5,1},{6,2},{7,3},{8,12},{9,13},{10,... | collective-permute-start | bytes 9437192 | tf_op jit(solution)/shard_map/ppermute | solution.py:173
  976.5 14.4 %collective-permute-start.34 = (bf16[32,4096]{1,0:T(8,128)(2,1)S(1)}, bf16[32,4096]{1,0:T(8,128)(2,1)S(1)}, u32[]{:S(2)}, u32[]{:S(2)}) collective-permute-start(bf16[32,4096]{1,0:T(8,128)(2,1)S(1)} %broadcast_select_fusion.6), channel_id=1, source_target_pairs={{0,1},{1,0},{2,3},{3,2},{4,5},{5,4},{6,7},{7,6},{8,9},{9,8},{10,11... | collective-permute-start | bytes 786440 | tf_op jit(solution)/shard_map/ppermute | solution.py:186
  997.2 20.5 %collective-permute-start.21 = (bf16[256,3072]{1,0:T(8,128)(2,1)S(1)}, bf16[256,3072]{1,0:T(8,128)(2,1)S(1)}, u32[]{:S(2)}, u32[]{:S(2)}) collective-permute-start(bf16[256,3072]{1,0:T(8,128)(2,1)S(1)} %add_convert_fusion.10), channel_id=1, source_target_pairs={{0,8},{1,9},{2,10},{3,11},{4,20},{5,21},{6,22},{7,23},{8,0},{9,1},... | collective-permute-start | bytes 4718600 | tf_op jit(solution)/shard_map/ppermute | solution.py:176
  1019.4 12.4 %collective-permute-start.22 = (bf16[128,3072]{1,0:T(8,128)(2,1)}, bf16[128,3072]{1,0:T(8,128)(2,1)}, u32[]{:S(2)}, u32[]{:S(2)}) collective-permute-start(bf16[128,3072]{1,0:T(8,128)(2,1)} %slice.343), channel_id=1, source_target_pairs={{0,16},{1,17},{2,18},{3,19},{4,12},{5,13},{6,14},{7,15},{8,24},{9,... | collective-permute-start | bytes 2359304 | tf_op jit(solution)/shard_map/ppermute | solution.py:180
  1023.0 15.4 %all-to-all-start = ((f32[32,1,128]{2,1,0:T(1,128)}), f32[32,1,128]{2,1,0:T(1,128)}, u32[]{:S(2)}, u32[]{:S(2)}) async-start(f32[32,1,128]{2,1,0:T(1,128)} %bitcast.31), calls=%async_computation.1 | async-start | bytes 32768 | tf_op jit(solution)/shard_map/all_to_all | solution.py:198
  1035.1 17.7 %collective-permute-start.23 = (bf16[64,3072]{1,0:T(8,128)(2,1)}, bf16[64,3072]{1,0:T(8,128)(2,1)S(1)}, u32[]{:S(2)}, u32[]{:S(2)}) collective-permute-start(bf16[64,3072]{1,0:T(8,128)(2,1)} %broadcast_select_fusion.3), channel_id=1, source_target_pairs={{0,2},{1,3},{2,0},{3,1},{4,6},{5,7},{6,4},{7,5},{8,10},{9,11},{10,... | collective-permute-start | bytes 1179656 | tf_op jit(solution)/shard_map/ppermute | solution.py:186
  1054.1 6.9 collective-permute-start.24
  (92 other events, 1220.9 us)
Sparse Core Ops, SparseCore 0:
  174.4 81.3 all-gather.6
  292.2 81.3 all-gather.4
  738.9 147.2 reduce-scatter.1

commit v2 on v1

v2 whole, which is shorter than its diff:
```python
import functools
import math

import numpy as np

import jax
import jax.numpy as jnp
from jax import lax
from jax.experimental import pallas as pl
from jax.experimental.pallas import tpu as pltpu
from jax.sharding import PartitionSpec as P

H = 16
HD = 64
L = 2048


epsilon = 1e-05
masked_score = -1e30


def layer_norm(values, gain, shift):
    centre = values - jnp.mean(values, axis=-1, keepdims=True)
    spread = jnp.mean(centre * centre, axis=-1, keepdims=True)
    return centre * lax.rsqrt(spread + epsilon) * gain + shift


def rotary_tables(positions):
    half = HD // 2
    turns = jnp.arange(2 * HD, dtype=jnp.int32) % half
    freqs = jnp.exp(turns.astype(jnp.float32) * (-2.0 * math.log(10000.0) / HD))
    angles = positions.astype(jnp.float32)[:, None] * freqs[None, :]
    return (jnp.cos(angles), jnp.sin(angles))


AXES = ("dp", "ctx")
BF = jnp.bfloat16


class Plan:
    def __init__(self, mesh):
        self.dp, self.ctx = mesh.shape["dp"], mesh.shape["ctx"]
        self.stages = self.dp.bit_length() - 2
        self.ctx_bits = self.ctx.bit_length() - 1
        orders = (list(range(1, self.stages + 1)), list(range(self.stages, 0, -1)))
        self.core = self.pairs(lambda d, z: (d ^ 1, z))
        self.stage = [
            self.pairs(lambda d, z, t=t: (d ^ (1 << orders[d & 1][t]), z)) for t in range(self.stages)
        ]
        self.across = [self.pairs(lambda d, z, k=k: (d, z ^ k)) for k in range(self.ctx)]
        half = self.dp // 2
        table = np.zeros((self.dp, self.dp), np.int32)
        for d in range(self.dp):
            for j in range(self.dp):
                owner = d ^ 1 if j >= half else d
                block = owner
                for t in range(self.stages):
                    if (j % half) >> (self.stages - 1 - t) & 1:
                        block ^= 1 << orders[owner & 1][t]
                table[d, j] = block
        self.table = table

    def pairs(self, target):
        found = []
        for d in range(self.dp):
            for z in range(self.ctx):
                other, place = target(d, z)
                found.append((d * self.ctx + z, other * self.ctx + place))
        return found

    def slots(self):
        return jnp.asarray(self.table)[lax.axis_index("dp")]


def assemble(slots, pieces, rows):
    blocks = slots.shape[0]
    width = pieces[0].shape[1]
    sizes = [piece.shape[0] // rows for piece in pieces]
    starts = [sum(sizes[:i]) for i in range(len(sizes))]

    def body(order, *refs):
        slot = pl.program_id(0)
        out = refs[-1]
        for piece, start, size in zip(refs, starts, sizes):

            @pl.when((slot >= start) & (slot < start + size))
            def _(piece=piece):
                out[...] = piece[...]

    specs = [
        pl.BlockSpec(
            (rows, width),
            lambda j, order, start=start, size=size: (jnp.clip(j - start, 0, size - 1), 0),
        )
        for start, size in zip(starts, sizes)
    ]
    return pl.pallas_call(
        body,
        out_shape=jax.ShapeDtypeStruct((blocks * rows, width), pieces[0].dtype),
        grid_spec=pltpu.PrefetchScalarGridSpec(
            num_scalar_prefetch=1,
            grid=(blocks,),
            in_specs=specs,
            out_specs=pl.BlockSpec((rows, width), lambda j, order: (order[j], 0)),
        ),
        name="assemble",
    )(slots, *pieces)


def tie(values, others):
    leaves, tree = jax.tree.flatten((values, others))
    return jax.tree.unflatten(tree, lax.optimization_barrier(leaves))


class Chain:
    def __init__(self, steps):
        self.steps = steps
        self.flying, self.sent = next(steps)
        self.done = False
        self.value = None

    def land(self, came):
        if self.done:
            return
        try:
            self.flying, self.sent = self.steps.send(came)
        except StopIteration as stop:
            self.flying, self.sent, self.done, self.value = [], [], True, stop.value


def step(main, *chains):
    main, came = tie(main, [chain.flying for chain in chains])
    for chain, arrays in zip(chains, came):
        chain.land(arrays)
    return tie(main, [chain.sent for chain in chains])[0]


def begin(main, steps):
    chain = Chain(steps)
    return tie(main, chain.sent)[0], chain


def finish(main, *chains):
    while not all(chain.done for chain in chains):
        main = step(main, *chains)
    return main


def gather_steps(plan, shard):
    place = lax.axis_index("ctx")
    blocks = yield (
        [lax.ppermute(shard, AXES, plan.across[k]) for k in range(1, plan.ctx)],
        [shard],
    )
    blocks = [shard, *blocks]
    for bit in range(plan.ctx_bits):
        upper = (place >> bit) & 1 == 1
        blocks = [
            jnp.where(upper, jnp.concatenate([b, a]), jnp.concatenate([a, b]))
            for a, b in zip(blocks[::2], blocks[1::2])
        ]
    run = blocks[0]
    pieces = [run]
    for pairs in reversed(plan.stage):
        (other,) = yield [lax.ppermute(run, AXES, pairs)], [run]
        pieces.append(other)
        run = jnp.concatenate([run, other])
    (other,) = yield [lax.ppermute(run, AXES, plan.core)], [run]
    pieces.append(other)
    return run, pieces


def sum_steps(plan, product):
    place = lax.axis_index("ctx")
    half = plan.dp // 2

    def total(a, b):
        return (a.astype(jnp.float32) + b.astype(jnp.float32)).astype(BF)

    send = product(half, plan.dp)
    (other,) = yield [lax.ppermute(send, AXES, plan.core)], [send]
    rows = other.shape[0] // half
    size = half // 2
    send = product(size, half, other[size * rows :])
    flying = [lax.ppermute(send, AXES, plan.stage[0])]
    keep = product(0, size, other[: size * rows])
    (other,) = yield flying, [send, keep]
    held = total(keep, other)
    for pairs in plan.stage[1:]:
        size //= 2
        send = held[size * rows :]
        (other,) = yield [lax.ppermute(send, AXES, pairs)], [send]
        held = total(held[: size * rows], other)
    cut = held.shape[0] // plan.ctx
    parts = [lax.dynamic_slice_in_dim(held, (place ^ k) * cut, cut, 0) for k in range(plan.ctx)]
    others = yield (
        [lax.ppermute(parts[k], AXES, plan.across[k]) for k in range(1, plan.ctx)],
        parts[1:],
    )
    return sum((other.astype(jnp.float32) for other in others), parts[0].astype(jnp.float32))


def sum_vectors(plan, vectors):
    count = plan.dp * plan.ctx
    packed = jnp.stack(vectors).reshape(len(vectors), count, -1).transpose(1, 0, 2)
    part = packed.shape[2]
    packed = packed.reshape(count, len(vectors) * part)
    came = lax.all_to_all(packed, AXES, split_axis=0, concat_axis=0, tiled=True)
    whole = jnp.sum(came, axis=0)
    return [whole[i * part : (i + 1) * part] for i in range(len(vectors))]


def nt(a, b):
    return lax.dot_general(a, b, (((1,), (1,)), ((), ())), preferred_element_type=jnp.float32)


def turn(values, cosine, sine):
    lane = lax.broadcasted_iota(jnp.int32, values.shape, 1)
    ahead = pltpu.roll(values, 128 - HD // 2, 1)
    behind = pltpu.roll(values, HD // 2, 1)
    turned = jnp.where(lane % HD < HD // 2, -ahead, behind)
    return values * cosine + turned * sine


def head_parts(values):
    lane = lax.broadcasted_iota(jnp.int32, values.shape, 1)
    zero = jnp.zeros_like(values)
    return [jnp.where(lane < HD, values, zero), jnp.where(lane < HD, zero, values)]


def product_of(plan, groups):
    def product(start, end, add=None):
        columns = []
        low = 0
        for terms in groups:
            found = 0.0
            for flipped, right in terms:
                rows = flipped.shape[0] // plan.dp
                part = flipped[start * rows : end * rows]
                found = found + jnp.dot(part, right, preferred_element_type=jnp.float32)
            high = low + found.shape[1]
            if add is not None:
                found = found + add[:, low:high].astype(jnp.float32)
            columns.append(found.astype(BF))
            low = high
        return columns[0] if len(columns) == 1 else jnp.concatenate(columns, axis=1)

    return product


def whole(shape):
    return pl.BlockSpec(shape, lambda *at: (0,) * len(shape))


def call(body, order, grid, ins, outs, operands, name, flops, scratch=(), transcendentals=0):
    size = lambda a: math.prod(a.shape) * jnp.dtype(a.dtype).itemsize
    out_shape = [shape for spec, shape in outs]
    return pl.pallas_call(
        body,
        out_shape=out_shape,
        grid_spec=pltpu.PrefetchScalarGridSpec(
            num_scalar_prefetch=1,
            grid=grid,
            in_specs=ins,
            out_specs=[spec for spec, shape in outs],
            scratch_shapes=list(scratch),
        ),
        cost_estimate=pl.CostEstimate(
            flops=flops,
            bytes_accessed=sum(size(a) for a in [*operands, *out_shape]),
            transcendentals=transcendentals,
        ),
        name=name,
    )(order, *operands)


def array(shape, dtype=BF):
    return jax.ShapeDtypeStruct(shape, dtype)


def spread(order, source, target, rows):
    blocks = order.shape[0]
    part = source.shape[1] // blocks
    for j in range(blocks):
        at = pl.multiple_of(order[j] * part, 128)
        target[rows, j * part : (j + 1) * part] = source[rows, pl.ds(at, part)].astype(target.dtype)


def collect(order, source, target):
    blocks = order.shape[0]
    part = source.shape[1] // blocks
    for j in range(blocks):
        at = pl.multiple_of(order[j] * part, 128)
        target[:, pl.ds(at, part)] = source[:, j * part : (j + 1) * part].astype(target.dtype)


def by_pieces(left, pieces):
    found, low = 0.0, 0
    for piece in pieces:
        high = low + piece.shape[0]
        found = found + jnp.dot(left[:, low:high], piece[...], preferred_element_type=jnp.float32)
        low = high
    return found


def project(order, source, gain, shift, mixed, cosine, sine, block):
    rows, width = source.shape
    tile = 512
    tiles = width // tile
    skip = 0 if block == 0 else tiles
    count = len(mixed)
    scale = 1.0 / math.sqrt(HD)

    def body(order_ref, source_ref, gain_ref, shift_ref, cos_ref, sin_ref, *refs):
        weights = refs[:count]
        outs, normed = refs[count:-1], refs[-1]
        at = pl.program_id(0) + skip

        @pl.when(at == skip)
        def _():
            spread(order_ref, source_ref, normed, slice(None))
            chunk = math.gcd(rows, 128)

            def one(i, unused):
                here = pl.ds(pl.multiple_of(i * chunk, chunk), chunk)
                found = normed[here, :].astype(jnp.float32)
                normed[here, :] = layer_norm(found, gain_ref[...], shift_ref[...]).astype(BF)
                return unused

            lax.fori_loop(0, rows // chunk, one, 0)
            outs[0][...] = normed[...].T

        found = by_pieces(normed, weights)

        def turned(c):
            return turn(found[:, c : c + 128], cos_ref[...], sin_ref[...]).astype(BF)

        if block == 0:

            @pl.when(at < tiles)
            def _():
                for c in range(0, tile, 128):
                    outs[1][:, c : c + 128] = (turned(c).astype(jnp.float32) * scale).astype(BF)

        @pl.when(at >= tiles)
        def _():
            for c in range(0, tile, 256):
                outs[-1][:, c : c + 128] = turned(c)
                outs[-1][:, c + 128 : c + 256] = found[:, c + 128 : c + 256].astype(BF)

    table = pl.BlockSpec((rows, 128), lambda j, order: (block, 0))
    outs = [(whole((width, rows)), array((width, rows)))]
    if block == 0:
        outs.append(
            (
                pl.BlockSpec((rows, tile), lambda j, order: (0, jnp.minimum(j, tiles - 1))),
                array((rows, width)),
            )
        )
    outs.append(
        (
            pl.BlockSpec((rows, tile), lambda j, order: (0, jnp.maximum(j + skip - tiles, 0))),
            array((rows, 2 * width)),
        )
    )
    return call(
        body,
        order,
        (3 * tiles - skip,),
        [whole((rows, width)), whole((1, width)), whole((1, width)), table, table]
        + [
            pl.BlockSpec((piece.shape[0], tile), lambda j, order: (0, j + skip)) for piece in mixed
        ],
        outs,
        (source, gain[None, :], shift[None, :], cosine, sine, *mixed),
        f"project{block}",
        2 * rows * width * width * (2 if block else 3),
        scratch=[pltpu.VMEM((rows, width), BF)],
    )


def attend(order, valid, block, state, last, queries, both):
    rows, width = queries.shape
    pairs = width // 128
    first = state is None

    def body(order_ref, valid_ref, q_ref, kv_ref, *refs):
        outs = refs if first else refs[2:]
        parts = head_parts(q_ref[...])
        keys = kv_ref[:, :128]
        flipped = kv_ref[:, 128:].T
        tops, masses, sums = [], [], []
        for head in range(2):
            scores = nt(keys, parts[head])
            seat = lax.broadcasted_iota(jnp.int32, scores.shape, 0)
            scores = jnp.where(seat < valid_ref[block], scores, masked_score)
            top = jnp.max(scores, axis=0, keepdims=True)
            if not first:
                top = jnp.maximum(top, refs[0][0, head : head + 1, :])
            expo = jnp.exp(scores - top)
            mass = jnp.sum(expo, axis=0, keepdims=True)
            held = jnp.dot(
                flipped[head * HD : (head + 1) * HD, :],
                expo.astype(BF),
                preferred_element_type=jnp.float32,
            )
            if not first:
                factor = jnp.exp(refs[0][0, head : head + 1, :] - top)
                mass = mass + refs[0][0, head + 2 : head + 3, :] * factor
                held = held + refs[1][head * HD : (head + 1) * HD, :] * factor
            tops.append(top)
            masses.append(mass)
            sums.append(held)
        blank = jnp.zeros((4, rows), jnp.float32)
        if last:
            found = jnp.concatenate([s / m for s, m in zip(sums, masses)], axis=0)
            outs[1][...] = found.astype(BF)
            found = found.T
            outs[0][...] = found.astype(BF)
            outs[2][...] = found
            lse = [t + jnp.log(m) for t, m in zip(tops, masses)]
            outs[3][...] = jnp.concatenate(lse + masses + [blank], axis=0)[None]
        else:
            outs[0][...] = jnp.concatenate(tops + masses + [blank], axis=0)[None]
            outs[1][...] = jnp.concatenate(sums, axis=0)

    column = pl.BlockSpec((rows, 128), lambda j, order: (0, j))
    stats = pl.BlockSpec((1, 8, rows), lambda j, order: (j, 0, 0))
    carried = pl.BlockSpec((128, rows), lambda j, order: (j, 0))
    stats_shape = array((pairs, 8, rows), jnp.float32)
    if last:
        outs = [
            (column, array((rows, width))),
            (carried, array((width, rows))),
            (column, array((rows, width), jnp.float32)),
            (stats, stats_shape),
        ]
    else:
        outs = [(stats, stats_shape), (carried, array((width, rows), jnp.float32))]
    return call(
        body,
        order,
        (pairs,),
        [
            pl.BlockSpec(memory_space=pltpu.SMEM),
            pl.BlockSpec((rows, 128), lambda j, order: (0, order[j])),
            pl.BlockSpec((rows, 256), lambda j, order: (0, order[j])),
        ]
        + ([] if first else [stats, carried]),
        outs,
        (valid, queries, both, *(() if first else state)),
        f"attend{block}",
        16 * rows * rows * width,
        transcendentals=16 * rows * rows,
    )


def attend_back(order, valid, block, held, last, queries, both, go, attended, lse, cosine, sine):
    rows, width = queries.shape
    pairs = width // 128
    scale = 1.0 / math.sqrt(HD)
    first = held is None

    def body(order_ref, valid_ref, q_ref, kv_ref, go_ref, o_ref, lse_ref, cos_ref, sin_ref, *refs):
        dq_ref, dkv_ref = refs[-2:]
        keys = kv_ref[:, :128]
        values = kv_ref[:, 128:]
        go_all = go_ref[...]
        q_parts = head_parts(q_ref[...])
        go_parts = head_parts(go_all)
        crossed = (go_all.astype(jnp.float32) * o_ref[...]).T
        flipped = keys.T
        dk = jnp.zeros((rows, 128), jnp.float32)
        dv = jnp.zeros((rows, 128), jnp.float32)
        dq = []
        for head in range(2):
            delta = jnp.sum(crossed[head * HD : (head + 1) * HD, :], axis=0, keepdims=True)
            scores = nt(keys, q_parts[head])
            seat = lax.broadcasted_iota(jnp.int32, scores.shape, 0)
            scores = jnp.where(seat < valid_ref[block], scores, masked_score)
            probs = jnp.exp(scores - lse_ref[0, head : head + 1, :])
            grad_probs = nt(values, go_parts[head])
            grad_scores = (probs * (grad_probs - delta)).astype(BF)
            dv = dv + jnp.dot(probs.astype(BF), go_parts[head], preferred_element_type=jnp.float32)
            dk = dk + jnp.dot(grad_scores, q_parts[head], preferred_element_type=jnp.float32)
            dq.append(
                jnp.dot(
                    flipped[head * HD : (head + 1) * HD, :],
                    grad_scores,
                    preferred_element_type=jnp.float32,
                )
            )
        dkv_ref[:, :128] = turn(dk, cos_ref[...], -sin_ref[...]).astype(BF)
        dkv_ref[:, 128:] = dv.astype(BF)
        found = jnp.concatenate(dq, axis=0)
        if not first:
            found = found + refs[0][...]
        if last:
            dq_ref[...] = turn(found.T * scale, cos_ref[...], -sin_ref[...]).astype(BF)
        else:
            dq_ref[...] = found

    column = pl.BlockSpec((rows, 128), lambda j, order: (0, j))
    natural = pl.BlockSpec((rows, 128), lambda j, order: (0, order[j]))
    natural_both = pl.BlockSpec((rows, 256), lambda j, order: (0, order[j]))
    carried = pl.BlockSpec((128, rows), lambda j, order: (j, 0))
    table = pl.BlockSpec((rows, 128), lambda j, order: (block, 0))
    return call(
        body,
        order,
        (pairs,),
        [
            pl.BlockSpec(memory_space=pltpu.SMEM),
            natural,
            natural_both,
            column,
            column,
            pl.BlockSpec((1, 8, rows), lambda j, order: (j, 0, 0)),
            table,
            table,
        ]
        + ([] if first else [carried]),
        [
            (natural, array((rows, width))) if last else (carried, array((width, rows), jnp.float32)),
            (natural_both, array((rows, 2 * width))),
        ],
        (valid, queries, both, go, attended, lse, cosine, sine, *(() if first else (held,))),
        f"attend_back{block}",
        40 * rows * rows * width,
        transcendentals=16 * rows * rows,
    )


def middle(order, attended, mixed, tokens, gain, shift):
    rows, width = tokens.shape
    count = len(mixed)
    chunk = math.gcd(rows, 256)

    def body(order_ref, o_ref, x_ref, gain_ref, shift_ref, *refs):
        weights = refs[:count]
        resid_ref, two_ref, flipped_ref, held = refs[count:]
        found = x_ref[...].astype(jnp.float32) + by_pieces(o_ref, weights)
        resid_ref[...] = found
        spread(order_ref, resid_ref, held, slice(None))
        two = layer_norm(held[...], gain_ref[...], shift_ref[...]).astype(BF)
        two_ref[...] = two
        flipped_ref[...] = two.T

    line = pl.BlockSpec((chunk, width), lambda i, order: (i, 0))
    return call(
        body,
        order,
        (rows // chunk,),
        [line, line, whole((1, width)), whole((1, width))]
        + [pl.BlockSpec((piece.shape[0], width), lambda i, order: (0, 3)) for piece in mixed],
        [
            (line, array((rows, width), jnp.float32)),
            (line, array((rows, width))),
            (pl.BlockSpec((width, chunk), lambda i, order: (0, i)), array((width, rows))),
        ],
        (attended, tokens, gain[None, :], shift[None, :], *mixed),
        "middle",
        2 * rows * width * width,
        scratch=[pltpu.VMEM((chunk, width), jnp.float32)],
    )


def feed(order, two, pair):
    rows, width = two.shape
    blocks = order.shape[0]
    hidden = pair[0].shape[1] // 2
    part = hidden // blocks
    count = len(pair)

    def body(order_ref, two_ref, *refs):
        gate_ref, up_ref, hidden_ref, flipped_ref = refs[count:]
        found = by_pieces(two_ref, refs[:count])
        gate, up = found[:, :part], found[:, part:]
        made = (gate / (1.0 + jnp.exp(-gate)) * up).astype(BF)
        gate_ref[...] = gate.astype(BF)
        up_ref[...] = up.astype(BF)
        hidden_ref[...] = made
        flipped_ref[...] = made.T

    tile = pl.BlockSpec((rows, part), lambda j, order: (0, j))
    shape = array((rows, hidden))
    return call(
        body,
        order,
        (blocks,),
        [whole((rows, width))]
        + [
            pl.BlockSpec((piece.shape[0], 2 * part), lambda j, order: (0, order[j]))
            for piece in pair
        ],
        [
            (tile, shape),
            (tile, shape),
            (tile, shape),
            (pl.BlockSpec((part, rows), lambda j, order: (j, 0)), array((hidden, rows))),
        ],
        (two, *pair),
        "feed",
        4 * rows * width * hidden,
        transcendentals=rows * hidden,
    )


def feed_back(order, upstream, gate, up, made, resid, pair, down):
    rows, width = upstream.shape
    blocks = order.shape[0]
    hidden = gate.shape[1]
    part = hidden // blocks
    count, downs = len(pair), len(down)
    each = blocks // downs

    def body(order_ref, m_ref, gate_ref, up_ref, made_ref, resid_ref, *refs):
        pairs, lows = refs[:count], refs[count : count + downs]
        out_ref, grads_ref, two_ref, total, result = refs[count + downs :]
        at = pl.program_id(0)

        @pl.when(at == 0)
        def _():
            total[...] = jnp.zeros_like(total)
            result[...] = resid_ref[...]

        def one(low):
            gate_all = gate_ref[...].astype(jnp.float32)
            up_all = up_ref[...].astype(jnp.float32)
            sigma = 1.0 / (1.0 + jnp.exp(-gate_all))
            made_grad = nt(m_ref[...], low[...])
            result[...] += jnp.dot(made_ref[...], low[...], preferred_element_type=jnp.float32)
            gate_grad = made_grad * up_all * sigma * (1.0 + gate_all * (1.0 - sigma))
            grads_ref[:, :part] = gate_grad.astype(BF)
            grads_ref[:, part:] = (made_grad * gate_all * sigma).astype(BF)

        for i in range(downs):

            @pl.when((at >= i * each) & (at < (i + 1) * each))
            def _(i=i):
                one(lows[i])

        grads = grads_ref[...]
        low = 0
        for piece in pairs:
            high = low + piece.shape[0]
            total[:, low:high] += nt(grads, piece[...])
            low = high

        @pl.when(at == blocks - 1)
        def _():
            out_ref[...] = result[...].astype(BF)
            collect(order_ref, total, two_ref)

    tile = pl.BlockSpec((rows, part), lambda j, order: (0, j))
    return call(
        body,
        order,
        (blocks,),
        [whole((rows, width)), tile, tile, tile, whole((rows, width))]
        + [
            pl.BlockSpec((piece.shape[0], 2 * part), lambda j, order: (0, order[j]))
            for piece in pair
        ]
        + [
            pl.BlockSpec(
                (part, width), lambda j, order, i=i: (jnp.clip(j - i * each, 0, each - 1), 0)
            )
            for i in range(downs)
        ],
        [
            (whole((rows, width)), array((rows, width))),
            (
                pl.BlockSpec((rows, 2 * part), lambda j, order: (0, order[j])),
                array((rows, 2 * hidden)),
            ),
            (whole((rows, width)), array((rows, width), jnp.float32)),
        ],
        (upstream, gate, up, made, resid, *pair, *down),
        "feed_back",
        8 * rows * width * hidden,
        scratch=[pltpu.VMEM((rows, width), jnp.float32), pltpu.VMEM((rows, width), jnp.float32)],
        transcendentals=rows * hidden,
    )


def norm_back(values, grads, gain):
    centre = values - jnp.mean(values, axis=-1, keepdims=True)
    scale = lax.rsqrt(jnp.mean(centre * centre, axis=-1, keepdims=True) + epsilon)
    normed = centre * scale
    scaled = grads * gain
    inner = jnp.mean(scaled * normed, axis=-1, keepdims=True)
    found = (scaled - jnp.mean(scaled, axis=-1, keepdims=True) - normed * inner) * scale
    return (
        found,
        jnp.sum(grads * normed, axis=0, keepdims=True),
        jnp.sum(grads, axis=0, keepdims=True),
    )


def middle_back(order, grads, resid, upstream, mixed, gain):
    rows, width = resid.shape
    count = len(mixed)
    chunk = math.gcd(rows, 256)

    def body(order_ref, grads_ref, resid_ref, m_ref, gain_ref, *refs):
        weights = refs[:count]
        y_ref, a_ref, go_ref, edge_ref = refs[count:]

        @pl.when(pl.program_id(0) == 0)
        def _():
            edge_ref[...] = jnp.zeros_like(edge_ref)

        found, gain_grad, shift_grad = norm_back(resid_ref[...], grads_ref[...], gain_ref[...])
        found = m_ref[...].astype(jnp.float32) + found
        edge_ref[0:1, :] += gain_grad
        edge_ref[1:2, :] += shift_grad
        y_ref[...] = found
        a_ref[...] = found.astype(BF)
        low = 0
        for weight in weights:
            high = low + weight.shape[0]
            go_ref[:, low:high] = nt(a_ref[...], weight[...]).astype(BF)
            low = high

    line = pl.BlockSpec((chunk, width), lambda i, order: (i, 0))
    return call(
        body,
        order,
        (rows // chunk,),
        [line, line, line, whole((1, width))]
        + [pl.BlockSpec((piece.shape[0], width), lambda i, order: (0, 3)) for piece in mixed],
        [
            (line, array((rows, width), jnp.float32)),
            (line, array((rows, width))),
            (line, array((rows, width))),
            (whole((8, width)), array((8, width), jnp.float32)),
        ],
        (grads, resid, upstream, gain[None, :], *mixed),
        "middle_back",
        2 * rows * width * width,
    )


def pull(order, dq, both, mixed, block):
    rows, width = both.shape[0], both.shape[1] // 2
    tile = 512
    tiles = width // tile
    count = len(mixed)
    skip = 0 if block == 0 else tiles
    steps = 3 * tiles - skip
    dtype = BF if block else jnp.float32

    def body(order_ref, *refs):
        lefts = refs[: 1 if block else 2]
        weights = refs[len(lefts) : len(lefts) + count]
        out_ref, total = refs[len(lefts) + count :]
        at = pl.program_id(0)

        @pl.when(at == 0)
        def _():
            total[...] = jnp.zeros_like(total)

        def one(left):
            low = 0
            for weight in weights:
                high = low + weight.shape[0]
                total[:, low:high] += nt(left[...], weight[...])
                low = high

        if block:
            one(lefts[0])
        else:

            @pl.when(at < tiles)
            def _():
                one(lefts[0])

            @pl.when(at >= tiles)
            def _():
                one(lefts[1])

        @pl.when(at == steps - 1)
        def _():
            out_ref[...] = total[...].astype(dtype)

    lefts = [] if block else [pl.BlockSpec((rows, tile), lambda j, order: (0, jnp.minimum(j, tiles - 1)))]
    lefts.append(pl.BlockSpec((rows, tile), lambda j, order: (0, jnp.maximum(j + skip - tiles, 0))))
    return call(
        body,
        order,
        (steps,),
        lefts
        + [
            pl.BlockSpec((piece.shape[0], tile), lambda j, order: (0, j + skip)) for piece in mixed
        ],
        [(whole((rows, width)), array((rows, width), dtype))],
        ((both,) if block else (dq, both)) + tuple(mixed),
        f"pull{block}",
        2 * rows * width * width * (2 if block else 3),
        scratch=[pltpu.VMEM((rows, width), jnp.float32)],
    )[0]


def end_back(order, parts, tokens, grads, gain):
    rows, width = tokens.shape
    count = len(parts)
    chunk = math.gcd(rows, 256)

    def body(order_ref, x_ref, y_ref, gain_ref, *refs):
        sources = refs[:count]
        out_ref, edge_ref, held, total = refs[count:]

        @pl.when(pl.program_id(0) == 0)
        def _():
            edge_ref[...] = jnp.zeros_like(edge_ref)

        held[...] = sum(source[...].astype(jnp.float32) for source in sources)
        collect(order_ref, held, total)
        found, gain_grad, shift_grad = norm_back(
            x_ref[...].astype(jnp.float32), total[...], gain_ref[...]
        )
        edge_ref[0:1, :] += gain_grad
        edge_ref[1:2, :] += shift_grad
        out_ref[...] = (y_ref[...] + found).astype(BF)

    line = pl.BlockSpec((chunk, width), lambda i, order: (i, 0))
    return call(
        body,
        order,
        (rows // chunk,),
        [line, line, whole((1, width))] + [line] * count,
        [(line, array((rows, width))), (whole((8, width)), array((8, width), jnp.float32))],
        (tokens, grads, gain[None, :], *parts),
        "end_back",
        0,
        scratch=[pltpu.VMEM((chunk, width), jnp.float32), pltpu.VMEM((chunk, width), jnp.float32)],
    )


def join(first, second, part):
    rows, width = first.shape
    stacked = jnp.stack([first.reshape(rows, -1, part), second.reshape(rows, -1, part)], axis=2)
    return stacked.reshape(rows, 2 * width)


def part_ways(both, part):
    rows, width = both.shape
    cut = both.reshape(rows, -1, 2, part)
    return cut[:, :, 0].reshape(rows, width // 2), cut[:, :, 1].reshape(rows, width // 2)


def shards(
    plan,
    tokens,
    lengths,
    cotangent,
    query_weight,
    key_weight,
    value_weight,
    output_weight,
    gate_weight,
    up_weight,
    down_weight,
    attention_gain,
    attention_shift,
    feed_gain,
    feed_shift,
):
    slots = plan.slots()
    windows, local_len, width = tokens.shape
    rows = windows * local_len
    hidden = gate_weight.shape[1]
    place = lax.axis_index("ctx")
    exact = (width // plan.dp) % 128 == 0
    order = slots if exact else jnp.arange(8, dtype=jnp.int32)
    part = hidden // order.shape[0]

    def pieces_of(chain, shard):
        run, pieces = chain.value
        if exact:
            return [run, pieces[-1]]
        return [assemble(slots, pieces, shard.shape[0] * plan.ctx)]

    def in_slots(flipped):
        if exact:
            return flipped
        cut = flipped.reshape(plan.dp, -1, flipped.shape[1])
        return jnp.take(cut, slots, axis=0).reshape(flipped.shape)

    edge = jnp.stack([attention_gain, attention_shift, feed_gain, feed_shift], axis=1)
    edge = jnp.pad(edge, ((0, 0), (0, 124)))
    both = join(key_weight, value_weight, 128)
    mixed = jnp.concatenate([query_weight, both, output_weight, edge], axis=1)
    mix = Chain(gather_steps(plan, mixed))

    seats = jnp.arange(local_len, dtype=jnp.int32)
    starts = (place ^ jnp.arange(plan.ctx, dtype=jnp.int32)) * local_len
    valid = jnp.clip(lengths[0] - starts, 0, local_len)
    cosine, sine = rotary_tables((starts[:, None] + seats[None, :]).reshape(-1))
    real = (place * local_len + seats < lengths[0])[:, None]
    upstream = jnp.where(real, cotangent.reshape(rows, width), 0)
    own = tokens.reshape(rows, width)

    pair_own = join(gate_weight, up_weight, part)
    pair_own = step(pair_own, mix)
    pair = Chain(gather_steps(plan, pair_own))
    own = step(own, mix)
    own = step(own, mix)
    own = step(own, pair)
    came = {k: lax.ppermute(own, AXES, plan.across[k]) for k in range(1, plan.ctx)}
    own = finish(own, mix)
    mixed_w = pieces_of(mix, mixed)
    cols = jnp.concatenate([piece[:, 4 * width : 4 * width + 4] for piece in mixed_w])
    cols = cols.T.astype(jnp.float32)
    back = jnp.argsort(order)
    natural = cols.reshape(4, order.shape[0], -1)[:, back].reshape(4, width)

    flipped, both = {}, {}
    flipped[0], queries, both[0] = project(order, own, cols[0], cols[1], mixed_w, cosine, sine, 0)
    state = attend(order, valid, 0, None, plan.ctx == 1, queries, both[0])
    down = None
    for k in range(1, plan.ctx):
        state, came[k] = tie(state, came[k])
        if k == 1:
            state = step(state, pair)
        if k == 2:
            down_own, state = tie(down_weight, state)
            down = Chain(gather_steps(plan, down_own))
        if k == 3:
            state = step(state, pair, down)
        flipped[k], both[k] = project(
            order, came[k], cols[0], cols[1], mixed_w, cosine, sine, k
        )
        state = attend(order, valid, k, state, k == plan.ctx - 1, queries, both[k])
    state = step(state, down)
    low, low_flipped, attended, lse = state
    resid, two, two_flipped = middle(order, low, mixed_w, own, cols[2], cols[3])
    two = finish(two, pair)
    two = step(two, down)
    pair_w = pieces_of(pair, pair_own)
    gate, up, made, made_flipped = feed(order, two, pair_w)
    made, down_sum = begin(
        made, sum_steps(plan, product_of(plan, [[(in_slots(made_flipped), upstream)]]))
    )
    made = finish(made, down)
    down_w = pieces_of(down, down_weight)
    output, pair_grads, two_grads = feed_back(
        order, upstream, gate, up, made, resid, pair_w, down_w
    )
    output = output.reshape(windows, local_len, width)

    two_grads = step(two_grads, down_sum)
    two_grads, pair_sum = begin(
        two_grads, sum_steps(plan, product_of(plan, [[(in_slots(two_flipped), pair_grads)]]))
    )
    y_grads, low_grads, go, edge_two = middle_back(
        order, two_grads, resid, upstream, mixed_w, natural[2]
    )
    go = step(go, pair_sum)
    go, output_sum = begin(
        go, sum_steps(plan, product_of(plan, [[(in_slots(low_flipped), low_grads)]]))
    )
    held = None
    grads, sends = {}, []
    for k in reversed(range(plan.ctx)):
        held, grads[k] = attend_back(
            order, valid, k, held, k == 0, queries, both[k], go, attended, lse, cosine, sine
        )
        if k == plan.ctx - 1:
            held = step(held, down_sum, output_sum)
        elif k == plan.ctx - 2:
            held = step(held, down_sum, output_sum, pair_sum)
        elif k:
            held = step(held, down_sum, output_sum, pair_sum)
        else:
            held = step(held, output_sum, pair_sum)
        part_grads = pull(order, held, grads[k], mixed_w, k)
        if k:
            held, part_grads = tie(held, part_grads)
            sends.append(lax.ppermute(part_grads, AXES, plan.across[k]))
    flipped = {k: in_slots(flipped[k]) for k in flipped}
    last = product_of(
        plan, [[(flipped[0], held)], [(flipped[k], grads[k]) for k in range(plan.ctx)]]
    )
    part_grads, last_sum = begin(part_grads, sum_steps(plan, last))
    part_grads = finish(part_grads, down_sum, output_sum, pair_sum)
    part_grads = step(part_grads, last_sum)
    tokens_grad, edge_one = end_back(
        order, [part_grads, *sends], own, y_grads, natural[0]
    )
    vectors = sum_vectors(plan, (edge_one[0], edge_one[1], edge_two[0], edge_two[1]))
    finish((), last_sum)
    gate_grad, up_grad = part_ways(pair_sum.value, part)
    key_grad, value_grad = part_ways(last_sum.value[:, width:], 128)
    return (
        output,
        tokens_grad.reshape(windows, local_len, width),
        last_sum.value[:, :width],
        key_grad,
        value_grad,
        output_sum.value,
        gate_grad,
        up_grad,
        down_sum.value,
        *vectors,
    )


def solution(mesh):
    return jax.shard_map(
        functools.partial(shards, Plan(mesh)),
        mesh=mesh,
        in_specs=(
            P("dp", "ctx", None),
            P("dp"),
            P("dp", "ctx", None),
            P(("dp", "ctx"), None),
            P(("dp", "ctx"), None),
            P(("dp", "ctx"), None),
            P(("dp", "ctx"), None),
            P(("dp", "ctx"), None),
            P(("dp", "ctx"), None),
            P(("dp", "ctx"), None),
            P(("dp", "ctx")),
            P(("dp", "ctx")),
            P(("dp", "ctx")),
            P(("dp", "ctx")),
        ),
        out_specs=(
            P("dp", "ctx", None),
            P("dp", "ctx", None),
            P(("dp", "ctx"), None),
            P(("dp", "ctx"), None),
            P(("dp", "ctx"), None),
            P(("dp", "ctx"), None),
            P(("dp", "ctx"), None),
            P(("dp", "ctx"), None),
            P(("dp", "ctx"), None),
            P(("dp", "ctx")),
            P(("dp", "ctx")),
            P(("dp", "ctx")),
            P(("dp", "ctx")),
        ),
        check_vma=False,
    )
```

time: 1080 us -> 753 us (0.70)
  matrix products: 344 us -> 88.4 us
  Pallas kernels: 69.5 us -> 265 us
  waiting for transfers between devices: 347 us -> 239 us
  other arithmetic: 121 us -> 55.9 us
  local copies, waits for them, and re-layouts: 90.4 us -> 33.4 us
  between operations: 16 us -> 2.44 us
  loops' own time: 11.4 us -> 0 us
  starting transfers between devices: 70.1 us -> 59 us
    dot_general x85 -> x24, matrix products: 344 us -> 88.4 us  [product(): found = found + jnp.dot(part, right, preferred_element_type=jnp.float32)]
    pallas_call x8 -> x21, Pallas kernels: 69.5 us -> 265 us  [call(): pl.pallas_call(body, out_shape=out_shape, grid_spec=pltpu.PrefetchScalarG...]
    ppermute x45 -> x48, waiting for transfers between devices: 326 us -> 235 us  [the longest x6 54.4 us: gather_steps(): other, = (yield ([lax.ppermute(run, AXES, pairs)], [run]))]
    dynamic_slice x32 -> x4, local copies, waits for them, and re-layouts: 29.9 us -> 2.83 us  [sum_steps(): lax.dynamic_slice_in_dim(held, (place ^ k) * cut, cut, 0)]
    reduce_sum x14 -> x0, other arithmetic: 22.4 us -> none  [the longest x8 18.1 us: one_block(): totals = totals * factor + jnp.sum(expo, axis=-1)]
    all_gather x2 -> x0, waiting for transfers between devices: 21 us -> none  [the longest x1 20.9 us: shards(): key_piece = lax.all_gather(keys_flat, 'ctx', axis=1, tiled=True)]
    unnamed x156 -> x93, local copies, waits for them, and re-layouts: 25 us -> 6.14 us
    convert_element_type x16 -> x0, other arithmetic: 15.9 us -> none  [the longest x1 5.23 us: shards(): keys_flat = rotate(key_raw.reshape(windows, local_len, H, HD), cosine, si...]
  transfers between devices with their start and end apart: 49 -> 49, of which waited for: 27 -> 15; matrix products, arithmetic and copies ran while one was open for 17% -> 17% of each run, Pallas kernels for 6% -> 31%
where the time goes in v2:
time: 753 us; the launch traced here: 742 us
  Pallas kernels  265 us (35%)
  waiting for transfers between devices  239 us (32%)
  matrix products  88.4 us (12%)
  starting transfers between devices  59 us (8%)
  other arithmetic  55.9 us (7%)
  local copies, waits for them, and re-layouts  33.4 us (4%)
    pallas_call x21, Pallas kernels, call(): pl.pallas_call(body, out_shape=out_shape, grid_spec=pltpu.PrefetchScalarG...  265 us
    dot_general x24, matrix products, product(): found = found + jnp.dot(part, right, preferred_element_type=jnp.float32)  88.4 us
    ppermute x6, waiting for transfers between devices, gather_steps(): other, = (yield ([lax.ppermute(run, AXES, pairs)], [run]))  54.4 us
    ppermute x9, waiting for transfers between devices, gather_steps(): lax.ppermute(shard, AXES, plan.across[k])  48.4 us
    ppermute x3, waiting for transfers between devices, shards(): lax.ppermute(own, AXES, plan.across[k])  42.1 us
    ppermute x3, waiting for transfers between devices, shards(): sends.append(lax.ppermute(part_grads, AXES, plan.across[k]))  31.9 us
    ppermute x12, waiting for transfers between devices, sum_steps(): lax.ppermute(parts[k], AXES, plan.across[k])  31 us
    concatenate x6, other arithmetic, gather_steps(): run = jnp.concatenate([run, other])  21.6 us
  transfers between devices with their start and end apart: 49, of which 15 were waited for; matrix products, arithmetic and copies ran while one was open for 17% of the time, Pallas kernels for 31%

profile of v2, /device:TPU:0, one launch (start us, length us, event | category | flops | bytes accessed | tf_op | source)
XLA Modules:
  0.0 742.4 jit_solution(365014637504556952)
XLA Ops:
  4.6 5.1 collective-permute-start.2
  17.2 15.5 %collective-permute-done.1 = bf16[32,4224]{1,0:T(8,128)(2,1)S(1)} collective-permute-done((bf16[32,4224]{1,0:T(8,128)(2,1)S(1)}, bf16[32,4224]{1,0:T(8,128)(2,1)S(1)}, u32[]{:S(2)}, u32[]{:S(2)}) %collective-permute-start.1) | collective-permute-done | bytes 270368 | tf_op jit(solution)/shard_map/ppermute | solution.py:152
  34.7 13.6 %collective-permute-done.3 = bf16[128,4224]{1,0:T(8,128)(2,1)S(1)} collective-permute-done((bf16[128,4224]{1,0:T(8,128)(2,1)S(1)}, bf16[128,4224]{1,0:T(8,128)(2,1)S(1)}, u32[]{:S(2)}, u32[]{:S(2)}) %collective-permute-start.3) | collective-permute-done | bytes 1081376 | tf_op jit(solution)/shard_map/ppermute | solution.py:165
  54.5 20.9 %collective-permute-done.4 = bf16[256,4224]{1,0:T(8,128)(2,1)S(1)} collective-permute-done((bf16[256,4224]{1,0:T(8,128)(2,1)S(1)}, bf16[256,4224]{1,0:T(8,128)(2,1)S(1)}, u32[]{:S(2)}, u32[]{:S(2)}) %collective-permute-start.4) | collective-permute-done | bytes 2162720 | tf_op jit(solution)/shard_map/ppermute | solution.py:165
  75.3 5.7 pad_maximum_fusion.1.refs_0_.refs_1_.refs_2_
  81.7 12.9 %collective-permute-done.6 = bf16[32,8192]{1,0:T(8,128)(2,1)S(1)} collective-permute-done((bf16[32,8192]{1,0:T(8,128)(2,1)S(1)}, bf16[32,8192]{1,0:T(8,128)(2,1)S(1)}, u32[]{:S(2)}, u32[]{:S(2)}) %collective-permute-start.6) | collective-permute-done | bytes 524320 | tf_op jit(solution)/shard_map/ppermute | solution.py:152
  96.6 5.6 multiply_sine_fusion
  106.0 13.1 %project0.1 = (bf16[1024,512]{1,0:T(8,128)(2,1)}, bf16[512,1024]{1,0:T(8,128)(2,1)}, bf16[512,2048]{1,0:T(8,128)(2,1)}) custom-call(s32[8]{0:T(128)} %fusion.56.order_ref, bf16[512,1024]{1,0:T(8,128)(2,1)} %bitcast.67, f32[1,1024]{1,0:T(1,128)} %get-tuple-element.330.gain_ref, f32[1,1024]{1,0:T(1,128)} %get-tuple-element.329.shift_ref, ...), custom_call_target="tpu_custom_call" | custom-call | flops 3221225472 | bytes 15998976 | tf_op jit(solution)/shard_map/project0/pallas_call | solution.py:258
  119.1 12.4 %attend0.1 = (f32[8,8,512]{2,1,0:T(8,128)}, f32[1024,512]{1,0:T(8,128)}) custom-call(s32[8]{0:T(128)} %fusion.56.order_ref, s32[4]{0:T(128)} %get-tuple-element.339.valid_ref, bf16[512,1024]{1,0:T(8,128)(2,1)} %get-tuple-element.179.q_ref, bf16[512,2048]{1,0:T(8,128)(2,1)} %get-tuple-element.180.kv_ref), custom_call_target="tpu_custom_call" | custom-call | flops 4294967296 | bytes 5373968 | tf_op jit(solution)/shard_map/attend0/pallas_call | solution.py:258
  141.5 10.1 %project1.1 = (bf16[1024,512]{1,0:T(8,128)(2,1)}, bf16[512,2048]{1,0:T(8,128)(2,1)}) custom-call(s32[8]{0:T(128)} %fusion.56.order_ref, bf16[512,1024]{1,0:T(8,128)(2,1)} %collective-permute-done.9.source_ref, f32[1,1024]{1,0:T(1,128)} %get-tuple-element.330.gain_ref, f32[1,1024]{1,0:T(1,128)} %get-tuple-element.329.shift_ref, ...), custom_call_target="tpu_custom_call" | custom-call | flops 2147483648 | bytes 14950400 | tf_op jit(solution)/shard_map/project1/pallas_call | solution.py:258
  151.6 12.8 %attend1.1 = (f32[8,8,512]{2,1,0:T(8,128)}, f32[1024,512]{1,0:T(8,128)}) custom-call(s32[8]{0:T(128)} %fusion.56.order_ref, s32[4]{0:T(128)} %get-tuple-element.339.valid_ref, bf16[512,1024]{1,0:T(8,128)(2,1)} %get-tuple-element.179.q_ref, bf16[512,2048]{1,0:T(8,128)(2,1)} %get-tuple-element.184.kv_ref, f32[8,8,512]{2,1,0:T(8,128)} %get-tuple-element.190.refs_0_, ...), custom_call_target="tpu_custom_call" | custom-call | flops 4294967296 | bytes 7602192 | tf_op jit(solution)/shard_map/attend1/pallas_call | solution.py:258
  164.4 42.1 %collective-permute-done.11.source_ref = bf16[512,1024]{1,0:T(8,128)(2,1)} collective-permute-done((bf16[512,1024]{1,0:T(8,128)(2,1)S(1)}, bf16[512,1024]{1,0:T(8,128)(2,1)}, u32[]{:S(2)}, u32[]{:S(2)}) %collective-permute-start.11) | collective-permute-done | bytes 1048608 | tf_op jit(solution)/shard_map/ppermute | solution.py:911
  211.0 9.9 %project2.1 = (bf16[1024,512]{1,0:T(8,128)(2,1)}, bf16[512,2048]{1,0:T(8,128)(2,1)}) custom-call(s32[8]{0:T(128)} %fusion.56.order_ref, bf16[512,1024]{1,0:T(8,128)(2,1)} %collective-permute-done.11.source_ref, f32[1,1024]{1,0:T(1,128)} %get-tuple-element.330.gain_ref, f32[1,1024]{1,0:T(1,128)} %get-tuple-element.329.shift_ref, ...), custom_call_target="tpu_custom_call" | custom-call | flops 2147483648 | bytes 14950400 | tf_op jit(solution)/shard_map/project2/pallas_call | solution.py:258
  220.9 12.7 %attend2.1 = (f32[8,8,512]{2,1,0:T(8,128)}, f32[1024,512]{1,0:T(8,128)}) custom-call(s32[8]{0:T(128)} %fusion.56.order_ref, s32[4]{0:T(128)} %get-tuple-element.339.valid_ref, bf16[512,1024]{1,0:T(8,128)(2,1)} %get-tuple-element.179.q_ref, bf16[512,2048]{1,0:T(8,128)(2,1)} %get-tuple-element.195.kv_ref, f32[8,8,512]{2,1,0:T(8,128)} %get-tuple-element.198.refs_0_, ...), custom_call_target="tpu_custom_call" | custom-call | flops 4294967296 | bytes 7602192 | tf_op jit(solution)/shard_map/attend2/pallas_call | solution.py:258
  233.6 16.7 %collective-permute-done.15 = bf16[128,1024]{1,0:T(8,128)(2,1)} collective-permute-done((bf16[128,1024]{1,0:T(8,128)(2,1)S(1)}, bf16[128,1024]{1,0:T(8,128)(2,1)}, u32[]{:S(2)}, u32[]{:S(2)}) %collective-permute-start.15) | collective-permute-done | bytes 262176 | tf_op jit(solution)/shard_map/ppermute | solution.py:152
  250.3 6.6 pad_maximum_fusion.refs_0_
  261.8 10.0 %project3.1 = (bf16[1024,512]{1,0:T(8,128)(2,1)}, bf16[512,2048]{1,0:T(8,128)(2,1)}) custom-call(s32[8]{0:T(128)} %fusion.56.order_ref, bf16[512,1024]{1,0:T(8,128)(2,1)} %collective-permute-done.12.source_ref, f32[1,1024]{1,0:T(1,128)} %get-tuple-element.330.gain_ref, f32[1,1024]{1,0:T(1,128)} %get-tuple-element.329.shift_ref, ...), custom_call_target="tpu_custom_call" | custom-call | flops 2147483648 | bytes 14950400 | tf_op jit(solution)/shard_map/project3/pallas_call | solution.py:258
  271.7 13.4 %attend3.1 = (bf16[512,1024]{1,0:T(8,128)(2,1)}, bf16[1024,512]{1,0:T(8,128)(2,1)}, f32[512,1024]{1,0:T(8,128)}, f32[8,8,512]{2,1,0:T(8,128)}) custom-call(s32[8]{0:T(128)} %fusion.56.order_ref, s32[4]{0:T(128)} %get-tuple-element.339.valid_ref, bf16[512,1024]{1,0:T(8,128)(2,1)} %get-tuple-element.179.q_ref, bf16[512,2048]{1,0:T(8,128)(2,1)} %get-tuple-element.203.kv_ref, ...), custom_call_target="tpu_custom_call" | custom-call | flops 4294967296 | bytes 9699344 | tf_op jit(solution)/shard_map/attend3/pallas_call | solution.py:258
  287.0 6.1 middle.1
  293.1 19.9 %collective-permute-done.19 = bf16[1024,1024]{1,0:T(8,128)(2,1)} collective-permute-done((bf16[1024,1024]{1,0:T(8,128)(2,1)}, bf16[1024,1024]{1,0:T(8,128)(2,1)}, u32[]{:S(2)}, u32[]{:S(2)}) %collective-permute-start.19) | collective-permute-done | bytes 2097184 | tf_op jit(solution)/shard_map/ppermute | solution.py:165
  316.7 18.7 %feed.1 = (bf16[512,4096]{1,0:T(8,128)(2,1)}, bf16[512,4096]{1,0:T(8,128)(2,1)}, bf16[512,4096]{1,0:T(8,128)(2,1)}, bf16[4096,512]{1,0:T(8,128)(2,1)}) custom-call(s32[8]{0:T(128)} %fusion.56.order_ref, bf16[512,1024]{1,0:T(8,128)(2,1)} %get-tuple-element.229.two_ref, bf16[512,8192]{1,0:T(8,128)(2,1)} %pad_maximum_fusion.refs_0_, ...), custom_call_target="tpu_custom_call" | custom-call | flops 8589934592 | bytes 34603008 | tf_op jit(solution)/shard_map/feed/pallas_call | solution.py:258
  335.4 5.9 convolution_convert_fusion.1
  341.3 32.0 %feed_back.1 = (bf16[512,1024]{1,0:T(8,128)(2,1)}, bf16[512,8192]{1,0:T(8,128)(2,1)}, f32[512,1024]{1,0:T(8,128)}) custom-call(s32[8]{0:T(128)} %fusion.56.order_ref, bf16[512,1024]{1,0:T(8,128)(2,1)} %copy-done.15, bf16[512,4096]{1,0:T(8,128)(2,1)} %get-tuple-element.231.gate_ref, bf16[512,4096]{1,0:T(8,128)(2,1)} %get-tuple-element.232.up_ref, ...), custom_call_target="tpu_custom_call" | custom-call | flops 17179869184 | bytes 52428800 | tf_op jit(solution)/shard_map/feed_back/pallas_call | solution.py:258
  373.4 10.2 %convolution_convert_fusion = bf16[512,8192]{1,0:T(8,128)(2,1)} fusion(bf16[512,8192]{1,0:T(8,128)(2,1)} %get-tuple-element.245, bf16[1024,512]{1,0:T(8,128)(2,1)S(1)} %copy-done.38), kind=kOutput, calls=%fused_computation.1 | convolution fusion | flops 4299161600 | bytes 17301504 | tf_op jit(solution)/shard_map/dot_general | solution.py:240
  386.3 16.9 %collective-permute-done.21 = bf16[2048,1024]{1,0:T(8,128)(2,1)} collective-permute-done((bf16[2048,1024]{1,0:T(8,128)(2,1)}, bf16[2048,1024]{1,0:T(8,128)(2,1)}, u32[]{:S(2)}, u32[]{:S(2)}) %collective-permute-start.21) | collective-permute-done | bytes 4194336 | tf_op jit(solution)/shard_map/ppermute | solution.py:181
  403.2 4.5 add_convert_fusion.7
  408.0 4.5 add_convert_fusion.6
  412.5 7.5 %middle_back.1 = (f32[512,1024]{1,0:T(8,128)}, bf16[512,1024]{1,0:T(8,128)(2,1)}, bf16[512,1024]{1,0:T(8,128)(2,1)}, f32[8,1024]{1,0:T(8,128)}) custom-call(s32[8]{0:T(128)} %fusion.56.order_ref, f32[512,1024]{1,0:T(8,128)} %get-tuple-element.246.grads_ref, f32[512,1024]{1,0:T(8,128)} %get-tuple-element.237.resid_ref, bf16[512,1024]{1,0:T(8,128)(2,1)} %copy-done.15, ...), custom_call_target="tpu_custom_call" | custom-call | flops 1073741824 | bytes 18124800 | tf_op jit(solution)/shard_map/middle_back/pallas_call | solution.py:258
  423.2 9.3 %add_convert_fusion.2 = bf16[256,8192]{1,0:T(8,128)(2,1)} fusion(bf16[512,8192]{1,0:T(8,128)(2,1)} %collective-permute-done.22, bf16[512,8192]{1,0:T(8,128)(2,1)} %get-tuple-element.245, bf16[1024,512]{1,0:T(8,128)(2,1)S(1)} %copy-done.39), kind=kOutput, calls=%fused_computation.5 | convolution fusion | flops 2153775104 | bytes 17039360 | tf_op jit(solution)/shard_map/dot_general | solution.py:240
  434.1 6.8 add_convert_fusion.1
  440.9 16.5 %attend_back3.1 = (f32[1024,512]{1,0:T(8,128)}, bf16[512,2048]{1,0:T(8,128)(2,1)}) custom-call(s32[8]{0:T(128)} %fusion.56.order_ref, s32[4]{0:T(128)} %get-tuple-element.339.valid_ref, bf16[512,1024]{1,0:T(8,128)(2,1)} %get-tuple-element.179.q_ref, bf16[512,2048]{1,0:T(8,128)(2,1)} %get-tuple-element.203.kv_ref, ...), custom_call_target="tpu_custom_call" | custom-call | flops 10737418240 | bytes 12714000 | tf_op jit(solution)/shard_map/attend_back3/pallas_call | solution.py:258
  466.5 7.0 pull3.1
  473.5 16.5 %attend_back2.1 = (f32[1024,512]{1,0:T(8,128)}, bf16[512,2048]{1,0:T(8,128)(2,1)}) custom-call(s32[8]{0:T(128)} %fusion.56.order_ref, s32[4]{0:T(128)} %get-tuple-element.339.valid_ref, bf16[512,1024]{1,0:T(8,128)(2,1)} %get-tuple-element.179.q_ref, bf16[512,2048]{1,0:T(8,128)(2,1)} %get-tuple-element.195.kv_ref, ...), custom_call_target="tpu_custom_call" | custom-call | flops 10737418240 | bytes 14811152 | tf_op jit(solution)/shard_map/attend_back2/pallas_call | solution.py:258
  490.0 7.4 pull2.1
  497.3 4.5 fusion.12
  501.8 4.1 add_convert_fusion
  518.8 16.5 %attend_back1.1 = (f32[1024,512]{1,0:T(8,128)}, bf16[512,2048]{1,0:T(8,128)(2,1)}) custom-call(s32[8]{0:T(128)} %fusion.56.order_ref, s32[4]{0:T(128)} %get-tuple-element.339.valid_ref, bf16[512,1024]{1,0:T(8,128)(2,1)} %get-tuple-element.179.q_ref, bf16[512,2048]{1,0:T(8,128)(2,1)} %get-tuple-element.184.kv_ref, ...), custom_call_target="tpu_custom_call" | custom-call | flops 10737418240 | bytes 14811152 | tf_op jit(solution)/shard_map/attend_back1/pallas_call | solution.py:258
  535.3 5.0 fusion.14
  540.3 7.0 pull1.1
  559.4 18.7 %attend_back0.1 = (bf16[512,1024]{1,0:T(8,128)(2,1)}, bf16[512,2048]{1,0:T(8,128)(2,1)}) custom-call(s32[8]{0:T(128)} %fusion.56.order_ref, s32[4]{0:T(128)} %get-tuple-element.339.valid_ref, bf16[512,1024]{1,0:T(8,128)(2,1)} %get-tuple-element.179.q_ref, bf16[512,2048]{1,0:T(8,128)(2,1)} %get-tuple-element.180.kv_ref, ...), custom_call_target="tpu_custom_call" | custom-call | flops 10737418240 | bytes 13762576 | tf_op jit(solution)/shard_map/attend_back0/pallas_call | solution.py:258
  588.1 16.7 %collective-permute-done.37 = bf16[32,8192]{1,0:T(8,128)(2,1)} collective-permute-done((bf16[32,8192]{1,0:T(8,128)(2,1)}, bf16[32,8192]{1,0:T(8,128)(2,1)}, u32[]{:S(2)}, u32[]{:S(2)}) %collective-permute-start.37) | collective-permute-done | bytes 524320 | tf_op jit(solution)/shard_map/ppermute | solution.py:197
  623.2 10.0 %pull0.1.refs_0_ = f32[512,1024]{1,0:T(8,128)} custom-call(s32[8]{0:T(128)} %fusion.56.order_ref, bf16[512,1024]{1,0:T(8,128)(2,1)} %get-tuple-element.281.refs_0_, bf16[512,2048]{1,0:T(8,128)(2,1)} %get-tuple-element.282.refs_1_, bf16[512,4224]{1,0:T(8,128)(2,1)} %pad_maximum_fusion.1.refs_0_.refs_1_.refs_2_, ...), custom_call_target="tpu_custom_call" | custom-call | flops 3221225472 | bytes 13893632 | tf_op jit(solution)/shard_map/pull0/pallas_call | solution.py:258
  647.7 10.3 %collective-permute-done.43 = bf16[256,3072]{1,0:T(8,128)(2,1)S(1)} collective-permute-done((bf16[256,3072]{1,0:T(8,128)(2,1)S(1)}, bf16[256,3072]{1,0:T(8,128)(2,1)S(1)}, u32[]{:S(2)}, u32[]{:S(2)}) %collective-permute-start.43) | collective-permute-done | bytes 1572896 | tf_op jit(solution)/shard_map/ppermute | solution.py:185
  663.3 4.5 slice_reduce_fusion
  667.9 31.9 %collective-permute-done.41.refs_2_ = bf16[512,1024]{1,0:T(8,128)(2,1)} collective-permute-done((bf16[512,1024]{1,0:T(8,128)(2,1)}, bf16[512,1024]{1,0:T(8,128)(2,1)}, u32[]{:S(2)}, u32[]{:S(2)}) %collective-permute-start.41) | collective-permute-done | bytes 1048608 | tf_op jit(solution)/shard_map/ppermute | solution.py:981
  699.8 6.6 end_back.1
  724.9 4.7 collective-permute-done.47
  729.6 9.6 %collective-permute-done.46 = bf16[32,3072]{1,0:T(8,128)(2,1)S(1)} collective-permute-done((bf16[32,3072]{1,0:T(8,128)(2,1)S(1)}, bf16[32,3072]{1,0:T(8,128)(2,1)S(1)}, u32[]{:S(2)}, u32[]{:S(2)}) %collective-permute-start.46) | collective-permute-done | bytes 196640 | tf_op jit(solution)/shard_map/ppermute | solution.py:197
  (270 shorter events, 161.2 us)
Async XLA Ops:
  4.6 12.6 %collective-permute-start.2 = (bf16[32,4224]{1,0:T(8,128)(2,1)S(1)}, bf16[32,4224]{1,0:T(8,128)(2,1)S(1)}, u32[]{:S(2)}, u32[]{:S(2)}) collective-permute-start(bf16[32,4224]{1,0:T(8,128)(2,1)S(1)} %pad_maximum_fusion.10), channel_id=1, source_target_pairs={{0,3},{1,2},{2,1},{3,0},{4,7},{5,6},{6,5},{7,4},{8,11},{9,10},{10,... | collective-permute-start | bytes 811016 | tf_op jit(solution)/shard_map/ppermute | solution.py:152
  9.8 23.0 %collective-permute-start.1 = (bf16[32,4224]{1,0:T(8,128)(2,1)S(1)}, bf16[32,4224]{1,0:T(8,128)(2,1)S(1)}, u32[]{:S(2)}, u32[]{:S(2)}) collective-permute-start(bf16[32,4224]{1,0:T(8,128)(2,1)S(1)} %pad_maximum_fusion.10), channel_id=1, source_target_pairs={{0,2},{1,3},{2,0},{3,1},{4,6},{5,7},{6,4},{7,5},{8,10},{9,11},{10,... | collective-permute-start | bytes 811016 | tf_op jit(solution)/shard_map/ppermute | solution.py:152
  9.8 23.0 %collective-permute-start = (bf16[32,4224]{1,0:T(8,128)(2,1)S(1)}, bf16[32,4224]{1,0:T(8,128)(2,1)S(1)}, u32[]{:S(2)}, u32[]{:S(2)}) collective-permute-start(bf16[32,4224]{1,0:T(8,128)(2,1)S(1)} %pad_maximum_fusion.10), channel_id=1, source_target_pairs={{0,1},{1,0},{2,3},{3,2},{4,5},{5,4},{6,7},{7,6},{8,9},{9,8},{10,11... | collective-permute-start | bytes 811016 | tf_op jit(solution)/shard_map/ppermute | solution.py:152
  33.2 15.2 %collective-permute-start.3 = (bf16[128,4224]{1,0:T(8,128)(2,1)S(1)}, bf16[128,4224]{1,0:T(8,128)(2,1)S(1)}, u32[]{:S(2)}, u32[]{:S(2)}) collective-permute-start(bf16[128,4224]{1,0:T(8,128)(2,1)S(1)} %maximum_select_fusion.1), channel_id=1, source_target_pairs={{0,16},{1,17},{2,18},{3,19},{4,12},{5,13},{6,14},{7,15},{8,24},{9,... | collective-permute-start | bytes 3244040 | tf_op jit(solution)/shard_map/ppermute | solution.py:165
  48.5 26.8 %collective-permute-start.4 = (bf16[256,4224]{1,0:T(8,128)(2,1)S(1)}, bf16[256,4224]{1,0:T(8,128)(2,1)S(1)}, u32[]{:S(2)}, u32[]{:S(2)}) collective-permute-start(bf16[256,4224]{1,0:T(8,128)(2,1)S(1)} %pad_maximum_fusion.5), channel_id=1, source_target_pairs={{0,8},{1,9},{2,10},{3,11},{4,20},{5,21},{6,22},{7,23},{8,0},{9,1},... | collective-permute-start | bytes 6488072 | tf_op jit(solution)/shard_map/ppermute | solution.py:165
  50.1 31.6 %collective-permute-start.7 = (bf16[32,8192]{1,0:T(8,128)(2,1)S(1)}, bf16[32,8192]{1,0:T(8,128)(2,1)S(1)}, u32[]{:S(2)}, u32[]{:S(2)}) collective-permute-start(bf16[32,8192]{1,0:T(8,128)(2,1)S(1)} %reshape.102), channel_id=1, source_target_pairs={{0,3},{1,2},{2,1},{3,0},{4,7},{5,6},{6,5},{7,4},{8,11},{9,10},{10,... | collective-permute-start | bytes 1572872 | tf_op jit(solution)/shard_map/ppermute | solution.py:152
  52.6 42.0 %collective-permute-start.6 = (bf16[32,8192]{1,0:T(8,128)(2,1)S(1)}, bf16[32,8192]{1,0:T(8,128)(2,1)S(1)}, u32[]{:S(2)}, u32[]{:S(2)}) collective-permute-start(bf16[32,8192]{1,0:T(8,128)(2,1)S(1)} %reshape.102), channel_id=1, source_target_pairs={{0,2},{1,3},{2,0},{3,1},{4,6},{5,7},{6,4},{7,5},{8,10},{9,11},{10,... | collective-permute-start | bytes 1572872 | tf_op jit(solution)/shard_map/ppermute | solution.py:152
  52.6 42.0 %collective-permute-start.5 = (bf16[32,8192]{1,0:T(8,128)(2,1)S(1)}, bf16[32,8192]{1,0:T(8,128)(2,1)S(1)}, u32[]{:S(2)}, u32[]{:S(2)}) collective-permute-start(bf16[32,8192]{1,0:T(8,128)(2,1)S(1)} %reshape.102), channel_id=1, source_target_pairs={{0,1},{1,0},{2,3},{3,2},{4,5},{5,4},{6,7},{7,6},{8,9},{9,8},{10,11... | collective-permute-start | bytes 1572872 | tf_op jit(solution)/shard_map/ppermute | solution.py:152
  81.1 23.3 %collective-permute-start.8 = (bf16[512,4224]{1,0:T(8,128)(2,1)}, bf16[512,4224]{1,0:T(8,128)(2,1)}, u32[]{:S(2)}, u32[]{:S(2)}) collective-permute-start(bf16[512,4224]{1,0:T(8,128)(2,1)} %pad_maximum_fusion.1.refs_0_.refs_1_.refs_2_), channel_id=1, source_target_pairs={{0,4},{1,5},{2,6},{3,7},{4,0},{5,1},{6,2},{7,3},{8,12},{9,13},{10,... | collective-permute-start | bytes 12976136 | tf_op jit(solution)/shard_map/ppermute | solution.py:168
  95.4 36.1 %collective-permute-start.10 = (bf16[128,8192]{1,0:T(8,128)(2,1)S(1)}, bf16[128,8192]{1,0:T(8,128)(2,1)}, u32[]{:S(2)}, u32[]{:S(2)}) collective-permute-start(bf16[128,8192]{1,0:T(8,128)(2,1)S(1)} %maximum_select_fusion), channel_id=1, source_target_pairs={{0,16},{1,17},{2,18},{3,19},{4,12},{5,13},{6,14},{7,15},{8,24},{9,... | collective-permute-start | bytes 6291464 | tf_op jit(solution)/shard_map/ppermute | solution.py:165
  102.1 29.4 %collective-permute-start.9 = (bf16[512,1024]{1,0:T(8,128)(2,1)S(1)}, bf16[512,1024]{1,0:T(8,128)(2,1)}, u32[]{:S(2)}, u32[]{:S(2)}) collective-permute-start(bf16[512,1024]{1,0:T(8,128)(2,1)S(1)} %bitcast.70), channel_id=1, source_target_pairs={{0,1},{1,0},{2,3},{3,2},{4,5},{5,4},{6,7},{7,6},{8,9},{9,8},{10,11... | collective-permute-start | bytes 3145736 | tf_op jit(solution)/shard_map/ppermute | solution.py:911
  135.6 114.7 %collective-permute-start.13 = (bf16[256,8192]{1,0:T(8,128)(2,1)}, bf16[256,8192]{1,0:T(8,128)(2,1)}, u32[]{:S(2)}, u32[]{:S(2)}) collective-permute-start(bf16[256,8192]{1,0:T(8,128)(2,1)} %pad_maximum_fusion.2), channel_id=1, source_target_pairs={{0,8},{1,9},{2,10},{3,11},{4,20},{5,21},{6,22},{7,23},{8,0},{9,1},... | collective-permute-start | bytes 12582920 | tf_op jit(solution)/shard_map/ppermute | solution.py:165
  137.1 69.5 %collective-permute-start.11 = (bf16[512,1024]{1,0:T(8,128)(2,1)S(1)}, bf16[512,1024]{1,0:T(8,128)(2,1)}, u32[]{:S(2)}, u32[]{:S(2)}) collective-permute-start(bf16[512,1024]{1,0:T(8,128)(2,1)S(1)} %bitcast.71), channel_id=1, source_target_pairs={{0,2},{1,3},{2,0},{3,1},{4,6},{5,7},{6,4},{7,5},{8,10},{9,11},{10,... | collective-permute-start | bytes 3145736 | tf_op jit(solution)/shard_map/ppermute | solution.py:911
  139.2 94.4 %collective-permute-start.12 = (bf16[512,1024]{1,0:T(8,128)(2,1)S(1)}, bf16[512,1024]{1,0:T(8,128)(2,1)}, u32[]{:S(2)}, u32[]{:S(2)}) collective-permute-start(bf16[512,1024]{1,0:T(8,128)(2,1)S(1)} %bitcast.72), channel_id=1, source_target_pairs={{0,3},{1,2},{2,1},{3,0},{4,7},{5,6},{6,5},{7,4},{8,11},{9,10},{10,... | collective-permute-start | bytes 3145736 | tf_op jit(solution)/shard_map/ppermute | solution.py:911
  206.6 27.0 %collective-permute-start.16 = (bf16[128,1024]{1,0:T(8,128)(2,1)S(1)}, bf16[128,1024]{1,0:T(8,128)(2,1)}, u32[]{:S(2)}, u32[]{:S(2)}) collective-permute-start(bf16[128,1024]{1,0:T(8,128)(2,1)S(1)} %copy-done.36), channel_id=1, source_target_pairs={{0,3},{1,2},{2,1},{3,0},{4,7},{5,6},{6,5},{7,4},{8,11},{9,10},{10,... | collective-permute-start | bytes 786440 | tf_op jit(solution)/shard_map/ppermute | solution.py:152
  208.4 41.9 %collective-permute-start.15 = (bf16[128,1024]{1,0:T(8,128)(2,1)S(1)}, bf16[128,1024]{1,0:T(8,128)(2,1)}, u32[]{:S(2)}, u32[]{:S(2)}) collective-permute-start(bf16[128,1024]{1,0:T(8,128)(2,1)S(1)} %copy-done.36), channel_id=1, source_target_pairs={{0,2},{1,3},{2,0},{3,1},{4,6},{5,7},{6,4},{7,5},{8,10},{9,11},{10,... | collective-permute-start | bytes 786440 | tf_op jit(solution)/shard_map/ppermute | solution.py:152
  208.4 41.9 %collective-permute-start.14 = (bf16[128,1024]{1,0:T(8,128)(2,1)S(1)}, bf16[128,1024]{1,0:T(8,128)(2,1)}, u32[]{:S(2)}, u32[]{:S(2)}) collective-permute-start(bf16[128,1024]{1,0:T(8,128)(2,1)S(1)} %copy-done.36), channel_id=1, source_target_pairs={{0,1},{1,0},{2,3},{3,2},{4,5},{5,4},{6,7},{7,6},{8,9},{9,8},{10,11... | collective-permute-start | bytes 786440 | tf_op jit(solution)/shard_map/ppermute | solution.py:152
  256.8 36.3 %collective-permute-start.18 = (bf16[512,8192]{1,0:T(8,128)(2,1)}, bf16[512,8192]{1,0:T(8,128)(2,1)}, u32[]{:S(2)}, u32[]{:S(2)}) collective-permute-start(bf16[512,8192]{1,0:T(8,128)(2,1)} %pad_maximum_fusion.refs_0_), channel_id=1, source_target_pairs={{0,4},{1,5},{2,6},{3,7},{4,0},{5,1},{6,2},{7,3},{8,12},{9,13},{10,... | collective-permute-start | bytes 25165832 | tf_op jit(solution)/shard_map/ppermute | solution.py:168
  259.9 25.2 %collective-permute-start.17 = (bf16[512,1024]{1,0:T(8,128)(2,1)S(1)}, bf16[512,1024]{1,0:T(8,128)(2,1)S(1)}, u32[]{:S(2)}, u32[]{:S(2)}) collective-permute-start(bf16[512,1024]{1,0:T(8,128)(2,1)S(1)} %maximum_select_fusion.4), channel_id=1, source_target_pairs={{0,16},{1,17},{2,18},{3,19},{4,12},{5,13},{6,14},{7,15},{8,24},{9,... | collective-permute-start | bytes 3145736 | tf_op jit(solution)/shard_map/ppermute | solution.py:165
  286.7 26.4 %collective-permute-start.19 = (bf16[1024,1024]{1,0:T(8,128)(2,1)}, bf16[1024,1024]{1,0:T(8,128)(2,1)}, u32[]{:S(2)}, u32[]{:S(2)}) collective-permute-start(bf16[1024,1024]{1,0:T(8,128)(2,1)} %pad_maximum_fusion.6), channel_id=1, source_target_pairs={{0,8},{1,9},{2,10},{3,11},{4,20},{5,21},{6,22},{7,23},{8,0},{9,1},... | collective-permute-start | bytes 6291464 | tf_op jit(solution)/shard_map/ppermute | solution.py:165
  316.5 24.8 %collective-permute-start.20 = (bf16[2048,1024]{1,0:T(8,128)(2,1)}, bf16[2048,1024]{1,0:T(8,128)(2,1)}, u32[]{:S(2)}, u32[]{:S(2)}) collective-permute-start(bf16[2048,1024]{1,0:T(8,128)(2,1)} %pad_maximum_fusion.3.refs_2_), channel_id=1, source_target_pairs={{0,4},{1,5},{2,6},{3,7},{4,0},{5,1},{6,2},{7,3},{8,12},{9,13},{10,... | collective-permute-start | bytes 12582920 | tf_op jit(solution)/shard_map/ppermute | solution.py:168
  383.6 39.6 %collective-permute-start.22 = (bf16[512,8192]{1,0:T(8,128)(2,1)}, bf16[512,8192]{1,0:T(8,128)(2,1)}, u32[]{:S(2)}, u32[]{:S(2)}) collective-permute-start(bf16[512,8192]{1,0:T(8,128)(2,1)} %convolution_convert_fusion), channel_id=1, source_target_pairs={{0,4},{1,5},{2,6},{3,7},{4,0},{5,1},{6,2},{7,3},{8,12},{9,13},{10,... | collective-permute-start | bytes 25165832 | tf_op jit(solution)/shard_map/ppermute | solution.py:181
  384.1 19.1 %collective-permute-start.21 = (bf16[2048,1024]{1,0:T(8,128)(2,1)}, bf16[2048,1024]{1,0:T(8,128)(2,1)}, u32[]{:S(2)}, u32[]{:S(2)}) collective-permute-start(bf16[2048,1024]{1,0:T(8,128)(2,1)} %convolution_convert_fusion.1), channel_id=1, source_target_pairs={{0,4},{1,5},{2,6},{3,7},{4,0},{5,1},{6,2},{7,3},{8,12},{9,13},{10,... | collective-permute-start | bytes 12582920 | tf_op jit(solution)/shard_map/ppermute | solution.py:181
  407.7 49.7 %collective-permute-start.23 = (bf16[1024,1024]{1,0:T(8,128)(2,1)}, bf16[1024,1024]{1,0:T(8,128)(2,1)S(1)}, u32[]{:S(2)}, u32[]{:S(2)}) collective-permute-start(bf16[1024,1024]{1,0:T(8,128)(2,1)} %add_convert_fusion.7), channel_id=1, source_target_pairs={{0,8},{1,9},{2,10},{3,11},{4,20},{5,21},{6,22},{7,23},{8,0},{9,1},... | collective-permute-start | bytes 6291464 | tf_op jit(solution)/shard_map/ppermute | solution.py:185
  423.1 34.3 %collective-permute-start.24 = (bf16[512,1024]{1,0:T(8,128)(2,1)}, bf16[512,1024]{1,0:T(8,128)(2,1)}, u32[]{:S(2)}, u32[]{:S(2)}) collective-permute-start(bf16[512,1024]{1,0:T(8,128)(2,1)} %convolution_convert_fusion.3), channel_id=1, source_target_pairs={{0,4},{1,5},{2,6},{3,7},{4,0},{5,1},{6,2},{7,3},{8,12},{9,13},{10,... | collective-permute-start | bytes 3145736 | tf_op jit(solution)/shard_map/ppermute | solution.py:181
  432.5 69.3 %collective-permute-start.27 = (bf16[256,8192]{1,0:T(8,128)(2,1)}, bf16[256,8192]{1,0:T(8,128)(2,1)}, u32[]{:S(2)}, u32[]{:S(2)}) collective-permute-start(bf16[256,8192]{1,0:T(8,128)(2,1)} %add_convert_fusion.2), channel_id=1, source_target_pairs={{0,8},{1,9},{2,10},{3,11},{4,20},{5,21},{6,22},{7,23},{8,0},{9,1},... | collective-permute-start | bytes 12582920 | tf_op jit(solution)/shard_map/ppermute | solution.py:185
  459.9 41.9 %collective-permute-start.26 = (bf16[256,1024]{1,0:T(8,128)(2,1)}, bf16[256,1024]{1,0:T(8,128)(2,1)}, u32[]{:S(2)}, u32[]{:S(2)}) collective-permute-start(bf16[256,1024]{1,0:T(8,128)(2,1)} %add_convert_fusion.15), channel_id=1, source_target_pairs={{0,8},{1,9},{2,10},{3,11},{4,20},{5,21},{6,22},{7,23},{8,0},{9,1},... | collective-permute-start | bytes 1572872 | tf_op jit(solution)/shard_map/ppermute | solution.py:185
  462.4 39.4 %collective-permute-start.25 = (bf16[512,1024]{1,0:T(8,128)(2,1)}, bf16[512,1024]{1,0:T(8,128)(2,1)S(1)}, u32[]{:S(2)}, u32[]{:S(2)}) collective-permute-start(bf16[512,1024]{1,0:T(8,128)(2,1)} %slice.272), channel_id=1, source_target_pairs={{0,16},{1,17},{2,18},{3,19},{4,12},{5,13},{6,14},{7,15},{8,24},{9,... | collective-permute-start | bytes 3145736 | tf_op jit(solution)/shard_map/ppermute | solution.py:192
  508.9 38.4 %collective-permute-start.32 = (bf16[128,8192]{1,0:T(8,128)(2,1)}, bf16[128,8192]{1,0:T(8,128)(2,1)S(1)}, u32[]{:S(2)}, u32[]{:S(2)}) collective-permute-start(bf16[128,8192]{1,0:T(8,128)(2,1)} %slice.275), channel_id=1, source_target_pairs={{0,16},{1,17},{2,18},{3,19},{4,12},{5,13},{6,14},{7,15},{8,24},{9,... | collective-permute-start | bytes 6291464 | tf_op jit(solution)/shard_map/ppermute | solution.py:192
  511.4 36.0 %collective-permute-start.31 = (bf16[128,1024]{1,0:T(8,128)(2,1)}, bf16[128,1024]{1,0:T(8,128)(2,1)S(1)}, u32[]{:S(2)}, u32[]{:S(2)}) collective-permute-start(bf16[128,1024]{1,0:T(8,128)(2,1)} %slice.274), channel_id=1, source_target_pairs={{0,16},{1,17},{2,18},{3,19},{4,12},{5,13},{6,14},{7,15},{8,24},{9,... | collective-permute-start | bytes 786440 | tf_op jit(solution)/shard_map/ppermute | solution.py:192
  514.4 32.9 %collective-permute-start.30 = (bf16[128,1024]{1,0:T(8,128)(2,1)}, bf16[128,1024]{1,0:T(8,128)(2,1)}, u32[]{:S(2)}, u32[]{:S(2)}) collective-permute-start(bf16[128,1024]{1,0:T(8,128)(2,1)} %get-tuple-element.316), channel_id=1, source_target_pairs={{0,3},{1,2},{2,1},{3,0},{4,7},{5,6},{6,5},{7,4},{8,11},{9,10},{10,... | collective-permute-start | bytes 786440 | tf_op jit(solution)/shard_map/ppermute | solution.py:197
  516.1 31.2 %collective-permute-start.29 = (bf16[128,1024]{1,0:T(8,128)(2,1)}, bf16[128,1024]{1,0:T(8,128)(2,1)}, u32[]{:S(2)}, u32[]{:S(2)}) collective-permute-start(bf16[128,1024]{1,0:T(8,128)(2,1)} %get-tuple-element.317), channel_id=1, source_target_pairs={{0,2},{1,3},{2,0},{3,1},{4,6},{5,7},{6,4},{7,5},{8,10},{9,11},{10,... | collective-permute-start | bytes 786440 | tf_op jit(solution)/shard_map/ppermute | solution.py:197
  516.1 31.2 %collective-permute-start.28 = (bf16[128,1024]{1,0:T(8,128)(2,1)}, bf16[128,1024]{1,0:T(8,128)(2,1)}, u32[]{:S(2)}, u32[]{:S(2)}) collective-permute-start(bf16[128,1024]{1,0:T(8,128)(2,1)} %get-tuple-element.318), channel_id=1, source_target_pairs={{0,1},{1,0},{2,3},{3,2},{4,5},{5,4},{6,7},{7,6},{8,9},{9,8},{10,11... | collective-permute-start | bytes 786440 | tf_op jit(solution)/shard_map/ppermute | solution.py:197
  552.1 29.1 %collective-permute-start.35 = (bf16[32,1024]{1,0:T(8,128)(2,1)}, bf16[32,1024]{1,0:T(8,128)(2,1)S(1)}, u32[]{:S(2)}, u32[]{:S(2)}) collective-permute-start(bf16[32,1024]{1,0:T(8,128)(2,1)} %get-tuple-element.322), channel_id=1, source_target_pairs={{0,3},{1,2},{2,1},{3,0},{4,7},{5,6},{6,5},{7,4},{8,11},{9,10},{10,... | collective-permute-start | bytes 196616 | tf_op jit(solution)/shard_map/ppermute | solution.py:197
  553.9 34.2 %collective-permute-start.34 = (bf16[32,1024]{1,0:T(8,128)(2,1)}, bf16[32,1024]{1,0:T(8,128)(2,1)S(1)}, u32[]{:S(2)}, u32[]{:S(2)}) collective-permute-start(bf16[32,1024]{1,0:T(8,128)(2,1)} %get-tuple-element.323), channel_id=1, source_target_pairs={{0,2},{1,3},{2,0},{3,1},{4,6},{5,7},{6,4},{7,5},{8,10},{9,11},{10,... | collective-permute-start | bytes 196616 | tf_op jit(solution)/shard_map/ppermute | solution.py:197
  553.9 34.2 %collective-permute-start.33 = (bf16[32,1024]{1,0:T(8,128)(2,1)}, bf16[32,1024]{1,0:T(8,128)(2,1)}, u32[]{:S(2)}, u32[]{:S(2)}) collective-permute-start(bf16[32,1024]{1,0:T(8,128)(2,1)} %get-tuple-element.324), channel_id=1, source_target_pairs={{0,1},{1,0},{2,3},{3,2},{4,5},{5,4},{6,7},{7,6},{8,9},{9,8},{10,11... | collective-permute-start | bytes 196616 | tf_op jit(solution)/shard_map/ppermute | solution.py:197
  557.7 30.4 %collective-permute-start.38 = (bf16[32,8192]{1,0:T(8,128)(2,1)}, bf16[32,8192]{1,0:T(8,128)(2,1)}, u32[]{:S(2)}, u32[]{:S(2)}) collective-permute-start(bf16[32,8192]{1,0:T(8,128)(2,1)} %get-tuple-element.313), channel_id=1, source_target_pairs={{0,3},{1,2},{2,1},{3,0},{4,7},{5,6},{6,5},{7,4},{8,11},{9,10},{10,... | collective-permute-start | bytes 1572872 | tf_op jit(solution)/shard_map/ppermute | solution.py:197
  559.4 45.4 %collective-permute-start.37 = (bf16[32,8192]{1,0:T(8,128)(2,1)}, bf16[32,8192]{1,0:T(8,128)(2,1)}, u32[]{:S(2)}, u32[]{:S(2)}) collective-permute-start(bf16[32,8192]{1,0:T(8,128)(2,1)} %get-tuple-element.314), channel_id=1, source_target_pairs={{0,2},{1,3},{2,0},{3,1},{4,6},{5,7},{6,4},{7,5},{8,10},{9,11},{10,... | collective-permute-start | bytes 1572872 | tf_op jit(solution)/shard_map/ppermute | solution.py:197
  581.3 23.5 %collective-permute-start.36 = (bf16[32,8192]{1,0:T(8,128)(2,1)S(1)}, bf16[32,8192]{1,0:T(8,128)(2,1)S(1)}, u32[]{:S(2)}, u32[]{:S(2)}) collective-permute-start(bf16[32,8192]{1,0:T(8,128)(2,1)S(1)} %copy-done.28), channel_id=1, source_target_pairs={{0,1},{1,0},{2,3},{3,2},{4,5},{5,4},{6,7},{7,6},{8,9},{9,8},{10,11... | collective-permute-start | bytes 1572872 | tf_op jit(solution)/shard_map/ppermute | solution.py:197
  607.4 25.8 %collective-permute-start.39 = (bf16[512,3072]{1,0:T(8,128)(2,1)}, bf16[512,3072]{1,0:T(8,128)(2,1)}, u32[]{:S(2)}, u32[]{:S(2)}) collective-permute-start(bf16[512,3072]{1,0:T(8,128)(2,1)} %pad_maximum_fusion.4), channel_id=1, source_target_pairs={{0,4},{1,5},{2,6},{3,7},{4,0},{5,1},{6,2},{7,3},{8,12},{9,13},{10,... | collective-permute-start | bytes 9437192 | tf_op jit(solution)/shard_map/ppermute | solution.py:181
  608.2 59.7 %collective-permute-start.40 = (bf16[512,1024]{1,0:T(8,128)(2,1)}, bf16[512,1024]{1,0:T(8,128)(2,1)}, u32[]{:S(2)}, u32[]{:S(2)}) collective-permute-start(bf16[512,1024]{1,0:T(8,128)(2,1)} %pull3.1), channel_id=1, source_target_pairs={{0,3},{1,2},{2,1},{3,0},{4,7},{5,6},{6,5},{7,4},{8,11},{9,10},{10,... | collective-permute-start | bytes 3145736 | tf_op jit(solution)/shard_map/ppermute | solution.py:981
  609.9 89.9 %collective-permute-start.41 = (bf16[512,1024]{1,0:T(8,128)(2,1)}, bf16[512,1024]{1,0:T(8,128)(2,1)}, u32[]{:S(2)}, u32[]{:S(2)}) collective-permute-start(bf16[512,1024]{1,0:T(8,128)(2,1)} %pull2.1), channel_id=1, source_target_pairs={{0,2},{1,3},{2,0},{3,1},{4,6},{5,7},{6,4},{7,5},{8,10},{9,11},{10,... | collective-permute-start | bytes 3145736 | tf_op jit(solution)/shard_map/ppermute | solution.py:981
  609.9 89.9 %collective-permute-start.42 = (bf16[512,1024]{1,0:T(8,128)(2,1)}, bf16[512,1024]{1,0:T(8,128)(2,1)}, u32[]{:S(2)}, u32[]{:S(2)}) collective-permute-start(bf16[512,1024]{1,0:T(8,128)(2,1)} %pull1.1), channel_id=1, source_target_pairs={{0,1},{1,0},{2,3},{3,2},{4,5},{5,4},{6,7},{7,6},{8,9},{9,8},{10,11... | collective-permute-start | bytes 3145736 | tf_op jit(solution)/shard_map/ppermute | solution.py:981
  637.6 20.5 %collective-permute-start.43 = (bf16[256,3072]{1,0:T(8,128)(2,1)S(1)}, bf16[256,3072]{1,0:T(8,128)(2,1)S(1)}, u32[]{:S(2)}, u32[]{:S(2)}) collective-permute-start(bf16[256,3072]{1,0:T(8,128)(2,1)S(1)} %pad_maximum_fusion.7), channel_id=1, source_target_pairs={{0,8},{1,9},{2,10},{3,11},{4,20},{5,21},{6,22},{7,23},{8,0},{9,1},... | collective-permute-start | bytes 4718600 | tf_op jit(solution)/shard_map/ppermute | solution.py:185
  659.6 58.9 %collective-permute-start.44 = (bf16[128,3072]{1,0:T(8,128)(2,1)}, bf16[128,3072]{1,0:T(8,128)(2,1)}, u32[]{:S(2)}, u32[]{:S(2)}) collective-permute-start(bf16[128,3072]{1,0:T(8,128)(2,1)} %slice.279), channel_id=1, source_target_pairs={{0,16},{1,17},{2,18},{3,19},{4,12},{5,13},{6,14},{7,15},{8,24},{9,... | collective-permute-start | bytes 2359304 | tf_op jit(solution)/shard_map/ppermute | solution.py:192
  708.0 10.4 %all-to-all-start = ((f32[32,1,128]{2,1,0:T(1,128)}), f32[32,1,128]{2,1,0:T(1,128)S(1)}, u32[]{:S(2)}, u32[]{:S(2)}) async-start(f32[32,1,128]{2,1,0:T(1,128)} %bitcast.16), calls=%async_computation | async-start | bytes 32768 | tf_op jit(solution)/shard_map/all_to_all | solution.py:208
  720.5 18.6 %collective-permute-start.46 = (bf16[32,3072]{1,0:T(8,128)(2,1)S(1)}, bf16[32,3072]{1,0:T(8,128)(2,1)S(1)}, u32[]{:S(2)}, u32[]{:S(2)}) collective-permute-start(bf16[32,3072]{1,0:T(8,128)(2,1)S(1)} %get-tuple-element.320), channel_id=1, source_target_pairs={{0,2},{1,3},{2,0},{3,1},{4,6},{5,7},{6,4},{7,5},{8,10},{9,11},{10,... | collective-permute-start | bytes 589832 | tf_op jit(solution)/shard_map/ppermute | solution.py:197
  721.8 17.4 %collective-permute-start.45 = (bf16[32,3072]{1,0:T(8,128)(2,1)S(1)}, bf16[32,3072]{1,0:T(8,128)(2,1)S(1)}, u32[]{:S(2)}, u32[]{:S(2)}) collective-permute-start(bf16[32,3072]{1,0:T(8,128)(2,1)S(1)} %get-tuple-element.321), channel_id=1, source_target_pairs={{0,1},{1,0},{2,3},{3,2},{4,5},{5,4},{6,7},{7,6},{8,9},{9,8},{10,11... | collective-permute-start | bytes 589832 | tf_op jit(solution)/shard_map/ppermute | solution.py:197
  (45 other events, 447.8 us)

commit v3 on v2

--- a/solution.py
+++ b/solution.py
@@ -48,6 +48,14 @@
             self.pairs(lambda d, z, t=t: (d ^ (1 << orders[d & 1][t]), z)) for t in range(self.stages)
         ]
         self.across = [self.pairs(lambda d, z, k=k: (d, z ^ k)) for k in range(self.ctx)]
+        self.line = self.ctx == 4
+        self.inner = self.pairs(lambda d, z: (d, z ^ 3), (1, 2))
+        self.outward = self.pairs(lambda d, z: (d, z ^ 1), (1, 2))
+        self.inward = self.pairs(lambda d, z: (d, z ^ 1), (0, 3))
+        self.blocks = np.arange(self.ctx)[:, None] ^ np.arange(self.ctx)[None, :]
+        if self.line:
+            self.blocks = np.array([[0, 1, 2, 3], [1, 0, 2, 3], [2, 3, 1, 0], [3, 2, 1, 0]])
+        self.blocks = self.blocks.astype(np.int32)
         half = self.dp // 2
         table = np.zeros((self.dp, self.dp), np.int32)
         for d in range(self.dp):
@@ -59,11 +67,12 @@
                         block ^= 1 << orders[owner & 1][t]
                 table[d, j] = block
         self.table = table
-
-    def pairs(self, target):
+        self.back = np.argsort(table, axis=1).astype(np.int32)
+
+    def pairs(self, target, places=None):
         found = []
         for d in range(self.dp):
-            for z in range(self.ctx):
+            for z in range(self.ctx) if places is None else places:
                 other, place = target(d, z)
                 found.append((d * self.ctx + z, other * self.ctx + place))
         return found
@@ -170,12 +179,51 @@
     return run, pieces
 
 
+def add(a, b):
+    return (a.astype(jnp.float32) + b.astype(jnp.float32)).astype(BF)
+
+
+def window_steps(plan, own, came):
+    if not plan.line:
+        others = yield [lax.ppermute(own, AXES, plan.across[k]) for k in range(1, plan.ctx)], [own]
+        came.update(enumerate(others, 1))
+        return
+    near, middle = yield (
+        [lax.ppermute(own, AXES, plan.across[1]), lax.ppermute(own, AXES, plan.inner)],
+        [own],
+    )
+    came[1] = near
+    far, cross = yield (
+        [lax.ppermute(middle, AXES, plan.outward), lax.ppermute(near, AXES, plan.inner)],
+        [middle, near],
+    )
+    came[2] = middle + far
+    (last,) = yield [lax.ppermute(cross, AXES, plan.outward)], [cross]
+    came[3] = cross + last
+
+
+def return_steps(plan, parts):
+    (came,) = yield [lax.ppermute(parts[3], AXES, plan.inward)], [parts[3]]
+    run = add(parts[3], came)
+    near, cross = yield (
+        [lax.ppermute(parts[2], AXES, plan.inward), lax.ppermute(run, AXES, plan.inner)],
+        [parts[2], run],
+    )
+    run, last = add(parts[2], near), add(parts[1], cross)
+    return (
+        yield (
+            [
+                lax.ppermute(run, AXES, plan.inner),
+                lax.ppermute(last, AXES, plan.across[1]),
+            ],
+            [run, last],
+        )
+    )
+
+
 def sum_steps(plan, product):
     place = lax.axis_index("ctx")
     half = plan.dp // 2
-
-    def total(a, b):
-        return (a.astype(jnp.float32) + b.astype(jnp.float32)).astype(BF)
 
     send = product(half, plan.dp)
     (other,) = yield [lax.ppermute(send, AXES, plan.core)], [send]
@@ -185,19 +233,20 @@
     flying = [lax.ppermute(send, AXES, plan.stage[0])]
     keep = product(0, size, other[: size * rows])
     (other,) = yield flying, [send, keep]
-    held = total(keep, other)
+    held = add(keep, other)
     for pairs in plan.stage[1:]:
         size //= 2
         send = held[size * rows :]
         (other,) = yield [lax.ppermute(send, AXES, pairs)], [send]
-        held = total(held[: size * rows], other)
-    cut = held.shape[0] // plan.ctx
-    parts = [lax.dynamic_slice_in_dim(held, (place ^ k) * cut, cut, 0) for k in range(plan.ctx)]
-    others = yield (
-        [lax.ppermute(parts[k], AXES, plan.across[k]) for k in range(1, plan.ctx)],
-        parts[1:],
-    )
-    return sum((other.astype(jnp.float32) for other in others), parts[0].astype(jnp.float32))
+        held = add(held[: size * rows], other)
+    for bit in reversed(range(plan.ctx_bits)):
+        cut = held.shape[0] // 2
+        upper = (place >> bit) & 1
+        send = lax.dynamic_slice_in_dim(held, (1 - upper) * cut, cut, 0)
+        keep = lax.dynamic_slice_in_dim(held, upper * cut, cut, 0)
+        (other,) = yield [lax.ppermute(send, AXES, plan.across[1 << bit])], [send]
+        held = add(keep, other) if bit else keep.astype(jnp.float32) + other.astype(jnp.float32)
+    return held
 
 
 def sum_vectors(plan, vectors):
@@ -229,7 +278,7 @@
 
 
 def product_of(plan, groups):
-    def product(start, end, add=None):
+    def product(start, end, more=None):
         columns = []
         low = 0
         for terms in groups:
@@ -239,8 +288,8 @@
                 part = flipped[start * rows : end * rows]
                 found = found + jnp.dot(part, right, preferred_element_type=jnp.float32)
             high = low + found.shape[1]
-            if add is not None:
-                found = found + add[:, low:high].astype(jnp.float32)
+            if more is not None:
+                found = found + more[:, low:high].astype(jnp.float32)
             columns.append(found.astype(BF))
             low = high
         return columns[0] if len(columns) == 1 else jnp.concatenate(columns, axis=1)
@@ -797,7 +846,7 @@
         [(whole((rows, width)), array((rows, width), dtype))],
         ((both,) if block else (dq, both)) + tuple(mixed),
         f"pull{block}",
-        2 * rows * width * width * (2 if block else 3),
+        rows * width,
         scratch=[pltpu.VMEM((rows, width), jnp.float32)],
     )[0]
 
@@ -895,7 +944,7 @@
     mix = Chain(gather_steps(plan, mixed))
 
     seats = jnp.arange(local_len, dtype=jnp.int32)
-    starts = (place ^ jnp.arange(plan.ctx, dtype=jnp.int32)) * local_len
+    starts = jnp.asarray(plan.blocks)[place] * local_len
     valid = jnp.clip(lengths[0] - starts, 0, local_len)
     cosine, sine = rotary_tables((starts[:, None] + seats[None, :]).reshape(-1))
     real = (place * local_len + seats < lengths[0])[:, None]
@@ -903,17 +952,19 @@
     own = tokens.reshape(rows, width)
 
     pair_own = join(gate_weight, up_weight, part)
-    pair_own = step(pair_own, mix)
+    early = (pair_own, cosine, sine, upstream)
+    pair_own, cosine, sine, upstream = step(early, mix)
     pair = Chain(gather_steps(plan, pair_own))
     own = step(own, mix)
+    came = {}
+    own, window = begin(own, window_steps(plan, own, came))
     own = step(own, mix)
     own = step(own, pair)
-    came = {k: lax.ppermute(own, AXES, plan.across[k]) for k in range(1, plan.ctx)}
     own = finish(own, mix)
     mixed_w = pieces_of(mix, mixed)
     cols = jnp.concatenate([piece[:, 4 * width : 4 * width + 4] for piece in mixed_w])
     cols = cols.T.astype(jnp.float32)
-    back = jnp.argsort(order)
+    back = jnp.asarray(plan.back)[lax.axis_index("dp")] if exact else order
     natural = cols.reshape(4, order.shape[0], -1)[:, back].reshape(4, width)
 
     flipped, both = {}, {}
@@ -921,14 +972,13 @@
     state = attend(order, valid, 0, None, plan.ctx == 1, queries, both[0])
     down = None
     for k in range(1, plan.ctx):
-        state, came[k] = tie(state, came[k])
-        if k == 1:
-            state = step(state, pair)
+        while k not in came:
+            state = step(state, window, pair) if k == 1 else step(state, window)
         if k == 2:
             down_own, state = tie(down_weight, state)
             down = Chain(gather_steps(plan, down_own))
         if k == 3:
-            state = step(state, pair, down)
+            state = step(state, pair)
         flipped[k], both[k] = project(
             order, came[k], cols[0], cols[1], mixed_w, cosine, sine, k
         )
@@ -950,7 +1000,7 @@
     )
     output = output.reshape(windows, local_len, width)
 
-    two_grads = step(two_grads, down_sum)
+    two_grads, pair_grads = step((two_grads, pair_grads), down_sum)
     two_grads, pair_sum = begin(
         two_grads, sum_steps(plan, product_of(plan, [[(in_slots(two_flipped), pair_grads)]]))
     )
@@ -961,36 +1011,38 @@
     go, output_sum = begin(
         go, sum_steps(plan, product_of(plan, [[(in_slots(low_flipped), low_grads)]]))
     )
-    held = None
-    grads, sends = {}, []
+    held, back_way = None, None
+    grads, parts = {}, {}
+    flipped = {k: in_slots(flipped[k]) for k in flipped}
     for k in reversed(range(plan.ctx)):
         held, grads[k] = attend_back(
             order, valid, k, held, k == 0, queries, both[k], go, attended, lse, cosine, sine
         )
-        if k == plan.ctx - 1:
-            held = step(held, down_sum, output_sum)
-        elif k == plan.ctx - 2:
-            held = step(held, down_sum, output_sum, pair_sum)
-        elif k:
-            held = step(held, down_sum, output_sum, pair_sum)
-        else:
-            held = step(held, output_sum, pair_sum)
-        part_grads = pull(order, held, grads[k], mixed_w, k)
         if k:
-            held, part_grads = tie(held, part_grads)
-            sends.append(lax.ppermute(part_grads, AXES, plan.across[k]))
-    flipped = {k: in_slots(flipped[k]) for k in flipped}
-    last = product_of(
-        plan, [[(flipped[0], held)], [(flipped[k], grads[k]) for k in range(plan.ctx)]]
-    )
-    part_grads, last_sum = begin(part_grads, sum_steps(plan, last))
-    part_grads = finish(part_grads, down_sum, output_sum, pair_sum)
+            held = step(held, down_sum, output_sum, *([] if k == plan.ctx - 1 else [pair_sum]))
+            parts[k] = pull(order, held, grads[k], mixed_w, k)
+            held, parts[k] = tie(held, parts[k])
+            if plan.line:
+                if back_way is None:
+                    held, back_way = begin(held, return_steps(plan, parts))
+                else:
+                    held = step(held, back_way)
+    groups = [[(flipped[0], held)], [(flipped[k], grads[k]) for k in range(plan.ctx)]]
+    held, last_sum = begin(held, sum_steps(plan, product_of(plan, groups)))
+    held = step(held, output_sum, pair_sum)
+    part_grads = pull(order, held, grads[0], mixed_w, 0)
     part_grads = step(part_grads, last_sum)
+    if plan.line:
+        part_grads = finish(part_grads, back_way)
+        sends = back_way.value
+    else:
+        sends = [lax.ppermute(parts[k], AXES, plan.across[k]) for k in range(1, plan.ctx)]
     tokens_grad, edge_one = end_back(
         order, [part_grads, *sends], own, y_grads, natural[0]
     )
     vectors = sum_vectors(plan, (edge_one[0], edge_one[1], edge_two[0], edge_two[1]))
     finish((), last_sum)
+    finish((), down_sum, output_sum, pair_sum)
     gate_grad, up_grad = part_ways(pair_sum.value, part)
     key_grad, value_grad = part_ways(last_sum.value[:, width:], 128)
     return (

time: 753 us -> 637 us (0.85)
  waiting for transfers between devices: 239 us -> 106 us
  other arithmetic: 55.9 us -> 70 us
  matrix products: 88.4 us -> 80.3 us
    ppermute x18, waiting for transfers between devices: 105 us -> 23.8 us  [the longest x8 22.9 us: sum_steps(): other, = (yield ([lax.ppermute(send, AXES, plan.across[1 << bit])], [send]))]
    ppermute x9, waiting for transfers between devices: 48.4 us -> 24.7 us  [gather_steps(): lax.ppermute(shard, AXES, plan.across[k])]
    ppermute x4, waiting for transfers between devices: 16.9 us -> 0.01 us  [sum_steps(): other, = (yield ([lax.ppermute(send, AXES, plan.core)], [send]))]
    convert_element_type x8 -> x15, other arithmetic: 12 us -> 24 us  [add(): return (a.astype(jnp.float32) + b.astype(jnp.float32)).astype(BF)]
    ppermute x6, waiting for transfers between devices: 54.4 us -> 43.2 us  [gather_steps(): other, = (yield ([lax.ppermute(run, AXES, pairs)], [run]))]
    ppermute x4, waiting for transfers between devices: 10.3 us -> 0.01 us  [sum_steps(): flying = [lax.ppermute(send, AXES, plan.stage[0])]]
    dot_general x24, matrix products: 88.4 us -> 80.3 us  [product(): found = found + jnp.dot(part, right, preferred_element_type=jnp.float32)]
  transfers between devices with their start and end apart: 49 -> 49, of which waited for: 15 -> 13; matrix products, arithmetic and copies ran while one was open for 17% -> 23% of each run, Pallas kernels for 31% -> 42%
where the time goes in v3:
time: 637 us; the launch traced here: 625 us
  Pallas kernels  264 us (41%)
  waiting for transfers between devices  106 us (17%)
  matrix products  80.3 us (13%)
  other arithmetic  70 us (11%)
  starting transfers between devices  64 us (10%)
  local copies, waits for them, and re-layouts  38.2 us (6%)
    pallas_call x21, Pallas kernels, call(): pl.pallas_call(body, out_shape=out_shape, grid_spec=pltpu.PrefetchScalarG...  264 us
    dot_general x24, matrix products, product(): found = found + jnp.dot(part, right, preferred_element_type=jnp.float32)  80.3 us
    ppermute x6, waiting for transfers between devices, gather_steps(): other, = (yield ([lax.ppermute(run, AXES, pairs)], [run]))  43.2 us
    ppermute x9, waiting for transfers between devices, gather_steps(): lax.ppermute(shard, AXES, plan.across[k])  24.7 us
    convert_element_type x15, other arithmetic, add(): return (a.astype(jnp.float32) + b.astype(jnp.float32)).astype(BF)  24 us
    ppermute x8, waiting for transfers between devices, sum_steps(): other, = (yield ([lax.ppermute(send, AXES, plan.across[1 << bit])], [send]))  22.9 us
    concatenate x6, other arithmetic, gather_steps(): run = jnp.concatenate([run, other])  19.8 us
    ppermute x9, starting transfers between devices, gather_steps(): lax.ppermute(shard, AXES, plan.across[k])  16.2 us
  transfers between devices with their start and end apart: 49, of which 13 were waited for; matrix products, arithmetic and copies ran while one was open for 23% of the time, Pallas kernels for 42%

profile of v3, /device:TPU:0, one launch (start us, length us, event | category | flops | bytes accessed | tf_op | source)
XLA Modules:
  0.0 625.3 jit_solution(7500289989252331299)
XLA Ops:
  5.3 5.1 collective-permute-start.2
  15.9 5.6 multiply_sine_fusion
  22.6 11.0 %collective-permute-done.1 = bf16[32,4224]{1,0:T(8,128)(2,1)S(1)} collective-permute-done((bf16[32,4224]{1,0:T(8,128)(2,1)}, bf16[32,4224]{1,0:T(8,128)(2,1)S(1)}, u32[]{:S(2)}, u32[]{:S(2)}) %collective-permute-start.1) | collective-permute-done | bytes 270368 | tf_op jit(solution)/shard_map/ppermute | solution.py:161
  36.6 13.6 %collective-permute-done.3 = bf16[128,4224]{1,0:T(8,128)(2,1)S(1)} collective-permute-done((bf16[128,4224]{1,0:T(8,128)(2,1)S(1)}, bf16[128,4224]{1,0:T(8,128)(2,1)S(1)}, u32[]{:S(2)}, u32[]{:S(2)}) %collective-permute-start.3) | collective-permute-done | bytes 1081376 | tf_op jit(solution)/shard_map/ppermute | solution.py:174
  56.4 20.9 %collective-permute-done.4 = bf16[256,4224]{1,0:T(8,128)(2,1)S(1)} collective-permute-done((bf16[256,4224]{1,0:T(8,128)(2,1)S(1)}, bf16[256,4224]{1,0:T(8,128)(2,1)S(1)}, u32[]{:S(2)}, u32[]{:S(2)}) %collective-permute-start.4) | collective-permute-done | bytes 2162720 | tf_op jit(solution)/shard_map/ppermute | solution.py:174
  77.2 5.7 pad_maximum_fusion.1.refs_0_.refs_1_.refs_2_
  82.9 13.6 %collective-permute-done.6 = bf16[32,8192]{1,0:T(8,128)(2,1)S(1)} collective-permute-done((bf16[32,8192]{1,0:T(8,128)(2,1)S(1)}, bf16[32,8192]{1,0:T(8,128)(2,1)S(1)}, u32[]{:S(2)}, u32[]{:S(2)}) %collective-permute-start.6) | collective-permute-done | bytes 524320 | tf_op jit(solution)/shard_map/ppermute | solution.py:161
  105.1 13.1 %project0.1 = (bf16[1024,512]{1,0:T(8,128)(2,1)}, bf16[512,1024]{1,0:T(8,128)(2,1)}, bf16[512,2048]{1,0:T(8,128)(2,1)}) custom-call(s32[8]{0:T(128)} %fusion.61.order_ref, bf16[512,1024]{1,0:T(8,128)(2,1)} %bitcast.77, f32[1,1024]{1,0:T(1,128)} %get-tuple-element.357.gain_ref, f32[1,1024]{1,0:T(1,128)} %get-tuple-element.356.shift_ref, ...), custom_call_target="tpu_custom_call" | custom-call | flops 3221225472 | bytes 15998976 | tf_op jit(solution)/shard_map/project0/pallas_call | solution.py:307
  118.2 12.4 %attend0.1 = (f32[8,8,512]{2,1,0:T(8,128)}, f32[1024,512]{1,0:T(8,128)}) custom-call(s32[8]{0:T(128)} %fusion.61.order_ref, s32[4]{0:T(128)} %subtract_clamp_fusion.valid_ref, bf16[512,1024]{1,0:T(8,128)(2,1)} %get-tuple-element.206.q_ref, bf16[512,2048]{1,0:T(8,128)(2,1)} %get-tuple-element.207.kv_ref), custom_call_target="tpu_custom_call" | custom-call | flops 4294967296 | bytes 5373968 | tf_op jit(solution)/shard_map/attend0/pallas_call | solution.py:307
  130.6 4.0 pad_maximum_fusion.2
  138.5 10.0 %project1.1 = (bf16[1024,512]{1,0:T(8,128)(2,1)}, bf16[512,2048]{1,0:T(8,128)(2,1)}) custom-call(s32[8]{0:T(128)} %fusion.61.order_ref, bf16[512,1024]{1,0:T(8,128)(2,1)} %collective-permute-done.9.source_ref, f32[1,1024]{1,0:T(1,128)} %get-tuple-element.357.gain_ref, f32[1,1024]{1,0:T(1,128)} %get-tuple-element.356.shift_ref, ...), custom_call_target="tpu_custom_call" | custom-call | flops 2147483648 | bytes 14950400 | tf_op jit(solution)/shard_map/project1/pallas_call | solution.py:307
  148.5 12.7 %attend1.1 = (f32[8,8,512]{2,1,0:T(8,128)}, f32[1024,512]{1,0:T(8,128)}) custom-call(s32[8]{0:T(128)} %fusion.61.order_ref, s32[4]{0:T(128)} %subtract_clamp_fusion.valid_ref, bf16[512,1024]{1,0:T(8,128)(2,1)} %get-tuple-element.206.q_ref, bf16[512,2048]{1,0:T(8,128)(2,1)} %get-tuple-element.211.kv_ref, f32[8,8,512]{2,1,0:T(8,128)} %get-tuple-element.216.refs_0_, ...), custom_call_target="tpu_custom_call" | custom-call | flops 4294967296 | bytes 7602192 | tf_op jit(solution)/shard_map/attend1/pallas_call | solution.py:307
  166.2 9.9 %project2.1 = (bf16[1024,512]{1,0:T(8,128)(2,1)}, bf16[512,2048]{1,0:T(8,128)(2,1)}) custom-call(s32[8]{0:T(128)} %fusion.61.order_ref, bf16[512,1024]{1,0:T(8,128)(2,1)} %add.218.source_ref, f32[1,1024]{1,0:T(1,128)} %get-tuple-element.357.gain_ref, f32[1,1024]{1,0:T(1,128)} %get-tuple-element.356.shift_ref, f32[2048,128]{1,0:T(8,128)} %get-tuple-element.204.cos_ref, ...), custom_call_target="tpu_custom_call" | custom-call | flops 2147483648 | bytes 14950400 | tf_op jit(solution)/shard_map/project2/pallas_call | solution.py:307
  176.1 12.7 %attend2.1 = (f32[8,8,512]{2,1,0:T(8,128)}, f32[1024,512]{1,0:T(8,128)}) custom-call(s32[8]{0:T(128)} %fusion.61.order_ref, s32[4]{0:T(128)} %subtract_clamp_fusion.valid_ref, bf16[512,1024]{1,0:T(8,128)(2,1)} %get-tuple-element.206.q_ref, bf16[512,2048]{1,0:T(8,128)(2,1)} %get-tuple-element.222.kv_ref, f32[8,8,512]{2,1,0:T(8,128)} %get-tuple-element.227.refs_0_, ...), custom_call_target="tpu_custom_call" | custom-call | flops 4294967296 | bytes 7602192 | tf_op jit(solution)/shard_map/attend2/pallas_call | solution.py:307
  188.8 6.6 %pad_maximum_fusion.refs_0_ = bf16[512,8192]{1,0:T(8,128)(2,1)} fusion(bf16[256,8192]{1,0:T(8,128)(2,1)} %collective-permute-done.15, bf16[128,8192]{1,0:T(8,128)(2,1)} %collective-permute-done.11, bf16[128,8192]{1,0:T(8,128)(2,1)S(1)} %maximum_select_fusion), kind=kLoop, calls=%fused_computation.2 | loop fusion | flops 25165824 | bytes 16777216 | tf_op jit(solution)/shard_map/concatenate | solution.py:176
  197.6 4.0 collective-permute-start.17
  204.2 9.9 %project3.1 = (bf16[1024,512]{1,0:T(8,128)(2,1)}, bf16[512,2048]{1,0:T(8,128)(2,1)}) custom-call(s32[8]{0:T(128)} %fusion.61.order_ref, bf16[512,1024]{1,0:T(8,128)(2,1)} %add.219.source_ref, f32[1,1024]{1,0:T(1,128)} %get-tuple-element.357.gain_ref, f32[1,1024]{1,0:T(1,128)} %get-tuple-element.356.shift_ref, f32[2048,128]{1,0:T(8,128)} %get-tuple-element.204.cos_ref, ...), custom_call_target="tpu_custom_call" | custom-call | flops 2147483648 | bytes 14950400 | tf_op jit(solution)/shard_map/project3/pallas_call | solution.py:307
  214.1 13.4 %attend3.1 = (bf16[512,1024]{1,0:T(8,128)(2,1)}, bf16[1024,512]{1,0:T(8,128)(2,1)}, f32[512,1024]{1,0:T(8,128)}, f32[8,8,512]{2,1,0:T(8,128)}) custom-call(s32[8]{0:T(128)} %fusion.61.order_ref, s32[4]{0:T(128)} %subtract_clamp_fusion.valid_ref, bf16[512,1024]{1,0:T(8,128)(2,1)} %get-tuple-element.206.q_ref, bf16[512,2048]{1,0:T(8,128)(2,1)} %get-tuple-element.232.kv_ref, ...), custom_call_target="tpu_custom_call" | custom-call | flops 4294967296 | bytes 9699344 | tf_op jit(solution)/shard_map/attend3/pallas_call | solution.py:307
  230.0 6.1 middle.1
  236.1 7.1 %collective-permute-done.20 = bf16[512,1024]{1,0:T(8,128)(2,1)S(1)} collective-permute-done((bf16[512,1024]{1,0:T(8,128)(2,1)S(1)}, bf16[512,1024]{1,0:T(8,128)(2,1)S(1)}, u32[]{:S(2)}, u32[]{:S(2)}) %collective-permute-start.20) | collective-permute-done | bytes 1048608 | tf_op jit(solution)/shard_map/ppermute | solution.py:174
  245.3 18.3 %feed.1 = (bf16[512,4096]{1,0:T(8,128)(2,1)}, bf16[512,4096]{1,0:T(8,128)(2,1)}, bf16[512,4096]{1,0:T(8,128)(2,1)}, bf16[4096,512]{1,0:T(8,128)(2,1)}) custom-call(s32[8]{0:T(128)} %fusion.61.order_ref, bf16[512,1024]{1,0:T(8,128)(2,1)} %get-tuple-element.259.two_ref, bf16[512,8192]{1,0:T(8,128)(2,1)} %pad_maximum_fusion.refs_0_, ...), custom_call_target="tpu_custom_call" | custom-call | flops 8589934592 | bytes 34603008 | tf_op jit(solution)/shard_map/feed/pallas_call | solution.py:307
  263.6 5.9 convolution_convert_fusion.1
  273.5 6.6 %collective-permute-done.22.refs_3_ = bf16[2048,1024]{1,0:T(8,128)(2,1)S(1)} collective-permute-done((bf16[2048,1024]{1,0:T(8,128)(2,1)S(1)}, bf16[2048,1024]{1,0:T(8,128)(2,1)S(1)}, u32[]{:S(2)}, u32[]{:S(2)}) %collective-permute-start.22) | collective-permute-done | bytes 4194336 | tf_op jit(solution)/shard_map/ppermute | solution.py:177
  282.1 32.2 %feed_back.1 = (bf16[512,1024]{1,0:T(8,128)(2,1)}, bf16[512,8192]{1,0:T(8,128)(2,1)}, f32[512,1024]{1,0:T(8,128)}) custom-call(s32[8]{0:T(128)} %fusion.61.order_ref, bf16[512,1024]{1,0:T(8,128)(2,1)} %bitcast_select_fusion.m_ref, bf16[512,4096]{1,0:T(8,128)(2,1)} %get-tuple-element.261.gate_ref, bf16[512,4096]{1,0:T(8,128)(2,1)} %get-tuple-element.262.up_ref, ...), custom_call_target="tpu_custom_call" | custom-call | flops 17179869184 | bytes 52428800 | tf_op jit(solution)/shard_map/feed_back/pallas_call | solution.py:307
  317.6 4.5 add_convert_fusion.7
  322.1 6.7 %convolution_convert_fusion = bf16[512,8192]{1,0:T(8,128)(2,1)} fusion(bf16[512,8192]{1,0:T(8,128)(2,1)S(1)} %copy-done.50, bf16[1024,512]{1,0:T(8,128)(2,1)S(1)} %copy-done.46), kind=kOutput, calls=%fused_computation.1 | convolution fusion | flops 4299161600 | bytes 17301504 | tf_op jit(solution)/shard_map/dot_general | solution.py:289
  331.4 7.6 %middle_back.1 = (f32[512,1024]{1,0:T(8,128)}, bf16[512,1024]{1,0:T(8,128)(2,1)}, bf16[512,1024]{1,0:T(8,128)(2,1)}, f32[8,1024]{1,0:T(8,128)}) custom-call(s32[8]{0:T(128)} %fusion.61.order_ref, f32[512,1024]{1,0:T(8,128)} %get-tuple-element.281.grads_ref, f32[512,1024]{1,0:T(8,128)} %get-tuple-element.270.resid_ref, ...), custom_call_target="tpu_custom_call" | custom-call | flops 1073741824 | bytes 18124800 | tf_op jit(solution)/shard_map/middle_back/pallas_call | solution.py:307
  344.1 9.2 %add_convert_fusion.2 = bf16[256,8192]{1,0:T(8,128)(2,1)} fusion(bf16[512,8192]{1,0:T(8,128)(2,1)} %collective-permute-done.24, bf16[512,8192]{1,0:T(8,128)(2,1)} %get-tuple-element.280, bf16[1024,512]{1,0:T(8,128)(2,1)S(1)} %copy-done.47), kind=kOutput, calls=%fused_computation.5 | convolution fusion | flops 2153775104 | bytes 17039360 | tf_op jit(solution)/shard_map/dot_general | solution.py:289
  353.8 6.7 %add_convert_fusion.1 = bf16[256,8192]{1,0:T(8,128)(2,1)} fusion(bf16[512,8192]{1,0:T(8,128)(2,1)} %collective-permute-done.24, bf16[512,8192]{1,0:T(8,128)(2,1)S(1)} %bitcast.100, bf16[1024,512]{1,0:T(8,128)(2,1)S(1)} %copy-done.47), kind=kOutput, calls=%fused_computation.4 | convolution fusion | flops 2153775104 | bytes 17039360 | tf_op jit(solution)/shard_map/dot_general | solution.py:289
  360.5 16.5 %attend_back3.1 = (f32[1024,512]{1,0:T(8,128)}, bf16[512,2048]{1,0:T(8,128)(2,1)}) custom-call(s32[8]{0:T(128)} %fusion.61.order_ref, s32[4]{0:T(128)} %subtract_clamp_fusion.valid_ref, bf16[512,1024]{1,0:T(8,128)(2,1)} %get-tuple-element.206.q_ref, bf16[512,2048]{1,0:T(8,128)(2,1)} %get-tuple-element.232.kv_ref, ...), custom_call_target="tpu_custom_call" | custom-call | flops 10737418240 | bytes 12714000 | tf_op jit(solution)/shard_map/attend_back3/pallas_call | solution.py:307
  387.5 7.0 %pull3.1 = bf16[512,1024]{1,0:T(8,128)(2,1)} custom-call(s32[8]{0:T(128)} %fusion.61.order_ref, bf16[512,2048]{1,0:T(8,128)(2,1)} %get-tuple-element.297.refs_0_, bf16[512,4224]{1,0:T(8,128)(2,1)} %pad_maximum_fusion.1.refs_0_.refs_1_.refs_2_, bf16[512,4224]{1,0:T(8,128)(2,1)} %collective-permute-done.8.refs_1_.refs_2_.refs_3_), custom_call_target="tpu_custom_call" | custom-call | flops 524288 | bytes 11796480 | tf_op jit(solution)/shard_map/pull3/pallas_call | solution.py:307
  394.5 16.4 %attend_back2.1 = (f32[1024,512]{1,0:T(8,128)}, bf16[512,2048]{1,0:T(8,128)(2,1)}) custom-call(s32[8]{0:T(128)} %fusion.61.order_ref, s32[4]{0:T(128)} %subtract_clamp_fusion.valid_ref, bf16[512,1024]{1,0:T(8,128)(2,1)} %get-tuple-element.206.q_ref, bf16[512,2048]{1,0:T(8,128)(2,1)} %get-tuple-element.222.kv_ref, ...), custom_call_target="tpu_custom_call" | custom-call | flops 10737418240 | bytes 14811152 | tf_op jit(solution)/shard_map/attend_back2/pallas_call | solution.py:307
  410.9 4.9 collective-permute-start.30
  415.8 7.6 %pull2.1 = bf16[512,1024]{1,0:T(8,128)(2,1)} custom-call(s32[8]{0:T(128)} %fusion.61.order_ref, bf16[512,2048]{1,0:T(8,128)(2,1)} %get-tuple-element.305.refs_0_, bf16[512,4224]{1,0:T(8,128)(2,1)} %pad_maximum_fusion.1.refs_0_.refs_1_.refs_2_, bf16[512,4224]{1,0:T(8,128)(2,1)} %collective-permute-done.8.refs_1_.refs_2_.refs_3_), custom_call_target="tpu_custom_call" | custom-call | flops 524288 | bytes 11796480 | tf_op jit(solution)/shard_map/pull2/pallas_call | solution.py:307
  423.4 4.5 fusion.10
  444.4 6.6 %collective-permute-start.34 = (bf16[512,1024]{1,0:T(8,128)(2,1)S(1)}, bf16[512,1024]{1,0:T(8,128)(2,1)}, u32[]{:S(2)}, u32[]{:S(2)}) collective-permute-start(bf16[512,1024]{1,0:T(8,128)(2,1)S(1)} %copy-done.19), channel_id=1, source_target_pairs={{0,1},{3,2},{4,5},{7,6},{8,9},{11,10},{12,13},{15,14},{16,17},{19,... | collective-permute-start | bytes 3145736 | tf_op jit(solution)/shard_map/ppermute | solution.py:209
  450.9 16.5 %attend_back1.1 = (f32[1024,512]{1,0:T(8,128)}, bf16[512,2048]{1,0:T(8,128)(2,1)}) custom-call(s32[8]{0:T(128)} %fusion.61.order_ref, s32[4]{0:T(128)} %subtract_clamp_fusion.valid_ref, bf16[512,1024]{1,0:T(8,128)(2,1)} %get-tuple-element.206.q_ref, bf16[512,2048]{1,0:T(8,128)(2,1)} %get-tuple-element.211.kv_ref, ...), custom_call_target="tpu_custom_call" | custom-call | flops 10737418240 | bytes 14811152 | tf_op jit(solution)/shard_map/attend_back1/pallas_call | solution.py:307
  467.4 7.1 %pull1.1 = bf16[512,1024]{1,0:T(8,128)(2,1)} custom-call(s32[8]{0:T(128)} %fusion.61.order_ref, bf16[512,2048]{1,0:T(8,128)(2,1)} %get-tuple-element.318.refs_0_, bf16[512,4224]{1,0:T(8,128)(2,1)} %pad_maximum_fusion.1.refs_0_.refs_1_.refs_2_, bf16[512,4224]{1,0:T(8,128)(2,1)} %collective-permute-done.8.refs_1_.refs_2_.refs_3_), custom_call_target="tpu_custom_call" | custom-call | flops 524288 | bytes 11796480 | tf_op jit(solution)/shard_map/pull1/pallas_call | solution.py:307
  474.6 4.5 fusion.12
  494.1 18.6 %attend_back0.1 = (bf16[512,1024]{1,0:T(8,128)(2,1)}, bf16[512,2048]{1,0:T(8,128)(2,1)}) custom-call(s32[8]{0:T(128)} %fusion.61.order_ref, s32[4]{0:T(128)} %subtract_clamp_fusion.valid_ref, bf16[512,1024]{1,0:T(8,128)(2,1)} %get-tuple-element.206.q_ref, bf16[512,2048]{1,0:T(8,128)(2,1)} %get-tuple-element.207.kv_ref, ...), custom_call_target="tpu_custom_call" | custom-call | flops 10737418240 | bytes 13762576 | tf_op jit(solution)/shard_map/attend_back0/pallas_call | solution.py:307
  530.3 7.1 %collective-permute-done.37 = bf16[64,8192]{1,0:T(8,128)(2,1)} collective-permute-done((bf16[64,8192]{1,0:T(8,128)(2,1)}, bf16[64,8192]{1,0:T(8,128)(2,1)}, u32[]{:S(2)}, u32[]{:S(2)}) %collective-permute-start.37) | collective-permute-done | bytes 1048608 | tf_op jit(solution)/shard_map/ppermute | solution.py:247
  540.6 10.1 %pull0.1.refs_0_ = f32[512,1024]{1,0:T(8,128)} custom-call(s32[8]{0:T(128)} %fusion.61.order_ref, bf16[512,1024]{1,0:T(8,128)(2,1)} %get-tuple-element.335.refs_0_, bf16[512,2048]{1,0:T(8,128)(2,1)} %get-tuple-element.327.refs_1_, bf16[512,4224]{1,0:T(8,128)(2,1)} %pad_maximum_fusion.1.refs_0_.refs_1_.refs_2_, ...), custom_call_target="tpu_custom_call" | custom-call | flops 524288 | bytes 13893632 | tf_op jit(solution)/shard_map/pull0/pallas_call | solution.py:307
  563.6 10.3 %collective-permute-done.46 = bf16[32,1024]{1,0:T(8,128)(2,1)S(1)} collective-permute-done((bf16[32,1024]{1,0:T(8,128)(2,1)S(1)}, bf16[32,1024]{1,0:T(8,128)(2,1)S(1)}, u32[]{:S(2)}, u32[]{:S(2)}) %collective-permute-start.46) | collective-permute-done | bytes 65568 | tf_op jit(solution)/shard_map/ppermute | solution.py:247
  583.2 5.6 slice_reduce_fusion
  595.9 6.3 %end_back.1 = (bf16[512,1024]{1,0:T(8,128)(2,1)}, f32[8,1024]{1,0:T(8,128)}) custom-call(s32[8]{0:T(128)} %fusion.61.order_ref, bf16[512,1024]{1,0:T(8,128)(2,1)} %bitcast.79, f32[512,1024]{1,0:T(8,128)} %get-tuple-element.282.y_ref, f32[1,1024]{1,0:T(1,128)} %get-tuple-element.352.gain_ref, f32[512,1024]{1,0:T(8,128)} %pull0.1.refs_0_, ...), custom_call_target="tpu_custom_call" | custom-call | bytes 8425472 | tf_op jit(solution)/shard_map/end_back/pallas_call | solution.py:307
  603.9 4.2 all-to-all-start
  611.0 4.2 all-to-all-done
  616.6 5.5 collective-permute-done.44
  (300 shorter events, 164.0 us)
Async XLA Ops:
  5.3 17.3 %collective-permute-start.2 = (bf16[32,4224]{1,0:T(8,128)(2,1)}, bf16[32,4224]{1,0:T(8,128)(2,1)S(1)}, u32[]{:S(2)}, u32[]{:S(2)}) collective-permute-start(bf16[32,4224]{1,0:T(8,128)(2,1)} %pad_maximum_fusion.10), channel_id=1, source_target_pairs={{0,3},{1,2},{2,1},{3,0},{4,7},{5,6},{6,5},{7,4},{8,11},{9,10},{10,... | collective-permute-start | bytes 811016 | tf_op jit(solution)/shard_map/ppermute | solution.py:161
  10.4 23.2 %collective-permute-start.1 = (bf16[32,4224]{1,0:T(8,128)(2,1)}, bf16[32,4224]{1,0:T(8,128)(2,1)S(1)}, u32[]{:S(2)}, u32[]{:S(2)}) collective-permute-start(bf16[32,4224]{1,0:T(8,128)(2,1)} %pad_maximum_fusion.10), channel_id=1, source_target_pairs={{0,2},{1,3},{2,0},{3,1},{4,6},{5,7},{6,4},{7,5},{8,10},{9,11},{10,... | collective-permute-start | bytes 811016 | tf_op jit(solution)/shard_map/ppermute | solution.py:161
  10.4 23.2 %collective-permute-start = (bf16[32,4224]{1,0:T(8,128)(2,1)}, bf16[32,4224]{1,0:T(8,128)(2,1)}, u32[]{:S(2)}, u32[]{:S(2)}) collective-permute-start(bf16[32,4224]{1,0:T(8,128)(2,1)} %pad_maximum_fusion.10), channel_id=1, source_target_pairs={{0,1},{1,0},{2,3},{3,2},{4,5},{5,4},{6,7},{7,6},{8,9},{9,8},{10,11... | collective-permute-start | bytes 811016 | tf_op jit(solution)/shard_map/ppermute | solution.py:161
  35.1 15.2 %collective-permute-start.3 = (bf16[128,4224]{1,0:T(8,128)(2,1)S(1)}, bf16[128,4224]{1,0:T(8,128)(2,1)S(1)}, u32[]{:S(2)}, u32[]{:S(2)}) collective-permute-start(bf16[128,4224]{1,0:T(8,128)(2,1)S(1)} %maximum_select_fusion.1), channel_id=1, source_target_pairs={{0,16},{1,17},{2,18},{3,19},{4,12},{5,13},{6,14},{7,15},{8,24},{9,... | collective-permute-start | bytes 3244040 | tf_op jit(solution)/shard_map/ppermute | solution.py:174
  50.4 26.8 %collective-permute-start.4 = (bf16[256,4224]{1,0:T(8,128)(2,1)S(1)}, bf16[256,4224]{1,0:T(8,128)(2,1)S(1)}, u32[]{:S(2)}, u32[]{:S(2)}) collective-permute-start(bf16[256,4224]{1,0:T(8,128)(2,1)S(1)} %pad_maximum_fusion.5), channel_id=1, source_target_pairs={{0,8},{1,9},{2,10},{3,11},{4,20},{5,21},{6,22},{7,23},{8,0},{9,1},... | collective-permute-start | bytes 6488072 | tf_op jit(solution)/shard_map/ppermute | solution.py:174
  52.0 31.0 %collective-permute-start.7 = (bf16[32,8192]{1,0:T(8,128)(2,1)S(1)}, bf16[32,8192]{1,0:T(8,128)(2,1)S(1)}, u32[]{:S(2)}, u32[]{:S(2)}) collective-permute-start(bf16[32,8192]{1,0:T(8,128)(2,1)S(1)} %reshape.130), channel_id=1, source_target_pairs={{0,3},{1,2},{2,1},{3,0},{4,7},{5,6},{6,5},{7,4},{8,11},{9,10},{10,... | collective-permute-start | bytes 1572872 | tf_op jit(solution)/shard_map/ppermute | solution.py:161
  54.4 42.1 %collective-permute-start.6 = (bf16[32,8192]{1,0:T(8,128)(2,1)S(1)}, bf16[32,8192]{1,0:T(8,128)(2,1)S(1)}, u32[]{:S(2)}, u32[]{:S(2)}) collective-permute-start(bf16[32,8192]{1,0:T(8,128)(2,1)S(1)} %reshape.130), channel_id=1, source_target_pairs={{0,2},{1,3},{2,0},{3,1},{4,6},{5,7},{6,4},{7,5},{8,10},{9,11},{10,... | collective-permute-start | bytes 1572872 | tf_op jit(solution)/shard_map/ppermute | solution.py:161
  54.5 42.1 %collective-permute-start.5 = (bf16[32,8192]{1,0:T(8,128)(2,1)S(1)}, bf16[32,8192]{1,0:T(8,128)(2,1)S(1)}, u32[]{:S(2)}, u32[]{:S(2)}) collective-permute-start(bf16[32,8192]{1,0:T(8,128)(2,1)S(1)} %reshape.130), channel_id=1, source_target_pairs={{0,1},{1,0},{2,3},{3,2},{4,5},{5,4},{6,7},{7,6},{8,9},{9,8},{10,11... | collective-permute-start | bytes 1572872 | tf_op jit(solution)/shard_map/ppermute | solution.py:161
  82.9 20.5 %collective-permute-start.8 = (bf16[512,4224]{1,0:T(8,128)(2,1)}, bf16[512,4224]{1,0:T(8,128)(2,1)}, u32[]{:S(2)}, u32[]{:S(2)}) collective-permute-start(bf16[512,4224]{1,0:T(8,128)(2,1)} %pad_maximum_fusion.1.refs_0_.refs_1_.refs_2_), channel_id=1, source_target_pairs={{0,4},{1,5},{2,6},{3,7},{4,0},{5,1},{6,2},{7,3},{8,12},{9,13},{10,... | collective-permute-start | bytes 12976136 | tf_op jit(solution)/shard_map/ppermute | solution.py:177
  97.4 33.3 %collective-permute-start.11 = (bf16[128,8192]{1,0:T(8,128)(2,1)S(1)}, bf16[128,8192]{1,0:T(8,128)(2,1)}, u32[]{:S(2)}, u32[]{:S(2)}) collective-permute-start(bf16[128,8192]{1,0:T(8,128)(2,1)S(1)} %maximum_select_fusion), channel_id=1, source_target_pairs={{0,16},{1,17},{2,18},{3,19},{4,12},{5,13},{6,14},{7,15},{8,24},{9,... | collective-permute-start | bytes 6291464 | tf_op jit(solution)/shard_map/ppermute | solution.py:174
  99.2 31.5 %collective-permute-start.10 = (bf16[512,1024]{1,0:T(8,128)(2,1)S(1)}, bf16[512,1024]{1,0:T(8,128)(2,1)}, u32[]{:S(2)}, u32[]{:S(2)}) collective-permute-start(bf16[512,1024]{1,0:T(8,128)(2,1)S(1)} %bitcast.80), channel_id=1, source_target_pairs={{1,2},{2,1},{5,6},{6,5},{9,10},{10,9},{13,14},{14,13},{17,18},{18,... | collective-permute-start | bytes 3145736 | tf_op jit(solution)/shard_map/ppermute | solution.py:192
  100.8 29.8 %collective-permute-start.9 = (bf16[512,1024]{1,0:T(8,128)(2,1)S(1)}, bf16[512,1024]{1,0:T(8,128)(2,1)}, u32[]{:S(2)}, u32[]{:S(2)}) collective-permute-start(bf16[512,1024]{1,0:T(8,128)(2,1)S(1)} %bitcast.81), channel_id=1, source_target_pairs={{0,1},{1,0},{2,3},{3,2},{4,5},{5,4},{6,7},{7,6},{8,9},{9,8},{10,11... | collective-permute-start | bytes 3145736 | tf_op jit(solution)/shard_map/ppermute | solution.py:192
  134.6 54.2 %collective-permute-start.15 = (bf16[256,8192]{1,0:T(8,128)(2,1)}, bf16[256,8192]{1,0:T(8,128)(2,1)}, u32[]{:S(2)}, u32[]{:S(2)}) collective-permute-start(bf16[256,8192]{1,0:T(8,128)(2,1)} %pad_maximum_fusion.2), channel_id=1, source_target_pairs={{0,8},{1,9},{2,10},{3,11},{4,20},{5,21},{6,22},{7,23},{8,0},{9,1},... | collective-permute-start | bytes 12582920 | tf_op jit(solution)/shard_map/ppermute | solution.py:174
  136.1 25.0 %collective-permute-start.13 = (bf16[512,1024]{1,0:T(8,128)(2,1)}, bf16[512,1024]{1,0:T(8,128)(2,1)S(1)}, u32[]{:S(2)}, u32[]{:S(2)}) collective-permute-start(bf16[512,1024]{1,0:T(8,128)(2,1)} %collective-permute-done.9.source_ref), channel_id=1, source_target_pairs={{1,2},{2,1},{5,6},{6,5},{9,10},{10,9},{13,14},{14,13},{17,18},{18,... | collective-permute-start | bytes 3145736 | tf_op jit(solution)/shard_map/ppermute | solution.py:197
  136.9 25.1 %collective-permute-start.12 = (bf16[512,1024]{1,0:T(8,128)(2,1)}, bf16[512,1024]{1,0:T(8,128)(2,1)}, u32[]{:S(2)}, u32[]{:S(2)}) collective-permute-start(bf16[512,1024]{1,0:T(8,128)(2,1)} %collective-permute-done.10), channel_id=1, source_target_pairs={{1,0},{2,3},{5,4},{6,7},{9,8},{10,11},{13,12},{14,15},{17,16},{18,... | collective-permute-start | bytes 3145736 | tf_op jit(solution)/shard_map/ppermute | solution.py:197
  162.0 26.8 %collective-permute-start.14 = (bf16[512,1024]{1,0:T(8,128)(2,1)S(1)}, bf16[512,1024]{1,0:T(8,128)(2,1)}, u32[]{:S(2)}, u32[]{:S(2)}) collective-permute-start(bf16[512,1024]{1,0:T(8,128)(2,1)S(1)} %collective-permute-done.13), channel_id=1, source_target_pairs={{1,0},{2,3},{5,4},{6,7},{9,8},{10,11},{13,12},{14,15},{17,16},{18,... | collective-permute-start | bytes 3145736 | tf_op jit(solution)/shard_map/ppermute | solution.py:201
  195.4 40.7 %collective-permute-start.19 = (bf16[512,8192]{1,0:T(8,128)(2,1)}, bf16[512,8192]{1,0:T(8,128)(2,1)}, u32[]{:S(2)}, u32[]{:S(2)}) collective-permute-start(bf16[512,8192]{1,0:T(8,128)(2,1)} %pad_maximum_fusion.refs_0_), channel_id=1, source_target_pairs={{0,4},{1,5},{2,6},{3,7},{4,0},{5,1},{6,2},{7,3},{8,12},{9,13},{10,... | collective-permute-start | bytes 25165832 | tf_op jit(solution)/shard_map/ppermute | solution.py:177
  195.4 32.1 %collective-permute-start.18 = (bf16[128,1024]{1,0:T(8,128)(2,1)S(1)}, bf16[128,1024]{1,0:T(8,128)(2,1)S(1)}, u32[]{:S(2)}, u32[]{:S(2)}) collective-permute-start(bf16[128,1024]{1,0:T(8,128)(2,1)S(1)} %copy-done.41), channel_id=1, source_target_pairs={{0,3},{1,2},{2,1},{3,0},{4,7},{5,6},{6,5},{7,4},{8,11},{9,10},{10,... | collective-permute-start | bytes 786440 | tf_op jit(solution)/shard_map/ppermute | solution.py:161
  197.6 30.0 %collective-permute-start.17 = (bf16[128,1024]{1,0:T(8,128)(2,1)S(1)}, bf16[128,1024]{1,0:T(8,128)(2,1)S(1)}, u32[]{:S(2)}, u32[]{:S(2)}) collective-permute-start(bf16[128,1024]{1,0:T(8,128)(2,1)S(1)} %copy-done.41), channel_id=1, source_target_pairs={{0,2},{1,3},{2,0},{3,1},{4,6},{5,7},{6,4},{7,5},{8,10},{9,11},{10,... | collective-permute-start | bytes 786440 | tf_op jit(solution)/shard_map/ppermute | solution.py:161
  201.6 26.0 %collective-permute-start.16 = (bf16[128,1024]{1,0:T(8,128)(2,1)S(1)}, bf16[128,1024]{1,0:T(8,128)(2,1)S(1)}, u32[]{:S(2)}, u32[]{:S(2)}) collective-permute-start(bf16[128,1024]{1,0:T(8,128)(2,1)S(1)} %copy-done.41), channel_id=1, source_target_pairs={{0,1},{1,0},{2,3},{3,2},{4,5},{5,4},{6,7},{7,6},{8,9},{9,8},{10,11... | collective-permute-start | bytes 786440 | tf_op jit(solution)/shard_map/ppermute | solution.py:161
  228.3 14.9 %collective-permute-start.20 = (bf16[512,1024]{1,0:T(8,128)(2,1)S(1)}, bf16[512,1024]{1,0:T(8,128)(2,1)S(1)}, u32[]{:S(2)}, u32[]{:S(2)}) collective-permute-start(bf16[512,1024]{1,0:T(8,128)(2,1)S(1)} %maximum_select_fusion.4), channel_id=1, source_target_pairs={{0,16},{1,17},{2,18},{3,19},{4,12},{5,13},{6,14},{7,15},{8,24},{9,... | collective-permute-start | bytes 3145736 | tf_op jit(solution)/shard_map/ppermute | solution.py:174
  244.7 26.4 %collective-permute-start.21 = (bf16[1024,1024]{1,0:T(8,128)(2,1)}, bf16[1024,1024]{1,0:T(8,128)(2,1)}, u32[]{:S(2)}, u32[]{:S(2)}) collective-permute-start(bf16[1024,1024]{1,0:T(8,128)(2,1)} %pad_maximum_fusion.6), channel_id=1, source_target_pairs={{0,8},{1,9},{2,10},{3,11},{4,20},{5,21},{6,22},{7,23},{8,0},{9,1},... | collective-permute-start | bytes 6291464 | tf_op jit(solution)/shard_map/ppermute | solution.py:174
  272.9 7.2 %collective-permute-start.22 = (bf16[2048,1024]{1,0:T(8,128)(2,1)S(1)}, bf16[2048,1024]{1,0:T(8,128)(2,1)S(1)}, u32[]{:S(2)}, u32[]{:S(2)}) collective-permute-start(bf16[2048,1024]{1,0:T(8,128)(2,1)S(1)} %pad_maximum_fusion.3.refs_2_), channel_id=1, source_target_pairs={{0,4},{1,5},{2,6},{3,7},{4,0},{5,1},{6,2},{7,3},{8,12},{9,13},{10,... | collective-permute-start | bytes 12582920 | tf_op jit(solution)/shard_map/ppermute | solution.py:177
  273.0 41.3 %collective-permute-start.23 = (bf16[2048,1024]{1,0:T(8,128)(2,1)}, bf16[2048,1024]{1,0:T(8,128)(2,1)}, u32[]{:S(2)}, u32[]{:S(2)}) collective-permute-start(bf16[2048,1024]{1,0:T(8,128)(2,1)} %convolution_convert_fusion.1), channel_id=1, source_target_pairs={{0,4},{1,5},{2,6},{3,7},{4,0},{5,1},{6,2},{7,3},{8,12},{9,13},{10,... | collective-permute-start | bytes 12582920 | tf_op jit(solution)/shard_map/ppermute | solution.py:229
  328.8 15.2 %collective-permute-start.24 = (bf16[512,8192]{1,0:T(8,128)(2,1)}, bf16[512,8192]{1,0:T(8,128)(2,1)}, u32[]{:S(2)}, u32[]{:S(2)}) collective-permute-start(bf16[512,8192]{1,0:T(8,128)(2,1)} %convolution_convert_fusion), channel_id=1, source_target_pairs={{0,4},{1,5},{2,6},{3,7},{4,0},{5,1},{6,2},{7,3},{8,12},{9,13},{10,... | collective-permute-start | bytes 25165832 | tf_op jit(solution)/shard_map/ppermute | solution.py:229
  330.8 46.2 %collective-permute-start.25 = (bf16[1024,1024]{1,0:T(8,128)(2,1)}, bf16[1024,1024]{1,0:T(8,128)(2,1)}, u32[]{:S(2)}, u32[]{:S(2)}) collective-permute-start(bf16[1024,1024]{1,0:T(8,128)(2,1)} %add_convert_fusion.7), channel_id=1, source_target_pairs={{0,8},{1,9},{2,10},{3,11},{4,20},{5,21},{6,22},{7,23},{8,0},{9,1},... | collective-permute-start | bytes 6291464 | tf_op jit(solution)/shard_map/ppermute | solution.py:233
  342.9 34.0 %collective-permute-start.26 = (bf16[512,1024]{1,0:T(8,128)(2,1)}, bf16[512,1024]{1,0:T(8,128)(2,1)}, u32[]{:S(2)}, u32[]{:S(2)}) collective-permute-start(bf16[512,1024]{1,0:T(8,128)(2,1)} %convolution_convert_fusion.3), channel_id=1, source_target_pairs={{0,4},{1,5},{2,6},{3,7},{4,0},{5,1},{6,2},{7,3},{8,12},{9,13},{10,... | collective-permute-start | bytes 3145736 | tf_op jit(solution)/shard_map/ppermute | solution.py:229
  353.3 74.6 %collective-permute-start.29 = (bf16[256,8192]{1,0:T(8,128)(2,1)}, bf16[256,8192]{1,0:T(8,128)(2,1)}, u32[]{:S(2)}, u32[]{:S(2)}) collective-permute-start(bf16[256,8192]{1,0:T(8,128)(2,1)} %add_convert_fusion.2), channel_id=1, source_target_pairs={{0,8},{1,9},{2,10},{3,11},{4,20},{5,21},{6,22},{7,23},{8,0},{9,1},... | collective-permute-start | bytes 12582920 | tf_op jit(solution)/shard_map/ppermute | solution.py:233
  379.4 48.5 %collective-permute-start.28 = (bf16[256,1024]{1,0:T(8,128)(2,1)}, bf16[256,1024]{1,0:T(8,128)(2,1)}, u32[]{:S(2)}, u32[]{:S(2)}) collective-permute-start(bf16[256,1024]{1,0:T(8,128)(2,1)} %add_convert_fusion.22), channel_id=1, source_target_pairs={{0,8},{1,9},{2,10},{3,11},{4,20},{5,21},{6,22},{7,23},{8,0},{9,1},... | collective-permute-start | bytes 1572872 | tf_op jit(solution)/shard_map/ppermute | solution.py:233
  384.6 43.3 %collective-permute-start.27 = (bf16[512,1024]{1,0:T(8,128)(2,1)}, bf16[512,1024]{1,0:T(8,128)(2,1)S(1)}, u32[]{:S(2)}, u32[]{:S(2)}) collective-permute-start(bf16[512,1024]{1,0:T(8,128)(2,1)} %slice.272), channel_id=1, source_target_pairs={{0,16},{1,17},{2,18},{3,19},{4,12},{5,13},{6,14},{7,15},{8,24},{9,... | collective-permute-start | bytes 3145736 | tf_op jit(solution)/shard_map/ppermute | solution.py:240
  410.9 28.8 %collective-permute-start.30 = (bf16[512,1024]{1,0:T(8,128)(2,1)}, bf16[512,1024]{1,0:T(8,128)(2,1)}, u32[]{:S(2)}, u32[]{:S(2)}) collective-permute-start(bf16[512,1024]{1,0:T(8,128)(2,1)} %pull3.1), channel_id=1, source_target_pairs={{0,1},{3,2},{4,5},{7,6},{8,9},{11,10},{12,13},{15,14},{16,17},{19,... | collective-permute-start | bytes 3145736 | tf_op jit(solution)/shard_map/ppermute | solution.py:206
  434.9 44.2 %collective-permute-start.32 = (bf16[128,1024]{1,0:T(8,128)(2,1)}, bf16[128,1024]{1,0:T(8,128)(2,1)S(1)}, u32[]{:S(2)}, u32[]{:S(2)}) collective-permute-start(bf16[128,1024]{1,0:T(8,128)(2,1)} %slice.274), channel_id=1, source_target_pairs={{0,16},{1,17},{2,18},{3,19},{4,12},{5,13},{6,14},{7,15},{8,24},{9,... | collective-permute-start | bytes 786440 | tf_op jit(solution)/shard_map/ppermute | solution.py:240
  438.0 41.1 %collective-permute-start.33 = (bf16[128,8192]{1,0:T(8,128)(2,1)}, bf16[128,8192]{1,0:T(8,128)(2,1)}, u32[]{:S(2)}, u32[]{:S(2)}) collective-permute-start(bf16[128,8192]{1,0:T(8,128)(2,1)} %slice.275), channel_id=1, source_target_pairs={{0,16},{1,17},{2,18},{3,19},{4,12},{5,13},{6,14},{7,15},{8,24},{9,... | collective-permute-start | bytes 6291464 | tf_op jit(solution)/shard_map/ppermute | solution.py:240
  439.7 39.4 %collective-permute-start.31 = (bf16[256,1024]{1,0:T(8,128)(2,1)}, bf16[256,1024]{1,0:T(8,128)(2,1)}, u32[]{:S(2)}, u32[]{:S(2)}) collective-permute-start(bf16[256,1024]{1,0:T(8,128)(2,1)} %constant_dynamic-slice_fusion.7), channel_id=1, source_target_pairs={{0,2},{1,3},{2,0},{3,1},{4,6},{5,7},{6,4},{7,5},{8,10},{9,11},{10,... | collective-permute-start | bytes 1572872 | tf_op jit(solution)/shard_map/ppermute | solution.py:247
  442.7 44.5 %collective-permute-start.35 = (bf16[512,1024]{1,0:T(8,128)(2,1)}, bf16[512,1024]{1,0:T(8,128)(2,1)}, u32[]{:S(2)}, u32[]{:S(2)}) collective-permute-start(bf16[512,1024]{1,0:T(8,128)(2,1)} %add_convert_fusion.14), channel_id=1, source_target_pairs={{1,2},{2,1},{5,6},{6,5},{9,10},{10,9},{13,14},{14,13},{17,18},{18,... | collective-permute-start | bytes 3145736 | tf_op jit(solution)/shard_map/ppermute | solution.py:209
  444.4 42.8 %collective-permute-start.34 = (bf16[512,1024]{1,0:T(8,128)(2,1)S(1)}, bf16[512,1024]{1,0:T(8,128)(2,1)}, u32[]{:S(2)}, u32[]{:S(2)}) collective-permute-start(bf16[512,1024]{1,0:T(8,128)(2,1)S(1)} %copy-done.19), channel_id=1, source_target_pairs={{0,1},{3,2},{4,5},{7,6},{8,9},{11,10},{12,13},{15,14},{16,17},{19,... | collective-permute-start | bytes 3145736 | tf_op jit(solution)/shard_map/ppermute | solution.py:209
  481.4 48.9 %collective-permute-start.36 = (bf16[64,1024]{1,0:T(8,128)(2,1)S(1)}, bf16[64,1024]{1,0:T(8,128)(2,1)S(1)}, u32[]{:S(2)}, u32[]{:S(2)}) collective-permute-start(bf16[64,1024]{1,0:T(8,128)(2,1)S(1)} %constant_dynamic-slice_fusion.5), channel_id=1, source_target_pairs={{0,2},{1,3},{2,0},{3,1},{4,6},{5,7},{6,4},{7,5},{8,10},{9,11},{10,... | collective-permute-start | bytes 393224 | tf_op jit(solution)/shard_map/ppermute | solution.py:247
  483.2 80.1 %collective-permute-start.45 = (bf16[128,1024]{1,0:T(8,128)(2,1)S(1)}, bf16[128,1024]{1,0:T(8,128)(2,1)}, u32[]{:S(2)}, u32[]{:S(2)}) collective-permute-start(bf16[128,1024]{1,0:T(8,128)(2,1)S(1)} %constant_dynamic-slice_fusion.6), channel_id=1, source_target_pairs={{0,1},{1,0},{2,3},{3,2},{4,5},{5,4},{6,7},{7,6},{8,9},{9,8},{10,11... | collective-permute-start | bytes 786440 | tf_op jit(solution)/shard_map/ppermute | solution.py:247
  486.8 50.7 %collective-permute-start.37 = (bf16[64,8192]{1,0:T(8,128)(2,1)}, bf16[64,8192]{1,0:T(8,128)(2,1)}, u32[]{:S(2)}, u32[]{:S(2)}) collective-permute-start(bf16[64,8192]{1,0:T(8,128)(2,1)} %constant_dynamic-slice_fusion.4), channel_id=1, source_target_pairs={{0,2},{1,3},{2,0},{3,1},{4,6},{5,7},{6,4},{7,5},{8,10},{9,11},{10,... | collective-permute-start | bytes 3145736 | tf_op jit(solution)/shard_map/ppermute | solution.py:247
  489.8 106.1 %collective-permute-start.39 = (bf16[512,1024]{1,0:T(8,128)(2,1)}, bf16[512,1024]{1,0:T(8,128)(2,1)}, u32[]{:S(2)}, u32[]{:S(2)}) collective-permute-start(bf16[512,1024]{1,0:T(8,128)(2,1)} %add_convert_fusion.13), channel_id=1, source_target_pairs={{1,2},{2,1},{5,6},{6,5},{9,10},{10,9},{13,14},{14,13},{17,18},{18,... | collective-permute-start | bytes 3145736 | tf_op jit(solution)/shard_map/ppermute | solution.py:216
  523.3 27.4 %collective-permute-start.38 = (bf16[512,3072]{1,0:T(8,128)(2,1)}, bf16[512,3072]{1,0:T(8,128)(2,1)}, u32[]{:S(2)}, u32[]{:S(2)}) collective-permute-start(bf16[512,3072]{1,0:T(8,128)(2,1)} %pad_maximum_fusion.4), channel_id=1, source_target_pairs={{0,4},{1,5},{2,6},{3,7},{4,0},{5,1},{6,2},{7,3},{8,12},{9,13},{10,... | collective-permute-start | bytes 9437192 | tf_op jit(solution)/shard_map/ppermute | solution.py:229
  555.2 23.0 %collective-permute-start.41 = (bf16[256,3072]{1,0:T(8,128)(2,1)S(1)}, bf16[256,3072]{1,0:T(8,128)(2,1)S(1)}, u32[]{:S(2)}, u32[]{:S(2)}) collective-permute-start(bf16[256,3072]{1,0:T(8,128)(2,1)S(1)} %pad_maximum_fusion.7), channel_id=1, source_target_pairs={{0,8},{1,9},{2,10},{3,11},{4,20},{5,21},{6,22},{7,23},{8,0},{9,1},... | collective-permute-start | bytes 4718600 | tf_op jit(solution)/shard_map/ppermute | solution.py:233
  557.6 16.3 %collective-permute-start.47 = (bf16[32,8192]{1,0:T(8,128)(2,1)S(1)}, bf16[32,8192]{1,0:T(8,128)(2,1)S(1)}, u32[]{:S(2)}, u32[]{:S(2)}) collective-permute-start(bf16[32,8192]{1,0:T(8,128)(2,1)S(1)} %constant_dynamic-slice_fusion.2), channel_id=1, source_target_pairs={{0,1},{1,0},{2,3},{3,2},{4,5},{5,4},{6,7},{7,6},{8,9},{9,8},{10,11... | collective-permute-start | bytes 1572872 | tf_op jit(solution)/shard_map/ppermute | solution.py:247
  559.6 14.3 %collective-permute-start.46 = (bf16[32,1024]{1,0:T(8,128)(2,1)S(1)}, bf16[32,1024]{1,0:T(8,128)(2,1)S(1)}, u32[]{:S(2)}, u32[]{:S(2)}) collective-permute-start(bf16[32,1024]{1,0:T(8,128)(2,1)S(1)} %copy-done.42), channel_id=1, source_target_pairs={{0,1},{1,0},{2,3},{3,2},{4,5},{5,4},{6,7},{7,6},{8,9},{9,8},{10,11... | collective-permute-start | bytes 196616 | tf_op jit(solution)/shard_map/ppermute | solution.py:247
  563.3 32.7 %collective-permute-start.40 = (bf16[512,1024]{1,0:T(8,128)(2,1)}, bf16[512,1024]{1,0:T(8,128)(2,1)}, u32[]{:S(2)}, u32[]{:S(2)}) collective-permute-start(bf16[512,1024]{1,0:T(8,128)(2,1)} %add_convert_fusion.12), channel_id=1, source_target_pairs={{0,1},{1,0},{2,3},{3,2},{4,5},{5,4},{6,7},{7,6},{8,9},{9,8},{10,11... | collective-permute-start | bytes 3145736 | tf_op jit(solution)/shard_map/ppermute | solution.py:217
  579.7 12.3 %collective-permute-start.42 = (bf16[128,3072]{1,0:T(8,128)(2,1)}, bf16[128,3072]{1,0:T(8,128)(2,1)}, u32[]{:S(2)}, u32[]{:S(2)}) collective-permute-start(bf16[128,3072]{1,0:T(8,128)(2,1)} %slice.279), channel_id=1, source_target_pairs={{0,16},{1,17},{2,18},{3,19},{4,12},{5,13},{6,14},{7,15},{8,24},{9,... | collective-permute-start | bytes 2359304 | tf_op jit(solution)/shard_map/ppermute | solution.py:240
  594.1 21.2 %collective-permute-start.43 = (bf16[64,3072]{1,0:T(8,128)(2,1)}, bf16[64,3072]{1,0:T(8,128)(2,1)S(1)}, u32[]{:S(2)}, u32[]{:S(2)}) collective-permute-start(bf16[64,3072]{1,0:T(8,128)(2,1)} %constant_dynamic-slice_fusion.1), channel_id=1, source_target_pairs={{0,2},{1,3},{2,0},{3,1},{4,6},{5,7},{6,4},{7,5},{8,10},{9,11},{10,... | collective-permute-start | bytes 1179656 | tf_op jit(solution)/shard_map/ppermute | solution.py:247
  603.9 11.4 %all-to-all-start = ((f32[32,1,128]{2,1,0:T(1,128)}), f32[32,1,128]{2,1,0:T(1,128)S(1)}, u32[]{:S(2)}, u32[]{:S(2)}) async-start(f32[32,1,128]{2,1,0:T(1,128)} %bitcast.19), calls=%async_computation | async-start | bytes 32768 | tf_op jit(solution)/shard_map/all_to_all | solution.py:257
  (54 other events, 382.1 us)

commit v4 on v3

--- a/solution.py
+++ b/solution.py
@@ -144,6 +144,20 @@
     return tie(main, [chain.sent for chain in chains])[0]
 
 
+def wait(main, *chains):
+    main, came = tie(main, [chain.flying for chain in chains])
+    for chain, arrays in zip(chains, came):
+        chain.came = arrays
+    return main
+
+
+def go_on(main, *chains):
+    main, came = tie(main, [chain.came for chain in chains])
+    for chain, arrays in zip(chains, came):
+        chain.land(arrays)
+    return tie(main, [chain.sent for chain in chains])[0]
+
+
 def begin(main, steps):
     chain = Chain(steps)
     return tie(main, chain.sent)[0], chain
@@ -155,28 +169,47 @@
     return main
 
 
-def gather_steps(plan, shard):
+def gather_steps(plan, shard, line=False):
     place = lax.axis_index("ctx")
-    blocks = yield (
-        [lax.ppermute(shard, AXES, plan.across[k]) for k in range(1, plan.ctx)],
-        [shard],
-    )
-    blocks = [shard, *blocks]
-    for bit in range(plan.ctx_bits):
-        upper = (place >> bit) & 1 == 1
-        blocks = [
-            jnp.where(upper, jnp.concatenate([b, a]), jnp.concatenate([a, b]))
-            for a, b in zip(blocks[::2], blocks[1::2])
-        ]
-    run = blocks[0]
-    pieces = [run]
-    for pairs in reversed(plan.stage):
+    if line and plan.line:
+        near, middle = yield (
+            [lax.ppermute(shard, AXES, plan.across[1]), lax.ppermute(shard, AXES, plan.inner)],
+            [shard],
+        )
+        far, cross = yield (
+            [lax.ppermute(middle, AXES, plan.outward), lax.ppermute(near, AXES, plan.inner)],
+            [middle, near],
+        )
+        (last,) = yield [lax.ppermute(cross, AXES, plan.outward)], [cross]
+        two, three = middle + far, cross + last
+        upper = place >= 2
+        blocks = [shard, near, jnp.where(upper, three, two), jnp.where(upper, two, three)]
+        odd = place % 2 == 1
+        run = jnp.where(
+            upper,
+            jnp.concatenate(blocks[2:] + [jnp.where(odd, near, shard), jnp.where(odd, shard, near)]),
+            jnp.concatenate([jnp.where(odd, near, shard), jnp.where(odd, shard, near)] + blocks[2:]),
+        )
+    else:
+        blocks = yield (
+            [lax.ppermute(shard, AXES, plan.across[k]) for k in range(1, plan.ctx)],
+            [shard],
+        )
+        blocks = [shard, *blocks]
+        for bit in range(plan.ctx_bits):
+            upper = (place >> bit) & 1 == 1
+            blocks = [
+                jnp.where(upper, jnp.concatenate([b, a]), jnp.concatenate([a, b]))
+                for a, b in zip(blocks[::2], blocks[1::2])
+            ]
+        run = blocks[0]
+    *early, final = reversed(plan.stage)
+    for pairs in early:
         (other,) = yield [lax.ppermute(run, AXES, pairs)], [run]
-        pieces.append(other)
         run = jnp.concatenate([run, other])
-    (other,) = yield [lax.ppermute(run, AXES, plan.core)], [run]
-    pieces.append(other)
-    return run, pieces
+    other, far = yield [lax.ppermute(run, AXES, final), lax.ppermute(run, AXES, plan.core)], [run]
+    (last,) = yield [lax.ppermute(other, AXES, plan.core)], [other]
+    return [run, other, far, last]
 
 
 def add(a, b):
@@ -221,11 +254,12 @@
     )
 
 
-def sum_steps(plan, product):
+def sum_steps(plan, product, send=None):
     place = lax.axis_index("ctx")
     half = plan.dp // 2
 
-    send = product(half, plan.dp)
+    if send is None:
+        send = product(half, plan.dp)
     (other,) = yield [lax.ppermute(send, AXES, plan.core)], [send]
     rows = other.shape[0] // half
     size = half // 2
@@ -239,13 +273,18 @@
         send = held[size * rows :]
         (other,) = yield [lax.ppermute(send, AXES, pairs)], [send]
         held = add(held[: size * rows], other)
-    for bit in reversed(range(plan.ctx_bits)):
-        cut = held.shape[0] // 2
-        upper = (place >> bit) & 1
-        send = lax.dynamic_slice_in_dim(held, (1 - upper) * cut, cut, 0)
-        keep = lax.dynamic_slice_in_dim(held, upper * cut, cut, 0)
+    width = held.shape[1]
+    for bit in range(plan.ctx_bits):
+        left = 1 << (plan.ctx_bits - bit - 1)
+        lower = (place >> bit) & 1
+        cut = held.reshape(left, 2, -1, width)
+        send = lax.dynamic_index_in_dim(cut, 1 - lower, 1, False).reshape(-1, width)
+        keep = lax.dynamic_index_in_dim(cut, lower, 1, False).reshape(-1, width)
         (other,) = yield [lax.ppermute(send, AXES, plan.across[1 << bit])], [send]
-        held = add(keep, other) if bit else keep.astype(jnp.float32) + other.astype(jnp.float32)
+        if left > 1:
+            held = add(keep, other)
+        else:
+            held = keep.astype(jnp.float32) + other.astype(jnp.float32)
     return held
 
 
@@ -352,7 +391,7 @@
     return found
 
 
-def project(order, source, gain, shift, mixed, cosine, sine, block):
+def project(order, source, cols, mixed, cosine, sine, block):
     rows, width = source.shape
     tile = 512
     tiles = width // tile
@@ -360,20 +399,27 @@
     count = len(mixed)
     scale = 1.0 / math.sqrt(HD)
 
-    def body(order_ref, source_ref, gain_ref, shift_ref, cos_ref, sin_ref, *refs):
-        weights = refs[:count]
-        outs, normed = refs[count:-1], refs[-1]
+    def body(order_ref, source_ref, cos_ref, sin_ref, *refs):
+        weights, edges = refs[:count], refs[count : -1 - found_outs]
+        outs, normed = refs[-1 - found_outs : -1], refs[-1]
+        cols_ref = outs[-1] if block == 0 else edges[0]
         at = pl.program_id(0) + skip
 
         @pl.when(at == skip)
         def _():
+            if block == 0:
+                low = 0
+                for edge in edges:
+                    high = low + edge.shape[0]
+                    cols_ref[:, low:high] = edge[...].astype(jnp.float32).T[:8]
+                    low = high
             spread(order_ref, source_ref, normed, slice(None))
             chunk = math.gcd(rows, 128)
 
             def one(i, unused):
                 here = pl.ds(pl.multiple_of(i * chunk, chunk), chunk)
                 found = normed[here, :].astype(jnp.float32)
-                normed[here, :] = layer_norm(found, gain_ref[...], shift_ref[...]).astype(BF)
+                normed[here, :] = layer_norm(found, cols_ref[0:1, :], cols_ref[1:2, :]).astype(BF)
                 return unused
 
             lax.fori_loop(0, rows // chunk, one, 0)
@@ -393,9 +439,10 @@
 
         @pl.when(at >= tiles)
         def _():
+            both_ref = outs[2] if block == 0 else outs[1]
             for c in range(0, tile, 256):
-                outs[-1][:, c : c + 128] = turned(c)
-                outs[-1][:, c + 128 : c + 256] = found[:, c + 128 : c + 256].astype(BF)
+                both_ref[:, c : c + 128] = turned(c)
+                both_ref[:, c + 128 : c + 256] = found[:, c + 128 : c + 256].astype(BF)
 
     table = pl.BlockSpec((rows, 128), lambda j, order: (block, 0))
     outs = [(whole((width, rows)), array((width, rows)))]
@@ -412,18 +459,28 @@
             array((rows, 2 * width)),
         )
     )
+    if block == 0:
+        outs.append((whole((8, width)), array((8, width), jnp.float32)))
+        edges = [
+            pl.BlockSpec((piece.shape[0], 128), lambda j, order: (0, 3 * width // 128))
+            for piece in mixed
+        ]
+    else:
+        edges = [whole((8, width))]
+    found_outs = len(outs)
     return call(
         body,
         order,
         (3 * tiles - skip,),
-        [whole((rows, width)), whole((1, width)), whole((1, width)), table, table]
+        [whole((rows, width)), table, table]
         + [
             pl.BlockSpec((piece.shape[0], tile), lambda j, order: (0, j + skip)) for piece in mixed
-        ],
+        ]
+        + edges,
         outs,
-        (source, gain[None, :], shift[None, :], cosine, sine, *mixed),
+        (source, cosine, sine, *mixed, *(mixed if block == 0 else [cols])),
         f"project{block}",
-        2 * rows * width * width * (2 if block else 3),
+        32 * rows * width * width * (2 if block else 3),
         scratch=[pltpu.VMEM((rows, width), BF)],
     )
 
@@ -499,7 +556,7 @@
         outs,
         (valid, queries, both, *(() if first else state)),
         f"attend{block}",
-        16 * rows * rows * width,
+        256 * rows * rows * width,
         transcendentals=16 * rows * rows,
     )
 
@@ -580,18 +637,19 @@
     )
 
 
-def middle(order, attended, mixed, tokens, gain, shift):
+def middle(order, attended, mixed, tokens, cols):
     rows, width = tokens.shape
     count = len(mixed)
+    last = mixed[0].shape[1] // width - 1
     chunk = math.gcd(rows, 256)
 
-    def body(order_ref, o_ref, x_ref, gain_ref, shift_ref, *refs):
+    def body(order_ref, o_ref, x_ref, cols_ref, *refs):
         weights = refs[:count]
         resid_ref, two_ref, flipped_ref, held = refs[count:]
         found = x_ref[...].astype(jnp.float32) + by_pieces(o_ref, weights)
         resid_ref[...] = found
         spread(order_ref, resid_ref, held, slice(None))
-        two = layer_norm(held[...], gain_ref[...], shift_ref[...]).astype(BF)
+        two = layer_norm(held[...], cols_ref[2:3, :], cols_ref[3:4, :]).astype(BF)
         two_ref[...] = two
         flipped_ref[...] = two.T
 
@@ -600,14 +658,14 @@
         body,
         order,
         (rows // chunk,),
-        [line, line, whole((1, width)), whole((1, width))]
-        + [pl.BlockSpec((piece.shape[0], width), lambda i, order: (0, 3)) for piece in mixed],
+        [line, line, whole((8, width))]
+        + [pl.BlockSpec((piece.shape[0], width), lambda i, order: (0, last)) for piece in mixed],
         [
             (line, array((rows, width), jnp.float32)),
             (line, array((rows, width))),
             (pl.BlockSpec((width, chunk), lambda i, order: (0, i)), array((width, rows))),
         ],
-        (attended, tokens, gain[None, :], shift[None, :], *mixed),
+        (attended, tokens, cols, *mixed),
         "middle",
         2 * rows * width * width,
         scratch=[pltpu.VMEM((chunk, width), jnp.float32)],
@@ -617,7 +675,7 @@
 def feed(order, two, pair):
     rows, width = two.shape
     blocks = order.shape[0]
-    hidden = pair[0].shape[1] // 2
+    hidden = (pair[0].shape[1] - width) // 2
     part = hidden // blocks
     count = len(pair)
 
@@ -750,6 +808,7 @@
 def middle_back(order, grads, resid, upstream, mixed, gain):
     rows, width = resid.shape
     count = len(mixed)
+    last = mixed[0].shape[1] // width - 1
     chunk = math.gcd(rows, 256)
 
     def body(order_ref, grads_ref, resid_ref, m_ref, gain_ref, *refs):
@@ -778,7 +837,7 @@
         order,
         (rows // chunk,),
         [line, line, line, whole((1, width))]
-        + [pl.BlockSpec((piece.shape[0], width), lambda i, order: (0, 3)) for piece in mixed],
+        + [pl.BlockSpec((piece.shape[0], width), lambda i, order: (0, last)) for piece in mixed],
         [
             (line, array((rows, width), jnp.float32)),
             (line, array((rows, width))),
@@ -926,10 +985,9 @@
     part = hidden // order.shape[0]
 
     def pieces_of(chain, shard):
-        run, pieces = chain.value
         if exact:
-            return [run, pieces[-1]]
-        return [assemble(slots, pieces, shard.shape[0] * plan.ctx)]
+            return chain.value
+        return [assemble(slots, chain.value, shard.shape[0] * plan.ctx)]
 
     def in_slots(flipped):
         if exact:
@@ -940,7 +998,7 @@
     edge = jnp.stack([attention_gain, attention_shift, feed_gain, feed_shift], axis=1)
     edge = jnp.pad(edge, ((0, 0), (0, 124)))
     both = join(key_weight, value_weight, 128)
-    mixed = jnp.concatenate([query_weight, both, output_weight, edge], axis=1)
+    mixed = jnp.concatenate([query_weight, both, edge], axis=1)
     mix = Chain(gather_steps(plan, mixed))
 
     seats = jnp.arange(local_len, dtype=jnp.int32)
@@ -951,49 +1009,46 @@
     upstream = jnp.where(real, cotangent.reshape(rows, width), 0)
     own = tokens.reshape(rows, width)
 
-    pair_own = join(gate_weight, up_weight, part)
+    pair_own = jnp.concatenate([join(gate_weight, up_weight, part), output_weight], axis=1)
     early = (pair_own, cosine, sine, upstream)
     pair_own, cosine, sine, upstream = step(early, mix)
-    pair = Chain(gather_steps(plan, pair_own))
-    own = step(own, mix)
+    pair = Chain(gather_steps(plan, pair_own, line=True))
+    own = step(own, mix, pair)
+    own = step(own, mix, pair)
     came = {}
     own, window = begin(own, window_steps(plan, own, came))
-    own = step(own, mix)
-    own = step(own, pair)
     own = finish(own, mix)
     mixed_w = pieces_of(mix, mixed)
-    cols = jnp.concatenate([piece[:, 4 * width : 4 * width + 4] for piece in mixed_w])
-    cols = cols.T.astype(jnp.float32)
     back = jnp.asarray(plan.back)[lax.axis_index("dp")] if exact else order
-    natural = cols.reshape(4, order.shape[0], -1)[:, back].reshape(4, width)
 
     flipped, both = {}, {}
-    flipped[0], queries, both[0] = project(order, own, cols[0], cols[1], mixed_w, cosine, sine, 0)
+    cols = None
+    flipped[0], queries, both[0], cols = project(order, own, cols, mixed_w, cosine, sine, 0)
+    both[0] = step(both[0], pair)
     state = attend(order, valid, 0, None, plan.ctx == 1, queries, both[0])
     down = None
     for k in range(1, plan.ctx):
         while k not in came:
-            state = step(state, window, pair) if k == 1 else step(state, window)
-        if k == 2:
+            state = step(state, window)
+        if k == min(3, plan.ctx - 1):
             down_own, state = tie(down_weight, state)
             down = Chain(gather_steps(plan, down_own))
-        if k == 3:
-            state = step(state, pair)
-        flipped[k], both[k] = project(
-            order, came[k], cols[0], cols[1], mixed_w, cosine, sine, k
-        )
+        flipped[k], both[k] = project(order, came[k], cols, mixed_w, cosine, sine, k)
+        if k == 1:
+            both[k] = step(both[k], pair)
         state = attend(order, valid, k, state, k == plan.ctx - 1, queries, both[k])
-    state = step(state, down)
+    state = step(state, pair, down)
+    state = finish(state, pair)
+    pair_w = pieces_of(pair, pair_own)
+    natural = cols[:4].reshape(4, order.shape[0], -1)[:, back].reshape(4, width)
     low, low_flipped, attended, lse = state
-    resid, two, two_flipped = middle(order, low, mixed_w, own, cols[2], cols[3])
-    two = finish(two, pair)
+    resid, two, two_flipped = middle(order, low, pair_w, own, cols)
     two = step(two, down)
-    pair_w = pieces_of(pair, pair_own)
     gate, up, made, made_flipped = feed(order, two, pair_w)
-    made, down_sum = begin(
-        made, sum_steps(plan, product_of(plan, [[(in_slots(made_flipped), upstream)]]))
-    )
-    made = finish(made, down)
+    product = product_of(plan, [[(in_slots(made_flipped), upstream)]])
+    first = product(plan.dp // 2, plan.dp)
+    made, first = finish((made, first), down)
+    made, down_sum = begin(made, sum_steps(plan, product, first))
     down_w = pieces_of(down, down_weight)
     output, pair_grads, two_grads = feed_back(
         order, upstream, gate, up, made, resid, pair_w, down_w
@@ -1005,7 +1060,7 @@
         two_grads, sum_steps(plan, product_of(plan, [[(in_slots(two_flipped), pair_grads)]]))
     )
     y_grads, low_grads, go, edge_two = middle_back(
-        order, two_grads, resid, upstream, mixed_w, natural[2]
+        order, two_grads, resid, upstream, pair_w, natural[2]
     )
     go = step(go, pair_sum)
     go, output_sum = begin(
@@ -1019,19 +1074,29 @@
             order, valid, k, held, k == 0, queries, both[k], go, attended, lse, cosine, sine
         )
         if k:
-            held = step(held, down_sum, output_sum, *([] if k == plan.ctx - 1 else [pair_sum]))
+            if k == plan.ctx - 1:
+                held = step(held, down_sum, output_sum)
+            else:
+                if plan.line:
+                    held = wait(held, back_way)
+                held = step(held, pair_sum)
+            held, grads[k] = tie(held, grads[k])
             parts[k] = pull(order, held, grads[k], mixed_w, k)
             held, parts[k] = tie(held, parts[k])
             if plan.line:
                 if back_way is None:
                     held, back_way = begin(held, return_steps(plan, parts))
                 else:
-                    held = step(held, back_way)
+                    held = go_on(held, back_way)
+            if k < plan.ctx - 1:
+                held = step(held, down_sum, output_sum)
+    finals = [down_sum, output_sum, pair_sum]
+    held = wait(held, *finals)
     groups = [[(flipped[0], held)], [(flipped[k], grads[k]) for k in range(plan.ctx)]]
     held, last_sum = begin(held, sum_steps(plan, product_of(plan, groups)))
-    held = step(held, output_sum, pair_sum)
+    held = go_on(held, down_sum, output_sum)
+    held = step(held, last_sum)
     part_grads = pull(order, held, grads[0], mixed_w, 0)
-    part_grads = step(part_grads, last_sum)
     if plan.line:
         part_grads = finish(part_grads, back_way)
         sends = back_way.value
@@ -1040,6 +1105,8 @@
     tokens_grad, edge_one = end_back(
         order, [part_grads, *sends], own, y_grads, natural[0]
     )
+    edge_one = step(edge_one, last_sum)
+    edge_one = go_on(edge_one, pair_sum)
     vectors = sum_vectors(plan, (edge_one[0], edge_one[1], edge_two[0], edge_two[1]))
     finish((), last_sum)
     finish((), down_sum, output_sum, pair_sum)

time: 637 us -> 606 us (0.951)
  waiting for transfers between devices: 106 us -> 91.2 us
  matrix products: 80.3 us -> 67 us
    ppermute x6 -> x3, waiting for transfers between devices: 43.2 us -> 1.82 us  [gather_steps(): other, = (yield ([lax.ppermute(run, AXES, pairs)], [run]))]
    ppermute x3 -> x14, waiting for transfers between devices: 6.65 us -> 39.5 us  [the longest x1 13.5 us: gather_steps(): lax.ppermute(shard, AXES, plan.across[1])]
    ppermute x9 -> x6, waiting for transfers between devices: 24.7 us -> 5.26 us  [gather_steps(): lax.ppermute(shard, AXES, plan.across[k])]
    all_to_all x1, waiting for transfers between devices: 4.23 us -> 18.3 us  [sum_vectors(): came = lax.all_to_all(packed, AXES, split_axis=0, concat_axis=0, tiled=True)]
    concatenate x6 -> x3, other arithmetic: 19.8 us -> 5.68 us  [gather_steps(): run = jnp.concatenate([run, other])]
    dot_general x24, matrix products: 80.3 us -> 67 us  [product(): found = found + jnp.dot(part, right, preferred_element_type=jnp.float32)]
    ppermute x8, waiting for transfers between devices: 22.9 us -> 12.9 us  [sum_steps(): other, = (yield ([lax.ppermute(send, AXES, plan.across[1 << bit])], [send]))]
    ppermute x3 -> x14, starting transfers between devices: 0.08 us -> 9.1 us  [the longest x3 2.64 us: gather_steps(): lax.ppermute(run, AXES, final)]
  transfers between devices with their start and end apart: 49 -> 54, of which waited for: 13 -> 16; matrix products, arithmetic and copies ran while one was open for 23% -> 22% of each run, Pallas kernels for 42% -> 45%
where the time goes in v4:
time: 606 us; the launch traced here: 597 us
  Pallas kernels  266 us (44%)
  waiting for transfers between devices  91.2 us (15%)
  starting transfers between devices  69.5 us (11%)
  matrix products  67 us (11%)
  other arithmetic  65.8 us (11%)
  local copies, waits for them, and re-layouts  34.9 us (6%)
    pallas_call x21, Pallas kernels, call(): pl.pallas_call(body, out_shape=out_shape, grid_spec=pltpu.PrefetchScalarG...  266 us
    dot_general x24, matrix products, product(): found = found + jnp.dot(part, right, preferred_element_type=jnp.float32)  67 us
    convert_element_type x15, other arithmetic, add(): return (a.astype(jnp.float32) + b.astype(jnp.float32)).astype(BF)  30 us
    all_to_all x1, waiting for transfers between devices, sum_vectors(): came = lax.all_to_all(packed, AXES, split_axis=0, concat_axis=0, tiled=True)  18.3 us
    ppermute x1, waiting for transfers between devices, gather_steps(): lax.ppermute(shard, AXES, plan.across[1])  13.5 us
    ppermute x1, waiting for transfers between devices, gather_steps(): lax.ppermute(middle, AXES, plan.outward)  13.1 us
    ppermute x8, waiting for transfers between devices, sum_steps(): other, = (yield ([lax.ppermute(send, AXES, plan.across[1 << bit])], [send]))  12.9 us
    unnamed x115, local copies, waits for them, and re-layouts  12.3 us
  transfers between devices with their start and end apart: 54, of which 16 were waited for; matrix products, arithmetic and copies ran while one was open for 22% of the time, Pallas kernels for 45%

profile of v4, /device:TPU:0, one launch (start us, length us, event | category | flops | bytes accessed | tf_op | source)
XLA Modules:
  0.0 596.7 jit_solution(12358624069843519653)
XLA Ops:
  5.3 5.1 collective-permute-start.2
  15.9 5.6 multiply_sine_fusion
  22.7 5.2 collective-permute-done.1
  32.0 13.5 %collective-permute-done.4 = bf16[32,9216]{1,0:T(8,128)(2,1)} collective-permute-done((bf16[32,9216]{1,0:T(8,128)(2,1)S(1)}, bf16[32,9216]{1,0:T(8,128)(2,1)}, u32[]{:S(2)}, u32[]{:S(2)}) %collective-permute-start.4) | collective-permute-done | bytes 589856 | tf_op jit(solution)/shard_map/ppermute | solution.py:176
  51.5 13.1 %collective-permute-done.8 = bf16[32,9216]{1,0:T(8,128)(2,1)} collective-permute-done((bf16[32,9216]{1,0:T(8,128)(2,1)}, bf16[32,9216]{1,0:T(8,128)(2,1)}, u32[]{:S(2)}, u32[]{:S(2)}) %collective-permute-start.8) | collective-permute-done | bytes 589856 | tf_op jit(solution)/shard_map/ppermute | solution.py:180
  72.3 5.5 collective-permute-start.12
  77.8 13.2 %project0.1 = (bf16[1024,512]{1,0:T(8,128)(2,1)}, bf16[512,1024]{1,0:T(8,128)(2,1)}, bf16[512,2048]{1,0:T(8,128)(2,1)}, f32[8,1024]{1,0:T(8,128)}) custom-call(s32[8]{0:T(128)} %fusion.61.order_ref, bf16[512,1024]{1,0:T(8,128)(2,1)} %bitcast.8.source_ref.x_ref, f32[2048,128]{1,0:T(8,128)} %get-tuple-element.241.cos_ref, ...), custom_call_target="tpu_custom_call" | custom-call | flops 51539607552 | bytes 20480000 | tf_op jit(solution)/shard_map/project0/pallas_call | solution.py:346
  94.8 12.4 %attend0.1 = (f32[8,8,512]{2,1,0:T(8,128)}, f32[1024,512]{1,0:T(8,128)}) custom-call(s32[8]{0:T(128)} %fusion.61.order_ref, s32[4]{0:T(128)} %subtract_clamp_fusion.valid_ref, bf16[512,1024]{1,0:T(8,128)(2,1)} %get-tuple-element.245.q_ref, bf16[512,2048]{1,0:T(8,128)(2,1)} %get-tuple-element.250.kv_ref), custom_call_target="tpu_custom_call" | custom-call | flops 68719476736 | bytes 5373968 | tf_op jit(solution)/shard_map/attend0/pallas_call | solution.py:346
  112.0 10.0 %project1.1 = (bf16[1024,512]{1,0:T(8,128)(2,1)}, bf16[512,2048]{1,0:T(8,128)(2,1)}) custom-call(s32[8]{0:T(128)} %fusion.61.order_ref, bf16[512,1024]{1,0:T(8,128)(2,1)} %collective-permute-done.12.source_ref, f32[2048,128]{1,0:T(8,128)} %get-tuple-element.241.cos_ref, f32[2048,128]{1,0:T(8,128)} %get-tuple-element.242.sin_ref, bf16[256,3200]{1,0:T(8,128)(2,1)} %copy-done, ...), custom_call_target="tpu_custom_call" | custom-call | flops 34359738368 | bytes 12877824 | tf_op jit(solution)/shard_map/project1/pallas_call | solution.py:346
  122.5 4.2 pad_maximum_fusion.refs_0_
  127.2 12.7 %attend1.1 = (f32[8,8,512]{2,1,0:T(8,128)}, f32[1024,512]{1,0:T(8,128)}) custom-call(s32[8]{0:T(128)} %fusion.61.order_ref, s32[4]{0:T(128)} %subtract_clamp_fusion.valid_ref, bf16[512,1024]{1,0:T(8,128)(2,1)} %get-tuple-element.245.q_ref, bf16[512,2048]{1,0:T(8,128)(2,1)} %get-tuple-element.258.kv_ref, f32[8,8,512]{2,1,0:T(8,128)} %get-tuple-element.262.refs_0_, ...), custom_call_target="tpu_custom_call" | custom-call | flops 68719476736 | bytes 7602192 | tf_op jit(solution)/shard_map/attend1/pallas_call | solution.py:346
  140.0 2.9 add.233.source_ref
  144.2 10.0 %project2.1 = (bf16[1024,512]{1,0:T(8,128)(2,1)}, bf16[512,2048]{1,0:T(8,128)(2,1)}) custom-call(s32[8]{0:T(128)} %fusion.61.order_ref, bf16[512,1024]{1,0:T(8,128)(2,1)} %add.233.source_ref, f32[2048,128]{1,0:T(8,128)} %get-tuple-element.241.cos_ref, f32[2048,128]{1,0:T(8,128)} %get-tuple-element.242.sin_ref, bf16[256,3200]{1,0:T(8,128)(2,1)} %copy-done, ...), custom_call_target="tpu_custom_call" | custom-call | flops 34359738368 | bytes 12877824 | tf_op jit(solution)/shard_map/project2/pallas_call | solution.py:346
  154.1 12.8 %attend2.1 = (f32[8,8,512]{2,1,0:T(8,128)}, f32[1024,512]{1,0:T(8,128)}) custom-call(s32[8]{0:T(128)} %fusion.61.order_ref, s32[4]{0:T(128)} %subtract_clamp_fusion.valid_ref, bf16[512,1024]{1,0:T(8,128)(2,1)} %get-tuple-element.245.q_ref, bf16[512,2048]{1,0:T(8,128)(2,1)} %get-tuple-element.268.kv_ref, f32[8,8,512]{2,1,0:T(8,128)} %get-tuple-element.271.refs_0_, ...), custom_call_target="tpu_custom_call" | custom-call | flops 68719476736 | bytes 7602192 | tf_op jit(solution)/shard_map/attend2/pallas_call | solution.py:346
  166.9 3.8 collective-permute-done.17
  176.5 10.0 %project3.1 = (bf16[1024,512]{1,0:T(8,128)(2,1)}, bf16[512,2048]{1,0:T(8,128)(2,1)}) custom-call(s32[8]{0:T(128)} %fusion.61.order_ref, bf16[512,1024]{1,0:T(8,128)(2,1)} %add.234.source_ref, f32[2048,128]{1,0:T(8,128)} %get-tuple-element.241.cos_ref, f32[2048,128]{1,0:T(8,128)} %get-tuple-element.242.sin_ref, bf16[256,3200]{1,0:T(8,128)(2,1)} %copy-done, ...), custom_call_target="tpu_custom_call" | custom-call | flops 34359738368 | bytes 12877824 | tf_op jit(solution)/shard_map/project3/pallas_call | solution.py:346
  186.5 13.4 %attend3.1 = (bf16[512,1024]{1,0:T(8,128)(2,1)}, bf16[1024,512]{1,0:T(8,128)(2,1)}, f32[512,1024]{1,0:T(8,128)}, f32[8,8,512]{2,1,0:T(8,128)}) custom-call(s32[8]{0:T(128)} %fusion.61.order_ref, s32[4]{0:T(128)} %subtract_clamp_fusion.valid_ref, bf16[512,1024]{1,0:T(8,128)(2,1)} %get-tuple-element.245.q_ref, bf16[512,2048]{1,0:T(8,128)(2,1)} %get-tuple-element.276.kv_ref, ...), custom_call_target="tpu_custom_call" | custom-call | flops 68719476736 | bytes 9699344 | tf_op jit(solution)/shard_map/attend3/pallas_call | solution.py:346
  202.4 5.9 collective-permute-done.23.refs_3_
  208.3 6.1 %middle.1 = (f32[512,1024]{1,0:T(8,128)}, bf16[512,1024]{1,0:T(8,128)(2,1)}, bf16[1024,512]{1,0:T(8,128)(2,1)}) custom-call(s32[8]{0:T(128)} %fusion.61.order_ref, bf16[512,1024]{1,0:T(8,128)(2,1)} %get-tuple-element.304.o_ref, bf16[512,1024]{1,0:T(8,128)(2,1)} %bitcast.8.source_ref.x_ref, f32[8,1024]{1,0:T(8,128)} %get-tuple-element.254.refs_4_.cols_ref, ...), custom_call_target="tpu_custom_call" | custom-call | flops 1073741824 | bytes 25198592 | tf_op jit(solution)/shard_map/middle/pallas_call | solution.py:346
  219.7 18.5 %feed.1 = (bf16[512,4096]{1,0:T(8,128)(2,1)}, bf16[512,4096]{1,0:T(8,128)(2,1)}, bf16[512,4096]{1,0:T(8,128)(2,1)}, bf16[4096,512]{1,0:T(8,128)(2,1)}) custom-call(s32[8]{0:T(128)} %fusion.61.order_ref, bf16[512,1024]{1,0:T(8,128)(2,1)} %get-tuple-element.310.two_ref, bf16[256,9216]{1,0:T(8,128)(2,1)} %pad_maximum_fusion.refs_0_, ...), custom_call_target="tpu_custom_call" | custom-call | flops 8589934592 | bytes 36700160 | tf_op jit(solution)/shard_map/feed/pallas_call | solution.py:346
  238.2 6.0 %convolution_convert_fusion.1 = bf16[2048,1024]{1,0:T(8,128)(2,1)} fusion(bf16[512,1024]{1,0:T(8,128)(2,1)S(1)} %copy-done.15, bf16[4096,512]{1,0:T(8,128)(2,1)} %get-tuple-element.314), kind=kOutput, calls=%fused_computation.11 | convolution fusion | flops 2149580800 | bytes 7340032 | tf_op jit(solution)/shard_map/dot_general | solution.py:328
  244.4 4.4 collective-permute-done.27.refs_7_
  250.1 33.7 %feed_back.1 = (bf16[512,1024]{1,0:T(8,128)(2,1)}, bf16[512,8192]{1,0:T(8,128)(2,1)}, f32[512,1024]{1,0:T(8,128)}) custom-call(s32[8]{0:T(128)} %fusion.61.order_ref, bf16[512,1024]{1,0:T(8,128)(2,1)} %bitcast_select_fusion.m_ref, bf16[512,4096]{1,0:T(8,128)(2,1)} %get-tuple-element.311.gate_ref, bf16[512,4096]{1,0:T(8,128)(2,1)} %get-tuple-element.312.up_ref, ...), custom_call_target="tpu_custom_call" | custom-call | flops 17179869184 | bytes 54525952 | tf_op jit(solution)/shard_map/feed_back/pallas_call | solution.py:346
  283.8 4.6 add_convert_fusion.6
  288.5 3.2 add_convert_fusion.7
  291.8 6.7 %convolution_convert_fusion = bf16[512,8192]{1,0:T(8,128)(2,1)} fusion(bf16[512,8192]{1,0:T(8,128)(2,1)S(1)} %copy-done.52, bf16[1024,512]{1,0:T(8,128)(2,1)S(1)} %copy-done.46), kind=kOutput, calls=%fused_computation.1 | convolution fusion | flops 4299161600 | bytes 17301504 | tf_op jit(solution)/shard_map/dot_general | solution.py:328
  301.9 7.5 %middle_back.1 = (f32[512,1024]{1,0:T(8,128)}, bf16[512,1024]{1,0:T(8,128)(2,1)}, bf16[512,1024]{1,0:T(8,128)(2,1)}, f32[8,1024]{1,0:T(8,128)}) custom-call(s32[8]{0:T(128)} %fusion.61.order_ref, f32[512,1024]{1,0:T(8,128)} %get-tuple-element.336.grads_ref, f32[512,1024]{1,0:T(8,128)} %get-tuple-element.323.resid_ref, ...), custom_call_target="tpu_custom_call" | custom-call | flops 1073741824 | bytes 28348416 | tf_op jit(solution)/shard_map/middle_back/pallas_call | solution.py:346
  312.0 9.1 %add_convert_fusion.2 = bf16[256,8192]{1,0:T(8,128)(2,1)} fusion(bf16[512,8192]{1,0:T(8,128)(2,1)} %collective-permute-done.29, bf16[512,8192]{1,0:T(8,128)(2,1)} %get-tuple-element.335, bf16[1024,512]{1,0:T(8,128)(2,1)S(1)} %copy-done.47), kind=kOutput, calls=%fused_computation.4 | convolution fusion | flops 2153775104 | bytes 17039360 | tf_op jit(solution)/shard_map/dot_general | solution.py:328
  324.2 6.8 %add_convert_fusion.1 = bf16[256,8192]{1,0:T(8,128)(2,1)} fusion(bf16[512,8192]{1,0:T(8,128)(2,1)} %collective-permute-done.29, bf16[512,8192]{1,0:T(8,128)(2,1)S(1)} %bitcast.156, bf16[1024,512]{1,0:T(8,128)(2,1)S(1)} %copy-done.47), kind=kOutput, calls=%fused_computation.3 | convolution fusion | flops 2153775104 | bytes 17039360 | tf_op jit(solution)/shard_map/dot_general | solution.py:328
  331.0 16.3 %attend_back3.1 = (f32[1024,512]{1,0:T(8,128)}, bf16[512,2048]{1,0:T(8,128)(2,1)}) custom-call(s32[8]{0:T(128)} %fusion.61.order_ref, s32[4]{0:T(128)} %subtract_clamp_fusion.valid_ref, bf16[512,1024]{1,0:T(8,128)(2,1)} %get-tuple-element.245.q_ref, bf16[512,2048]{1,0:T(8,128)(2,1)} %get-tuple-element.276.kv_ref, ...), custom_call_target="tpu_custom_call" | custom-call | flops 10737418240 | bytes 12714000 | tf_op jit(solution)/shard_map/attend_back3/pallas_call | solution.py:346
  347.4 3.3 add_convert_fusion.5
  356.3 7.0 %pull3.1 = bf16[512,1024]{1,0:T(8,128)(2,1)} custom-call(s32[8]{0:T(128)} %fusion.61.order_ref, bf16[512,2048]{1,0:T(8,128)(2,1)} %get-tuple-element.354.refs_0_, bf16[256,3200]{1,0:T(8,128)(2,1)} %copy-done, bf16[256,3200]{1,0:T(8,128)(2,1)} %collective-permute-done.6.refs_1_.refs_5_.refs_2_.refs_3_, bf16[256,3200]{1,0:T(8,128)(2,1)} %copy-done.8, ...), custom_call_target="tpu_custom_call" | custom-call | flops 524288 | bytes 9699328 | tf_op jit(solution)/shard_map/pull3/pallas_call | solution.py:346
  367.5 16.7 %attend_back2.1 = (f32[1024,512]{1,0:T(8,128)}, bf16[512,2048]{1,0:T(8,128)(2,1)}) custom-call(s32[8]{0:T(128)} %fusion.61.order_ref, s32[4]{0:T(128)} %subtract_clamp_fusion.valid_ref, bf16[512,1024]{1,0:T(8,128)(2,1)} %get-tuple-element.245.q_ref, bf16[512,2048]{1,0:T(8,128)(2,1)} %get-tuple-element.268.kv_ref, ...), custom_call_target="tpu_custom_call" | custom-call | flops 10737418240 | bytes 14811152 | tf_op jit(solution)/shard_map/attend_back2/pallas_call | solution.py:346
  384.2 4.5 collective-permute-done.32
  388.7 5.4 add_convert_fusion
  397.3 7.0 %pull2.1 = bf16[512,1024]{1,0:T(8,128)(2,1)} custom-call(s32[8]{0:T(128)} %fusion.61.order_ref, bf16[512,2048]{1,0:T(8,128)(2,1)} %get-tuple-element.364.refs_0_, bf16[256,3200]{1,0:T(8,128)(2,1)} %copy-done, bf16[256,3200]{1,0:T(8,128)(2,1)} %collective-permute-done.6.refs_1_.refs_5_.refs_2_.refs_3_, bf16[256,3200]{1,0:T(8,128)(2,1)} %copy-done.8, ...), custom_call_target="tpu_custom_call" | custom-call | flops 524288 | bytes 9699328 | tf_op jit(solution)/shard_map/pull2/pallas_call | solution.py:346
  404.4 3.0 add_convert_fusion.14
  409.0 7.0 %collective-permute-start.36 = (bf16[512,1024]{1,0:T(8,128)(2,1)S(1)}, bf16[512,1024]{1,0:T(8,128)(2,1)}, u32[]{:S(2)}, u32[]{:S(2)}) collective-permute-start(bf16[512,1024]{1,0:T(8,128)(2,1)S(1)} %copy-done.12), channel_id=1, source_target_pairs={{0,1},{3,2},{4,5},{7,6},{8,9},{11,10},{12,13},{15,14},{16,17},{19,... | collective-permute-start | bytes 3145736 | tf_op jit(solution)/shard_map/ppermute | solution.py:242
  422.2 3.3 fusion.15
  425.5 16.9 %attend_back1.1 = (f32[1024,512]{1,0:T(8,128)}, bf16[512,2048]{1,0:T(8,128)(2,1)}) custom-call(s32[8]{0:T(128)} %fusion.61.order_ref, s32[4]{0:T(128)} %subtract_clamp_fusion.valid_ref, bf16[512,1024]{1,0:T(8,128)(2,1)} %get-tuple-element.245.q_ref, bf16[512,2048]{1,0:T(8,128)(2,1)} %get-tuple-element.258.kv_ref, ...), custom_call_target="tpu_custom_call" | custom-call | flops 10737418240 | bytes 14811152 | tf_op jit(solution)/shard_map/attend_back1/pallas_call | solution.py:346
  448.3 7.2 %pull1.1 = bf16[512,1024]{1,0:T(8,128)(2,1)} custom-call(s32[8]{0:T(128)} %fusion.61.order_ref, bf16[512,2048]{1,0:T(8,128)(2,1)} %get-tuple-element.382.refs_0_, bf16[256,3200]{1,0:T(8,128)(2,1)} %copy-done, bf16[256,3200]{1,0:T(8,128)(2,1)} %collective-permute-done.6.refs_1_.refs_5_.refs_2_.refs_3_, bf16[256,3200]{1,0:T(8,128)(2,1)} %copy-done.8, ...), custom_call_target="tpu_custom_call" | custom-call | flops 524288 | bytes 9699328 | tf_op jit(solution)/shard_map/pull1/pallas_call | solution.py:346
  465.9 18.3 %attend_back0.1 = (bf16[512,1024]{1,0:T(8,128)(2,1)}, bf16[512,2048]{1,0:T(8,128)(2,1)}) custom-call(s32[8]{0:T(128)} %fusion.61.order_ref, s32[4]{0:T(128)} %subtract_clamp_fusion.valid_ref, bf16[512,1024]{1,0:T(8,128)(2,1)} %get-tuple-element.245.q_ref, bf16[512,2048]{1,0:T(8,128)(2,1)} %get-tuple-element.250.kv_ref, ...), custom_call_target="tpu_custom_call" | custom-call | flops 10737418240 | bytes 13762576 | tf_op jit(solution)/shard_map/attend_back0/pallas_call | solution.py:346
  514.4 9.8 %pull0.1.refs_0_ = f32[512,1024]{1,0:T(8,128)} custom-call(s32[8]{0:T(128)} %fusion.61.order_ref, bf16[512,1024]{1,0:T(8,128)(2,1)} %get-tuple-element.410.refs_0_, bf16[512,2048]{1,0:T(8,128)(2,1)} %get-tuple-element.398.refs_1_, bf16[256,3200]{1,0:T(8,128)(2,1)} %copy-done, bf16[256,3200]{1,0:T(8,128)(2,1)} %collective-permute-done.6.refs_1_.refs_5_.refs_2_.refs_3_, ...), custom_call_target="tpu_custom_call" | custom-call | flops 524288 | bytes 11796480 | tf_op jit(solution)/shard_map/pull0/pallas_call | solution.py:346
  524.2 6.2 %end_back.1 = (bf16[512,1024]{1,0:T(8,128)(2,1)}, f32[8,1024]{1,0:T(8,128)}) custom-call(s32[8]{0:T(128)} %fusion.61.order_ref, bf16[512,1024]{1,0:T(8,128)(2,1)} %bitcast.8.source_ref.x_ref, f32[512,1024]{1,0:T(8,128)} %get-tuple-element.337.y_ref, f32[1,1024]{1,0:T(1,128)} %get-tuple-element.443.gain_ref, f32[512,1024]{1,0:T(8,128)} %pull0.1.refs_0_, ...), custom_call_target="tpu_custom_call" | custom-call | bytes 8425472 | tf_op jit(solution)/shard_map/end_back/pallas_call | solution.py:346
  545.5 3.1 all-to-all-start
  550.5 18.3 %all-to-all-done = f32[32,1,128]{2,1,0:T(1,128)S(1)} async-done(((f32[32,1,128]{2,1,0:T(1,128)}), f32[32,1,128]{2,1,0:T(1,128)S(1)}, u32[]{:S(2)}, u32[]{:S(2)}) %all-to-all-start) | async-done | bytes 16416 | tf_op jit(solution)/shard_map/all_to_all | solution.py:296
  578.5 3.4 collective-permute-done.49
  584.5 9.4 %collective-permute-done.50 = bf16[32,3072]{1,0:T(8,128)(2,1)S(1)} collective-permute-done((bf16[32,3072]{1,0:T(8,128)(2,1)S(1)}, bf16[32,3072]{1,0:T(8,128)(2,1)S(1)}, u32[]{:S(2)}, u32[]{:S(2)}) %collective-permute-start.50) | collective-permute-done | bytes 196640 | tf_op jit(solution)/shard_map/ppermute | solution.py:283
  (307 shorter events, 161.8 us)
Async XLA Ops:
  5.3 17.4 %collective-permute-start.2 = (bf16[32,3200]{1,0:T(8,128)(2,1)}, bf16[32,3200]{1,0:T(8,128)(2,1)S(1)}, u32[]{:S(2)}, u32[]{:S(2)}) collective-permute-start(bf16[32,3200]{1,0:T(8,128)(2,1)} %pad_maximum_fusion.8), channel_id=1, source_target_pairs={{0,3},{1,2},{2,1},{3,0},{4,7},{5,6},{6,5},{7,4},{8,11},{9,10},{10,... | collective-permute-start | bytes 614408 | tf_op jit(solution)/shard_map/ppermute | solution.py:195
  10.3 17.6 %collective-permute-start.1 = (bf16[32,3200]{1,0:T(8,128)(2,1)}, bf16[32,3200]{1,0:T(8,128)(2,1)S(1)}, u32[]{:S(2)}, u32[]{:S(2)}) collective-permute-start(bf16[32,3200]{1,0:T(8,128)(2,1)} %pad_maximum_fusion.8), channel_id=1, source_target_pairs={{0,2},{1,3},{2,0},{3,1},{4,6},{5,7},{6,4},{7,5},{8,10},{9,11},{10,... | collective-permute-start | bytes 614408 | tf_op jit(solution)/shard_map/ppermute | solution.py:195
  10.3 17.6 %collective-permute-start = (bf16[32,3200]{1,0:T(8,128)(2,1)}, bf16[32,3200]{1,0:T(8,128)(2,1)S(1)}, u32[]{:S(2)}, u32[]{:S(2)}) collective-permute-start(bf16[32,3200]{1,0:T(8,128)(2,1)} %pad_maximum_fusion.8), channel_id=1, source_target_pairs={{0,1},{1,0},{2,3},{3,2},{4,5},{5,4},{6,7},{7,6},{8,9},{9,8},{10,11... | collective-permute-start | bytes 614408 | tf_op jit(solution)/shard_map/ppermute | solution.py:195
  28.2 17.3 %collective-permute-start.3 = (bf16[128,3200]{1,0:T(8,128)(2,1)S(1)}, bf16[128,3200]{1,0:T(8,128)(2,1)S(1)}, u32[]{:S(2)}, u32[]{:S(2)}) collective-permute-start(bf16[128,3200]{1,0:T(8,128)(2,1)S(1)} %maximum_select_fusion.2), channel_id=1, source_target_pairs={{0,16},{1,17},{2,18},{3,19},{4,12},{5,13},{6,14},{7,15},{8,24},{9,... | collective-permute-start | bytes 2457608 | tf_op jit(solution)/shard_map/ppermute | solution.py:208
  31.3 14.2 %collective-permute-start.4 = (bf16[32,9216]{1,0:T(8,128)(2,1)S(1)}, bf16[32,9216]{1,0:T(8,128)(2,1)}, u32[]{:S(2)}, u32[]{:S(2)}) collective-permute-start(bf16[32,9216]{1,0:T(8,128)(2,1)S(1)} %pad_maximum_fusion.6), channel_id=1, source_target_pairs={{0,1},{1,0},{2,3},{3,2},{4,5},{5,4},{6,7},{7,6},{8,9},{9,8},{10,11... | collective-permute-start | bytes 1769480 | tf_op jit(solution)/shard_map/ppermute | solution.py:176
  45.6 18.9 %collective-permute-start.7 = (bf16[256,3200]{1,0:T(8,128)(2,1)S(1)}, bf16[256,3200]{1,0:T(8,128)(2,1)S(1)}, u32[]{:S(2)}, u32[]{:S(2)}) collective-permute-start(bf16[256,3200]{1,0:T(8,128)(2,1)S(1)} %pad_maximum_fusion.3.refs_0_.refs_4_.refs_1_.refs_2_), channel_id=1, source_target_pairs={{0,4},{1,5},{2,6},{3,7},{4,0},{5,1},{6,2},{7,3},{8,12},{9,13},{10,... | collective-permute-start | bytes 4915208 | tf_op jit(solution)/shard_map/ppermute | solution.py:210
  45.7 21.3 %collective-permute-start.6 = (bf16[256,3200]{1,0:T(8,128)(2,1)S(1)}, bf16[256,3200]{1,0:T(8,128)(2,1)}, u32[]{:S(2)}, u32[]{:S(2)}) collective-permute-start(bf16[256,3200]{1,0:T(8,128)(2,1)S(1)} %pad_maximum_fusion.3.refs_0_.refs_4_.refs_1_.refs_2_), channel_id=1, source_target_pairs={{0,8},{1,9},{2,10},{3,11},{4,20},{5,21},{6,22},{7,23},{8,0},{9,1},... | collective-permute-start | bytes 4915208 | tf_op jit(solution)/shard_map/ppermute | solution.py:210
  46.3 18.2 %collective-permute-start.8 = (bf16[32,9216]{1,0:T(8,128)(2,1)}, bf16[32,9216]{1,0:T(8,128)(2,1)}, u32[]{:S(2)}, u32[]{:S(2)}) collective-permute-start(bf16[32,9216]{1,0:T(8,128)(2,1)} %collective-permute-done.5), channel_id=1, source_target_pairs={{1,0},{2,3},{5,4},{6,7},{9,8},{10,11},{13,12},{14,15},{17,16},{18,... | collective-permute-start | bytes 1769480 | tf_op jit(solution)/shard_map/ppermute | solution.py:180
  47.6 16.9 %collective-permute-start.9 = (bf16[32,9216]{1,0:T(8,128)(2,1)}, bf16[32,9216]{1,0:T(8,128)(2,1)}, u32[]{:S(2)}, u32[]{:S(2)}) collective-permute-start(bf16[32,9216]{1,0:T(8,128)(2,1)} %collective-permute-done.4), channel_id=1, source_target_pairs={{1,2},{2,1},{5,6},{6,5},{9,10},{10,9},{13,14},{14,13},{17,18},{18,... | collective-permute-start | bytes 1769480 | tf_op jit(solution)/shard_map/ppermute | solution.py:180
  69.3 21.7 %collective-permute-start.11 = (bf16[32,9216]{1,0:T(8,128)(2,1)}, bf16[32,9216]{1,0:T(8,128)(2,1)}, u32[]{:S(2)}, u32[]{:S(2)}) collective-permute-start(bf16[32,9216]{1,0:T(8,128)(2,1)} %collective-permute-done.9), channel_id=1, source_target_pairs={{1,0},{2,3},{5,4},{6,7},{9,8},{10,11},{13,12},{14,15},{17,16},{18,... | collective-permute-start | bytes 1769480 | tf_op jit(solution)/shard_map/ppermute | solution.py:183
  70.6 36.6 %collective-permute-start.13 = (bf16[512,1024]{1,0:T(8,128)(2,1)}, bf16[512,1024]{1,0:T(8,128)(2,1)}, u32[]{:S(2)}, u32[]{:S(2)}) collective-permute-start(bf16[512,1024]{1,0:T(8,128)(2,1)} %bitcast.8.source_ref.x_ref), channel_id=1, source_target_pairs={{1,2},{2,1},{5,6},{6,5},{9,10},{10,9},{13,14},{14,13},{17,18},{18,... | collective-permute-start | bytes 3145736 | tf_op jit(solution)/shard_map/ppermute | solution.py:225
  72.3 37.5 %collective-permute-start.12 = (bf16[512,1024]{1,0:T(8,128)(2,1)}, bf16[512,1024]{1,0:T(8,128)(2,1)}, u32[]{:S(2)}, u32[]{:S(2)}) collective-permute-start(bf16[512,1024]{1,0:T(8,128)(2,1)} %bitcast.8.source_ref.x_ref), channel_id=1, source_target_pairs={{0,1},{1,0},{2,3},{3,2},{4,5},{5,4},{6,7},{7,6},{8,9},{9,8},{10,11... | collective-permute-start | bytes 3145736 | tf_op jit(solution)/shard_map/ppermute | solution.py:225
  93.5 29.0 %collective-permute-start.14 = (bf16[128,9216]{1,0:T(8,128)(2,1)S(1)}, bf16[128,9216]{1,0:T(8,128)(2,1)}, u32[]{:S(2)}, u32[]{:S(2)}) collective-permute-start(bf16[128,9216]{1,0:T(8,128)(2,1)S(1)} %maximum_select_fusion), channel_id=1, source_target_pairs={{0,16},{1,17},{2,18},{3,19},{4,12},{5,13},{6,14},{7,15},{8,24},{9,... | collective-permute-start | bytes 7077896 | tf_op jit(solution)/shard_map/ppermute | solution.py:208
  109.8 30.1 %collective-permute-start.16 = (bf16[512,1024]{1,0:T(8,128)(2,1)}, bf16[512,1024]{1,0:T(8,128)(2,1)S(1)}, u32[]{:S(2)}, u32[]{:S(2)}) collective-permute-start(bf16[512,1024]{1,0:T(8,128)(2,1)} %collective-permute-done.12.source_ref), channel_id=1, source_target_pairs={{1,2},{2,1},{5,6},{6,5},{9,10},{10,9},{13,14},{14,13},{17,18},{18,... | collective-permute-start | bytes 3145736 | tf_op jit(solution)/shard_map/ppermute | solution.py:230
  110.5 29.4 %collective-permute-start.15 = (bf16[512,1024]{1,0:T(8,128)(2,1)}, bf16[512,1024]{1,0:T(8,128)(2,1)}, u32[]{:S(2)}, u32[]{:S(2)}) collective-permute-start(bf16[512,1024]{1,0:T(8,128)(2,1)} %collective-permute-done.13), channel_id=1, source_target_pairs={{1,0},{2,3},{5,4},{6,7},{9,8},{10,11},{13,12},{14,15},{17,16},{18,... | collective-permute-start | bytes 3145736 | tf_op jit(solution)/shard_map/ppermute | solution.py:230
  126.7 73.2 %collective-permute-start.19 = (bf16[256,9216]{1,0:T(8,128)(2,1)}, bf16[256,9216]{1,0:T(8,128)(2,1)}, u32[]{:S(2)}, u32[]{:S(2)}) collective-permute-start(bf16[256,9216]{1,0:T(8,128)(2,1)} %pad_maximum_fusion.refs_0_), channel_id=1, source_target_pairs={{0,4},{1,5},{2,6},{3,7},{4,0},{5,1},{6,2},{7,3},{8,12},{9,13},{10,... | collective-permute-start | bytes 14155784 | tf_op jit(solution)/shard_map/ppermute | solution.py:210
  126.7 73.2 %collective-permute-start.18 = (bf16[256,9216]{1,0:T(8,128)(2,1)}, bf16[256,9216]{1,0:T(8,128)(2,1)}, u32[]{:S(2)}, u32[]{:S(2)}) collective-permute-start(bf16[256,9216]{1,0:T(8,128)(2,1)} %pad_maximum_fusion.refs_0_), channel_id=1, source_target_pairs={{0,8},{1,9},{2,10},{3,11},{4,20},{5,21},{6,22},{7,23},{8,0},{9,1},... | collective-permute-start | bytes 14155784 | tf_op jit(solution)/shard_map/ppermute | solution.py:210
  142.9 27.9 %collective-permute-start.17 = (bf16[512,1024]{1,0:T(8,128)(2,1)S(1)}, bf16[512,1024]{1,0:T(8,128)(2,1)S(1)}, u32[]{:S(2)}, u32[]{:S(2)}) collective-permute-start(bf16[512,1024]{1,0:T(8,128)(2,1)S(1)} %collective-permute-done.16), channel_id=1, source_target_pairs={{1,0},{2,3},{5,4},{6,7},{9,8},{10,11},{13,12},{14,15},{17,16},{18,... | collective-permute-start | bytes 3145736 | tf_op jit(solution)/shard_map/ppermute | solution.py:234
  170.8 29.2 %collective-permute-start.22 = (bf16[128,1024]{1,0:T(8,128)(2,1)S(1)}, bf16[128,1024]{1,0:T(8,128)(2,1)S(1)}, u32[]{:S(2)}, u32[]{:S(2)}) collective-permute-start(bf16[128,1024]{1,0:T(8,128)(2,1)S(1)} %copy-done.42), channel_id=1, source_target_pairs={{0,3},{1,2},{2,1},{3,0},{4,7},{5,6},{6,5},{7,4},{8,11},{9,10},{10,... | collective-permute-start | bytes 786440 | tf_op jit(solution)/shard_map/ppermute | solution.py:195
  173.0 26.9 %collective-permute-start.21 = (bf16[128,1024]{1,0:T(8,128)(2,1)S(1)}, bf16[128,1024]{1,0:T(8,128)(2,1)S(1)}, u32[]{:S(2)}, u32[]{:S(2)}) collective-permute-start(bf16[128,1024]{1,0:T(8,128)(2,1)S(1)} %copy-done.42), channel_id=1, source_target_pairs={{0,2},{1,3},{2,0},{3,1},{4,6},{5,7},{6,4},{7,5},{8,10},{9,11},{10,... | collective-permute-start | bytes 786440 | tf_op jit(solution)/shard_map/ppermute | solution.py:195
  173.0 26.9 %collective-permute-start.20 = (bf16[128,1024]{1,0:T(8,128)(2,1)S(1)}, bf16[128,1024]{1,0:T(8,128)(2,1)S(1)}, u32[]{:S(2)}, u32[]{:S(2)}) collective-permute-start(bf16[128,1024]{1,0:T(8,128)(2,1)S(1)} %copy-done.42), channel_id=1, source_target_pairs={{0,1},{1,0},{2,3},{3,2},{4,5},{5,4},{6,7},{7,6},{8,9},{9,8},{10,11... | collective-permute-start | bytes 786440 | tf_op jit(solution)/shard_map/ppermute | solution.py:195
  200.8 14.9 %collective-permute-start.24 = (bf16[512,1024]{1,0:T(8,128)(2,1)S(1)}, bf16[512,1024]{1,0:T(8,128)(2,1)S(1)}, u32[]{:S(2)}, u32[]{:S(2)}) collective-permute-start(bf16[512,1024]{1,0:T(8,128)(2,1)S(1)} %maximum_select_fusion.1), channel_id=1, source_target_pairs={{0,16},{1,17},{2,18},{3,19},{4,12},{5,13},{6,14},{7,15},{8,24},{9,... | collective-permute-start | bytes 3145736 | tf_op jit(solution)/shard_map/ppermute | solution.py:208
  218.1 26.1 %collective-permute-start.26 = (bf16[1024,1024]{1,0:T(8,128)(2,1)S(1)}, bf16[1024,1024]{1,0:T(8,128)(2,1)}, u32[]{:S(2)}, u32[]{:S(2)}) collective-permute-start(bf16[1024,1024]{1,0:T(8,128)(2,1)S(1)} %pad_maximum_fusion.2.refs_4_), channel_id=1, source_target_pairs={{0,4},{1,5},{2,6},{3,7},{4,0},{5,1},{6,2},{7,3},{8,12},{9,13},{10,... | collective-permute-start | bytes 6291464 | tf_op jit(solution)/shard_map/ppermute | solution.py:210
  218.1 26.2 %collective-permute-start.25 = (bf16[1024,1024]{1,0:T(8,128)(2,1)S(1)}, bf16[1024,1024]{1,0:T(8,128)(2,1)}, u32[]{:S(2)}, u32[]{:S(2)}) collective-permute-start(bf16[1024,1024]{1,0:T(8,128)(2,1)S(1)} %pad_maximum_fusion.2.refs_4_), channel_id=1, source_target_pairs={{0,8},{1,9},{2,10},{3,11},{4,20},{5,21},{6,22},{7,23},{8,0},{9,1},... | collective-permute-start | bytes 6291464 | tf_op jit(solution)/shard_map/ppermute | solution.py:210
  248.7 35.1 %collective-permute-start.28 = (bf16[2048,1024]{1,0:T(8,128)(2,1)}, bf16[2048,1024]{1,0:T(8,128)(2,1)}, u32[]{:S(2)}, u32[]{:S(2)}) collective-permute-start(bf16[2048,1024]{1,0:T(8,128)(2,1)} %convolution_convert_fusion.1), channel_id=1, source_target_pairs={{0,4},{1,5},{2,6},{3,7},{4,0},{5,1},{6,2},{7,3},{8,12},{9,13},{10,... | collective-permute-start | bytes 12582920 | tf_op jit(solution)/shard_map/ppermute | solution.py:263
  298.5 13.5 %collective-permute-start.29 = (bf16[512,8192]{1,0:T(8,128)(2,1)}, bf16[512,8192]{1,0:T(8,128)(2,1)}, u32[]{:S(2)}, u32[]{:S(2)}) collective-permute-start(bf16[512,8192]{1,0:T(8,128)(2,1)} %convolution_convert_fusion), channel_id=1, source_target_pairs={{0,4},{1,5},{2,6},{3,7},{4,0},{5,1},{6,2},{7,3},{8,12},{9,13},{10,... | collective-permute-start | bytes 25165832 | tf_op jit(solution)/shard_map/ppermute | solution.py:263
  300.5 46.9 %collective-permute-start.30 = (bf16[1024,1024]{1,0:T(8,128)(2,1)S(1)}, bf16[1024,1024]{1,0:T(8,128)(2,1)}, u32[]{:S(2)}, u32[]{:S(2)}) collective-permute-start(bf16[1024,1024]{1,0:T(8,128)(2,1)S(1)} %add_convert_fusion.7), channel_id=1, source_target_pairs={{0,8},{1,9},{2,10},{3,11},{4,20},{5,21},{6,22},{7,23},{8,0},{9,1},... | collective-permute-start | bytes 6291464 | tf_op jit(solution)/shard_map/ppermute | solution.py:267
  321.1 67.5 %collective-permute-start.33 = (bf16[256,8192]{1,0:T(8,128)(2,1)}, bf16[256,8192]{1,0:T(8,128)(2,1)}, u32[]{:S(2)}, u32[]{:S(2)}) collective-permute-start(bf16[256,8192]{1,0:T(8,128)(2,1)} %add_convert_fusion.2), channel_id=1, source_target_pairs={{0,8},{1,9},{2,10},{3,11},{4,20},{5,21},{6,22},{7,23},{8,0},{9,1},... | collective-permute-start | bytes 12582920 | tf_op jit(solution)/shard_map/ppermute | solution.py:267
  324.2 23.2 %collective-permute-start.31 = (bf16[512,1024]{1,0:T(8,128)(2,1)}, bf16[512,1024]{1,0:T(8,128)(2,1)}, u32[]{:S(2)}, u32[]{:S(2)}) collective-permute-start(bf16[512,1024]{1,0:T(8,128)(2,1)} %convolution_convert_fusion.3), channel_id=1, source_target_pairs={{0,4},{1,5},{2,6},{3,7},{4,0},{5,1},{6,2},{7,3},{8,12},{9,13},{10,... | collective-permute-start | bytes 3145736 | tf_op jit(solution)/shard_map/ppermute | solution.py:263
  363.4 25.3 %collective-permute-start.32 = (bf16[512,1024]{1,0:T(8,128)(2,1)}, bf16[512,1024]{1,0:T(8,128)(2,1)S(1)}, u32[]{:S(2)}, u32[]{:S(2)}) collective-permute-start(bf16[512,1024]{1,0:T(8,128)(2,1)} %pull3.1), channel_id=1, source_target_pairs={{0,1},{3,2},{4,5},{7,6},{8,9},{11,10},{12,13},{15,14},{16,17},{19,... | collective-permute-start | bytes 3145736 | tf_op jit(solution)/shard_map/ppermute | solution.py:239
  365.3 50.6 %collective-permute-start.35 = (bf16[256,1024]{1,0:T(8,128)(2,1)}, bf16[256,1024]{1,0:T(8,128)(2,1)}, u32[]{:S(2)}, u32[]{:S(2)}) collective-permute-start(bf16[256,1024]{1,0:T(8,128)(2,1)} %add_convert_fusion.18), channel_id=1, source_target_pairs={{0,8},{1,9},{2,10},{3,11},{4,20},{5,21},{6,22},{7,23},{8,0},{9,1},... | collective-permute-start | bytes 1572872 | tf_op jit(solution)/shard_map/ppermute | solution.py:267
  366.2 49.8 %collective-permute-start.34 = (bf16[512,1024]{1,0:T(8,128)(2,1)}, bf16[512,1024]{1,0:T(8,128)(2,1)}, u32[]{:S(2)}, u32[]{:S(2)}) collective-permute-start(bf16[512,1024]{1,0:T(8,128)(2,1)} %slice.241), channel_id=1, source_target_pairs={{0,16},{1,17},{2,18},{3,19},{4,12},{5,13},{6,14},{7,15},{8,24},{9,... | collective-permute-start | bytes 3145736 | tf_op jit(solution)/shard_map/ppermute | solution.py:274
  396.7 45.6 %collective-permute-start.38 = (bf16[128,8192]{1,0:T(8,128)(2,1)}, bf16[128,8192]{1,0:T(8,128)(2,1)}, u32[]{:S(2)}, u32[]{:S(2)}) collective-permute-start(bf16[128,8192]{1,0:T(8,128)(2,1)} %slice.242), channel_id=1, source_target_pairs={{0,16},{1,17},{2,18},{3,19},{4,12},{5,13},{6,14},{7,15},{8,24},{9,... | collective-permute-start | bytes 6291464 | tf_op jit(solution)/shard_map/ppermute | solution.py:274
  407.4 34.9 %collective-permute-start.37 = (bf16[512,1024]{1,0:T(8,128)(2,1)}, bf16[512,1024]{1,0:T(8,128)(2,1)}, u32[]{:S(2)}, u32[]{:S(2)}) collective-permute-start(bf16[512,1024]{1,0:T(8,128)(2,1)} %add_convert_fusion.14), channel_id=1, source_target_pairs={{1,2},{2,1},{5,6},{6,5},{9,10},{10,9},{13,14},{14,13},{17,18},{18,... | collective-permute-start | bytes 3145736 | tf_op jit(solution)/shard_map/ppermute | solution.py:242
  409.0 33.3 %collective-permute-start.36 = (bf16[512,1024]{1,0:T(8,128)(2,1)S(1)}, bf16[512,1024]{1,0:T(8,128)(2,1)}, u32[]{:S(2)}, u32[]{:S(2)}) collective-permute-start(bf16[512,1024]{1,0:T(8,128)(2,1)S(1)} %copy-done.12), channel_id=1, source_target_pairs={{0,1},{3,2},{4,5},{7,6},{8,9},{11,10},{12,13},{15,14},{16,17},{19,... | collective-permute-start | bytes 3145736 | tf_op jit(solution)/shard_map/ppermute | solution.py:242
  418.1 42.7 %collective-permute-start.40 = (bf16[128,1024]{1,0:T(8,128)(2,1)}, bf16[128,1024]{1,0:T(8,128)(2,1)S(1)}, u32[]{:S(2)}, u32[]{:S(2)}) collective-permute-start(bf16[128,1024]{1,0:T(8,128)(2,1)} %slice.244), channel_id=1, source_target_pairs={{0,16},{1,17},{2,18},{3,19},{4,12},{5,13},{6,14},{7,15},{8,24},{9,... | collective-permute-start | bytes 786440 | tf_op jit(solution)/shard_map/ppermute | solution.py:274
  422.2 38.7 %collective-permute-start.39 = (bf16[256,1024]{1,0:T(8,128)(2,1)}, bf16[256,1024]{1,0:T(8,128)(2,1)}, u32[]{:S(2)}, u32[]{:S(2)}) collective-permute-start(bf16[256,1024]{1,0:T(8,128)(2,1)} %bitcast.17), channel_id=1, source_target_pairs={{0,1},{1,0},{2,3},{3,2},{4,5},{5,4},{6,7},{7,6},{8,9},{9,8},{10,11... | collective-permute-start | bytes 1572872 | tf_op jit(solution)/shard_map/ppermute | solution.py:283
  446.3 44.7 %collective-permute-start.43 = (bf16[64,8192]{1,0:T(8,128)(2,1)}, bf16[64,8192]{1,0:T(8,128)(2,1)}, u32[]{:S(2)}, u32[]{:S(2)}) collective-permute-start(bf16[64,8192]{1,0:T(8,128)(2,1)} %bitcast.19), channel_id=1, source_target_pairs={{0,1},{1,0},{2,3},{3,2},{4,5},{5,4},{6,7},{7,6},{8,9},{9,8},{10,11... | collective-permute-start | bytes 3145736 | tf_op jit(solution)/shard_map/ppermute | solution.py:283
  461.0 30.0 %collective-permute-start.42 = (bf16[64,1024]{1,0:T(8,128)(2,1)S(1)}, bf16[64,1024]{1,0:T(8,128)(2,1)S(1)}, u32[]{:S(2)}, u32[]{:S(2)}) collective-permute-start(bf16[64,1024]{1,0:T(8,128)(2,1)S(1)} %bitcast.146), channel_id=1, source_target_pairs={{0,1},{1,0},{2,3},{3,2},{4,5},{5,4},{6,7},{7,6},{8,9},{9,8},{10,11... | collective-permute-start | bytes 393224 | tf_op jit(solution)/shard_map/ppermute | solution.py:283
  463.8 27.1 %collective-permute-start.41 = (bf16[128,1024]{1,0:T(8,128)(2,1)}, bf16[128,1024]{1,0:T(8,128)(2,1)}, u32[]{:S(2)}, u32[]{:S(2)}) collective-permute-start(bf16[128,1024]{1,0:T(8,128)(2,1)} %dynamic-slice_bitcast_fusion.1), channel_id=1, source_target_pairs={{0,2},{1,3},{2,0},{3,1},{4,6},{5,7},{6,4},{7,5},{8,10},{9,11},{10,... | collective-permute-start | bytes 786440 | tf_op jit(solution)/shard_map/ppermute | solution.py:283
  494.4 29.9 %collective-permute-start.45 = (bf16[512,1024]{1,0:T(8,128)(2,1)}, bf16[512,1024]{1,0:T(8,128)(2,1)}, u32[]{:S(2)}, u32[]{:S(2)}) collective-permute-start(bf16[512,1024]{1,0:T(8,128)(2,1)} %add_convert_fusion.12), channel_id=1, source_target_pairs={{1,2},{2,1},{5,6},{6,5},{9,10},{10,9},{13,14},{14,13},{17,18},{18,... | collective-permute-start | bytes 3145736 | tf_op jit(solution)/shard_map/ppermute | solution.py:249
  496.3 27.9 %collective-permute-start.46 = (bf16[512,1024]{1,0:T(8,128)(2,1)}, bf16[512,1024]{1,0:T(8,128)(2,1)}, u32[]{:S(2)}, u32[]{:S(2)}) collective-permute-start(bf16[512,1024]{1,0:T(8,128)(2,1)} %add_convert_fusion.11), channel_id=1, source_target_pairs={{0,1},{1,0},{2,3},{3,2},{4,5},{5,4},{6,7},{7,6},{8,9},{9,8},{10,11... | collective-permute-start | bytes 3145736 | tf_op jit(solution)/shard_map/ppermute | solution.py:250
  508.8 25.8 %collective-permute-start.47 = (bf16[256,3072]{1,0:T(8,128)(2,1)}, bf16[256,3072]{1,0:T(8,128)(2,1)}, u32[]{:S(2)}, u32[]{:S(2)}) collective-permute-start(bf16[256,3072]{1,0:T(8,128)(2,1)} %pad_maximum_fusion.4), channel_id=1, source_target_pairs={{0,8},{1,9},{2,10},{3,11},{4,20},{5,21},{6,22},{7,23},{8,0},{9,1},... | collective-permute-start | bytes 4718600 | tf_op jit(solution)/shard_map/ppermute | solution.py:267
  513.4 56.1 %collective-permute-start.51 = (bf16[32,1024]{1,0:T(8,128)(2,1)S(1)}, bf16[32,1024]{1,0:T(8,128)(2,1)S(1)}, u32[]{:S(2)}, u32[]{:S(2)}) collective-permute-start(bf16[32,1024]{1,0:T(8,128)(2,1)S(1)} %dynamic-slice_bitcast_fusion.3), channel_id=1, source_target_pairs={{0,2},{1,3},{2,0},{3,1},{4,6},{5,7},{6,4},{7,5},{8,10},{9,11},{10,... | collective-permute-start | bytes 196616 | tf_op jit(solution)/shard_map/ppermute | solution.py:283
  537.6 31.9 %collective-permute-start.48 = (bf16[128,3072]{1,0:T(8,128)(2,1)}, bf16[128,3072]{1,0:T(8,128)(2,1)}, u32[]{:S(2)}, u32[]{:S(2)}) collective-permute-start(bf16[128,3072]{1,0:T(8,128)(2,1)} %slice.248), channel_id=1, source_target_pairs={{0,16},{1,17},{2,18},{3,19},{4,12},{5,13},{6,14},{7,15},{8,24},{9,... | collective-permute-start | bytes 2359304 | tf_op jit(solution)/shard_map/ppermute | solution.py:274
  542.0 27.5 %collective-permute-start.52 = (bf16[32,8192]{1,0:T(8,128)(2,1)}, bf16[32,8192]{1,0:T(8,128)(2,1)}, u32[]{:S(2)}, u32[]{:S(2)}) collective-permute-start(bf16[32,8192]{1,0:T(8,128)(2,1)} %dynamic-slice_bitcast_fusion), channel_id=1, source_target_pairs={{0,2},{1,3},{2,0},{3,1},{4,6},{5,7},{6,4},{7,5},{8,10},{9,11},{10,... | collective-permute-start | bytes 1572872 | tf_op jit(solution)/shard_map/ppermute | solution.py:283
  545.5 23.3 %all-to-all-start = ((f32[32,1,128]{2,1,0:T(1,128)}), f32[32,1,128]{2,1,0:T(1,128)S(1)}, u32[]{:S(2)}, u32[]{:S(2)}) async-start(f32[32,1,128]{2,1,0:T(1,128)} %bitcast.42), calls=%async_computation | async-start | bytes 32768 | tf_op jit(solution)/shard_map/all_to_all | solution.py:296
  570.9 11.1 %collective-permute-start.49 = (bf16[64,3072]{1,0:T(8,128)(2,1)S(1)}, bf16[64,3072]{1,0:T(8,128)(2,1)}, u32[]{:S(2)}, u32[]{:S(2)}) collective-permute-start(bf16[64,3072]{1,0:T(8,128)(2,1)S(1)} %bitcast.142), channel_id=1, source_target_pairs={{0,1},{1,0},{2,3},{3,2},{4,5},{5,4},{6,7},{7,6},{8,9},{9,8},{10,11... | collective-permute-start | bytes 1179656 | tf_op jit(solution)/shard_map/ppermute | solution.py:283
  (61 other events, 461.4 us)

commit v5 on v4

--- a/solution.py
+++ b/solution.py
@@ -905,7 +905,7 @@
         [(whole((rows, width)), array((rows, width), dtype))],
         ((both,) if block else (dq, both)) + tuple(mixed),
         f"pull{block}",
-        rows * width,
+        rows * width * (1 if block else 96 * width),
         scratch=[pltpu.VMEM((rows, width), jnp.float32)],
     )[0]
 
@@ -1034,7 +1034,7 @@
             down_own, state = tie(down_weight, state)
             down = Chain(gather_steps(plan, down_own))
         flipped[k], both[k] = project(order, came[k], cols, mixed_w, cosine, sine, k)
-        if k == 1:
+        if k in (1, plan.ctx - 1):
             both[k] = step(both[k], pair)
         state = attend(order, valid, k, state, k == plan.ctx - 1, queries, both[k])
     state = step(state, pair, down)
@@ -1077,9 +1077,9 @@
             if k == plan.ctx - 1:
                 held = step(held, down_sum, output_sum)
             else:
+                held = step(held, pair_sum)
                 if plan.line:
                     held = wait(held, back_way)
-                held = step(held, pair_sum)
             held, grads[k] = tie(held, grads[k])
             parts[k] = pull(order, held, grads[k], mixed_w, k)
             held, parts[k] = tie(held, parts[k])
@@ -1096,17 +1096,20 @@
     held, last_sum = begin(held, sum_steps(plan, product_of(plan, groups)))
     held = go_on(held, down_sum, output_sum)
     held = step(held, last_sum)
+    held = go_on(held, pair_sum)
     part_grads = pull(order, held, grads[0], mixed_w, 0)
     if plan.line:
         part_grads = finish(part_grads, back_way)
+    part_grads = step(part_grads, last_sum)
+    if plan.line:
         sends = back_way.value
     else:
         sends = [lax.ppermute(parts[k], AXES, plan.across[k]) for k in range(1, plan.ctx)]
     tokens_grad, edge_one = end_back(
         order, [part_grads, *sends], own, y_grads, natural[0]
     )
+    edge_one = step(edge_one, pair_sum)
     edge_one = step(edge_one, last_sum)
-    edge_one = go_on(edge_one, pair_sum)
     vectors = sum_vectors(plan, (edge_one[0], edge_one[1], edge_two[0], edge_two[1]))
     finish((), last_sum)
     finish((), down_sum, output_sum, pair_sum)

time: 606 us -> 599 us (0.988)
    ppermute x8, waiting for transfers between devices: 12.9 us -> 32.7 us  [sum_steps(): other, = (yield ([lax.ppermute(send, AXES, plan.across[1 << bit])], [send]))]
    all_to_all x1, waiting for transfers between devices: 18.3 us -> 2.25 us  [sum_vectors(): came = lax.all_to_all(packed, AXES, split_axis=0, concat_axis=0, tiled=True)]
    unnamed x115 -> x105, local copies, waits for them, and re-layouts: 12.3 us -> 14.2 us
  transfers between devices with their start and end apart: 54 -> 54, of which waited for: 16 -> 15; matrix products, arithmetic and copies ran while one was open for 22% -> 20% of each run, Pallas kernels for 45% -> 45%
where the time goes in v5:
time: 599 us; the launch traced here: 590 us
  Pallas kernels  266 us (44%)
  waiting for transfers between devices  93.2 us (16%)
  starting transfers between devices  66.3 us (11%)
  matrix products  64.7 us (11%)
  other arithmetic  61.9 us (10%)
  local copies, waits for them, and re-layouts  35.4 us (6%)
    pallas_call x21, Pallas kernels, call(): pl.pallas_call(body, out_shape=out_shape, grid_spec=pltpu.PrefetchScalarG...  266 us
    dot_general x24, matrix products, product(): found = found + jnp.dot(part, right, preferred_element_type=jnp.float32)  64.7 us
    ppermute x8, waiting for transfers between devices, sum_steps(): other, = (yield ([lax.ppermute(send, AXES, plan.across[1 << bit])], [send]))  32.7 us
    convert_element_type x15, other arithmetic, add(): return (a.astype(jnp.float32) + b.astype(jnp.float32)).astype(BF)  28.8 us
    unnamed x105, local copies, waits for them, and re-layouts  14.2 us
    ppermute x1, waiting for transfers between devices, gather_steps(): lax.ppermute(shard, AXES, plan.across[1])  13.5 us
    ppermute x1, waiting for transfers between devices, gather_steps(): lax.ppermute(middle, AXES, plan.outward)  13.1 us
  transfers between devices with their start and end apart: 54, of which 15 were waited for; matrix products, arithmetic and copies ran while one was open for 20% of the time, Pallas kernels for 45%

profile of v5, /device:TPU:0, one launch (start us, length us, event | category | flops | bytes accessed | tf_op | source)
XLA Modules:
  0.0 589.9 jit_solution(9211891293376313908)
XLA Ops:
  5.3 5.1 collective-permute-start.2
  15.9 5.5 multiply_sine_fusion
  22.6 5.4 collective-permute-done.1
  32.0 13.5 %collective-permute-done.4 = bf16[32,9216]{1,0:T(8,128)(2,1)} collective-permute-done((bf16[32,9216]{1,0:T(8,128)(2,1)S(1)}, bf16[32,9216]{1,0:T(8,128)(2,1)}, u32[]{:S(2)}, u32[]{:S(2)}) %collective-permute-start.4) | collective-permute-done | bytes 589856 | tf_op jit(solution)/shard_map/ppermute | solution.py:176
  51.5 13.1 %collective-permute-done.8 = bf16[32,9216]{1,0:T(8,128)(2,1)} collective-permute-done((bf16[32,9216]{1,0:T(8,128)(2,1)}, bf16[32,9216]{1,0:T(8,128)(2,1)}, u32[]{:S(2)}, u32[]{:S(2)}) %collective-permute-start.8) | collective-permute-done | bytes 589856 | tf_op jit(solution)/shard_map/ppermute | solution.py:180
  72.3 5.5 collective-permute-start.12
  77.8 13.2 %project0.1 = (bf16[1024,512]{1,0:T(8,128)(2,1)}, bf16[512,1024]{1,0:T(8,128)(2,1)}, bf16[512,2048]{1,0:T(8,128)(2,1)}, f32[8,1024]{1,0:T(8,128)}) custom-call(s32[8]{0:T(128)} %fusion.61.order_ref, bf16[512,1024]{1,0:T(8,128)(2,1)} %bitcast.8.source_ref.x_ref, f32[2048,128]{1,0:T(8,128)} %get-tuple-element.238.cos_ref, ...), custom_call_target="tpu_custom_call" | custom-call | flops 51539607552 | bytes 20480000 | tf_op jit(solution)/shard_map/project0/pallas_call | solution.py:346
  94.8 12.4 %attend0.1 = (f32[8,8,512]{2,1,0:T(8,128)}, f32[1024,512]{1,0:T(8,128)}) custom-call(s32[8]{0:T(128)} %fusion.61.order_ref, s32[4]{0:T(128)} %subtract_clamp_fusion.valid_ref, bf16[512,1024]{1,0:T(8,128)(2,1)} %get-tuple-element.242.q_ref, bf16[512,2048]{1,0:T(8,128)(2,1)} %get-tuple-element.247.kv_ref), custom_call_target="tpu_custom_call" | custom-call | flops 68719476736 | bytes 5373968 | tf_op jit(solution)/shard_map/attend0/pallas_call | solution.py:346
  112.0 10.0 %project1.1 = (bf16[1024,512]{1,0:T(8,128)(2,1)}, bf16[512,2048]{1,0:T(8,128)(2,1)}) custom-call(s32[8]{0:T(128)} %fusion.61.order_ref, bf16[512,1024]{1,0:T(8,128)(2,1)} %collective-permute-done.12.source_ref, f32[2048,128]{1,0:T(8,128)} %get-tuple-element.238.cos_ref, f32[2048,128]{1,0:T(8,128)} %get-tuple-element.239.sin_ref, ...), custom_call_target="tpu_custom_call" | custom-call | flops 34359738368 | bytes 12877824 | tf_op jit(solution)/shard_map/project1/pallas_call | solution.py:346
  122.5 4.2 pad_maximum_fusion.refs_0_
  127.2 12.7 %attend1.1 = (f32[8,8,512]{2,1,0:T(8,128)}, f32[1024,512]{1,0:T(8,128)}) custom-call(s32[8]{0:T(128)} %fusion.61.order_ref, s32[4]{0:T(128)} %subtract_clamp_fusion.valid_ref, bf16[512,1024]{1,0:T(8,128)(2,1)} %get-tuple-element.242.q_ref, bf16[512,2048]{1,0:T(8,128)(2,1)} %get-tuple-element.255.kv_ref, f32[8,8,512]{2,1,0:T(8,128)} %get-tuple-element.259.refs_0_, ...), custom_call_target="tpu_custom_call" | custom-call | flops 68719476736 | bytes 7602192 | tf_op jit(solution)/shard_map/attend1/pallas_call | solution.py:346
  139.9 2.9 add.233.source_ref
  144.1 10.0 %project2.1 = (bf16[1024,512]{1,0:T(8,128)(2,1)}, bf16[512,2048]{1,0:T(8,128)(2,1)}) custom-call(s32[8]{0:T(128)} %fusion.61.order_ref, bf16[512,1024]{1,0:T(8,128)(2,1)} %add.233.source_ref, f32[2048,128]{1,0:T(8,128)} %get-tuple-element.238.cos_ref, f32[2048,128]{1,0:T(8,128)} %get-tuple-element.239.sin_ref, bf16[256,3200]{1,0:T(8,128)(2,1)} %copy-done.5, ...), custom_call_target="tpu_custom_call" | custom-call | flops 34359738368 | bytes 12877824 | tf_op jit(solution)/shard_map/project2/pallas_call | solution.py:346
  154.1 12.8 %attend2.1 = (f32[8,8,512]{2,1,0:T(8,128)}, f32[1024,512]{1,0:T(8,128)}) custom-call(s32[8]{0:T(128)} %fusion.61.order_ref, s32[4]{0:T(128)} %subtract_clamp_fusion.valid_ref, bf16[512,1024]{1,0:T(8,128)(2,1)} %get-tuple-element.242.q_ref, bf16[512,2048]{1,0:T(8,128)(2,1)} %get-tuple-element.265.kv_ref, f32[8,8,512]{2,1,0:T(8,128)} %get-tuple-element.268.refs_0_, ...), custom_call_target="tpu_custom_call" | custom-call | flops 68719476736 | bytes 7602192 | tf_op jit(solution)/shard_map/attend2/pallas_call | solution.py:346
  166.9 3.7 collective-permute-done.17
  176.4 10.0 %project3.1 = (bf16[1024,512]{1,0:T(8,128)(2,1)}, bf16[512,2048]{1,0:T(8,128)(2,1)}) custom-call(s32[8]{0:T(128)} %fusion.61.order_ref, bf16[512,1024]{1,0:T(8,128)(2,1)} %add.234.source_ref, f32[2048,128]{1,0:T(8,128)} %get-tuple-element.238.cos_ref, f32[2048,128]{1,0:T(8,128)} %get-tuple-element.239.sin_ref, bf16[256,3200]{1,0:T(8,128)(2,1)} %copy-done.5, ...), custom_call_target="tpu_custom_call" | custom-call | flops 34359738368 | bytes 12877824 | tf_op jit(solution)/shard_map/project3/pallas_call | solution.py:346
  186.5 13.4 %attend3.1 = (bf16[512,1024]{1,0:T(8,128)(2,1)}, bf16[1024,512]{1,0:T(8,128)(2,1)}, f32[512,1024]{1,0:T(8,128)}, f32[8,8,512]{2,1,0:T(8,128)}) custom-call(s32[8]{0:T(128)} %fusion.61.order_ref, s32[4]{0:T(128)} %subtract_clamp_fusion.valid_ref, bf16[512,1024]{1,0:T(8,128)(2,1)} %get-tuple-element.242.q_ref, bf16[512,2048]{1,0:T(8,128)(2,1)} %get-tuple-element.276.kv_ref, ...), custom_call_target="tpu_custom_call" | custom-call | flops 68719476736 | bytes 9699344 | tf_op jit(solution)/shard_map/attend3/pallas_call | solution.py:346
  202.3 6.1 %middle.1 = (f32[512,1024]{1,0:T(8,128)}, bf16[512,1024]{1,0:T(8,128)(2,1)}, bf16[1024,512]{1,0:T(8,128)(2,1)}) custom-call(s32[8]{0:T(128)} %fusion.61.order_ref, bf16[512,1024]{1,0:T(8,128)(2,1)} %get-tuple-element.295.o_ref, bf16[512,1024]{1,0:T(8,128)(2,1)} %bitcast.8.source_ref.x_ref, f32[8,1024]{1,0:T(8,128)} %get-tuple-element.251.refs_4_.cols_ref, ...), custom_call_target="tpu_custom_call" | custom-call | flops 1073741824 | bytes 25198592 | tf_op jit(solution)/shard_map/middle/pallas_call | solution.py:346
  208.4 7.2 %collective-permute-done.24 = bf16[512,1024]{1,0:T(8,128)(2,1)S(1)} collective-permute-done((bf16[512,1024]{1,0:T(8,128)(2,1)S(1)}, bf16[512,1024]{1,0:T(8,128)(2,1)S(1)}, u32[]{:S(2)}, u32[]{:S(2)}) %collective-permute-start.24) | collective-permute-done | bytes 1048608 | tf_op jit(solution)/shard_map/ppermute | solution.py:208
  219.6 18.5 %feed.1 = (bf16[512,4096]{1,0:T(8,128)(2,1)}, bf16[512,4096]{1,0:T(8,128)(2,1)}, bf16[512,4096]{1,0:T(8,128)(2,1)}, bf16[4096,512]{1,0:T(8,128)(2,1)}) custom-call(s32[8]{0:T(128)} %fusion.61.order_ref, bf16[512,1024]{1,0:T(8,128)(2,1)} %get-tuple-element.301.two_ref, bf16[256,9216]{1,0:T(8,128)(2,1)} %pad_maximum_fusion.refs_0_, ...), custom_call_target="tpu_custom_call" | custom-call | flops 8589934592 | bytes 36700160 | tf_op jit(solution)/shard_map/feed/pallas_call | solution.py:346
  238.1 6.0 %convolution_convert_fusion.1 = bf16[2048,1024]{1,0:T(8,128)(2,1)} fusion(bf16[512,1024]{1,0:T(8,128)(2,1)S(1)} %copy-done.13, bf16[4096,512]{1,0:T(8,128)(2,1)} %get-tuple-element.305), kind=kOutput, calls=%fused_computation.11 | convolution fusion | flops 2149580800 | bytes 7340032 | tf_op jit(solution)/shard_map/dot_general | solution.py:328
  244.3 4.4 collective-permute-done.27.refs_7_
  250.0 33.8 %feed_back.1 = (bf16[512,1024]{1,0:T(8,128)(2,1)}, bf16[512,8192]{1,0:T(8,128)(2,1)}, f32[512,1024]{1,0:T(8,128)}) custom-call(s32[8]{0:T(128)} %fusion.61.order_ref, bf16[512,1024]{1,0:T(8,128)(2,1)} %bitcast_select_fusion.m_ref, bf16[512,4096]{1,0:T(8,128)(2,1)} %get-tuple-element.302.gate_ref, bf16[512,4096]{1,0:T(8,128)(2,1)} %get-tuple-element.303.up_ref, ...), custom_call_target="tpu_custom_call" | custom-call | flops 17179869184 | bytes 54525952 | tf_op jit(solution)/shard_map/feed_back/pallas_call | solution.py:346
  283.8 4.6 add_convert_fusion.6
  288.4 4.6 add_convert_fusion.7
  293.1 6.7 %convolution_convert_fusion = bf16[512,8192]{1,0:T(8,128)(2,1)} fusion(bf16[512,8192]{1,0:T(8,128)(2,1)S(1)} %copy-done.47, bf16[1024,512]{1,0:T(8,128)(2,1)S(1)} %copy-done.41), kind=kOutput, calls=%fused_computation.1 | convolution fusion | flops 4299161600 | bytes 17301504 | tf_op jit(solution)/shard_map/dot_general | solution.py:328
  303.2 7.4 %middle_back.1 = (f32[512,1024]{1,0:T(8,128)}, bf16[512,1024]{1,0:T(8,128)(2,1)}, bf16[512,1024]{1,0:T(8,128)(2,1)}, f32[8,1024]{1,0:T(8,128)}) custom-call(s32[8]{0:T(128)} %fusion.61.order_ref, f32[512,1024]{1,0:T(8,128)} %get-tuple-element.327.grads_ref, f32[512,1024]{1,0:T(8,128)} %get-tuple-element.314.resid_ref, ...), custom_call_target="tpu_custom_call" | custom-call | flops 1073741824 | bytes 28348416 | tf_op jit(solution)/shard_map/middle_back/pallas_call | solution.py:346
  313.3 9.1 %add_convert_fusion.2 = bf16[256,8192]{1,0:T(8,128)(2,1)} fusion(bf16[512,8192]{1,0:T(8,128)(2,1)} %collective-permute-done.29, bf16[512,8192]{1,0:T(8,128)(2,1)} %get-tuple-element.326, bf16[1024,512]{1,0:T(8,128)(2,1)S(1)} %copy-done.41), kind=kOutput, calls=%fused_computation.4 | convolution fusion | flops 2153775104 | bytes 17039360 | tf_op jit(solution)/shard_map/dot_general | solution.py:328
  325.5 6.8 %add_convert_fusion.1 = bf16[256,8192]{1,0:T(8,128)(2,1)} fusion(bf16[512,8192]{1,0:T(8,128)(2,1)} %collective-permute-done.29, bf16[512,8192]{1,0:T(8,128)(2,1)S(1)} %bitcast.156, bf16[1024,512]{1,0:T(8,128)(2,1)S(1)} %copy-done.41), kind=kOutput, calls=%fused_computation.3 | convolution fusion | flops 2153775104 | bytes 17039360 | tf_op jit(solution)/shard_map/dot_general | solution.py:328
  332.3 16.5 %attend_back3.1 = (f32[1024,512]{1,0:T(8,128)}, bf16[512,2048]{1,0:T(8,128)(2,1)}) custom-call(s32[8]{0:T(128)} %fusion.61.order_ref, s32[4]{0:T(128)} %subtract_clamp_fusion.valid_ref, bf16[512,1024]{1,0:T(8,128)(2,1)} %get-tuple-element.242.q_ref, bf16[512,2048]{1,0:T(8,128)(2,1)} %get-tuple-element.276.kv_ref, ...), custom_call_target="tpu_custom_call" | custom-call | flops 10737418240 | bytes 12714000 | tf_op jit(solution)/shard_map/attend_back3/pallas_call | solution.py:346
  348.9 3.1 add_convert_fusion.18
  360.0 7.0 %pull3.1 = bf16[512,1024]{1,0:T(8,128)(2,1)} custom-call(s32[8]{0:T(128)} %fusion.61.order_ref, bf16[512,2048]{1,0:T(8,128)(2,1)} %get-tuple-element.345.refs_0_, bf16[256,3200]{1,0:T(8,128)(2,1)} %copy-done.5, bf16[256,3200]{1,0:T(8,128)(2,1)} %collective-permute-done.6.refs_1_.refs_5_.refs_2_.refs_3_, bf16[256,3200]{1,0:T(8,128)(2,1)} %copy-done.9, ...), custom_call_target="tpu_custom_call" | custom-call | flops 524288 | bytes 9699328 | tf_op jit(solution)/shard_map/pull3/pallas_call | solution.py:346
  368.9 16.7 %attend_back2.1 = (f32[1024,512]{1,0:T(8,128)}, bf16[512,2048]{1,0:T(8,128)(2,1)}) custom-call(s32[8]{0:T(128)} %fusion.61.order_ref, s32[4]{0:T(128)} %subtract_clamp_fusion.valid_ref, bf16[512,1024]{1,0:T(8,128)(2,1)} %get-tuple-element.242.q_ref, bf16[512,2048]{1,0:T(8,128)(2,1)} %get-tuple-element.265.kv_ref, ...), custom_call_target="tpu_custom_call" | custom-call | flops 10737418240 | bytes 14811152 | tf_op jit(solution)/shard_map/attend_back2/pallas_call | solution.py:346
  385.6 5.0 add_convert_fusion
  395.1 7.1 %pull2.1 = bf16[512,1024]{1,0:T(8,128)(2,1)} custom-call(s32[8]{0:T(128)} %fusion.61.order_ref, bf16[512,2048]{1,0:T(8,128)(2,1)} %get-tuple-element.355.refs_0_, bf16[256,3200]{1,0:T(8,128)(2,1)} %copy-done.5, bf16[256,3200]{1,0:T(8,128)(2,1)} %collective-permute-done.6.refs_1_.refs_5_.refs_2_.refs_3_, bf16[256,3200]{1,0:T(8,128)(2,1)} %copy-done.9, ...), custom_call_target="tpu_custom_call" | custom-call | flops 524288 | bytes 9699328 | tf_op jit(solution)/shard_map/pull2/pallas_call | solution.py:346
  406.6 4.5 collective-permute-start.37
  415.8 3.3 fusion.15
  419.1 16.8 %attend_back1.1 = (f32[1024,512]{1,0:T(8,128)}, bf16[512,2048]{1,0:T(8,128)(2,1)}) custom-call(s32[8]{0:T(128)} %fusion.61.order_ref, s32[4]{0:T(128)} %subtract_clamp_fusion.valid_ref, bf16[512,1024]{1,0:T(8,128)(2,1)} %get-tuple-element.242.q_ref, bf16[512,2048]{1,0:T(8,128)(2,1)} %get-tuple-element.255.kv_ref, ...), custom_call_target="tpu_custom_call" | custom-call | flops 10737418240 | bytes 14811152 | tf_op jit(solution)/shard_map/attend_back1/pallas_call | solution.py:346
  436.0 2.7 add_convert_fusion.4
  441.9 7.0 %pull1.1 = bf16[512,1024]{1,0:T(8,128)(2,1)} custom-call(s32[8]{0:T(128)} %fusion.61.order_ref, bf16[512,2048]{1,0:T(8,128)(2,1)} %get-tuple-element.373.refs_0_, bf16[256,3200]{1,0:T(8,128)(2,1)} %copy-done.5, bf16[256,3200]{1,0:T(8,128)(2,1)} %collective-permute-done.6.refs_1_.refs_5_.refs_2_.refs_3_, bf16[256,3200]{1,0:T(8,128)(2,1)} %copy-done.9, ...), custom_call_target="tpu_custom_call" | custom-call | flops 524288 | bytes 9699328 | tf_op jit(solution)/shard_map/pull1/pallas_call | solution.py:346
  448.9 3.0 add_convert_fusion.12
  458.5 18.3 %attend_back0.1 = (bf16[512,1024]{1,0:T(8,128)(2,1)}, bf16[512,2048]{1,0:T(8,128)(2,1)}) custom-call(s32[8]{0:T(128)} %fusion.61.order_ref, s32[4]{0:T(128)} %subtract_clamp_fusion.valid_ref, bf16[512,1024]{1,0:T(8,128)(2,1)} %get-tuple-element.242.q_ref, bf16[512,2048]{1,0:T(8,128)(2,1)} %get-tuple-element.247.kv_ref, ...), custom_call_target="tpu_custom_call" | custom-call | flops 10737418240 | bytes 13762576 | tf_op jit(solution)/shard_map/attend_back0/pallas_call | solution.py:346
  505.0 10.0 %pull0.1.refs_0_ = f32[512,1024]{1,0:T(8,128)} custom-call(s32[8]{0:T(128)} %fusion.61.order_ref, bf16[512,1024]{1,0:T(8,128)(2,1)} %get-tuple-element.405.refs_0_, bf16[512,2048]{1,0:T(8,128)(2,1)} %get-tuple-element.389.refs_1_, bf16[256,3200]{1,0:T(8,128)(2,1)} %copy-done.5, bf16[256,3200]{1,0:T(8,128)(2,1)} %collective-permute-done.6.refs_1_.refs_5_.refs_2_.refs_3_, ...), custom_call_target="tpu_custom_call" | custom-call | flops 51539607552 | bytes 11796480 | tf_op jit(solution)/shard_map/pull0/pallas_call | solution.py:346
  530.1 22.2 %collective-permute-done.52 = bf16[32,1024]{1,0:T(8,128)(2,1)S(1)} collective-permute-done((bf16[32,1024]{1,0:T(8,128)(2,1)}, bf16[32,1024]{1,0:T(8,128)(2,1)S(1)}, u32[]{:S(2)}, u32[]{:S(2)}) %collective-permute-start.52) | collective-permute-done | bytes 65568 | tf_op jit(solution)/shard_map/ppermute | solution.py:283
  553.0 6.2 %end_back.1 = (bf16[512,1024]{1,0:T(8,128)(2,1)}, f32[8,1024]{1,0:T(8,128)}) custom-call(s32[8]{0:T(128)} %fusion.61.order_ref, bf16[512,1024]{1,0:T(8,128)(2,1)} %bitcast.8.source_ref.x_ref, f32[512,1024]{1,0:T(8,128)} %get-tuple-element.328.y_ref, f32[1,1024]{1,0:T(1,128)} %get-tuple-element.437.gain_ref, f32[512,1024]{1,0:T(8,128)} %pull0.1.refs_0_, ...), custom_call_target="tpu_custom_call" | custom-call | bytes 8425472 | tf_op jit(solution)/shard_map/end_back/pallas_call | solution.py:346
  563.4 3.7 all-to-all-start
  567.1 2.7 slice_reduce_fusion
  576.7 10.5 %collective-permute-done.51 = bf16[32,3072]{1,0:T(8,128)(2,1)S(1)} collective-permute-done((bf16[32,3072]{1,0:T(8,128)(2,1)S(1)}, bf16[32,3072]{1,0:T(8,128)(2,1)S(1)}, u32[]{:S(2)}, u32[]{:S(2)}) %collective-permute-start.51) | collective-permute-done | bytes 196640 | tf_op jit(solution)/shard_map/ppermute | solution.py:283
  (297 shorter events, 152.4 us)
Async XLA Ops:
  5.3 17.3 %collective-permute-start.2 = (bf16[32,3200]{1,0:T(8,128)(2,1)}, bf16[32,3200]{1,0:T(8,128)(2,1)S(1)}, u32[]{:S(2)}, u32[]{:S(2)}) collective-permute-start(bf16[32,3200]{1,0:T(8,128)(2,1)} %pad_maximum_fusion.8), channel_id=1, source_target_pairs={{0,3},{1,2},{2,1},{3,0},{4,7},{5,6},{6,5},{7,4},{8,11},{9,10},{10,... | collective-permute-start | bytes 614408 | tf_op jit(solution)/shard_map/ppermute | solution.py:195
  10.3 17.6 %collective-permute-start.1 = (bf16[32,3200]{1,0:T(8,128)(2,1)}, bf16[32,3200]{1,0:T(8,128)(2,1)S(1)}, u32[]{:S(2)}, u32[]{:S(2)}) collective-permute-start(bf16[32,3200]{1,0:T(8,128)(2,1)} %pad_maximum_fusion.8), channel_id=1, source_target_pairs={{0,2},{1,3},{2,0},{3,1},{4,6},{5,7},{6,4},{7,5},{8,10},{9,11},{10,... | collective-permute-start | bytes 614408 | tf_op jit(solution)/shard_map/ppermute | solution.py:195
  10.3 17.6 %collective-permute-start = (bf16[32,3200]{1,0:T(8,128)(2,1)}, bf16[32,3200]{1,0:T(8,128)(2,1)S(1)}, u32[]{:S(2)}, u32[]{:S(2)}) collective-permute-start(bf16[32,3200]{1,0:T(8,128)(2,1)} %pad_maximum_fusion.8), channel_id=1, source_target_pairs={{0,1},{1,0},{2,3},{3,2},{4,5},{5,4},{6,7},{7,6},{8,9},{9,8},{10,11... | collective-permute-start | bytes 614408 | tf_op jit(solution)/shard_map/ppermute | solution.py:195
  28.2 17.3 %collective-permute-start.3 = (bf16[128,3200]{1,0:T(8,128)(2,1)S(1)}, bf16[128,3200]{1,0:T(8,128)(2,1)S(1)}, u32[]{:S(2)}, u32[]{:S(2)}) collective-permute-start(bf16[128,3200]{1,0:T(8,128)(2,1)S(1)} %maximum_select_fusion.2), channel_id=1, source_target_pairs={{0,16},{1,17},{2,18},{3,19},{4,12},{5,13},{6,14},{7,15},{8,24},{9,... | collective-permute-start | bytes 2457608 | tf_op jit(solution)/shard_map/ppermute | solution.py:208
  31.3 14.2 %collective-permute-start.4 = (bf16[32,9216]{1,0:T(8,128)(2,1)S(1)}, bf16[32,9216]{1,0:T(8,128)(2,1)}, u32[]{:S(2)}, u32[]{:S(2)}) collective-permute-start(bf16[32,9216]{1,0:T(8,128)(2,1)S(1)} %pad_maximum_fusion.6), channel_id=1, source_target_pairs={{0,1},{1,0},{2,3},{3,2},{4,5},{5,4},{6,7},{7,6},{8,9},{9,8},{10,11... | collective-permute-start | bytes 1769480 | tf_op jit(solution)/shard_map/ppermute | solution.py:176
  45.6 18.9 %collective-permute-start.7 = (bf16[256,3200]{1,0:T(8,128)(2,1)S(1)}, bf16[256,3200]{1,0:T(8,128)(2,1)S(1)}, u32[]{:S(2)}, u32[]{:S(2)}) collective-permute-start(bf16[256,3200]{1,0:T(8,128)(2,1)S(1)} %pad_maximum_fusion.3.refs_0_.refs_4_.refs_1_.refs_2_), channel_id=1, source_target_pairs={{0,4},{1,5},{2,6},{3,7},{4,0},{5,1},{6,2},{7,3},{8,12},{9,13},{10,... | collective-permute-start | bytes 4915208 | tf_op jit(solution)/shard_map/ppermute | solution.py:210
  45.7 21.3 %collective-permute-start.6 = (bf16[256,3200]{1,0:T(8,128)(2,1)S(1)}, bf16[256,3200]{1,0:T(8,128)(2,1)}, u32[]{:S(2)}, u32[]{:S(2)}) collective-permute-start(bf16[256,3200]{1,0:T(8,128)(2,1)S(1)} %pad_maximum_fusion.3.refs_0_.refs_4_.refs_1_.refs_2_), channel_id=1, source_target_pairs={{0,8},{1,9},{2,10},{3,11},{4,20},{5,21},{6,22},{7,23},{8,0},{9,1},... | collective-permute-start | bytes 4915208 | tf_op jit(solution)/shard_map/ppermute | solution.py:210
  46.3 18.2 %collective-permute-start.8 = (bf16[32,9216]{1,0:T(8,128)(2,1)}, bf16[32,9216]{1,0:T(8,128)(2,1)}, u32[]{:S(2)}, u32[]{:S(2)}) collective-permute-start(bf16[32,9216]{1,0:T(8,128)(2,1)} %collective-permute-done.5), channel_id=1, source_target_pairs={{1,0},{2,3},{5,4},{6,7},{9,8},{10,11},{13,12},{14,15},{17,16},{18,... | collective-permute-start | bytes 1769480 | tf_op jit(solution)/shard_map/ppermute | solution.py:180
  47.6 16.9 %collective-permute-start.9 = (bf16[32,9216]{1,0:T(8,128)(2,1)}, bf16[32,9216]{1,0:T(8,128)(2,1)}, u32[]{:S(2)}, u32[]{:S(2)}) collective-permute-start(bf16[32,9216]{1,0:T(8,128)(2,1)} %collective-permute-done.4), channel_id=1, source_target_pairs={{1,2},{2,1},{5,6},{6,5},{9,10},{10,9},{13,14},{14,13},{17,18},{18,... | collective-permute-start | bytes 1769480 | tf_op jit(solution)/shard_map/ppermute | solution.py:180
  69.3 21.6 %collective-permute-start.11 = (bf16[32,9216]{1,0:T(8,128)(2,1)}, bf16[32,9216]{1,0:T(8,128)(2,1)}, u32[]{:S(2)}, u32[]{:S(2)}) collective-permute-start(bf16[32,9216]{1,0:T(8,128)(2,1)} %collective-permute-done.9), channel_id=1, source_target_pairs={{1,0},{2,3},{5,4},{6,7},{9,8},{10,11},{13,12},{14,15},{17,16},{18,... | collective-permute-start | bytes 1769480 | tf_op jit(solution)/shard_map/ppermute | solution.py:183
  70.6 36.6 %collective-permute-start.13 = (bf16[512,1024]{1,0:T(8,128)(2,1)}, bf16[512,1024]{1,0:T(8,128)(2,1)}, u32[]{:S(2)}, u32[]{:S(2)}) collective-permute-start(bf16[512,1024]{1,0:T(8,128)(2,1)} %bitcast.8.source_ref.x_ref), channel_id=1, source_target_pairs={{1,2},{2,1},{5,6},{6,5},{9,10},{10,9},{13,14},{14,13},{17,18},{18,... | collective-permute-start | bytes 3145736 | tf_op jit(solution)/shard_map/ppermute | solution.py:225
  72.3 37.5 %collective-permute-start.12 = (bf16[512,1024]{1,0:T(8,128)(2,1)}, bf16[512,1024]{1,0:T(8,128)(2,1)}, u32[]{:S(2)}, u32[]{:S(2)}) collective-permute-start(bf16[512,1024]{1,0:T(8,128)(2,1)} %bitcast.8.source_ref.x_ref), channel_id=1, source_target_pairs={{0,1},{1,0},{2,3},{3,2},{4,5},{5,4},{6,7},{7,6},{8,9},{9,8},{10,11... | collective-permute-start | bytes 3145736 | tf_op jit(solution)/shard_map/ppermute | solution.py:225
  93.5 29.0 %collective-permute-start.14 = (bf16[128,9216]{1,0:T(8,128)(2,1)S(1)}, bf16[128,9216]{1,0:T(8,128)(2,1)}, u32[]{:S(2)}, u32[]{:S(2)}) collective-permute-start(bf16[128,9216]{1,0:T(8,128)(2,1)S(1)} %maximum_select_fusion), channel_id=1, source_target_pairs={{0,16},{1,17},{2,18},{3,19},{4,12},{5,13},{6,14},{7,15},{8,24},{9,... | collective-permute-start | bytes 7077896 | tf_op jit(solution)/shard_map/ppermute | solution.py:208
  109.8 30.1 %collective-permute-start.16 = (bf16[512,1024]{1,0:T(8,128)(2,1)}, bf16[512,1024]{1,0:T(8,128)(2,1)S(1)}, u32[]{:S(2)}, u32[]{:S(2)}) collective-permute-start(bf16[512,1024]{1,0:T(8,128)(2,1)} %collective-permute-done.12.source_ref), channel_id=1, source_target_pairs={{1,2},{2,1},{5,6},{6,5},{9,10},{10,9},{13,14},{14,13},{17,18},{18,... | collective-permute-start | bytes 3145736 | tf_op jit(solution)/shard_map/ppermute | solution.py:230
  110.5 29.4 %collective-permute-start.15 = (bf16[512,1024]{1,0:T(8,128)(2,1)}, bf16[512,1024]{1,0:T(8,128)(2,1)}, u32[]{:S(2)}, u32[]{:S(2)}) collective-permute-start(bf16[512,1024]{1,0:T(8,128)(2,1)} %collective-permute-done.13), channel_id=1, source_target_pairs={{1,0},{2,3},{5,4},{6,7},{9,8},{10,11},{13,12},{14,15},{17,16},{18,... | collective-permute-start | bytes 3145736 | tf_op jit(solution)/shard_map/ppermute | solution.py:230
  126.7 59.7 %collective-permute-start.19 = (bf16[256,9216]{1,0:T(8,128)(2,1)}, bf16[256,9216]{1,0:T(8,128)(2,1)}, u32[]{:S(2)}, u32[]{:S(2)}) collective-permute-start(bf16[256,9216]{1,0:T(8,128)(2,1)} %pad_maximum_fusion.refs_0_), channel_id=1, source_target_pairs={{0,4},{1,5},{2,6},{3,7},{4,0},{5,1},{6,2},{7,3},{8,12},{9,13},{10,... | collective-permute-start | bytes 14155784 | tf_op jit(solution)/shard_map/ppermute | solution.py:210
  126.7 59.7 %collective-permute-start.18 = (bf16[256,9216]{1,0:T(8,128)(2,1)}, bf16[256,9216]{1,0:T(8,128)(2,1)}, u32[]{:S(2)}, u32[]{:S(2)}) collective-permute-start(bf16[256,9216]{1,0:T(8,128)(2,1)} %pad_maximum_fusion.refs_0_), channel_id=1, source_target_pairs={{0,8},{1,9},{2,10},{3,11},{4,20},{5,21},{6,22},{7,23},{8,0},{9,1},... | collective-permute-start | bytes 14155784 | tf_op jit(solution)/shard_map/ppermute | solution.py:210
  142.8 27.8 %collective-permute-start.17 = (bf16[512,1024]{1,0:T(8,128)(2,1)S(1)}, bf16[512,1024]{1,0:T(8,128)(2,1)S(1)}, u32[]{:S(2)}, u32[]{:S(2)}) collective-permute-start(bf16[512,1024]{1,0:T(8,128)(2,1)S(1)} %collective-permute-done.16), channel_id=1, source_target_pairs={{1,0},{2,3},{5,4},{6,7},{9,8},{10,11},{13,12},{14,15},{17,16},{18,... | collective-permute-start | bytes 3145736 | tf_op jit(solution)/shard_map/ppermute | solution.py:234
  170.7 29.3 %collective-permute-start.23 = (bf16[128,1024]{1,0:T(8,128)(2,1)S(1)}, bf16[128,1024]{1,0:T(8,128)(2,1)S(1)}, u32[]{:S(2)}, u32[]{:S(2)}) collective-permute-start(bf16[128,1024]{1,0:T(8,128)(2,1)S(1)} %copy-done.37), channel_id=1, source_target_pairs={{0,3},{1,2},{2,1},{3,0},{4,7},{5,6},{6,5},{7,4},{8,11},{9,10},{10,... | collective-permute-start | bytes 786440 | tf_op jit(solution)/shard_map/ppermute | solution.py:195
  172.9 27.0 %collective-permute-start.22 = (bf16[128,1024]{1,0:T(8,128)(2,1)S(1)}, bf16[128,1024]{1,0:T(8,128)(2,1)S(1)}, u32[]{:S(2)}, u32[]{:S(2)}) collective-permute-start(bf16[128,1024]{1,0:T(8,128)(2,1)S(1)} %copy-done.37), channel_id=1, source_target_pairs={{0,2},{1,3},{2,0},{3,1},{4,6},{5,7},{6,4},{7,5},{8,10},{9,11},{10,... | collective-permute-start | bytes 786440 | tf_op jit(solution)/shard_map/ppermute | solution.py:195
  172.9 27.0 %collective-permute-start.21 = (bf16[128,1024]{1,0:T(8,128)(2,1)S(1)}, bf16[128,1024]{1,0:T(8,128)(2,1)S(1)}, u32[]{:S(2)}, u32[]{:S(2)}) collective-permute-start(bf16[128,1024]{1,0:T(8,128)(2,1)S(1)} %copy-done.37), channel_id=1, source_target_pairs={{0,1},{1,0},{2,3},{3,2},{4,5},{5,4},{6,7},{7,6},{8,9},{9,8},{10,11... | collective-permute-start | bytes 786440 | tf_op jit(solution)/shard_map/ppermute | solution.py:195
  186.4 13.5 %collective-permute-start.20 = (bf16[256,9216]{1,0:T(8,128)(2,1)}, bf16[256,9216]{1,0:T(8,128)(2,1)}, u32[]{:S(2)}, u32[]{:S(2)}) collective-permute-start(bf16[256,9216]{1,0:T(8,128)(2,1)} %collective-permute-done.18.refs_1_), channel_id=1, source_target_pairs={{0,4},{1,5},{2,6},{3,7},{4,0},{5,1},{6,2},{7,3},{8,12},{9,13},{10,... | collective-permute-start | bytes 14155784 | tf_op jit(solution)/shard_map/ppermute | solution.py:211
  200.7 14.9 %collective-permute-start.24 = (bf16[512,1024]{1,0:T(8,128)(2,1)S(1)}, bf16[512,1024]{1,0:T(8,128)(2,1)S(1)}, u32[]{:S(2)}, u32[]{:S(2)}) collective-permute-start(bf16[512,1024]{1,0:T(8,128)(2,1)S(1)} %maximum_select_fusion.1), channel_id=1, source_target_pairs={{0,16},{1,17},{2,18},{3,19},{4,12},{5,13},{6,14},{7,15},{8,24},{9,... | collective-permute-start | bytes 3145736 | tf_op jit(solution)/shard_map/ppermute | solution.py:208
  218.0 26.1 %collective-permute-start.26 = (bf16[1024,1024]{1,0:T(8,128)(2,1)S(1)}, bf16[1024,1024]{1,0:T(8,128)(2,1)}, u32[]{:S(2)}, u32[]{:S(2)}) collective-permute-start(bf16[1024,1024]{1,0:T(8,128)(2,1)S(1)} %pad_maximum_fusion.2.refs_4_), channel_id=1, source_target_pairs={{0,4},{1,5},{2,6},{3,7},{4,0},{5,1},{6,2},{7,3},{8,12},{9,13},{10,... | collective-permute-start | bytes 6291464 | tf_op jit(solution)/shard_map/ppermute | solution.py:210
  218.0 26.2 %collective-permute-start.25 = (bf16[1024,1024]{1,0:T(8,128)(2,1)S(1)}, bf16[1024,1024]{1,0:T(8,128)(2,1)}, u32[]{:S(2)}, u32[]{:S(2)}) collective-permute-start(bf16[1024,1024]{1,0:T(8,128)(2,1)S(1)} %pad_maximum_fusion.2.refs_4_), channel_id=1, source_target_pairs={{0,8},{1,9},{2,10},{3,11},{4,20},{5,21},{6,22},{7,23},{8,0},{9,1},... | collective-permute-start | bytes 6291464 | tf_op jit(solution)/shard_map/ppermute | solution.py:210
  248.6 35.2 %collective-permute-start.28 = (bf16[2048,1024]{1,0:T(8,128)(2,1)}, bf16[2048,1024]{1,0:T(8,128)(2,1)}, u32[]{:S(2)}, u32[]{:S(2)}) collective-permute-start(bf16[2048,1024]{1,0:T(8,128)(2,1)} %convolution_convert_fusion.1), channel_id=1, source_target_pairs={{0,4},{1,5},{2,6},{3,7},{4,0},{5,1},{6,2},{7,3},{8,12},{9,13},{10,... | collective-permute-start | bytes 12582920 | tf_op jit(solution)/shard_map/ppermute | solution.py:263
  299.8 13.5 %collective-permute-start.29 = (bf16[512,8192]{1,0:T(8,128)(2,1)}, bf16[512,8192]{1,0:T(8,128)(2,1)}, u32[]{:S(2)}, u32[]{:S(2)}) collective-permute-start(bf16[512,8192]{1,0:T(8,128)(2,1)} %convolution_convert_fusion), channel_id=1, source_target_pairs={{0,4},{1,5},{2,6},{3,7},{4,0},{5,1},{6,2},{7,3},{8,12},{9,13},{10,... | collective-permute-start | bytes 25165832 | tf_op jit(solution)/shard_map/ppermute | solution.py:263
  301.8 47.1 %collective-permute-start.30 = (bf16[1024,1024]{1,0:T(8,128)(2,1)}, bf16[1024,1024]{1,0:T(8,128)(2,1)S(1)}, u32[]{:S(2)}, u32[]{:S(2)}) collective-permute-start(bf16[1024,1024]{1,0:T(8,128)(2,1)} %add_convert_fusion.7), channel_id=1, source_target_pairs={{0,8},{1,9},{2,10},{3,11},{4,20},{5,21},{6,22},{7,23},{8,0},{9,1},... | collective-permute-start | bytes 6291464 | tf_op jit(solution)/shard_map/ppermute | solution.py:267
  322.4 63.2 %collective-permute-start.32 = (bf16[256,8192]{1,0:T(8,128)(2,1)}, bf16[256,8192]{1,0:T(8,128)(2,1)}, u32[]{:S(2)}, u32[]{:S(2)}) collective-permute-start(bf16[256,8192]{1,0:T(8,128)(2,1)} %add_convert_fusion.2), channel_id=1, source_target_pairs={{0,8},{1,9},{2,10},{3,11},{4,20},{5,21},{6,22},{7,23},{8,0},{9,1},... | collective-permute-start | bytes 12582920 | tf_op jit(solution)/shard_map/ppermute | solution.py:267
  325.5 23.3 %collective-permute-start.31 = (bf16[512,1024]{1,0:T(8,128)(2,1)}, bf16[512,1024]{1,0:T(8,128)(2,1)}, u32[]{:S(2)}, u32[]{:S(2)}) collective-permute-start(bf16[512,1024]{1,0:T(8,128)(2,1)} %convolution_convert_fusion.3), channel_id=1, source_target_pairs={{0,4},{1,5},{2,6},{3,7},{4,0},{5,1},{6,2},{7,3},{8,12},{9,13},{10,... | collective-permute-start | bytes 3145736 | tf_op jit(solution)/shard_map/ppermute | solution.py:263
  352.0 59.1 %collective-permute-start.35 = (bf16[256,1024]{1,0:T(8,128)(2,1)}, bf16[256,1024]{1,0:T(8,128)(2,1)}, u32[]{:S(2)}, u32[]{:S(2)}) collective-permute-start(bf16[256,1024]{1,0:T(8,128)(2,1)} %add_convert_fusion.18), channel_id=1, source_target_pairs={{0,8},{1,9},{2,10},{3,11},{4,20},{5,21},{6,22},{7,23},{8,0},{9,1},... | collective-permute-start | bytes 1572872 | tf_op jit(solution)/shard_map/ppermute | solution.py:267
  356.2 54.9 %collective-permute-start.34 = (bf16[512,1024]{1,0:T(8,128)(2,1)}, bf16[512,1024]{1,0:T(8,128)(2,1)}, u32[]{:S(2)}, u32[]{:S(2)}) collective-permute-start(bf16[512,1024]{1,0:T(8,128)(2,1)} %slice.241), channel_id=1, source_target_pairs={{0,16},{1,17},{2,18},{3,19},{4,12},{5,13},{6,14},{7,15},{8,24},{9,... | collective-permute-start | bytes 3145736 | tf_op jit(solution)/shard_map/ppermute | solution.py:274
  367.0 27.1 %collective-permute-start.33 = (bf16[512,1024]{1,0:T(8,128)(2,1)}, bf16[512,1024]{1,0:T(8,128)(2,1)S(1)}, u32[]{:S(2)}, u32[]{:S(2)}) collective-permute-start(bf16[512,1024]{1,0:T(8,128)(2,1)} %pull3.1), channel_id=1, source_target_pairs={{0,1},{3,2},{4,5},{7,6},{8,9},{11,10},{12,13},{15,14},{16,17},{19,... | collective-permute-start | bytes 3145736 | tf_op jit(solution)/shard_map/ppermute | solution.py:239
  393.3 42.7 %collective-permute-start.36 = (bf16[128,8192]{1,0:T(8,128)(2,1)}, bf16[128,8192]{1,0:T(8,128)(2,1)}, u32[]{:S(2)}, u32[]{:S(2)}) collective-permute-start(bf16[128,8192]{1,0:T(8,128)(2,1)} %slice.242), channel_id=1, source_target_pairs={{0,16},{1,17},{2,18},{3,19},{4,12},{5,13},{6,14},{7,15},{8,24},{9,... | collective-permute-start | bytes 6291464 | tf_op jit(solution)/shard_map/ppermute | solution.py:274
  404.9 37.0 %collective-permute-start.38 = (bf16[512,1024]{1,0:T(8,128)(2,1)}, bf16[512,1024]{1,0:T(8,128)(2,1)}, u32[]{:S(2)}, u32[]{:S(2)}) collective-permute-start(bf16[512,1024]{1,0:T(8,128)(2,1)} %add_convert_fusion.14), channel_id=1, source_target_pairs={{1,2},{2,1},{5,6},{6,5},{9,10},{10,9},{13,14},{14,13},{17,18},{18,... | collective-permute-start | bytes 3145736 | tf_op jit(solution)/shard_map/ppermute | solution.py:242
  406.6 35.3 %collective-permute-start.37 = (bf16[512,1024]{1,0:T(8,128)(2,1)}, bf16[512,1024]{1,0:T(8,128)(2,1)}, u32[]{:S(2)}, u32[]{:S(2)}) collective-permute-start(bf16[512,1024]{1,0:T(8,128)(2,1)} %pull2.1), channel_id=1, source_target_pairs={{0,1},{3,2},{4,5},{7,6},{8,9},{11,10},{12,13},{15,14},{16,17},{19,... | collective-permute-start | bytes 3145736 | tf_op jit(solution)/shard_map/ppermute | solution.py:242
  413.1 41.5 %collective-permute-start.40 = (bf16[128,1024]{1,0:T(8,128)(2,1)}, bf16[128,1024]{1,0:T(8,128)(2,1)S(1)}, u32[]{:S(2)}, u32[]{:S(2)}) collective-permute-start(bf16[128,1024]{1,0:T(8,128)(2,1)} %slice.244), channel_id=1, source_target_pairs={{0,16},{1,17},{2,18},{3,19},{4,12},{5,13},{6,14},{7,15},{8,24},{9,... | collective-permute-start | bytes 786440 | tf_op jit(solution)/shard_map/ppermute | solution.py:274
  415.7 38.8 %collective-permute-start.39 = (bf16[256,1024]{1,0:T(8,128)(2,1)S(1)}, bf16[256,1024]{1,0:T(8,128)(2,1)S(1)}, u32[]{:S(2)}, u32[]{:S(2)}) collective-permute-start(bf16[256,1024]{1,0:T(8,128)(2,1)S(1)} %bitcast.142), channel_id=1, source_target_pairs={{0,1},{1,0},{2,3},{3,2},{4,5},{5,4},{6,7},{7,6},{8,9},{9,8},{10,11... | collective-permute-start | bytes 1572872 | tf_op jit(solution)/shard_map/ppermute | solution.py:283
  439.9 43.7 %collective-permute-start.43 = (bf16[64,8192]{1,0:T(8,128)(2,1)}, bf16[64,8192]{1,0:T(8,128)(2,1)}, u32[]{:S(2)}, u32[]{:S(2)}) collective-permute-start(bf16[64,8192]{1,0:T(8,128)(2,1)} %bitcast.19), channel_id=1, source_target_pairs={{0,1},{1,0},{2,3},{3,2},{4,5},{5,4},{6,7},{7,6},{8,9},{9,8},{10,11... | collective-permute-start | bytes 3145736 | tf_op jit(solution)/shard_map/ppermute | solution.py:283
  455.3 28.2 %collective-permute-start.42 = (bf16[64,1024]{1,0:T(8,128)(2,1)}, bf16[64,1024]{1,0:T(8,128)(2,1)}, u32[]{:S(2)}, u32[]{:S(2)}) collective-permute-start(bf16[64,1024]{1,0:T(8,128)(2,1)} %bitcast.24), channel_id=1, source_target_pairs={{0,1},{1,0},{2,3},{3,2},{4,5},{5,4},{6,7},{7,6},{8,9},{9,8},{10,11... | collective-permute-start | bytes 393224 | tf_op jit(solution)/shard_map/ppermute | solution.py:283
  456.4 27.2 %collective-permute-start.41 = (bf16[128,1024]{1,0:T(8,128)(2,1)S(1)}, bf16[128,1024]{1,0:T(8,128)(2,1)}, u32[]{:S(2)}, u32[]{:S(2)}) collective-permute-start(bf16[128,1024]{1,0:T(8,128)(2,1)S(1)} %dynamic-slice_bitcast_fusion.1), channel_id=1, source_target_pairs={{0,2},{1,3},{2,0},{3,1},{4,6},{5,7},{6,4},{7,5},{8,10},{9,11},{10,... | collective-permute-start | bytes 786440 | tf_op jit(solution)/shard_map/ppermute | solution.py:283
  484.6 30.4 %collective-permute-start.45 = (bf16[512,1024]{1,0:T(8,128)(2,1)}, bf16[512,1024]{1,0:T(8,128)(2,1)}, u32[]{:S(2)}, u32[]{:S(2)}) collective-permute-start(bf16[512,1024]{1,0:T(8,128)(2,1)} %add_convert_fusion.12), channel_id=1, source_target_pairs={{1,2},{2,1},{5,6},{6,5},{9,10},{10,9},{13,14},{14,13},{17,18},{18,... | collective-permute-start | bytes 3145736 | tf_op jit(solution)/shard_map/ppermute | solution.py:249
  486.5 28.5 %collective-permute-start.46 = (bf16[512,1024]{1,0:T(8,128)(2,1)}, bf16[512,1024]{1,0:T(8,128)(2,1)}, u32[]{:S(2)}, u32[]{:S(2)}) collective-permute-start(bf16[512,1024]{1,0:T(8,128)(2,1)} %add_convert_fusion.11), channel_id=1, source_target_pairs={{0,1},{1,0},{2,3},{3,2},{4,5},{5,4},{6,7},{7,6},{8,9},{9,8},{10,11... | collective-permute-start | bytes 3145736 | tf_op jit(solution)/shard_map/ppermute | solution.py:250
  500.6 20.7 %collective-permute-start.47 = (bf16[256,3072]{1,0:T(8,128)(2,1)}, bf16[256,3072]{1,0:T(8,128)(2,1)}, u32[]{:S(2)}, u32[]{:S(2)}) collective-permute-start(bf16[256,3072]{1,0:T(8,128)(2,1)} %pad_maximum_fusion.4), channel_id=1, source_target_pairs={{0,8},{1,9},{2,10},{3,11},{4,20},{5,21},{6,22},{7,23},{8,0},{9,1},... | collective-permute-start | bytes 4718600 | tf_op jit(solution)/shard_map/ppermute | solution.py:267
  523.4 35.7 %collective-permute-start.49 = (bf16[128,3072]{1,0:T(8,128)(2,1)S(1)}, bf16[128,3072]{1,0:T(8,128)(2,1)}, u32[]{:S(2)}, u32[]{:S(2)}) collective-permute-start(bf16[128,3072]{1,0:T(8,128)(2,1)S(1)} %slice.247), channel_id=1, source_target_pairs={{0,16},{1,17},{2,18},{3,19},{4,12},{5,13},{6,14},{7,15},{8,24},{9,... | collective-permute-start | bytes 2359304 | tf_op jit(solution)/shard_map/ppermute | solution.py:274
  524.6 34.6 %collective-permute-start.48 = (bf16[32,8192]{1,0:T(8,128)(2,1)}, bf16[32,8192]{1,0:T(8,128)(2,1)S(1)}, u32[]{:S(2)}, u32[]{:S(2)}) collective-permute-start(bf16[32,8192]{1,0:T(8,128)(2,1)} %dynamic-slice_bitcast_fusion), channel_id=1, source_target_pairs={{0,2},{1,3},{2,0},{3,1},{4,6},{5,7},{6,4},{7,5},{8,10},{9,11},{10,... | collective-permute-start | bytes 1572872 | tf_op jit(solution)/shard_map/ppermute | solution.py:283
  526.5 25.8 %collective-permute-start.52 = (bf16[32,1024]{1,0:T(8,128)(2,1)}, bf16[32,1024]{1,0:T(8,128)(2,1)S(1)}, u32[]{:S(2)}, u32[]{:S(2)}) collective-permute-start(bf16[32,1024]{1,0:T(8,128)(2,1)} %dynamic-slice_bitcast_fusion.3), channel_id=1, source_target_pairs={{0,2},{1,3},{2,0},{3,1},{4,6},{5,7},{6,4},{7,5},{8,10},{9,11},{10,... | collective-permute-start | bytes 196616 | tf_op jit(solution)/shard_map/ppermute | solution.py:283
  560.7 13.7 %collective-permute-start.50 = (bf16[64,3072]{1,0:T(8,128)(2,1)S(1)}, bf16[64,3072]{1,0:T(8,128)(2,1)}, u32[]{:S(2)}, u32[]{:S(2)}) collective-permute-start(bf16[64,3072]{1,0:T(8,128)(2,1)S(1)} %bitcast.143), channel_id=1, source_target_pairs={{0,1},{1,0},{2,3},{3,2},{4,5},{5,4},{6,7},{7,6},{8,9},{9,8},{10,11... | collective-permute-start | bytes 1179656 | tf_op jit(solution)/shard_map/ppermute | solution.py:283
  (56 other events, 431.9 us)

commit v6 on v5

--- a/solution.py
+++ b/solution.py
@@ -1098,8 +1098,7 @@
     held = step(held, last_sum)
     held = go_on(held, pair_sum)
     part_grads = pull(order, held, grads[0], mixed_w, 0)
-    if plan.line:
-        part_grads = finish(part_grads, back_way)
+    part_grads = finish(part_grads, down_sum, output_sum, *([back_way] if plan.line else []))
     part_grads = step(part_grads, last_sum)
     if plan.line:
         sends = back_way.value
@@ -1111,9 +1110,12 @@
     edge_one = step(edge_one, pair_sum)
     edge_one = step(edge_one, last_sum)
     vectors = sum_vectors(plan, (edge_one[0], edge_one[1], edge_two[0], edge_two[1]))
+    finish((), pair_sum)
+    pair_grads = pair_sum.value
+    for _ in range(plan.ctx_bits - 1):
+        pair_grads = step(pair_grads, last_sum)
     finish((), last_sum)
-    finish((), down_sum, output_sum, pair_sum)
-    gate_grad, up_grad = part_ways(pair_sum.value, part)
+    gate_grad, up_grad = part_ways(pair_grads, part)
     key_grad, value_grad = part_ways(last_sum.value[:, width:], 128)
     return (
         output,

time: 599 us -> 591 us (0.987)
  waiting for transfers between devices: 93.2 us -> 83 us
    ppermute x8, waiting for transfers between devices: 32.7 us -> 17.9 us  [sum_steps(): other, = (yield ([lax.ppermute(send, AXES, plan.across[1 << bit])], [send]))]
    unnamed x105 -> x111, local copies, waits for them, and re-layouts: 14.2 us -> 15 us
  transfers between devices with their start and end apart: 54 -> 54, of which waited for: 15 -> 15; matrix products, arithmetic and copies ran while one was open for 20% -> 21% of each run, Pallas kernels for 45% -> 46%
where the time goes in v6:
time: 591 us; the launch traced here: 581 us
  Pallas kernels  266 us (45%)
  waiting for transfers between devices  83 us (14%)
  starting transfers between devices  66.6 us (11%)
  matrix products  64.8 us (11%)
  other arithmetic  62.9 us (11%)
  local copies, waits for them, and re-layouts  35.5 us (6%)
    pallas_call x21, Pallas kernels, call(): pl.pallas_call(body, out_shape=out_shape, grid_spec=pltpu.PrefetchScalarG...  266 us
    dot_general x24, matrix products, product(): found = found + jnp.dot(part, right, preferred_element_type=jnp.float32)  64.8 us
    convert_element_type x15, other arithmetic, add(): return (a.astype(jnp.float32) + b.astype(jnp.float32)).astype(BF)  28.9 us
    ppermute x8, waiting for transfers between devices, sum_steps(): other, = (yield ([lax.ppermute(send, AXES, plan.across[1 << bit])], [send]))  17.9 us
    unnamed x111, local copies, waits for them, and re-layouts  15 us
    ppermute x1, waiting for transfers between devices, gather_steps(): lax.ppermute(shard, AXES, plan.across[1])  13.5 us
    ppermute x1, waiting for transfers between devices, gather_steps(): lax.ppermute(middle, AXES, plan.outward)  13.1 us
  transfers between devices with their start and end apart: 54, of which 15 were waited for; matrix products, arithmetic and copies ran while one was open for 21% of the time, Pallas kernels for 46%

profile of v6, /device:TPU:0, one launch (start us, length us, event | category | flops | bytes accessed | tf_op | source)
XLA Modules:
  0.0 581.2 jit_solution(7635807415451794223)
XLA Ops:
  5.3 5.1 collective-permute-start.2
  15.9 5.6 multiply_sine_fusion
  22.7 5.3 collective-permute-done.1
  32.0 13.5 %collective-permute-done.4 = bf16[32,9216]{1,0:T(8,128)(2,1)} collective-permute-done((bf16[32,9216]{1,0:T(8,128)(2,1)S(1)}, bf16[32,9216]{1,0:T(8,128)(2,1)}, u32[]{:S(2)}, u32[]{:S(2)}) %collective-permute-start.4) | collective-permute-done | bytes 589856 | tf_op jit(solution)/shard_map/ppermute | solution.py:176
  51.5 13.1 %collective-permute-done.8 = bf16[32,9216]{1,0:T(8,128)(2,1)} collective-permute-done((bf16[32,9216]{1,0:T(8,128)(2,1)}, bf16[32,9216]{1,0:T(8,128)(2,1)}, u32[]{:S(2)}, u32[]{:S(2)}) %collective-permute-start.8) | collective-permute-done | bytes 589856 | tf_op jit(solution)/shard_map/ppermute | solution.py:180
  72.3 5.5 collective-permute-start.12
  77.8 13.2 %project0.1 = (bf16[1024,512]{1,0:T(8,128)(2,1)}, bf16[512,1024]{1,0:T(8,128)(2,1)}, bf16[512,2048]{1,0:T(8,128)(2,1)}, f32[8,1024]{1,0:T(8,128)}) custom-call(s32[8]{0:T(128)} %fusion.61.order_ref, bf16[512,1024]{1,0:T(8,128)(2,1)} %bitcast.8.source_ref.x_ref, f32[2048,128]{1,0:T(8,128)} %get-tuple-element.242.cos_ref, ...), custom_call_target="tpu_custom_call" | custom-call | flops 51539607552 | bytes 20480000 | tf_op jit(solution)/shard_map/project0/pallas_call | solution.py:346
  94.8 12.4 %attend0.1 = (f32[8,8,512]{2,1,0:T(8,128)}, f32[1024,512]{1,0:T(8,128)}) custom-call(s32[8]{0:T(128)} %fusion.61.order_ref, s32[4]{0:T(128)} %subtract_clamp_fusion.valid_ref, bf16[512,1024]{1,0:T(8,128)(2,1)} %get-tuple-element.246.q_ref, bf16[512,2048]{1,0:T(8,128)(2,1)} %get-tuple-element.251.kv_ref), custom_call_target="tpu_custom_call" | custom-call | flops 68719476736 | bytes 5373968 | tf_op jit(solution)/shard_map/attend0/pallas_call | solution.py:346
  112.0 10.0 %project1.1 = (bf16[1024,512]{1,0:T(8,128)(2,1)}, bf16[512,2048]{1,0:T(8,128)(2,1)}) custom-call(s32[8]{0:T(128)} %fusion.61.order_ref, bf16[512,1024]{1,0:T(8,128)(2,1)} %collective-permute-done.12.source_ref, f32[2048,128]{1,0:T(8,128)} %get-tuple-element.242.cos_ref, f32[2048,128]{1,0:T(8,128)} %get-tuple-element.243.sin_ref, ...), custom_call_target="tpu_custom_call" | custom-call | flops 34359738368 | bytes 12877824 | tf_op jit(solution)/shard_map/project1/pallas_call | solution.py:346
  122.6 4.2 pad_maximum_fusion.refs_0_
  127.3 12.7 %attend1.1 = (f32[8,8,512]{2,1,0:T(8,128)}, f32[1024,512]{1,0:T(8,128)}) custom-call(s32[8]{0:T(128)} %fusion.61.order_ref, s32[4]{0:T(128)} %subtract_clamp_fusion.valid_ref, bf16[512,1024]{1,0:T(8,128)(2,1)} %get-tuple-element.246.q_ref, bf16[512,2048]{1,0:T(8,128)(2,1)} %get-tuple-element.259.kv_ref, f32[8,8,512]{2,1,0:T(8,128)} %get-tuple-element.263.refs_0_, ...), custom_call_target="tpu_custom_call" | custom-call | flops 68719476736 | bytes 7602192 | tf_op jit(solution)/shard_map/attend1/pallas_call | solution.py:346
  140.0 2.9 add.233.source_ref
  144.2 9.9 %project2.1 = (bf16[1024,512]{1,0:T(8,128)(2,1)}, bf16[512,2048]{1,0:T(8,128)(2,1)}) custom-call(s32[8]{0:T(128)} %fusion.61.order_ref, bf16[512,1024]{1,0:T(8,128)(2,1)} %add.233.source_ref, f32[2048,128]{1,0:T(8,128)} %get-tuple-element.242.cos_ref, f32[2048,128]{1,0:T(8,128)} %get-tuple-element.243.sin_ref, bf16[256,3200]{1,0:T(8,128)(2,1)} %copy-done.5, ...), custom_call_target="tpu_custom_call" | custom-call | flops 34359738368 | bytes 12877824 | tf_op jit(solution)/shard_map/project2/pallas_call | solution.py:346
  154.1 12.8 %attend2.1 = (f32[8,8,512]{2,1,0:T(8,128)}, f32[1024,512]{1,0:T(8,128)}) custom-call(s32[8]{0:T(128)} %fusion.61.order_ref, s32[4]{0:T(128)} %subtract_clamp_fusion.valid_ref, bf16[512,1024]{1,0:T(8,128)(2,1)} %get-tuple-element.246.q_ref, bf16[512,2048]{1,0:T(8,128)(2,1)} %get-tuple-element.269.kv_ref, f32[8,8,512]{2,1,0:T(8,128)} %get-tuple-element.272.refs_0_, ...), custom_call_target="tpu_custom_call" | custom-call | flops 68719476736 | bytes 7602192 | tf_op jit(solution)/shard_map/attend2/pallas_call | solution.py:346
  167.0 3.8 collective-permute-done.17
  176.5 10.0 %project3.1 = (bf16[1024,512]{1,0:T(8,128)(2,1)}, bf16[512,2048]{1,0:T(8,128)(2,1)}) custom-call(s32[8]{0:T(128)} %fusion.61.order_ref, bf16[512,1024]{1,0:T(8,128)(2,1)} %add.234.source_ref, f32[2048,128]{1,0:T(8,128)} %get-tuple-element.242.cos_ref, f32[2048,128]{1,0:T(8,128)} %get-tuple-element.243.sin_ref, bf16[256,3200]{1,0:T(8,128)(2,1)} %copy-done.5, ...), custom_call_target="tpu_custom_call" | custom-call | flops 34359738368 | bytes 12877824 | tf_op jit(solution)/shard_map/project3/pallas_call | solution.py:346
  186.6 13.4 %attend3.1 = (bf16[512,1024]{1,0:T(8,128)(2,1)}, bf16[1024,512]{1,0:T(8,128)(2,1)}, f32[512,1024]{1,0:T(8,128)}, f32[8,8,512]{2,1,0:T(8,128)}) custom-call(s32[8]{0:T(128)} %fusion.61.order_ref, s32[4]{0:T(128)} %subtract_clamp_fusion.valid_ref, bf16[512,1024]{1,0:T(8,128)(2,1)} %get-tuple-element.246.q_ref, bf16[512,2048]{1,0:T(8,128)(2,1)} %get-tuple-element.280.kv_ref, ...), custom_call_target="tpu_custom_call" | custom-call | flops 68719476736 | bytes 9699344 | tf_op jit(solution)/shard_map/attend3/pallas_call | solution.py:346
  202.4 6.1 %middle.1 = (f32[512,1024]{1,0:T(8,128)}, bf16[512,1024]{1,0:T(8,128)(2,1)}, bf16[1024,512]{1,0:T(8,128)(2,1)}) custom-call(s32[8]{0:T(128)} %fusion.61.order_ref, bf16[512,1024]{1,0:T(8,128)(2,1)} %get-tuple-element.299.o_ref, bf16[512,1024]{1,0:T(8,128)(2,1)} %bitcast.8.source_ref.x_ref, f32[8,1024]{1,0:T(8,128)} %get-tuple-element.255.refs_4_.cols_ref, ...), custom_call_target="tpu_custom_call" | custom-call | flops 1073741824 | bytes 25198592 | tf_op jit(solution)/shard_map/middle/pallas_call | solution.py:346
  208.5 7.2 %collective-permute-done.24 = bf16[512,1024]{1,0:T(8,128)(2,1)S(1)} collective-permute-done((bf16[512,1024]{1,0:T(8,128)(2,1)S(1)}, bf16[512,1024]{1,0:T(8,128)(2,1)S(1)}, u32[]{:S(2)}, u32[]{:S(2)}) %collective-permute-start.24) | collective-permute-done | bytes 1048608 | tf_op jit(solution)/shard_map/ppermute | solution.py:208
  219.7 18.4 %feed.1 = (bf16[512,4096]{1,0:T(8,128)(2,1)}, bf16[512,4096]{1,0:T(8,128)(2,1)}, bf16[512,4096]{1,0:T(8,128)(2,1)}, bf16[4096,512]{1,0:T(8,128)(2,1)}) custom-call(s32[8]{0:T(128)} %fusion.61.order_ref, bf16[512,1024]{1,0:T(8,128)(2,1)} %get-tuple-element.305.two_ref, bf16[256,9216]{1,0:T(8,128)(2,1)} %pad_maximum_fusion.refs_0_, ...), custom_call_target="tpu_custom_call" | custom-call | flops 8589934592 | bytes 36700160 | tf_op jit(solution)/shard_map/feed/pallas_call | solution.py:346
  238.1 6.0 %convolution_convert_fusion.1 = bf16[2048,1024]{1,0:T(8,128)(2,1)} fusion(bf16[512,1024]{1,0:T(8,128)(2,1)S(1)} %copy-done.13, bf16[4096,512]{1,0:T(8,128)(2,1)} %get-tuple-element.309), kind=kOutput, calls=%fused_computation.11 | convolution fusion | flops 2149580800 | bytes 7340032 | tf_op jit(solution)/shard_map/dot_general | solution.py:328
  244.3 4.4 collective-permute-done.27.refs_7_
  250.1 33.7 %feed_back.1 = (bf16[512,1024]{1,0:T(8,128)(2,1)}, bf16[512,8192]{1,0:T(8,128)(2,1)}, f32[512,1024]{1,0:T(8,128)}) custom-call(s32[8]{0:T(128)} %fusion.61.order_ref, bf16[512,1024]{1,0:T(8,128)(2,1)} %bitcast_select_fusion.m_ref, bf16[512,4096]{1,0:T(8,128)(2,1)} %get-tuple-element.306.gate_ref, bf16[512,4096]{1,0:T(8,128)(2,1)} %get-tuple-element.307.up_ref, ...), custom_call_target="tpu_custom_call" | custom-call | flops 17179869184 | bytes 54525952 | tf_op jit(solution)/shard_map/feed_back/pallas_call | solution.py:346
  283.8 4.6 add_convert_fusion.6
  288.4 4.6 add_convert_fusion.7
  293.1 6.8 %convolution_convert_fusion = bf16[512,8192]{1,0:T(8,128)(2,1)} fusion(bf16[512,8192]{1,0:T(8,128)(2,1)S(1)} %copy-done.50, bf16[1024,512]{1,0:T(8,128)(2,1)S(1)} %copy-done.44), kind=kOutput, calls=%fused_computation.1 | convolution fusion | flops 4299161600 | bytes 17301504 | tf_op jit(solution)/shard_map/dot_general | solution.py:328
  303.4 7.4 %middle_back.1 = (f32[512,1024]{1,0:T(8,128)}, bf16[512,1024]{1,0:T(8,128)(2,1)}, bf16[512,1024]{1,0:T(8,128)(2,1)}, f32[8,1024]{1,0:T(8,128)}) custom-call(s32[8]{0:T(128)} %fusion.61.order_ref, f32[512,1024]{1,0:T(8,128)} %get-tuple-element.331.grads_ref, f32[512,1024]{1,0:T(8,128)} %get-tuple-element.318.resid_ref, ...), custom_call_target="tpu_custom_call" | custom-call | flops 1073741824 | bytes 28348416 | tf_op jit(solution)/shard_map/middle_back/pallas_call | solution.py:346
  313.4 9.1 %add_convert_fusion.2 = bf16[256,8192]{1,0:T(8,128)(2,1)} fusion(bf16[512,8192]{1,0:T(8,128)(2,1)} %collective-permute-done.29, bf16[512,8192]{1,0:T(8,128)(2,1)} %get-tuple-element.330, bf16[1024,512]{1,0:T(8,128)(2,1)S(1)} %copy-done.44), kind=kOutput, calls=%fused_computation.4 | convolution fusion | flops 2153775104 | bytes 17039360 | tf_op jit(solution)/shard_map/dot_general | solution.py:328
  325.6 6.8 %add_convert_fusion.1 = bf16[256,8192]{1,0:T(8,128)(2,1)} fusion(bf16[512,8192]{1,0:T(8,128)(2,1)} %collective-permute-done.29, bf16[512,8192]{1,0:T(8,128)(2,1)S(1)} %bitcast.156, bf16[1024,512]{1,0:T(8,128)(2,1)S(1)} %copy-done.44), kind=kOutput, calls=%fused_computation.3 | convolution fusion | flops 2153775104 | bytes 17039360 | tf_op jit(solution)/shard_map/dot_general | solution.py:328
  332.4 16.5 %attend_back3.1 = (f32[1024,512]{1,0:T(8,128)}, bf16[512,2048]{1,0:T(8,128)(2,1)}) custom-call(s32[8]{0:T(128)} %fusion.61.order_ref, s32[4]{0:T(128)} %subtract_clamp_fusion.valid_ref, bf16[512,1024]{1,0:T(8,128)(2,1)} %get-tuple-element.246.q_ref, bf16[512,2048]{1,0:T(8,128)(2,1)} %get-tuple-element.280.kv_ref, ...), custom_call_target="tpu_custom_call" | custom-call | flops 10737418240 | bytes 12714000 | tf_op jit(solution)/shard_map/attend_back3/pallas_call | solution.py:346
  348.9 3.1 add_convert_fusion.18
  360.1 7.0 %pull3.1 = bf16[512,1024]{1,0:T(8,128)(2,1)} custom-call(s32[8]{0:T(128)} %fusion.61.order_ref, bf16[512,2048]{1,0:T(8,128)(2,1)} %get-tuple-element.349.refs_0_, bf16[256,3200]{1,0:T(8,128)(2,1)} %copy-done.5, bf16[256,3200]{1,0:T(8,128)(2,1)} %collective-permute-done.6.refs_1_.refs_5_.refs_2_.refs_3_, bf16[256,3200]{1,0:T(8,128)(2,1)} %copy-done.9, ...), custom_call_target="tpu_custom_call" | custom-call | flops 524288 | bytes 9699328 | tf_op jit(solution)/shard_map/pull3/pallas_call | solution.py:346
  369.1 16.7 %attend_back2.1 = (f32[1024,512]{1,0:T(8,128)}, bf16[512,2048]{1,0:T(8,128)(2,1)}) custom-call(s32[8]{0:T(128)} %fusion.61.order_ref, s32[4]{0:T(128)} %subtract_clamp_fusion.valid_ref, bf16[512,1024]{1,0:T(8,128)(2,1)} %get-tuple-element.246.q_ref, bf16[512,2048]{1,0:T(8,128)(2,1)} %get-tuple-element.269.kv_ref, ...), custom_call_target="tpu_custom_call" | custom-call | flops 10737418240 | bytes 14811152 | tf_op jit(solution)/shard_map/attend_back2/pallas_call | solution.py:346
  385.8 5.0 add_convert_fusion
  395.1 7.1 %pull2.1 = bf16[512,1024]{1,0:T(8,128)(2,1)} custom-call(s32[8]{0:T(128)} %fusion.61.order_ref, bf16[512,2048]{1,0:T(8,128)(2,1)} %get-tuple-element.359.refs_0_, bf16[256,3200]{1,0:T(8,128)(2,1)} %copy-done.5, bf16[256,3200]{1,0:T(8,128)(2,1)} %collective-permute-done.6.refs_1_.refs_5_.refs_2_.refs_3_, bf16[256,3200]{1,0:T(8,128)(2,1)} %copy-done.9, ...), custom_call_target="tpu_custom_call" | custom-call | flops 524288 | bytes 9699328 | tf_op jit(solution)/shard_map/pull2/pallas_call | solution.py:346
  406.6 4.6 collective-permute-start.37
  416.0 3.3 fusion.15
  419.2 16.8 %attend_back1.1 = (f32[1024,512]{1,0:T(8,128)}, bf16[512,2048]{1,0:T(8,128)(2,1)}) custom-call(s32[8]{0:T(128)} %fusion.61.order_ref, s32[4]{0:T(128)} %subtract_clamp_fusion.valid_ref, bf16[512,1024]{1,0:T(8,128)(2,1)} %get-tuple-element.246.q_ref, bf16[512,2048]{1,0:T(8,128)(2,1)} %get-tuple-element.259.kv_ref, ...), custom_call_target="tpu_custom_call" | custom-call | flops 10737418240 | bytes 14811152 | tf_op jit(solution)/shard_map/attend_back1/pallas_call | solution.py:346
  441.9 7.0 %pull1.1 = bf16[512,1024]{1,0:T(8,128)(2,1)} custom-call(s32[8]{0:T(128)} %fusion.61.order_ref, bf16[512,2048]{1,0:T(8,128)(2,1)} %get-tuple-element.377.refs_0_, bf16[256,3200]{1,0:T(8,128)(2,1)} %copy-done.5, bf16[256,3200]{1,0:T(8,128)(2,1)} %collective-permute-done.6.refs_1_.refs_5_.refs_2_.refs_3_, bf16[256,3200]{1,0:T(8,128)(2,1)} %copy-done.9, ...), custom_call_target="tpu_custom_call" | custom-call | flops 524288 | bytes 9699328 | tf_op jit(solution)/shard_map/pull1/pallas_call | solution.py:346
  449.0 3.0 add_convert_fusion.12
  458.6 18.3 %attend_back0.1 = (bf16[512,1024]{1,0:T(8,128)(2,1)}, bf16[512,2048]{1,0:T(8,128)(2,1)}) custom-call(s32[8]{0:T(128)} %fusion.61.order_ref, s32[4]{0:T(128)} %subtract_clamp_fusion.valid_ref, bf16[512,1024]{1,0:T(8,128)(2,1)} %get-tuple-element.246.q_ref, bf16[512,2048]{1,0:T(8,128)(2,1)} %get-tuple-element.251.kv_ref, ...), custom_call_target="tpu_custom_call" | custom-call | flops 10737418240 | bytes 13762576 | tf_op jit(solution)/shard_map/attend_back0/pallas_call | solution.py:346
  505.6 10.0 %pull0.1.refs_0_ = f32[512,1024]{1,0:T(8,128)} custom-call(s32[8]{0:T(128)} %fusion.61.order_ref, bf16[512,1024]{1,0:T(8,128)(2,1)} %get-tuple-element.409.refs_0_, bf16[512,2048]{1,0:T(8,128)(2,1)} %get-tuple-element.393.refs_1_, bf16[256,3200]{1,0:T(8,128)(2,1)} %copy-done.5, bf16[256,3200]{1,0:T(8,128)(2,1)} %collective-permute-done.6.refs_1_.refs_5_.refs_2_.refs_3_, ...), custom_call_target="tpu_custom_call" | custom-call | flops 51539607552 | bytes 11796480 | tf_op jit(solution)/shard_map/pull0/pallas_call | solution.py:346
  531.1 6.2 %end_back.1 = (bf16[512,1024]{1,0:T(8,128)(2,1)}, f32[8,1024]{1,0:T(8,128)}) custom-call(s32[8]{0:T(128)} %fusion.61.order_ref, bf16[512,1024]{1,0:T(8,128)(2,1)} %bitcast.8.source_ref.x_ref, f32[512,1024]{1,0:T(8,128)} %get-tuple-element.332.y_ref, f32[1,1024]{1,0:T(1,128)} %get-tuple-element.445.gain_ref, f32[512,1024]{1,0:T(8,128)} %pull0.1.refs_0_, ...), custom_call_target="tpu_custom_call" | custom-call | bytes 8425472 | tf_op jit(solution)/shard_map/end_back/pallas_call | solution.py:346
  537.3 12.8 %collective-permute-done.49 = bf16[32,8192]{1,0:T(8,128)(2,1)S(1)} collective-permute-done((bf16[32,8192]{1,0:T(8,128)(2,1)}, bf16[32,8192]{1,0:T(8,128)(2,1)S(1)}, u32[]{:S(2)}, u32[]{:S(2)}) %collective-permute-start.49) | collective-permute-done | bytes 524320 | tf_op jit(solution)/shard_map/ppermute | solution.py:283
  554.1 3.7 all-to-all-start
  558.0 7.0 %all-to-all-done = f32[32,1,128]{2,1,0:T(1,128)S(1)} async-done(((f32[32,1,128]{2,1,0:T(1,128)}), f32[32,1,128]{2,1,0:T(1,128)S(1)}, u32[]{:S(2)}, u32[]{:S(2)}) %all-to-all-start) | async-done | bytes 16416 | tf_op jit(solution)/shard_map/all_to_all | solution.py:296
  568.5 2.7 slice_reduce_fusion
  573.4 5.0 collective-permute-done.52
  (303 shorter events, 154.1 us)
Async XLA Ops:
  5.3 17.4 %collective-permute-start.2 = (bf16[32,3200]{1,0:T(8,128)(2,1)}, bf16[32,3200]{1,0:T(8,128)(2,1)S(1)}, u32[]{:S(2)}, u32[]{:S(2)}) collective-permute-start(bf16[32,3200]{1,0:T(8,128)(2,1)} %pad_maximum_fusion.8), channel_id=1, source_target_pairs={{0,3},{1,2},{2,1},{3,0},{4,7},{5,6},{6,5},{7,4},{8,11},{9,10},{10,... | collective-permute-start | bytes 614408 | tf_op jit(solution)/shard_map/ppermute | solution.py:195
  10.3 17.6 %collective-permute-start.1 = (bf16[32,3200]{1,0:T(8,128)(2,1)}, bf16[32,3200]{1,0:T(8,128)(2,1)S(1)}, u32[]{:S(2)}, u32[]{:S(2)}) collective-permute-start(bf16[32,3200]{1,0:T(8,128)(2,1)} %pad_maximum_fusion.8), channel_id=1, source_target_pairs={{0,2},{1,3},{2,0},{3,1},{4,6},{5,7},{6,4},{7,5},{8,10},{9,11},{10,... | collective-permute-start | bytes 614408 | tf_op jit(solution)/shard_map/ppermute | solution.py:195
  10.3 17.6 %collective-permute-start = (bf16[32,3200]{1,0:T(8,128)(2,1)}, bf16[32,3200]{1,0:T(8,128)(2,1)S(1)}, u32[]{:S(2)}, u32[]{:S(2)}) collective-permute-start(bf16[32,3200]{1,0:T(8,128)(2,1)} %pad_maximum_fusion.8), channel_id=1, source_target_pairs={{0,1},{1,0},{2,3},{3,2},{4,5},{5,4},{6,7},{7,6},{8,9},{9,8},{10,11... | collective-permute-start | bytes 614408 | tf_op jit(solution)/shard_map/ppermute | solution.py:195
  28.2 17.3 %collective-permute-start.3 = (bf16[128,3200]{1,0:T(8,128)(2,1)S(1)}, bf16[128,3200]{1,0:T(8,128)(2,1)S(1)}, u32[]{:S(2)}, u32[]{:S(2)}) collective-permute-start(bf16[128,3200]{1,0:T(8,128)(2,1)S(1)} %maximum_select_fusion.2), channel_id=1, source_target_pairs={{0,16},{1,17},{2,18},{3,19},{4,12},{5,13},{6,14},{7,15},{8,24},{9,... | collective-permute-start | bytes 2457608 | tf_op jit(solution)/shard_map/ppermute | solution.py:208
  31.3 14.2 %collective-permute-start.4 = (bf16[32,9216]{1,0:T(8,128)(2,1)S(1)}, bf16[32,9216]{1,0:T(8,128)(2,1)}, u32[]{:S(2)}, u32[]{:S(2)}) collective-permute-start(bf16[32,9216]{1,0:T(8,128)(2,1)S(1)} %pad_maximum_fusion.6), channel_id=1, source_target_pairs={{0,1},{1,0},{2,3},{3,2},{4,5},{5,4},{6,7},{7,6},{8,9},{9,8},{10,11... | collective-permute-start | bytes 1769480 | tf_op jit(solution)/shard_map/ppermute | solution.py:176
  45.6 18.9 %collective-permute-start.7 = (bf16[256,3200]{1,0:T(8,128)(2,1)S(1)}, bf16[256,3200]{1,0:T(8,128)(2,1)S(1)}, u32[]{:S(2)}, u32[]{:S(2)}) collective-permute-start(bf16[256,3200]{1,0:T(8,128)(2,1)S(1)} %pad_maximum_fusion.3.refs_0_.refs_4_.refs_1_.refs_2_), channel_id=1, source_target_pairs={{0,4},{1,5},{2,6},{3,7},{4,0},{5,1},{6,2},{7,3},{8,12},{9,13},{10,... | collective-permute-start | bytes 4915208 | tf_op jit(solution)/shard_map/ppermute | solution.py:210
  45.7 21.3 %collective-permute-start.6 = (bf16[256,3200]{1,0:T(8,128)(2,1)S(1)}, bf16[256,3200]{1,0:T(8,128)(2,1)}, u32[]{:S(2)}, u32[]{:S(2)}) collective-permute-start(bf16[256,3200]{1,0:T(8,128)(2,1)S(1)} %pad_maximum_fusion.3.refs_0_.refs_4_.refs_1_.refs_2_), channel_id=1, source_target_pairs={{0,8},{1,9},{2,10},{3,11},{4,20},{5,21},{6,22},{7,23},{8,0},{9,1},... | collective-permute-start | bytes 4915208 | tf_op jit(solution)/shard_map/ppermute | solution.py:210
  46.3 18.2 %collective-permute-start.8 = (bf16[32,9216]{1,0:T(8,128)(2,1)}, bf16[32,9216]{1,0:T(8,128)(2,1)}, u32[]{:S(2)}, u32[]{:S(2)}) collective-permute-start(bf16[32,9216]{1,0:T(8,128)(2,1)} %collective-permute-done.5), channel_id=1, source_target_pairs={{1,0},{2,3},{5,4},{6,7},{9,8},{10,11},{13,12},{14,15},{17,16},{18,... | collective-permute-start | bytes 1769480 | tf_op jit(solution)/shard_map/ppermute | solution.py:180
  47.6 16.9 %collective-permute-start.9 = (bf16[32,9216]{1,0:T(8,128)(2,1)}, bf16[32,9216]{1,0:T(8,128)(2,1)}, u32[]{:S(2)}, u32[]{:S(2)}) collective-permute-start(bf16[32,9216]{1,0:T(8,128)(2,1)} %collective-permute-done.4), channel_id=1, source_target_pairs={{1,2},{2,1},{5,6},{6,5},{9,10},{10,9},{13,14},{14,13},{17,18},{18,... | collective-permute-start | bytes 1769480 | tf_op jit(solution)/shard_map/ppermute | solution.py:180
  69.3 21.7 %collective-permute-start.11 = (bf16[32,9216]{1,0:T(8,128)(2,1)}, bf16[32,9216]{1,0:T(8,128)(2,1)}, u32[]{:S(2)}, u32[]{:S(2)}) collective-permute-start(bf16[32,9216]{1,0:T(8,128)(2,1)} %collective-permute-done.9), channel_id=1, source_target_pairs={{1,0},{2,3},{5,4},{6,7},{9,8},{10,11},{13,12},{14,15},{17,16},{18,... | collective-permute-start | bytes 1769480 | tf_op jit(solution)/shard_map/ppermute | solution.py:183
  70.6 36.6 %collective-permute-start.13 = (bf16[512,1024]{1,0:T(8,128)(2,1)}, bf16[512,1024]{1,0:T(8,128)(2,1)}, u32[]{:S(2)}, u32[]{:S(2)}) collective-permute-start(bf16[512,1024]{1,0:T(8,128)(2,1)} %bitcast.8.source_ref.x_ref), channel_id=1, source_target_pairs={{1,2},{2,1},{5,6},{6,5},{9,10},{10,9},{13,14},{14,13},{17,18},{18,... | collective-permute-start | bytes 3145736 | tf_op jit(solution)/shard_map/ppermute | solution.py:225
  72.3 37.5 %collective-permute-start.12 = (bf16[512,1024]{1,0:T(8,128)(2,1)}, bf16[512,1024]{1,0:T(8,128)(2,1)}, u32[]{:S(2)}, u32[]{:S(2)}) collective-permute-start(bf16[512,1024]{1,0:T(8,128)(2,1)} %bitcast.8.source_ref.x_ref), channel_id=1, source_target_pairs={{0,1},{1,0},{2,3},{3,2},{4,5},{5,4},{6,7},{7,6},{8,9},{9,8},{10,11... | collective-permute-start | bytes 3145736 | tf_op jit(solution)/shard_map/ppermute | solution.py:225
  93.5 29.0 %collective-permute-start.14 = (bf16[128,9216]{1,0:T(8,128)(2,1)S(1)}, bf16[128,9216]{1,0:T(8,128)(2,1)}, u32[]{:S(2)}, u32[]{:S(2)}) collective-permute-start(bf16[128,9216]{1,0:T(8,128)(2,1)S(1)} %maximum_select_fusion), channel_id=1, source_target_pairs={{0,16},{1,17},{2,18},{3,19},{4,12},{5,13},{6,14},{7,15},{8,24},{9,... | collective-permute-start | bytes 7077896 | tf_op jit(solution)/shard_map/ppermute | solution.py:208
  109.8 30.2 %collective-permute-start.16 = (bf16[512,1024]{1,0:T(8,128)(2,1)}, bf16[512,1024]{1,0:T(8,128)(2,1)S(1)}, u32[]{:S(2)}, u32[]{:S(2)}) collective-permute-start(bf16[512,1024]{1,0:T(8,128)(2,1)} %collective-permute-done.12.source_ref), channel_id=1, source_target_pairs={{1,2},{2,1},{5,6},{6,5},{9,10},{10,9},{13,14},{14,13},{17,18},{18,... | collective-permute-start | bytes 3145736 | tf_op jit(solution)/shard_map/ppermute | solution.py:230
  110.5 29.4 %collective-permute-start.15 = (bf16[512,1024]{1,0:T(8,128)(2,1)}, bf16[512,1024]{1,0:T(8,128)(2,1)}, u32[]{:S(2)}, u32[]{:S(2)}) collective-permute-start(bf16[512,1024]{1,0:T(8,128)(2,1)} %collective-permute-done.13), channel_id=1, source_target_pairs={{1,0},{2,3},{5,4},{6,7},{9,8},{10,11},{13,12},{14,15},{17,16},{18,... | collective-permute-start | bytes 3145736 | tf_op jit(solution)/shard_map/ppermute | solution.py:230
  126.7 59.8 %collective-permute-start.19 = (bf16[256,9216]{1,0:T(8,128)(2,1)}, bf16[256,9216]{1,0:T(8,128)(2,1)}, u32[]{:S(2)}, u32[]{:S(2)}) collective-permute-start(bf16[256,9216]{1,0:T(8,128)(2,1)} %pad_maximum_fusion.refs_0_), channel_id=1, source_target_pairs={{0,4},{1,5},{2,6},{3,7},{4,0},{5,1},{6,2},{7,3},{8,12},{9,13},{10,... | collective-permute-start | bytes 14155784 | tf_op jit(solution)/shard_map/ppermute | solution.py:210
  126.7 59.8 %collective-permute-start.18 = (bf16[256,9216]{1,0:T(8,128)(2,1)}, bf16[256,9216]{1,0:T(8,128)(2,1)}, u32[]{:S(2)}, u32[]{:S(2)}) collective-permute-start(bf16[256,9216]{1,0:T(8,128)(2,1)} %pad_maximum_fusion.refs_0_), channel_id=1, source_target_pairs={{0,8},{1,9},{2,10},{3,11},{4,20},{5,21},{6,22},{7,23},{8,0},{9,1},... | collective-permute-start | bytes 14155784 | tf_op jit(solution)/shard_map/ppermute | solution.py:210
  142.9 27.8 %collective-permute-start.17 = (bf16[512,1024]{1,0:T(8,128)(2,1)S(1)}, bf16[512,1024]{1,0:T(8,128)(2,1)S(1)}, u32[]{:S(2)}, u32[]{:S(2)}) collective-permute-start(bf16[512,1024]{1,0:T(8,128)(2,1)S(1)} %collective-permute-done.16), channel_id=1, source_target_pairs={{1,0},{2,3},{5,4},{6,7},{9,8},{10,11},{13,12},{14,15},{17,16},{18,... | collective-permute-start | bytes 3145736 | tf_op jit(solution)/shard_map/ppermute | solution.py:234
  170.7 29.3 %collective-permute-start.23 = (bf16[128,1024]{1,0:T(8,128)(2,1)S(1)}, bf16[128,1024]{1,0:T(8,128)(2,1)S(1)}, u32[]{:S(2)}, u32[]{:S(2)}) collective-permute-start(bf16[128,1024]{1,0:T(8,128)(2,1)S(1)} %copy-done.39), channel_id=1, source_target_pairs={{0,3},{1,2},{2,1},{3,0},{4,7},{5,6},{6,5},{7,4},{8,11},{9,10},{10,... | collective-permute-start | bytes 786440 | tf_op jit(solution)/shard_map/ppermute | solution.py:195
  173.0 27.0 %collective-permute-start.22 = (bf16[128,1024]{1,0:T(8,128)(2,1)S(1)}, bf16[128,1024]{1,0:T(8,128)(2,1)S(1)}, u32[]{:S(2)}, u32[]{:S(2)}) collective-permute-start(bf16[128,1024]{1,0:T(8,128)(2,1)S(1)} %copy-done.39), channel_id=1, source_target_pairs={{0,2},{1,3},{2,0},{3,1},{4,6},{5,7},{6,4},{7,5},{8,10},{9,11},{10,... | collective-permute-start | bytes 786440 | tf_op jit(solution)/shard_map/ppermute | solution.py:195
  173.0 27.0 %collective-permute-start.21 = (bf16[128,1024]{1,0:T(8,128)(2,1)S(1)}, bf16[128,1024]{1,0:T(8,128)(2,1)S(1)}, u32[]{:S(2)}, u32[]{:S(2)}) collective-permute-start(bf16[128,1024]{1,0:T(8,128)(2,1)S(1)} %copy-done.39), channel_id=1, source_target_pairs={{0,1},{1,0},{2,3},{3,2},{4,5},{5,4},{6,7},{7,6},{8,9},{9,8},{10,11... | collective-permute-start | bytes 786440 | tf_op jit(solution)/shard_map/ppermute | solution.py:195
  186.5 13.5 %collective-permute-start.20 = (bf16[256,9216]{1,0:T(8,128)(2,1)}, bf16[256,9216]{1,0:T(8,128)(2,1)}, u32[]{:S(2)}, u32[]{:S(2)}) collective-permute-start(bf16[256,9216]{1,0:T(8,128)(2,1)} %collective-permute-done.18.refs_1_), channel_id=1, source_target_pairs={{0,4},{1,5},{2,6},{3,7},{4,0},{5,1},{6,2},{7,3},{8,12},{9,13},{10,... | collective-permute-start | bytes 14155784 | tf_op jit(solution)/shard_map/ppermute | solution.py:211
  200.8 14.9 %collective-permute-start.24 = (bf16[512,1024]{1,0:T(8,128)(2,1)S(1)}, bf16[512,1024]{1,0:T(8,128)(2,1)S(1)}, u32[]{:S(2)}, u32[]{:S(2)}) collective-permute-start(bf16[512,1024]{1,0:T(8,128)(2,1)S(1)} %maximum_select_fusion.1), channel_id=1, source_target_pairs={{0,16},{1,17},{2,18},{3,19},{4,12},{5,13},{6,14},{7,15},{8,24},{9,... | collective-permute-start | bytes 3145736 | tf_op jit(solution)/shard_map/ppermute | solution.py:208
  218.1 26.0 %collective-permute-start.26 = (bf16[1024,1024]{1,0:T(8,128)(2,1)S(1)}, bf16[1024,1024]{1,0:T(8,128)(2,1)}, u32[]{:S(2)}, u32[]{:S(2)}) collective-permute-start(bf16[1024,1024]{1,0:T(8,128)(2,1)S(1)} %pad_maximum_fusion.2.refs_4_), channel_id=1, source_target_pairs={{0,4},{1,5},{2,6},{3,7},{4,0},{5,1},{6,2},{7,3},{8,12},{9,13},{10,... | collective-permute-start | bytes 6291464 | tf_op jit(solution)/shard_map/ppermute | solution.py:210
  218.1 26.2 %collective-permute-start.25 = (bf16[1024,1024]{1,0:T(8,128)(2,1)S(1)}, bf16[1024,1024]{1,0:T(8,128)(2,1)}, u32[]{:S(2)}, u32[]{:S(2)}) collective-permute-start(bf16[1024,1024]{1,0:T(8,128)(2,1)S(1)} %pad_maximum_fusion.2.refs_4_), channel_id=1, source_target_pairs={{0,8},{1,9},{2,10},{3,11},{4,20},{5,21},{6,22},{7,23},{8,0},{9,1},... | collective-permute-start | bytes 6291464 | tf_op jit(solution)/shard_map/ppermute | solution.py:210
  248.7 35.1 %collective-permute-start.28 = (bf16[2048,1024]{1,0:T(8,128)(2,1)}, bf16[2048,1024]{1,0:T(8,128)(2,1)}, u32[]{:S(2)}, u32[]{:S(2)}) collective-permute-start(bf16[2048,1024]{1,0:T(8,128)(2,1)} %convolution_convert_fusion.1), channel_id=1, source_target_pairs={{0,4},{1,5},{2,6},{3,7},{4,0},{5,1},{6,2},{7,3},{8,12},{9,13},{10,... | collective-permute-start | bytes 12582920 | tf_op jit(solution)/shard_map/ppermute | solution.py:263
  299.9 13.5 %collective-permute-start.29 = (bf16[512,8192]{1,0:T(8,128)(2,1)}, bf16[512,8192]{1,0:T(8,128)(2,1)}, u32[]{:S(2)}, u32[]{:S(2)}) collective-permute-start(bf16[512,8192]{1,0:T(8,128)(2,1)} %convolution_convert_fusion), channel_id=1, source_target_pairs={{0,4},{1,5},{2,6},{3,7},{4,0},{5,1},{6,2},{7,3},{8,12},{9,13},{10,... | collective-permute-start | bytes 25165832 | tf_op jit(solution)/shard_map/ppermute | solution.py:263
  301.9 47.0 %collective-permute-start.30 = (bf16[1024,1024]{1,0:T(8,128)(2,1)}, bf16[1024,1024]{1,0:T(8,128)(2,1)S(1)}, u32[]{:S(2)}, u32[]{:S(2)}) collective-permute-start(bf16[1024,1024]{1,0:T(8,128)(2,1)} %add_convert_fusion.7), channel_id=1, source_target_pairs={{0,8},{1,9},{2,10},{3,11},{4,20},{5,21},{6,22},{7,23},{8,0},{9,1},... | collective-permute-start | bytes 6291464 | tf_op jit(solution)/shard_map/ppermute | solution.py:267
  322.5 63.3 %collective-permute-start.32 = (bf16[256,8192]{1,0:T(8,128)(2,1)}, bf16[256,8192]{1,0:T(8,128)(2,1)}, u32[]{:S(2)}, u32[]{:S(2)}) collective-permute-start(bf16[256,8192]{1,0:T(8,128)(2,1)} %add_convert_fusion.2), channel_id=1, source_target_pairs={{0,8},{1,9},{2,10},{3,11},{4,20},{5,21},{6,22},{7,23},{8,0},{9,1},... | collective-permute-start | bytes 12582920 | tf_op jit(solution)/shard_map/ppermute | solution.py:267
  325.6 23.3 %collective-permute-start.31 = (bf16[512,1024]{1,0:T(8,128)(2,1)}, bf16[512,1024]{1,0:T(8,128)(2,1)}, u32[]{:S(2)}, u32[]{:S(2)}) collective-permute-start(bf16[512,1024]{1,0:T(8,128)(2,1)} %convolution_convert_fusion.3), channel_id=1, source_target_pairs={{0,4},{1,5},{2,6},{3,7},{4,0},{5,1},{6,2},{7,3},{8,12},{9,13},{10,... | collective-permute-start | bytes 3145736 | tf_op jit(solution)/shard_map/ppermute | solution.py:263
  352.0 59.2 %collective-permute-start.35 = (bf16[256,1024]{1,0:T(8,128)(2,1)}, bf16[256,1024]{1,0:T(8,128)(2,1)}, u32[]{:S(2)}, u32[]{:S(2)}) collective-permute-start(bf16[256,1024]{1,0:T(8,128)(2,1)} %add_convert_fusion.18), channel_id=1, source_target_pairs={{0,8},{1,9},{2,10},{3,11},{4,20},{5,21},{6,22},{7,23},{8,0},{9,1},... | collective-permute-start | bytes 1572872 | tf_op jit(solution)/shard_map/ppermute | solution.py:267
  356.2 55.0 %collective-permute-start.34 = (bf16[512,1024]{1,0:T(8,128)(2,1)}, bf16[512,1024]{1,0:T(8,128)(2,1)}, u32[]{:S(2)}, u32[]{:S(2)}) collective-permute-start(bf16[512,1024]{1,0:T(8,128)(2,1)} %slice.241), channel_id=1, source_target_pairs={{0,16},{1,17},{2,18},{3,19},{4,12},{5,13},{6,14},{7,15},{8,24},{9,... | collective-permute-start | bytes 3145736 | tf_op jit(solution)/shard_map/ppermute | solution.py:274
  367.2 26.9 %collective-permute-start.33 = (bf16[512,1024]{1,0:T(8,128)(2,1)}, bf16[512,1024]{1,0:T(8,128)(2,1)S(1)}, u32[]{:S(2)}, u32[]{:S(2)}) collective-permute-start(bf16[512,1024]{1,0:T(8,128)(2,1)} %pull3.1), channel_id=1, source_target_pairs={{0,1},{3,2},{4,5},{7,6},{8,9},{11,10},{12,13},{15,14},{16,17},{19,... | collective-permute-start | bytes 3145736 | tf_op jit(solution)/shard_map/ppermute | solution.py:239
  393.5 42.6 %collective-permute-start.36 = (bf16[128,8192]{1,0:T(8,128)(2,1)}, bf16[128,8192]{1,0:T(8,128)(2,1)}, u32[]{:S(2)}, u32[]{:S(2)}) collective-permute-start(bf16[128,8192]{1,0:T(8,128)(2,1)} %slice.242), channel_id=1, source_target_pairs={{0,16},{1,17},{2,18},{3,19},{4,12},{5,13},{6,14},{7,15},{8,24},{9,... | collective-permute-start | bytes 6291464 | tf_op jit(solution)/shard_map/ppermute | solution.py:274
  404.9 37.1 %collective-permute-start.38 = (bf16[512,1024]{1,0:T(8,128)(2,1)}, bf16[512,1024]{1,0:T(8,128)(2,1)}, u32[]{:S(2)}, u32[]{:S(2)}) collective-permute-start(bf16[512,1024]{1,0:T(8,128)(2,1)} %add_convert_fusion.14), channel_id=1, source_target_pairs={{1,2},{2,1},{5,6},{6,5},{9,10},{10,9},{13,14},{14,13},{17,18},{18,... | collective-permute-start | bytes 3145736 | tf_op jit(solution)/shard_map/ppermute | solution.py:242
  406.6 35.4 %collective-permute-start.37 = (bf16[512,1024]{1,0:T(8,128)(2,1)}, bf16[512,1024]{1,0:T(8,128)(2,1)}, u32[]{:S(2)}, u32[]{:S(2)}) collective-permute-start(bf16[512,1024]{1,0:T(8,128)(2,1)} %pull2.1), channel_id=1, source_target_pairs={{0,1},{3,2},{4,5},{7,6},{8,9},{11,10},{12,13},{15,14},{16,17},{19,... | collective-permute-start | bytes 3145736 | tf_op jit(solution)/shard_map/ppermute | solution.py:242
  413.2 41.4 %collective-permute-start.40 = (bf16[128,1024]{1,0:T(8,128)(2,1)}, bf16[128,1024]{1,0:T(8,128)(2,1)S(1)}, u32[]{:S(2)}, u32[]{:S(2)}) collective-permute-start(bf16[128,1024]{1,0:T(8,128)(2,1)} %slice.244), channel_id=1, source_target_pairs={{0,16},{1,17},{2,18},{3,19},{4,12},{5,13},{6,14},{7,15},{8,24},{9,... | collective-permute-start | bytes 786440 | tf_op jit(solution)/shard_map/ppermute | solution.py:274
  415.9 38.8 %collective-permute-start.39 = (bf16[256,1024]{1,0:T(8,128)(2,1)S(1)}, bf16[256,1024]{1,0:T(8,128)(2,1)S(1)}, u32[]{:S(2)}, u32[]{:S(2)}) collective-permute-start(bf16[256,1024]{1,0:T(8,128)(2,1)S(1)} %bitcast.142), channel_id=1, source_target_pairs={{0,1},{1,0},{2,3},{3,2},{4,5},{5,4},{6,7},{7,6},{8,9},{9,8},{10,11... | collective-permute-start | bytes 1572872 | tf_op jit(solution)/shard_map/ppermute | solution.py:283
  440.0 43.7 %collective-permute-start.43 = (bf16[64,8192]{1,0:T(8,128)(2,1)}, bf16[64,8192]{1,0:T(8,128)(2,1)}, u32[]{:S(2)}, u32[]{:S(2)}) collective-permute-start(bf16[64,8192]{1,0:T(8,128)(2,1)} %bitcast.19), channel_id=1, source_target_pairs={{0,1},{1,0},{2,3},{3,2},{4,5},{5,4},{6,7},{7,6},{8,9},{9,8},{10,11... | collective-permute-start | bytes 3145736 | tf_op jit(solution)/shard_map/ppermute | solution.py:283
  455.4 28.2 %collective-permute-start.42 = (bf16[64,1024]{1,0:T(8,128)(2,1)}, bf16[64,1024]{1,0:T(8,128)(2,1)}, u32[]{:S(2)}, u32[]{:S(2)}) collective-permute-start(bf16[64,1024]{1,0:T(8,128)(2,1)} %bitcast.24), channel_id=1, source_target_pairs={{0,1},{1,0},{2,3},{3,2},{4,5},{5,4},{6,7},{7,6},{8,9},{9,8},{10,11... | collective-permute-start | bytes 393224 | tf_op jit(solution)/shard_map/ppermute | solution.py:283
  456.5 27.2 %collective-permute-start.41 = (bf16[128,1024]{1,0:T(8,128)(2,1)S(1)}, bf16[128,1024]{1,0:T(8,128)(2,1)}, u32[]{:S(2)}, u32[]{:S(2)}) collective-permute-start(bf16[128,1024]{1,0:T(8,128)(2,1)S(1)} %dynamic-slice_bitcast_fusion.1), channel_id=1, source_target_pairs={{0,2},{1,3},{2,0},{3,1},{4,6},{5,7},{6,4},{7,5},{8,10},{9,11},{10,... | collective-permute-start | bytes 786440 | tf_op jit(solution)/shard_map/ppermute | solution.py:283
  484.6 13.7 %collective-permute-start.44 = (bf16[512,3072]{1,0:T(8,128)(2,1)S(1)}, bf16[512,3072]{1,0:T(8,128)(2,1)S(1)}, u32[]{:S(2)}, u32[]{:S(2)}) collective-permute-start(bf16[512,3072]{1,0:T(8,128)(2,1)S(1)} %pad_maximum_fusion.1), channel_id=1, source_target_pairs={{0,4},{1,5},{2,6},{3,7},{4,0},{5,1},{6,2},{7,3},{8,12},{9,13},{10,... | collective-permute-start | bytes 9437192 | tf_op jit(solution)/shard_map/ppermute | solution.py:263
  484.7 30.9 %collective-permute-start.46 = (bf16[512,1024]{1,0:T(8,128)(2,1)}, bf16[512,1024]{1,0:T(8,128)(2,1)}, u32[]{:S(2)}, u32[]{:S(2)}) collective-permute-start(bf16[512,1024]{1,0:T(8,128)(2,1)} %add_convert_fusion.12), channel_id=1, source_target_pairs={{1,2},{2,1},{5,6},{6,5},{9,10},{10,9},{13,14},{14,13},{17,18},{18,... | collective-permute-start | bytes 3145736 | tf_op jit(solution)/shard_map/ppermute | solution.py:249
  486.5 29.1 %collective-permute-start.47 = (bf16[512,1024]{1,0:T(8,128)(2,1)}, bf16[512,1024]{1,0:T(8,128)(2,1)}, u32[]{:S(2)}, u32[]{:S(2)}) collective-permute-start(bf16[512,1024]{1,0:T(8,128)(2,1)} %add_convert_fusion.11), channel_id=1, source_target_pairs={{0,1},{1,0},{2,3},{3,2},{4,5},{5,4},{6,7},{7,6},{8,9},{9,8},{10,11... | collective-permute-start | bytes 3145736 | tf_op jit(solution)/shard_map/ppermute | solution.py:250
  497.1 18.5 %collective-permute-start.45 = (bf16[32,1024]{1,0:T(8,128)(2,1)S(1)}, bf16[32,1024]{1,0:T(8,128)(2,1)S(1)}, u32[]{:S(2)}, u32[]{:S(2)}) collective-permute-start(bf16[32,1024]{1,0:T(8,128)(2,1)S(1)} %dynamic-slice_bitcast_fusion.3), channel_id=1, source_target_pairs={{0,2},{1,3},{2,0},{3,1},{4,6},{5,7},{6,4},{7,5},{8,10},{9,11},{10,... | collective-permute-start | bytes 196616 | tf_op jit(solution)/shard_map/ppermute | solution.py:283
  501.3 20.7 %collective-permute-start.48 = (bf16[256,3072]{1,0:T(8,128)(2,1)}, bf16[256,3072]{1,0:T(8,128)(2,1)}, u32[]{:S(2)}, u32[]{:S(2)}) collective-permute-start(bf16[256,3072]{1,0:T(8,128)(2,1)} %pad_maximum_fusion.4), channel_id=1, source_target_pairs={{0,8},{1,9},{2,10},{3,11},{4,20},{5,21},{6,22},{7,23},{8,0},{9,1},... | collective-permute-start | bytes 4718600 | tf_op jit(solution)/shard_map/ppermute | solution.py:267
  524.1 26.8 %collective-permute-start.50 = (bf16[128,3072]{1,0:T(8,128)(2,1)S(1)}, bf16[128,3072]{1,0:T(8,128)(2,1)}, u32[]{:S(2)}, u32[]{:S(2)}) collective-permute-start(bf16[128,3072]{1,0:T(8,128)(2,1)S(1)} %slice.247), channel_id=1, source_target_pairs={{0,16},{1,17},{2,18},{3,19},{4,12},{5,13},{6,14},{7,15},{8,24},{9,... | collective-permute-start | bytes 2359304 | tf_op jit(solution)/shard_map/ppermute | solution.py:274
  525.3 24.8 %collective-permute-start.49 = (bf16[32,8192]{1,0:T(8,128)(2,1)}, bf16[32,8192]{1,0:T(8,128)(2,1)S(1)}, u32[]{:S(2)}, u32[]{:S(2)}) collective-permute-start(bf16[32,8192]{1,0:T(8,128)(2,1)} %dynamic-slice_bitcast_fusion), channel_id=1, source_target_pairs={{0,2},{1,3},{2,0},{3,1},{4,6},{5,7},{6,4},{7,5},{8,10},{9,11},{10,... | collective-permute-start | bytes 1572872 | tf_op jit(solution)/shard_map/ppermute | solution.py:283
  (59 other events, 447.9 us)

commit v7 on v6

--- a/solution.py
+++ b/solution.py
@@ -1055,10 +1055,11 @@
     )
     output = output.reshape(windows, local_len, width)
 
-    two_grads, pair_grads = step((two_grads, pair_grads), down_sum)
-    two_grads, pair_sum = begin(
-        two_grads, sum_steps(plan, product_of(plan, [[(in_slots(two_flipped), pair_grads)]]))
-    )
+    product = product_of(plan, [[(in_slots(two_flipped), pair_grads)]])
+    first = product(plan.dp // 2, plan.dp)
+    first, two_grads = wait((first, two_grads), down_sum)
+    two_grads, pair_sum = begin(two_grads, sum_steps(plan, product, first))
+    two_grads = go_on(two_grads, down_sum)
     y_grads, low_grads, go, edge_two = middle_back(
         order, two_grads, resid, upstream, pair_w, natural[2]
     )

time: 591 us -> 591 us (level)
    unnamed x111 -> x113, local copies, waits for them, and re-layouts: 15 us -> 15 us
  transfers between devices with their start and end apart: 54 -> 54, of which waited for: 15 -> 14; matrix products, arithmetic and copies ran while one was open for 21% -> 24% of each run, Pallas kernels for 46% -> 46%
where the time goes in v7:
time: 591 us; the launch traced here: 581 us
  Pallas kernels  266 us (45%)
  waiting for transfers between devices  80.7 us (14%)
  matrix products  67.8 us (11%)
  starting transfers between devices  66 us (11%)
  other arithmetic  62.7 us (11%)
  local copies, waits for them, and re-layouts  35.6 us (6%)
    pallas_call x21, Pallas kernels, call(): pl.pallas_call(body, out_shape=out_shape, grid_spec=pltpu.PrefetchScalarG...  266 us
    dot_general x24, matrix products, product(): found = found + jnp.dot(part, right, preferred_element_type=jnp.float32)  67.8 us
    convert_element_type x15, other arithmetic, add(): return (a.astype(jnp.float32) + b.astype(jnp.float32)).astype(BF)  28.7 us
    ppermute x8, waiting for transfers between devices, sum_steps(): other, = (yield ([lax.ppermute(send, AXES, plan.across[1 << bit])], [send]))  18.2 us
    unnamed x113, local copies, waits for them, and re-layouts  15 us
    ppermute x1, waiting for transfers between devices, gather_steps(): lax.ppermute(shard, AXES, plan.across[1])  13.5 us
    ppermute x1, waiting for transfers between devices, gather_steps(): lax.ppermute(middle, AXES, plan.outward)  13 us
  transfers between devices with their start and end apart: 54, of which 14 were waited for; matrix products, arithmetic and copies ran while one was open for 24% of the time, Pallas kernels for 46%

profile of v7, /device:TPU:0, one launch (start us, length us, event | category | flops | bytes accessed | tf_op | source)
XLA Modules:
  0.0 581.4 jit_solution(10026212271791823328)
XLA Ops:
  5.3 5.1 collective-permute-start.2
  15.9 5.6 multiply_sine_fusion
  22.6 5.3 collective-permute-done.1
  32.0 13.5 %collective-permute-done.4 = bf16[32,9216]{1,0:T(8,128)(2,1)} collective-permute-done((bf16[32,9216]{1,0:T(8,128)(2,1)S(1)}, bf16[32,9216]{1,0:T(8,128)(2,1)}, u32[]{:S(2)}, u32[]{:S(2)}) %collective-permute-start.4) | collective-permute-done | bytes 589856 | tf_op jit(solution)/shard_map/ppermute | solution.py:176
  51.5 13.0 %collective-permute-done.8 = bf16[32,9216]{1,0:T(8,128)(2,1)} collective-permute-done((bf16[32,9216]{1,0:T(8,128)(2,1)}, bf16[32,9216]{1,0:T(8,128)(2,1)}, u32[]{:S(2)}, u32[]{:S(2)}) %collective-permute-start.8) | collective-permute-done | bytes 589856 | tf_op jit(solution)/shard_map/ppermute | solution.py:180
  72.3 5.5 collective-permute-start.12
  77.7 13.3 %project0.1 = (bf16[1024,512]{1,0:T(8,128)(2,1)}, bf16[512,1024]{1,0:T(8,128)(2,1)}, bf16[512,2048]{1,0:T(8,128)(2,1)}, f32[8,1024]{1,0:T(8,128)}) custom-call(s32[8]{0:T(128)} %fusion.55.order_ref, bf16[512,1024]{1,0:T(8,128)(2,1)} %bitcast.8.source_ref.x_ref, f32[2048,128]{1,0:T(8,128)} %get-tuple-element.243.cos_ref, ...), custom_call_target="tpu_custom_call" | custom-call | flops 51539607552 | bytes 20480000 | tf_op jit(solution)/shard_map/project0/pallas_call | solution.py:346
  94.8 12.5 %attend0.1 = (f32[8,8,512]{2,1,0:T(8,128)}, f32[1024,512]{1,0:T(8,128)}) custom-call(s32[8]{0:T(128)} %fusion.55.order_ref, s32[4]{0:T(128)} %subtract_clamp_fusion.valid_ref, bf16[512,1024]{1,0:T(8,128)(2,1)} %get-tuple-element.247.q_ref, bf16[512,2048]{1,0:T(8,128)(2,1)} %get-tuple-element.252.kv_ref), custom_call_target="tpu_custom_call" | custom-call | flops 68719476736 | bytes 5373968 | tf_op jit(solution)/shard_map/attend0/pallas_call | solution.py:346
  112.0 10.0 %project1.1 = (bf16[1024,512]{1,0:T(8,128)(2,1)}, bf16[512,2048]{1,0:T(8,128)(2,1)}) custom-call(s32[8]{0:T(128)} %fusion.55.order_ref, bf16[512,1024]{1,0:T(8,128)(2,1)} %collective-permute-done.12.source_ref, f32[2048,128]{1,0:T(8,128)} %get-tuple-element.243.cos_ref, f32[2048,128]{1,0:T(8,128)} %get-tuple-element.244.sin_ref, ...), custom_call_target="tpu_custom_call" | custom-call | flops 34359738368 | bytes 12877824 | tf_op jit(solution)/shard_map/project1/pallas_call | solution.py:346
  122.6 4.2 pad_maximum_fusion.refs_0_
  127.3 12.7 %attend1.1 = (f32[8,8,512]{2,1,0:T(8,128)}, f32[1024,512]{1,0:T(8,128)}) custom-call(s32[8]{0:T(128)} %fusion.55.order_ref, s32[4]{0:T(128)} %subtract_clamp_fusion.valid_ref, bf16[512,1024]{1,0:T(8,128)(2,1)} %get-tuple-element.247.q_ref, bf16[512,2048]{1,0:T(8,128)(2,1)} %get-tuple-element.260.kv_ref, f32[8,8,512]{2,1,0:T(8,128)} %get-tuple-element.264.refs_0_, ...), custom_call_target="tpu_custom_call" | custom-call | flops 68719476736 | bytes 7602192 | tf_op jit(solution)/shard_map/attend1/pallas_call | solution.py:346
  140.0 2.9 add.233.source_ref
  144.2 10.0 %project2.1 = (bf16[1024,512]{1,0:T(8,128)(2,1)}, bf16[512,2048]{1,0:T(8,128)(2,1)}) custom-call(s32[8]{0:T(128)} %fusion.55.order_ref, bf16[512,1024]{1,0:T(8,128)(2,1)} %add.233.source_ref, f32[2048,128]{1,0:T(8,128)} %get-tuple-element.243.cos_ref, f32[2048,128]{1,0:T(8,128)} %get-tuple-element.244.sin_ref, bf16[256,3200]{1,0:T(8,128)(2,1)} %copy-done.5, ...), custom_call_target="tpu_custom_call" | custom-call | flops 34359738368 | bytes 12877824 | tf_op jit(solution)/shard_map/project2/pallas_call | solution.py:346
  154.1 12.8 %attend2.1 = (f32[8,8,512]{2,1,0:T(8,128)}, f32[1024,512]{1,0:T(8,128)}) custom-call(s32[8]{0:T(128)} %fusion.55.order_ref, s32[4]{0:T(128)} %subtract_clamp_fusion.valid_ref, bf16[512,1024]{1,0:T(8,128)(2,1)} %get-tuple-element.247.q_ref, bf16[512,2048]{1,0:T(8,128)(2,1)} %get-tuple-element.270.kv_ref, f32[8,8,512]{2,1,0:T(8,128)} %get-tuple-element.273.refs_0_, ...), custom_call_target="tpu_custom_call" | custom-call | flops 68719476736 | bytes 7602192 | tf_op jit(solution)/shard_map/attend2/pallas_call | solution.py:346
  166.9 3.8 collective-permute-done.17
  176.5 9.9 %project3.1 = (bf16[1024,512]{1,0:T(8,128)(2,1)}, bf16[512,2048]{1,0:T(8,128)(2,1)}) custom-call(s32[8]{0:T(128)} %fusion.55.order_ref, bf16[512,1024]{1,0:T(8,128)(2,1)} %add.234.source_ref, f32[2048,128]{1,0:T(8,128)} %get-tuple-element.243.cos_ref, f32[2048,128]{1,0:T(8,128)} %get-tuple-element.244.sin_ref, bf16[256,3200]{1,0:T(8,128)(2,1)} %copy-done.5, ...), custom_call_target="tpu_custom_call" | custom-call | flops 34359738368 | bytes 12877824 | tf_op jit(solution)/shard_map/project3/pallas_call | solution.py:346
  186.5 13.4 %attend3.1 = (bf16[512,1024]{1,0:T(8,128)(2,1)}, bf16[1024,512]{1,0:T(8,128)(2,1)}, f32[512,1024]{1,0:T(8,128)}, f32[8,8,512]{2,1,0:T(8,128)}) custom-call(s32[8]{0:T(128)} %fusion.55.order_ref, s32[4]{0:T(128)} %subtract_clamp_fusion.valid_ref, bf16[512,1024]{1,0:T(8,128)(2,1)} %get-tuple-element.247.q_ref, bf16[512,2048]{1,0:T(8,128)(2,1)} %get-tuple-element.281.kv_ref, ...), custom_call_target="tpu_custom_call" | custom-call | flops 68719476736 | bytes 9699344 | tf_op jit(solution)/shard_map/attend3/pallas_call | solution.py:346
  202.3 6.2 %middle.1 = (f32[512,1024]{1,0:T(8,128)}, bf16[512,1024]{1,0:T(8,128)(2,1)}, bf16[1024,512]{1,0:T(8,128)(2,1)}) custom-call(s32[8]{0:T(128)} %fusion.55.order_ref, bf16[512,1024]{1,0:T(8,128)(2,1)} %get-tuple-element.300.o_ref, bf16[512,1024]{1,0:T(8,128)(2,1)} %bitcast.8.source_ref.x_ref, f32[8,1024]{1,0:T(8,128)} %get-tuple-element.256.refs_4_.cols_ref, ...), custom_call_target="tpu_custom_call" | custom-call | flops 1073741824 | bytes 25198592 | tf_op jit(solution)/shard_map/middle/pallas_call | solution.py:346
  208.4 7.1 %collective-permute-done.24 = bf16[512,1024]{1,0:T(8,128)(2,1)S(1)} collective-permute-done((bf16[512,1024]{1,0:T(8,128)(2,1)S(1)}, bf16[512,1024]{1,0:T(8,128)(2,1)S(1)}, u32[]{:S(2)}, u32[]{:S(2)}) %collective-permute-start.24) | collective-permute-done | bytes 1048608 | tf_op jit(solution)/shard_map/ppermute | solution.py:208
  219.6 18.5 %feed.1 = (bf16[512,4096]{1,0:T(8,128)(2,1)}, bf16[512,4096]{1,0:T(8,128)(2,1)}, bf16[512,4096]{1,0:T(8,128)(2,1)}, bf16[4096,512]{1,0:T(8,128)(2,1)}) custom-call(s32[8]{0:T(128)} %fusion.55.order_ref, bf16[512,1024]{1,0:T(8,128)(2,1)} %get-tuple-element.306.two_ref, bf16[256,9216]{1,0:T(8,128)(2,1)} %pad_maximum_fusion.refs_0_, ...), custom_call_target="tpu_custom_call" | custom-call | flops 8589934592 | bytes 36700160 | tf_op jit(solution)/shard_map/feed/pallas_call | solution.py:346
  238.1 5.9 %convolution_convert_fusion.1 = bf16[2048,1024]{1,0:T(8,128)(2,1)} fusion(bf16[512,1024]{1,0:T(8,128)(2,1)S(1)} %copy-done.13, bf16[4096,512]{1,0:T(8,128)(2,1)} %get-tuple-element.310), kind=kOutput, calls=%fused_computation.11 | convolution fusion | flops 2149580800 | bytes 7340032 | tf_op jit(solution)/shard_map/dot_general | solution.py:328
  244.3 4.4 collective-permute-done.27.refs_7_
  250.0 33.7 %feed_back.1 = (bf16[512,1024]{1,0:T(8,128)(2,1)}, bf16[512,8192]{1,0:T(8,128)(2,1)}, f32[512,1024]{1,0:T(8,128)}) custom-call(s32[8]{0:T(128)} %fusion.55.order_ref, bf16[512,1024]{1,0:T(8,128)(2,1)} %bitcast_select_fusion.m_ref, bf16[512,4096]{1,0:T(8,128)(2,1)} %get-tuple-element.307.gate_ref, bf16[512,4096]{1,0:T(8,128)(2,1)} %get-tuple-element.308.up_ref, ...), custom_call_target="tpu_custom_call" | custom-call | flops 17179869184 | bytes 54525952 | tf_op jit(solution)/shard_map/feed_back/pallas_call | solution.py:346
  283.7 10.2 %convolution_convert_fusion = bf16[512,8192]{1,0:T(8,128)(2,1)} fusion(bf16[512,8192]{1,0:T(8,128)(2,1)} %get-tuple-element.324, bf16[1024,512]{1,0:T(8,128)(2,1)S(1)} %copy-done.44), kind=kOutput, calls=%fused_computation.1 | convolution fusion | flops 4299161600 | bytes 17301504 | tf_op jit(solution)/shard_map/dot_general | solution.py:328
  295.9 4.5 add_convert_fusion.7
  301.9 4.5 add_convert_fusion.6
  306.4 7.5 %middle_back.1 = (f32[512,1024]{1,0:T(8,128)}, bf16[512,1024]{1,0:T(8,128)(2,1)}, bf16[512,1024]{1,0:T(8,128)(2,1)}, f32[8,1024]{1,0:T(8,128)}) custom-call(s32[8]{0:T(128)} %fusion.55.order_ref, f32[512,1024]{1,0:T(8,128)} %get-tuple-element.333.grads_ref, f32[512,1024]{1,0:T(8,128)} %get-tuple-element.319.resid_ref, ...), custom_call_target="tpu_custom_call" | custom-call | flops 1073741824 | bytes 28348416 | tf_op jit(solution)/shard_map/middle_back/pallas_call | solution.py:346
  314.0 9.1 %add_convert_fusion.2 = bf16[256,8192]{1,0:T(8,128)(2,1)} fusion(bf16[512,8192]{1,0:T(8,128)(2,1)} %collective-permute-done.29, bf16[512,8192]{1,0:T(8,128)(2,1)} %get-tuple-element.324, bf16[1024,512]{1,0:T(8,128)(2,1)S(1)} %copy-done.45), kind=kOutput, calls=%fused_computation.4 | convolution fusion | flops 2153775104 | bytes 17039360 | tf_op jit(solution)/shard_map/dot_general | solution.py:328
  325.3 6.8 %add_convert_fusion.1 = bf16[256,8192]{1,0:T(8,128)(2,1)} fusion(bf16[512,8192]{1,0:T(8,128)(2,1)} %collective-permute-done.29, bf16[512,8192]{1,0:T(8,128)(2,1)S(1)} %bitcast.156, bf16[1024,512]{1,0:T(8,128)(2,1)S(1)} %copy-done.45), kind=kOutput, calls=%fused_computation.3 | convolution fusion | flops 2153775104 | bytes 17039360 | tf_op jit(solution)/shard_map/dot_general | solution.py:328
  332.1 16.5 %attend_back3.1 = (f32[1024,512]{1,0:T(8,128)}, bf16[512,2048]{1,0:T(8,128)(2,1)}) custom-call(s32[8]{0:T(128)} %fusion.55.order_ref, s32[4]{0:T(128)} %subtract_clamp_fusion.valid_ref, bf16[512,1024]{1,0:T(8,128)(2,1)} %get-tuple-element.247.q_ref, bf16[512,2048]{1,0:T(8,128)(2,1)} %get-tuple-element.281.kv_ref, ...), custom_call_target="tpu_custom_call" | custom-call | flops 10737418240 | bytes 12714000 | tf_op jit(solution)/shard_map/attend_back3/pallas_call | solution.py:346
  348.6 3.1 add_convert_fusion.18
  359.8 7.0 %pull3.1 = bf16[512,1024]{1,0:T(8,128)(2,1)} custom-call(s32[8]{0:T(128)} %fusion.55.order_ref, bf16[512,2048]{1,0:T(8,128)(2,1)} %get-tuple-element.351.refs_0_, bf16[256,3200]{1,0:T(8,128)(2,1)} %copy-done.5, bf16[256,3200]{1,0:T(8,128)(2,1)} %collective-permute-done.6.refs_1_.refs_5_.refs_2_.refs_3_, bf16[256,3200]{1,0:T(8,128)(2,1)} %copy-done.9, ...), custom_call_target="tpu_custom_call" | custom-call | flops 524288 | bytes 9699328 | tf_op jit(solution)/shard_map/pull3/pallas_call | solution.py:346
  368.8 16.7 %attend_back2.1 = (f32[1024,512]{1,0:T(8,128)}, bf16[512,2048]{1,0:T(8,128)(2,1)}) custom-call(s32[8]{0:T(128)} %fusion.55.order_ref, s32[4]{0:T(128)} %subtract_clamp_fusion.valid_ref, bf16[512,1024]{1,0:T(8,128)(2,1)} %get-tuple-element.247.q_ref, bf16[512,2048]{1,0:T(8,128)(2,1)} %get-tuple-element.270.kv_ref, ...), custom_call_target="tpu_custom_call" | custom-call | flops 10737418240 | bytes 14811152 | tf_op jit(solution)/shard_map/attend_back2/pallas_call | solution.py:346
  385.5 5.0 add_convert_fusion
  395.6 7.1 %pull2.1 = bf16[512,1024]{1,0:T(8,128)(2,1)} custom-call(s32[8]{0:T(128)} %fusion.55.order_ref, bf16[512,2048]{1,0:T(8,128)(2,1)} %get-tuple-element.361.refs_0_, bf16[256,3200]{1,0:T(8,128)(2,1)} %copy-done.5, bf16[256,3200]{1,0:T(8,128)(2,1)} %collective-permute-done.6.refs_1_.refs_5_.refs_2_.refs_3_, bf16[256,3200]{1,0:T(8,128)(2,1)} %copy-done.9, ...), custom_call_target="tpu_custom_call" | custom-call | flops 524288 | bytes 9699328 | tf_op jit(solution)/shard_map/pull2/pallas_call | solution.py:346
  407.1 3.9 collective-permute-start.37
  416.2 3.3 fusion.9
  419.5 16.8 %attend_back1.1 = (f32[1024,512]{1,0:T(8,128)}, bf16[512,2048]{1,0:T(8,128)(2,1)}) custom-call(s32[8]{0:T(128)} %fusion.55.order_ref, s32[4]{0:T(128)} %subtract_clamp_fusion.valid_ref, bf16[512,1024]{1,0:T(8,128)(2,1)} %get-tuple-element.247.q_ref, bf16[512,2048]{1,0:T(8,128)(2,1)} %get-tuple-element.260.kv_ref, ...), custom_call_target="tpu_custom_call" | custom-call | flops 10737418240 | bytes 14811152 | tf_op jit(solution)/shard_map/attend_back1/pallas_call | solution.py:346
  442.3 7.0 %pull1.1 = bf16[512,1024]{1,0:T(8,128)(2,1)} custom-call(s32[8]{0:T(128)} %fusion.55.order_ref, bf16[512,2048]{1,0:T(8,128)(2,1)} %get-tuple-element.379.refs_0_, bf16[256,3200]{1,0:T(8,128)(2,1)} %copy-done.5, bf16[256,3200]{1,0:T(8,128)(2,1)} %collective-permute-done.6.refs_1_.refs_5_.refs_2_.refs_3_, bf16[256,3200]{1,0:T(8,128)(2,1)} %copy-done.9, ...), custom_call_target="tpu_custom_call" | custom-call | flops 524288 | bytes 9699328 | tf_op jit(solution)/shard_map/pull1/pallas_call | solution.py:346
  449.3 3.0 add_convert_fusion.12
  459.0 18.3 %attend_back0.1 = (bf16[512,1024]{1,0:T(8,128)(2,1)}, bf16[512,2048]{1,0:T(8,128)(2,1)}) custom-call(s32[8]{0:T(128)} %fusion.55.order_ref, s32[4]{0:T(128)} %subtract_clamp_fusion.valid_ref, bf16[512,1024]{1,0:T(8,128)(2,1)} %get-tuple-element.247.q_ref, bf16[512,2048]{1,0:T(8,128)(2,1)} %get-tuple-element.252.kv_ref, ...), custom_call_target="tpu_custom_call" | custom-call | flops 10737418240 | bytes 13762576 | tf_op jit(solution)/shard_map/attend_back0/pallas_call | solution.py:346
  506.0 10.0 %pull0.1.refs_0_ = f32[512,1024]{1,0:T(8,128)} custom-call(s32[8]{0:T(128)} %fusion.55.order_ref, bf16[512,1024]{1,0:T(8,128)(2,1)} %get-tuple-element.411.refs_0_, bf16[512,2048]{1,0:T(8,128)(2,1)} %get-tuple-element.395.refs_1_, bf16[256,3200]{1,0:T(8,128)(2,1)} %copy-done.5, bf16[256,3200]{1,0:T(8,128)(2,1)} %collective-permute-done.6.refs_1_.refs_5_.refs_2_.refs_3_, ...), custom_call_target="tpu_custom_call" | custom-call | flops 51539607552 | bytes 11796480 | tf_op jit(solution)/shard_map/pull0/pallas_call | solution.py:346
  531.3 6.2 %end_back.1 = (bf16[512,1024]{1,0:T(8,128)(2,1)}, f32[8,1024]{1,0:T(8,128)}) custom-call(s32[8]{0:T(128)} %fusion.55.order_ref, bf16[512,1024]{1,0:T(8,128)(2,1)} %bitcast.8.source_ref.x_ref, f32[512,1024]{1,0:T(8,128)} %get-tuple-element.334.y_ref, f32[1,1024]{1,0:T(1,128)} %get-tuple-element.447.gain_ref, f32[512,1024]{1,0:T(8,128)} %pull0.1.refs_0_, ...), custom_call_target="tpu_custom_call" | custom-call | bytes 8425472 | tf_op jit(solution)/shard_map/end_back/pallas_call | solution.py:346
  537.5 13.1 %collective-permute-done.49 = bf16[32,8192]{1,0:T(8,128)(2,1)S(1)} collective-permute-done((bf16[32,8192]{1,0:T(8,128)(2,1)}, bf16[32,8192]{1,0:T(8,128)(2,1)S(1)}, u32[]{:S(2)}, u32[]{:S(2)}) %collective-permute-start.49) | collective-permute-done | bytes 524320 | tf_op jit(solution)/shard_map/ppermute | solution.py:283
  554.6 3.4 all-to-all-start
  558.1 7.0 %all-to-all-done = f32[32,1,128]{2,1,0:T(1,128)S(1)} async-done(((f32[32,1,128]{2,1,0:T(1,128)}), f32[32,1,128]{2,1,0:T(1,128)S(1)}, u32[]{:S(2)}, u32[]{:S(2)}) %all-to-all-start) | async-done | bytes 16416 | tf_op jit(solution)/shard_map/all_to_all | solution.py:296
  568.7 2.7 slice_reduce_fusion
  573.6 5.1 collective-permute-done.52
  (305 shorter events, 151.8 us)
Async XLA Ops:
  5.3 17.4 %collective-permute-start.2 = (bf16[32,3200]{1,0:T(8,128)(2,1)}, bf16[32,3200]{1,0:T(8,128)(2,1)S(1)}, u32[]{:S(2)}, u32[]{:S(2)}) collective-permute-start(bf16[32,3200]{1,0:T(8,128)(2,1)} %pad_maximum_fusion.8), channel_id=1, source_target_pairs={{0,3},{1,2},{2,1},{3,0},{4,7},{5,6},{6,5},{7,4},{8,11},{9,10},{10,... | collective-permute-start | bytes 614408 | tf_op jit(solution)/shard_map/ppermute | solution.py:195
  10.3 17.6 %collective-permute-start.1 = (bf16[32,3200]{1,0:T(8,128)(2,1)}, bf16[32,3200]{1,0:T(8,128)(2,1)S(1)}, u32[]{:S(2)}, u32[]{:S(2)}) collective-permute-start(bf16[32,3200]{1,0:T(8,128)(2,1)} %pad_maximum_fusion.8), channel_id=1, source_target_pairs={{0,2},{1,3},{2,0},{3,1},{4,6},{5,7},{6,4},{7,5},{8,10},{9,11},{10,... | collective-permute-start | bytes 614408 | tf_op jit(solution)/shard_map/ppermute | solution.py:195
  10.3 17.6 %collective-permute-start = (bf16[32,3200]{1,0:T(8,128)(2,1)}, bf16[32,3200]{1,0:T(8,128)(2,1)S(1)}, u32[]{:S(2)}, u32[]{:S(2)}) collective-permute-start(bf16[32,3200]{1,0:T(8,128)(2,1)} %pad_maximum_fusion.8), channel_id=1, source_target_pairs={{0,1},{1,0},{2,3},{3,2},{4,5},{5,4},{6,7},{7,6},{8,9},{9,8},{10,11... | collective-permute-start | bytes 614408 | tf_op jit(solution)/shard_map/ppermute | solution.py:195
  28.2 17.3 %collective-permute-start.3 = (bf16[128,3200]{1,0:T(8,128)(2,1)S(1)}, bf16[128,3200]{1,0:T(8,128)(2,1)S(1)}, u32[]{:S(2)}, u32[]{:S(2)}) collective-permute-start(bf16[128,3200]{1,0:T(8,128)(2,1)S(1)} %maximum_select_fusion.2), channel_id=1, source_target_pairs={{0,16},{1,17},{2,18},{3,19},{4,12},{5,13},{6,14},{7,15},{8,24},{9,... | collective-permute-start | bytes 2457608 | tf_op jit(solution)/shard_map/ppermute | solution.py:208
  31.3 14.2 %collective-permute-start.4 = (bf16[32,9216]{1,0:T(8,128)(2,1)S(1)}, bf16[32,9216]{1,0:T(8,128)(2,1)}, u32[]{:S(2)}, u32[]{:S(2)}) collective-permute-start(bf16[32,9216]{1,0:T(8,128)(2,1)S(1)} %pad_maximum_fusion.6), channel_id=1, source_target_pairs={{0,1},{1,0},{2,3},{3,2},{4,5},{5,4},{6,7},{7,6},{8,9},{9,8},{10,11... | collective-permute-start | bytes 1769480 | tf_op jit(solution)/shard_map/ppermute | solution.py:176
  45.6 18.9 %collective-permute-start.7 = (bf16[256,3200]{1,0:T(8,128)(2,1)S(1)}, bf16[256,3200]{1,0:T(8,128)(2,1)S(1)}, u32[]{:S(2)}, u32[]{:S(2)}) collective-permute-start(bf16[256,3200]{1,0:T(8,128)(2,1)S(1)} %pad_maximum_fusion.3.refs_0_.refs_4_.refs_1_.refs_2_), channel_id=1, source_target_pairs={{0,4},{1,5},{2,6},{3,7},{4,0},{5,1},{6,2},{7,3},{8,12},{9,13},{10,... | collective-permute-start | bytes 4915208 | tf_op jit(solution)/shard_map/ppermute | solution.py:210
  45.7 21.3 %collective-permute-start.6 = (bf16[256,3200]{1,0:T(8,128)(2,1)S(1)}, bf16[256,3200]{1,0:T(8,128)(2,1)}, u32[]{:S(2)}, u32[]{:S(2)}) collective-permute-start(bf16[256,3200]{1,0:T(8,128)(2,1)S(1)} %pad_maximum_fusion.3.refs_0_.refs_4_.refs_1_.refs_2_), channel_id=1, source_target_pairs={{0,8},{1,9},{2,10},{3,11},{4,20},{5,21},{6,22},{7,23},{8,0},{9,1},... | collective-permute-start | bytes 4915208 | tf_op jit(solution)/shard_map/ppermute | solution.py:210
  46.3 18.2 %collective-permute-start.8 = (bf16[32,9216]{1,0:T(8,128)(2,1)}, bf16[32,9216]{1,0:T(8,128)(2,1)}, u32[]{:S(2)}, u32[]{:S(2)}) collective-permute-start(bf16[32,9216]{1,0:T(8,128)(2,1)} %collective-permute-done.5), channel_id=1, source_target_pairs={{1,0},{2,3},{5,4},{6,7},{9,8},{10,11},{13,12},{14,15},{17,16},{18,... | collective-permute-start | bytes 1769480 | tf_op jit(solution)/shard_map/ppermute | solution.py:180
  47.6 16.9 %collective-permute-start.9 = (bf16[32,9216]{1,0:T(8,128)(2,1)}, bf16[32,9216]{1,0:T(8,128)(2,1)}, u32[]{:S(2)}, u32[]{:S(2)}) collective-permute-start(bf16[32,9216]{1,0:T(8,128)(2,1)} %collective-permute-done.4), channel_id=1, source_target_pairs={{1,2},{2,1},{5,6},{6,5},{9,10},{10,9},{13,14},{14,13},{17,18},{18,... | collective-permute-start | bytes 1769480 | tf_op jit(solution)/shard_map/ppermute | solution.py:180
  69.3 21.7 %collective-permute-start.11 = (bf16[32,9216]{1,0:T(8,128)(2,1)}, bf16[32,9216]{1,0:T(8,128)(2,1)}, u32[]{:S(2)}, u32[]{:S(2)}) collective-permute-start(bf16[32,9216]{1,0:T(8,128)(2,1)} %collective-permute-done.9), channel_id=1, source_target_pairs={{1,0},{2,3},{5,4},{6,7},{9,8},{10,11},{13,12},{14,15},{17,16},{18,... | collective-permute-start | bytes 1769480 | tf_op jit(solution)/shard_map/ppermute | solution.py:183
  70.6 36.7 %collective-permute-start.13 = (bf16[512,1024]{1,0:T(8,128)(2,1)}, bf16[512,1024]{1,0:T(8,128)(2,1)}, u32[]{:S(2)}, u32[]{:S(2)}) collective-permute-start(bf16[512,1024]{1,0:T(8,128)(2,1)} %bitcast.8.source_ref.x_ref), channel_id=1, source_target_pairs={{1,2},{2,1},{5,6},{6,5},{9,10},{10,9},{13,14},{14,13},{17,18},{18,... | collective-permute-start | bytes 3145736 | tf_op jit(solution)/shard_map/ppermute | solution.py:225
  72.3 37.5 %collective-permute-start.12 = (bf16[512,1024]{1,0:T(8,128)(2,1)}, bf16[512,1024]{1,0:T(8,128)(2,1)}, u32[]{:S(2)}, u32[]{:S(2)}) collective-permute-start(bf16[512,1024]{1,0:T(8,128)(2,1)} %bitcast.8.source_ref.x_ref), channel_id=1, source_target_pairs={{0,1},{1,0},{2,3},{3,2},{4,5},{5,4},{6,7},{7,6},{8,9},{9,8},{10,11... | collective-permute-start | bytes 3145736 | tf_op jit(solution)/shard_map/ppermute | solution.py:225
  93.5 29.0 %collective-permute-start.14 = (bf16[128,9216]{1,0:T(8,128)(2,1)S(1)}, bf16[128,9216]{1,0:T(8,128)(2,1)}, u32[]{:S(2)}, u32[]{:S(2)}) collective-permute-start(bf16[128,9216]{1,0:T(8,128)(2,1)S(1)} %maximum_select_fusion), channel_id=1, source_target_pairs={{0,16},{1,17},{2,18},{3,19},{4,12},{5,13},{6,14},{7,15},{8,24},{9,... | collective-permute-start | bytes 7077896 | tf_op jit(solution)/shard_map/ppermute | solution.py:208
  109.8 30.2 %collective-permute-start.16 = (bf16[512,1024]{1,0:T(8,128)(2,1)}, bf16[512,1024]{1,0:T(8,128)(2,1)S(1)}, u32[]{:S(2)}, u32[]{:S(2)}) collective-permute-start(bf16[512,1024]{1,0:T(8,128)(2,1)} %collective-permute-done.12.source_ref), channel_id=1, source_target_pairs={{1,2},{2,1},{5,6},{6,5},{9,10},{10,9},{13,14},{14,13},{17,18},{18,... | collective-permute-start | bytes 3145736 | tf_op jit(solution)/shard_map/ppermute | solution.py:230
  110.5 29.4 %collective-permute-start.15 = (bf16[512,1024]{1,0:T(8,128)(2,1)}, bf16[512,1024]{1,0:T(8,128)(2,1)}, u32[]{:S(2)}, u32[]{:S(2)}) collective-permute-start(bf16[512,1024]{1,0:T(8,128)(2,1)} %collective-permute-done.13), channel_id=1, source_target_pairs={{1,0},{2,3},{5,4},{6,7},{9,8},{10,11},{13,12},{14,15},{17,16},{18,... | collective-permute-start | bytes 3145736 | tf_op jit(solution)/shard_map/ppermute | solution.py:230
  126.7 59.7 %collective-permute-start.19 = (bf16[256,9216]{1,0:T(8,128)(2,1)}, bf16[256,9216]{1,0:T(8,128)(2,1)}, u32[]{:S(2)}, u32[]{:S(2)}) collective-permute-start(bf16[256,9216]{1,0:T(8,128)(2,1)} %pad_maximum_fusion.refs_0_), channel_id=1, source_target_pairs={{0,4},{1,5},{2,6},{3,7},{4,0},{5,1},{6,2},{7,3},{8,12},{9,13},{10,... | collective-permute-start | bytes 14155784 | tf_op jit(solution)/shard_map/ppermute | solution.py:210
  126.7 59.7 %collective-permute-start.18 = (bf16[256,9216]{1,0:T(8,128)(2,1)}, bf16[256,9216]{1,0:T(8,128)(2,1)}, u32[]{:S(2)}, u32[]{:S(2)}) collective-permute-start(bf16[256,9216]{1,0:T(8,128)(2,1)} %pad_maximum_fusion.refs_0_), channel_id=1, source_target_pairs={{0,8},{1,9},{2,10},{3,11},{4,20},{5,21},{6,22},{7,23},{8,0},{9,1},... | collective-permute-start | bytes 14155784 | tf_op jit(solution)/shard_map/ppermute | solution.py:210
  142.9 27.8 %collective-permute-start.17 = (bf16[512,1024]{1,0:T(8,128)(2,1)S(1)}, bf16[512,1024]{1,0:T(8,128)(2,1)S(1)}, u32[]{:S(2)}, u32[]{:S(2)}) collective-permute-start(bf16[512,1024]{1,0:T(8,128)(2,1)S(1)} %collective-permute-done.16), channel_id=1, source_target_pairs={{1,0},{2,3},{5,4},{6,7},{9,8},{10,11},{13,12},{14,15},{17,16},{18,... | collective-permute-start | bytes 3145736 | tf_op jit(solution)/shard_map/ppermute | solution.py:234
  170.7 29.2 %collective-permute-start.23 = (bf16[128,1024]{1,0:T(8,128)(2,1)S(1)}, bf16[128,1024]{1,0:T(8,128)(2,1)S(1)}, u32[]{:S(2)}, u32[]{:S(2)}) collective-permute-start(bf16[128,1024]{1,0:T(8,128)(2,1)S(1)} %copy-done.39), channel_id=1, source_target_pairs={{0,3},{1,2},{2,1},{3,0},{4,7},{5,6},{6,5},{7,4},{8,11},{9,10},{10,... | collective-permute-start | bytes 786440 | tf_op jit(solution)/shard_map/ppermute | solution.py:195
  173.0 26.9 %collective-permute-start.22 = (bf16[128,1024]{1,0:T(8,128)(2,1)S(1)}, bf16[128,1024]{1,0:T(8,128)(2,1)S(1)}, u32[]{:S(2)}, u32[]{:S(2)}) collective-permute-start(bf16[128,1024]{1,0:T(8,128)(2,1)S(1)} %copy-done.39), channel_id=1, source_target_pairs={{0,2},{1,3},{2,0},{3,1},{4,6},{5,7},{6,4},{7,5},{8,10},{9,11},{10,... | collective-permute-start | bytes 786440 | tf_op jit(solution)/shard_map/ppermute | solution.py:195
  173.0 26.9 %collective-permute-start.21 = (bf16[128,1024]{1,0:T(8,128)(2,1)S(1)}, bf16[128,1024]{1,0:T(8,128)(2,1)S(1)}, u32[]{:S(2)}, u32[]{:S(2)}) collective-permute-start(bf16[128,1024]{1,0:T(8,128)(2,1)S(1)} %copy-done.39), channel_id=1, source_target_pairs={{0,1},{1,0},{2,3},{3,2},{4,5},{5,4},{6,7},{7,6},{8,9},{9,8},{10,11... | collective-permute-start | bytes 786440 | tf_op jit(solution)/shard_map/ppermute | solution.py:195
  186.4 13.5 %collective-permute-start.20 = (bf16[256,9216]{1,0:T(8,128)(2,1)}, bf16[256,9216]{1,0:T(8,128)(2,1)}, u32[]{:S(2)}, u32[]{:S(2)}) collective-permute-start(bf16[256,9216]{1,0:T(8,128)(2,1)} %collective-permute-done.18.refs_1_), channel_id=1, source_target_pairs={{0,4},{1,5},{2,6},{3,7},{4,0},{5,1},{6,2},{7,3},{8,12},{9,13},{10,... | collective-permute-start | bytes 14155784 | tf_op jit(solution)/shard_map/ppermute | solution.py:211
  200.7 14.9 %collective-permute-start.24 = (bf16[512,1024]{1,0:T(8,128)(2,1)S(1)}, bf16[512,1024]{1,0:T(8,128)(2,1)S(1)}, u32[]{:S(2)}, u32[]{:S(2)}) collective-permute-start(bf16[512,1024]{1,0:T(8,128)(2,1)S(1)} %maximum_select_fusion.1), channel_id=1, source_target_pairs={{0,16},{1,17},{2,18},{3,19},{4,12},{5,13},{6,14},{7,15},{8,24},{9,... | collective-permute-start | bytes 3145736 | tf_op jit(solution)/shard_map/ppermute | solution.py:208
  218.0 26.0 %collective-permute-start.26 = (bf16[1024,1024]{1,0:T(8,128)(2,1)S(1)}, bf16[1024,1024]{1,0:T(8,128)(2,1)}, u32[]{:S(2)}, u32[]{:S(2)}) collective-permute-start(bf16[1024,1024]{1,0:T(8,128)(2,1)S(1)} %pad_maximum_fusion.2.refs_4_), channel_id=1, source_target_pairs={{0,4},{1,5},{2,6},{3,7},{4,0},{5,1},{6,2},{7,3},{8,12},{9,13},{10,... | collective-permute-start | bytes 6291464 | tf_op jit(solution)/shard_map/ppermute | solution.py:210
  218.1 26.2 %collective-permute-start.25 = (bf16[1024,1024]{1,0:T(8,128)(2,1)S(1)}, bf16[1024,1024]{1,0:T(8,128)(2,1)}, u32[]{:S(2)}, u32[]{:S(2)}) collective-permute-start(bf16[1024,1024]{1,0:T(8,128)(2,1)S(1)} %pad_maximum_fusion.2.refs_4_), channel_id=1, source_target_pairs={{0,8},{1,9},{2,10},{3,11},{4,20},{5,21},{6,22},{7,23},{8,0},{9,1},... | collective-permute-start | bytes 6291464 | tf_op jit(solution)/shard_map/ppermute | solution.py:210
  248.6 45.3 %collective-permute-start.28 = (bf16[2048,1024]{1,0:T(8,128)(2,1)}, bf16[2048,1024]{1,0:T(8,128)(2,1)}, u32[]{:S(2)}, u32[]{:S(2)}) collective-permute-start(bf16[2048,1024]{1,0:T(8,128)(2,1)} %convolution_convert_fusion.1), channel_id=1, source_target_pairs={{0,4},{1,5},{2,6},{3,7},{4,0},{5,1},{6,2},{7,3},{8,12},{9,13},{10,... | collective-permute-start | bytes 12582920 | tf_op jit(solution)/shard_map/ppermute | solution.py:263
  294.0 20.0 %collective-permute-start.29 = (bf16[512,8192]{1,0:T(8,128)(2,1)}, bf16[512,8192]{1,0:T(8,128)(2,1)}, u32[]{:S(2)}, u32[]{:S(2)}) collective-permute-start(bf16[512,8192]{1,0:T(8,128)(2,1)} %convolution_convert_fusion), channel_id=1, source_target_pairs={{0,4},{1,5},{2,6},{3,7},{4,0},{5,1},{6,2},{7,3},{8,12},{9,13},{10,... | collective-permute-start | bytes 25165832 | tf_op jit(solution)/shard_map/ppermute | solution.py:263
  300.4 48.2 %collective-permute-start.30 = (bf16[1024,1024]{1,0:T(8,128)(2,1)}, bf16[1024,1024]{1,0:T(8,128)(2,1)S(1)}, u32[]{:S(2)}, u32[]{:S(2)}) collective-permute-start(bf16[1024,1024]{1,0:T(8,128)(2,1)} %add_convert_fusion.7), channel_id=1, source_target_pairs={{0,8},{1,9},{2,10},{3,11},{4,20},{5,21},{6,22},{7,23},{8,0},{9,1},... | collective-permute-start | bytes 6291464 | tf_op jit(solution)/shard_map/ppermute | solution.py:267
  323.1 62.4 %collective-permute-start.32 = (bf16[256,8192]{1,0:T(8,128)(2,1)}, bf16[256,8192]{1,0:T(8,128)(2,1)}, u32[]{:S(2)}, u32[]{:S(2)}) collective-permute-start(bf16[256,8192]{1,0:T(8,128)(2,1)} %add_convert_fusion.2), channel_id=1, source_target_pairs={{0,8},{1,9},{2,10},{3,11},{4,20},{5,21},{6,22},{7,23},{8,0},{9,1},... | collective-permute-start | bytes 12582920 | tf_op jit(solution)/shard_map/ppermute | solution.py:267
  325.3 23.3 %collective-permute-start.31 = (bf16[512,1024]{1,0:T(8,128)(2,1)}, bf16[512,1024]{1,0:T(8,128)(2,1)}, u32[]{:S(2)}, u32[]{:S(2)}) collective-permute-start(bf16[512,1024]{1,0:T(8,128)(2,1)} %convolution_convert_fusion.3), channel_id=1, source_target_pairs={{0,4},{1,5},{2,6},{3,7},{4,0},{5,1},{6,2},{7,3},{8,12},{9,13},{10,... | collective-permute-start | bytes 3145736 | tf_op jit(solution)/shard_map/ppermute | solution.py:263
  351.7 59.3 %collective-permute-start.35 = (bf16[256,1024]{1,0:T(8,128)(2,1)}, bf16[256,1024]{1,0:T(8,128)(2,1)}, u32[]{:S(2)}, u32[]{:S(2)}) collective-permute-start(bf16[256,1024]{1,0:T(8,128)(2,1)} %add_convert_fusion.18), channel_id=1, source_target_pairs={{0,8},{1,9},{2,10},{3,11},{4,20},{5,21},{6,22},{7,23},{8,0},{9,1},... | collective-permute-start | bytes 1572872 | tf_op jit(solution)/shard_map/ppermute | solution.py:267
  356.8 54.2 %collective-permute-start.34 = (bf16[512,1024]{1,0:T(8,128)(2,1)}, bf16[512,1024]{1,0:T(8,128)(2,1)}, u32[]{:S(2)}, u32[]{:S(2)}) collective-permute-start(bf16[512,1024]{1,0:T(8,128)(2,1)} %slice.241), channel_id=1, source_target_pairs={{0,16},{1,17},{2,18},{3,19},{4,12},{5,13},{6,14},{7,15},{8,24},{9,... | collective-permute-start | bytes 3145736 | tf_op jit(solution)/shard_map/ppermute | solution.py:274
  366.8 27.8 %collective-permute-start.33 = (bf16[512,1024]{1,0:T(8,128)(2,1)}, bf16[512,1024]{1,0:T(8,128)(2,1)S(1)}, u32[]{:S(2)}, u32[]{:S(2)}) collective-permute-start(bf16[512,1024]{1,0:T(8,128)(2,1)} %pull3.1), channel_id=1, source_target_pairs={{0,1},{3,2},{4,5},{7,6},{8,9},{11,10},{12,13},{15,14},{16,17},{19,... | collective-permute-start | bytes 3145736 | tf_op jit(solution)/shard_map/ppermute | solution.py:239
  393.2 43.2 %collective-permute-start.36 = (bf16[128,8192]{1,0:T(8,128)(2,1)}, bf16[128,8192]{1,0:T(8,128)(2,1)}, u32[]{:S(2)}, u32[]{:S(2)}) collective-permute-start(bf16[128,8192]{1,0:T(8,128)(2,1)} %slice.242), channel_id=1, source_target_pairs={{0,16},{1,17},{2,18},{3,19},{4,12},{5,13},{6,14},{7,15},{8,24},{9,... | collective-permute-start | bytes 6291464 | tf_op jit(solution)/shard_map/ppermute | solution.py:274
  405.5 36.8 %collective-permute-start.38 = (bf16[512,1024]{1,0:T(8,128)(2,1)}, bf16[512,1024]{1,0:T(8,128)(2,1)}, u32[]{:S(2)}, u32[]{:S(2)}) collective-permute-start(bf16[512,1024]{1,0:T(8,128)(2,1)} %add_convert_fusion.14), channel_id=1, source_target_pairs={{1,2},{2,1},{5,6},{6,5},{9,10},{10,9},{13,14},{14,13},{17,18},{18,... | collective-permute-start | bytes 3145736 | tf_op jit(solution)/shard_map/ppermute | solution.py:242
  407.1 35.2 %collective-permute-start.37 = (bf16[512,1024]{1,0:T(8,128)(2,1)}, bf16[512,1024]{1,0:T(8,128)(2,1)}, u32[]{:S(2)}, u32[]{:S(2)}) collective-permute-start(bf16[512,1024]{1,0:T(8,128)(2,1)} %pull2.1), channel_id=1, source_target_pairs={{0,1},{3,2},{4,5},{7,6},{8,9},{11,10},{12,13},{15,14},{16,17},{19,... | collective-permute-start | bytes 3145736 | tf_op jit(solution)/shard_map/ppermute | solution.py:242
  413.0 42.0 %collective-permute-start.40 = (bf16[128,1024]{1,0:T(8,128)(2,1)}, bf16[128,1024]{1,0:T(8,128)(2,1)S(1)}, u32[]{:S(2)}, u32[]{:S(2)}) collective-permute-start(bf16[128,1024]{1,0:T(8,128)(2,1)} %slice.244), channel_id=1, source_target_pairs={{0,16},{1,17},{2,18},{3,19},{4,12},{5,13},{6,14},{7,15},{8,24},{9,... | collective-permute-start | bytes 786440 | tf_op jit(solution)/shard_map/ppermute | solution.py:274
  416.1 38.9 %collective-permute-start.39 = (bf16[256,1024]{1,0:T(8,128)(2,1)S(1)}, bf16[256,1024]{1,0:T(8,128)(2,1)S(1)}, u32[]{:S(2)}, u32[]{:S(2)}) collective-permute-start(bf16[256,1024]{1,0:T(8,128)(2,1)S(1)} %bitcast.142), channel_id=1, source_target_pairs={{0,1},{1,0},{2,3},{3,2},{4,5},{5,4},{6,7},{7,6},{8,9},{9,8},{10,11... | collective-permute-start | bytes 1572872 | tf_op jit(solution)/shard_map/ppermute | solution.py:283
  440.3 43.7 %collective-permute-start.43 = (bf16[64,8192]{1,0:T(8,128)(2,1)}, bf16[64,8192]{1,0:T(8,128)(2,1)}, u32[]{:S(2)}, u32[]{:S(2)}) collective-permute-start(bf16[64,8192]{1,0:T(8,128)(2,1)} %bitcast.19), channel_id=1, source_target_pairs={{0,1},{1,0},{2,3},{3,2},{4,5},{5,4},{6,7},{7,6},{8,9},{9,8},{10,11... | collective-permute-start | bytes 3145736 | tf_op jit(solution)/shard_map/ppermute | solution.py:283
  455.8 28.2 %collective-permute-start.42 = (bf16[64,1024]{1,0:T(8,128)(2,1)}, bf16[64,1024]{1,0:T(8,128)(2,1)}, u32[]{:S(2)}, u32[]{:S(2)}) collective-permute-start(bf16[64,1024]{1,0:T(8,128)(2,1)} %bitcast.24), channel_id=1, source_target_pairs={{0,1},{1,0},{2,3},{3,2},{4,5},{5,4},{6,7},{7,6},{8,9},{9,8},{10,11... | collective-permute-start | bytes 393224 | tf_op jit(solution)/shard_map/ppermute | solution.py:283
  456.9 27.2 %collective-permute-start.41 = (bf16[128,1024]{1,0:T(8,128)(2,1)S(1)}, bf16[128,1024]{1,0:T(8,128)(2,1)}, u32[]{:S(2)}, u32[]{:S(2)}) collective-permute-start(bf16[128,1024]{1,0:T(8,128)(2,1)S(1)} %dynamic-slice_bitcast_fusion.1), channel_id=1, source_target_pairs={{0,2},{1,3},{2,0},{3,1},{4,6},{5,7},{6,4},{7,5},{8,10},{9,11},{10,... | collective-permute-start | bytes 786440 | tf_op jit(solution)/shard_map/ppermute | solution.py:283
  485.0 13.8 %collective-permute-start.44 = (bf16[512,3072]{1,0:T(8,128)(2,1)S(1)}, bf16[512,3072]{1,0:T(8,128)(2,1)S(1)}, u32[]{:S(2)}, u32[]{:S(2)}) collective-permute-start(bf16[512,3072]{1,0:T(8,128)(2,1)S(1)} %pad_maximum_fusion.1), channel_id=1, source_target_pairs={{0,4},{1,5},{2,6},{3,7},{4,0},{5,1},{6,2},{7,3},{8,12},{9,13},{10,... | collective-permute-start | bytes 9437192 | tf_op jit(solution)/shard_map/ppermute | solution.py:263
  485.1 30.9 %collective-permute-start.46 = (bf16[512,1024]{1,0:T(8,128)(2,1)}, bf16[512,1024]{1,0:T(8,128)(2,1)}, u32[]{:S(2)}, u32[]{:S(2)}) collective-permute-start(bf16[512,1024]{1,0:T(8,128)(2,1)} %add_convert_fusion.12), channel_id=1, source_target_pairs={{1,2},{2,1},{5,6},{6,5},{9,10},{10,9},{13,14},{14,13},{17,18},{18,... | collective-permute-start | bytes 3145736 | tf_op jit(solution)/shard_map/ppermute | solution.py:249
  486.9 29.1 %collective-permute-start.47 = (bf16[512,1024]{1,0:T(8,128)(2,1)}, bf16[512,1024]{1,0:T(8,128)(2,1)}, u32[]{:S(2)}, u32[]{:S(2)}) collective-permute-start(bf16[512,1024]{1,0:T(8,128)(2,1)} %add_convert_fusion.11), channel_id=1, source_target_pairs={{0,1},{1,0},{2,3},{3,2},{4,5},{5,4},{6,7},{7,6},{8,9},{9,8},{10,11... | collective-permute-start | bytes 3145736 | tf_op jit(solution)/shard_map/ppermute | solution.py:250
  497.5 18.5 %collective-permute-start.45 = (bf16[32,1024]{1,0:T(8,128)(2,1)S(1)}, bf16[32,1024]{1,0:T(8,128)(2,1)S(1)}, u32[]{:S(2)}, u32[]{:S(2)}) collective-permute-start(bf16[32,1024]{1,0:T(8,128)(2,1)S(1)} %dynamic-slice_bitcast_fusion.3), channel_id=1, source_target_pairs={{0,2},{1,3},{2,0},{3,1},{4,6},{5,7},{6,4},{7,5},{8,10},{9,11},{10,... | collective-permute-start | bytes 196616 | tf_op jit(solution)/shard_map/ppermute | solution.py:283
  501.7 20.7 %collective-permute-start.48 = (bf16[256,3072]{1,0:T(8,128)(2,1)}, bf16[256,3072]{1,0:T(8,128)(2,1)}, u32[]{:S(2)}, u32[]{:S(2)}) collective-permute-start(bf16[256,3072]{1,0:T(8,128)(2,1)} %pad_maximum_fusion.4), channel_id=1, source_target_pairs={{0,8},{1,9},{2,10},{3,11},{4,20},{5,21},{6,22},{7,23},{8,0},{9,1},... | collective-permute-start | bytes 4718600 | tf_op jit(solution)/shard_map/ppermute | solution.py:267
  524.5 26.8 %collective-permute-start.50 = (bf16[128,3072]{1,0:T(8,128)(2,1)S(1)}, bf16[128,3072]{1,0:T(8,128)(2,1)}, u32[]{:S(2)}, u32[]{:S(2)}) collective-permute-start(bf16[128,3072]{1,0:T(8,128)(2,1)S(1)} %slice.247), channel_id=1, source_target_pairs={{0,16},{1,17},{2,18},{3,19},{4,12},{5,13},{6,14},{7,15},{8,24},{9,... | collective-permute-start | bytes 2359304 | tf_op jit(solution)/shard_map/ppermute | solution.py:274
  525.5 25.1 %collective-permute-start.49 = (bf16[32,8192]{1,0:T(8,128)(2,1)}, bf16[32,8192]{1,0:T(8,128)(2,1)S(1)}, u32[]{:S(2)}, u32[]{:S(2)}) collective-permute-start(bf16[32,8192]{1,0:T(8,128)(2,1)} %dynamic-slice_bitcast_fusion), channel_id=1, source_target_pairs={{0,2},{1,3},{2,0},{3,1},{4,6},{5,7},{6,4},{7,5},{8,10},{9,11},{10,... | collective-permute-start | bytes 1572872 | tf_op jit(solution)/shard_map/ppermute | solution.py:283
  (60 other events, 459.3 us)
